TPU v7x, 32 devices: a whole 2x2x4 slice. The times are simulated.
32 devices in a mesh: seq: 16 (over z, y, x), mlp: 2 (over core).
Axes of the slice: x: 2, y: 2, z: 4, core: 2. Of those that a mesh axis runs over, the one named last changes fastest.
Arguments:
- block_input: bfloat16 [2, 4096, 1024], P('mlp', 'seq'), may hold values from -6 to 6
- out_cotangent: bfloat16 [2, 4096, 1024], P('mlp', 'seq'), may hold values from -6 to 6
- attend_gain: bfloat16 [1024], replicated, may hold values from 0.5 to 1.5
- attend_shift: bfloat16 [1024], replicated, may hold values from -1.25 to 1.25
- query_key_value_weight: bfloat16 [1024, 3072], replicated, may hold values from -0.1875 to 0.1875
- query_key_value_bias: bfloat16 [3072], replicated, may hold values from -1.25 to 1.25
- attention_out_weight: bfloat16 [1024, 1024], replicated, may hold values from -1.5 to 1.5
- attention_out_bias: bfloat16 [1024], replicated, may hold values from -3 to 3
- feed_gain: bfloat16 [1024], replicated, may hold values from 0.5 to 1.5
- feed_shift: bfloat16 [1024], replicated, may hold values from -1.25 to 1.25
- expand_weight: bfloat16 [1024, 4096], P(None, 'mlp'), may hold values from -0.1875 to 0.1875
- expand_bias: bfloat16 [4096], P('mlp'), may hold values from -3 to 3
- contract_weight: bfloat16 [4096, 1024], P('mlp'), may hold values from -0.1875 to 0.1875
- contract_bias: bfloat16 [1024], replicated, may hold values from -3 to 3
Outputs:
- block_output: bfloat16 [2, 4096, 1024], P('mlp', 'seq')
- grad_input: float32 [2, 4096, 1024], P('mlp', 'seq')
- grad_attend_gain: float32 [1024], P(('seq', 'mlp'))
- grad_attend_shift: float32 [1024], P(('seq', 'mlp'))
- grad_merged_weight: float32 [1024, 3072], P(('seq', 'mlp'))
- grad_merged_bias: float32 [3072], P(('seq', 'mlp'))
- grad_dense_weight: float32 [1024, 1024], P(('seq', 'mlp'))
- grad_dense_bias: float32 [1024], P(('seq', 'mlp'))
- grad_feed_gain: float32 [1024], P(('seq', 'mlp'))
- grad_feed_shift: float32 [1024], P(('seq', 'mlp'))
- grad_hidden_weight: float32 [1024, 4096], P('seq', 'mlp')
- grad_hidden_bias: float32 [4096], P(('seq', 'mlp'))
- grad_output_weight: float32 [4096, 1024], P('mlp', 'seq')
- grad_output_bias: float32 [1024], P(('seq', 'mlp'))
All inputs are finite; a program needn't handle non-finite values.
Results may differ from a plain program's by a relative error of at most 0.03.
Values may be sent and summed in bfloat16 or wider, within the bound.
No kernel may reach another device: no remote copies, remote signals or barrier semaphores. Data moves between devices by JAX's collectives and lax.ppermute only.
A program may use at most 256 MiB of HBM per device.

v0:
```python
from functools import partial

import jax
import jax.numpy as jnp
from jax import lax
from jax.experimental import pallas as pl
from jax.experimental.pallas import tpu as pltpu
from jax.sharding import PartitionSpec as P

HEADS = 16
HEAD = 64
ROT = 16
PAIR = 2 * HEAD
GROUPS = HEADS // 2
EPS = 1e-05
NEGATIVE = -1e30

F32 = jnp.float32
BF16 = jnp.bfloat16
NT = (((1,), (1,)), ((), ()))
NN = (((1,), (0,)), ((), ()))
VMEM_LIMIT = 60 * 1024 * 1024


def dot32(a, b, dims=NN):
    return lax.dot_general(a, b, dims, preferred_element_type=F32)


def shape_of(shape, dtype):
    return jax.ShapeDtypeStruct(shape, dtype)


def fixed(shape):
    return pl.BlockSpec(shape, lambda *i: (0,) * len(shape))


def vector_row(ref):
    return ref[...].astype(F32).reshape(1, -1)


def two_heads(pair_a, pair_b, low):
    even = jnp.where(low, pair_a, pltpu.roll(pair_b, HEAD, 1))
    odd = jnp.where(low, pltpu.roll(pair_a, HEAD, 1), pair_b)
    return (even, odd)


def rotary_lanes(first, rows, inverse):
    shape = (rows, PAIR)
    lane = lax.broadcasted_iota(jnp.int32, shape, 1) % HEAD
    position = (lax.broadcasted_iota(jnp.int32, shape, 0) + first).astype(F32)
    angle = position * inverse
    cosine, sine = jnp.cos(angle), jnp.sin(angle)
    zero = jnp.zeros_like(sine)
    return (
        jnp.where(lane < ROT, cosine, 1.0),
        jnp.where(lane < ROT // 2, -sine, zero),
        jnp.where((lane >= ROT // 2) & (lane < ROT), sine, zero),
    )


def rotate_lanes(x, cosine, to_first, to_second):
    ahead = pltpu.roll(x, PAIR - ROT // 2, 1)
    behind = pltpu.roll(x, ROT // 2, 1)
    return x * cosine + ahead * to_first + behind * to_second


def unit_rows(x):
    average = jnp.mean(x, -1, keepdims=True)
    centred = x - average
    spread = jnp.mean(centred * centred, -1, keepdims=True)
    root = lax.rsqrt(spread + EPS)
    return (centred * root, root)


def open_kernel(
    first_ref, x_ref, g_ref, inv_ref, ga_ref, sa_ref, gf_ref, sf_ref, b_ref,
    wq_ref, wk_ref, wv_ref, wo_ref,
    out_ref, n1_ref, n2_ref, table_ref, n1t_ref, n2t_ref, gt_ref, bias_ref, *, parts,
):
    rows, width = x_ref.shape
    step = pl.program_id(0)
    cols = wq_ref.shape[1]

    @pl.when(step == 0)
    def _():
        unit, root = unit_rows(x_ref[...].astype(F32))
        n1_ref[...] = (unit * vector_row(ga_ref) + vector_row(sa_ref)).astype(BF16)
        n2_ref[...] = (unit * vector_row(gf_ref) + vector_row(sf_ref)).astype(BF16)
        for t, table in enumerate(rotary_lanes(first_ref[0], rows, inv_ref[...])):
            table_ref[t] = table
        bias_ref[...] = vector_row(b_ref)

    for at, source, target in ((1, n1_ref, n1t_ref), (2, n2_ref, n2t_ref), (3, g_ref, gt_ref)):

        @pl.when(step == at)
        def _(source=source, target=target):
            target[...] = jnp.transpose(source[...])

    def bias(third):
        return bias_ref[:, pl.ds(pl.multiple_of(third * width + step * cols, cols), cols)]

    normed = n1_ref[...]
    query = dot32(normed, wq_ref[...]) + bias(0)
    key = dot32(normed, wk_ref[...]) + bias(1)
    value = dot32(normed, wv_ref[...]) + bias(2)
    grad = dot32(g_ref[...], wo_ref[...], NT)
    tables = (table_ref[0], table_ref[1], table_ref[2])
    low = lax.broadcasted_iota(jnp.int32, (rows, PAIR), 1) < HEAD
    query_rows = rows // parts
    for c in range(cols // PAIR):
        cut = slice(c * PAIR, (c + 1) * PAIR)
        kv = two_heads(rotate_lanes(key[:, cut], *tables), value[:, cut], low)
        qg = two_heads(rotate_lanes(query[:, cut], *tables), grad[:, cut], low)
        for h in range(2):
            kv_h, qg_h = kv[h].astype(BF16), qg[h].astype(BF16)
            for p in range(parts):
                out_ref[2 * c + h, p, :rows] = kv_h
                out_ref[2 * c + h, p, rows:] = qg_h[p * query_rows : (p + 1) * query_rows]


def open_layer(x, g, first, vectors, weight, bias, out_weight, parts):
    rows, width = x.shape
    steps = 4
    cols = width // steps
    per = HEADS // steps
    inverse = 10000.0 ** (-(jnp.arange(ROT // 2, dtype=F32) * 2.0 / ROT))
    inverse = jnp.tile(inverse, PAIR // (ROT // 2)).reshape(1, PAIR)
    chunk = rows + rows // parts

    def third(t):
        return pl.BlockSpec((width, cols), lambda i: (0, t * steps + i))

    out, *others = pl.pallas_call(
        partial(open_kernel, parts=parts),
        grid=(steps,),
        out_shape=(
            shape_of((HEADS, parts, chunk, PAIR), BF16),
            shape_of((rows, width), BF16),
            shape_of((rows, width), BF16),
            shape_of((3, rows, PAIR), F32),
            shape_of((width, rows), BF16),
            shape_of((width, rows), BF16),
            shape_of((width, rows), BF16),
        ),
        in_specs=[
            pl.BlockSpec(memory_space=pltpu.SMEM),
            fixed((rows, width)),
            fixed((rows, width)),
            fixed((1, PAIR)),
            *[fixed((width,))] * 4,
            fixed((3 * width,)),
            third(0), third(1), third(2),
            pl.BlockSpec((cols, width), lambda i: (i, 0)),
        ],
        out_specs=(
            pl.BlockSpec((per, parts, chunk, PAIR), lambda i: (i, 0, 0, 0)),
            fixed((rows, width)),
            fixed((rows, width)),
            fixed((3, rows, PAIR)),
            fixed((width, rows)),
            fixed((width, rows)),
            fixed((width, rows)),
        ),
        scratch_shapes=[pltpu.VMEM((1, 3 * width), F32)],
        cost_estimate=pl.CostEstimate(
            flops=8 * rows * width * width,
            bytes_accessed=8 * width * width + 18 * rows * width,
            transcendentals=0,
        ),
        compiler_params=pltpu.CompilerParams(vmem_limit_bytes=VMEM_LIMIT),
        name="open_layer",
    )(first, x, g, inverse, *vectors, bias, weight, weight, weight, out_weight)
    return (out.reshape(HEADS * parts, chunk, PAIR), *others)


def head_kernel(part_ref, x_ref, y_ref, s_ref, p_ref, dkv_ref, *, group, key_rows, query_rows):
    blocks = x_ref.shape[0] // group
    keys = group * key_rows
    rows = group * query_rows
    scale = float(HEAD) ** -0.5
    lane = lax.broadcasted_iota(jnp.int32, (rows, PAIR), 1)
    low = lane < HEAD
    row = lax.broadcasted_iota(jnp.int32, (rows, keys), 0)
    col = lax.broadcasted_iota(jnp.int32, (rows, keys), 1)
    row_pos = (row // query_rows) * key_rows + row % query_rows + part_ref[0] * query_rows
    allowed = col <= row_pos

    dkv_ref[...] = jnp.zeros_like(dkv_ref)

    def key_value(j):
        return x_ref[pl.ds(j * group, group), :key_rows, :].reshape(keys, PAIR)

    def lanes_max(mx, s):
        for c in range(keys // 128):
            mx = jnp.maximum(mx, s[:, c * 128 : (c + 1) * 128])
        return mx

    def one_block(i, unused):
        qdo = x_ref[pl.ds(i * group, group), key_rows:, :].reshape(rows, PAIR)
        qdo32 = qdo.astype(F32)
        zero = jnp.zeros_like(qdo32)
        query = jnp.where(low, qdo32 * scale, zero).astype(BF16)

        def first(j, mx):
            s = dot32(query, key_value(j), NT)
            s_ref[j] = s
            return lanes_max(mx, s)

        mx = lax.fori_loop(0, i, first, jnp.full((rows, 128), NEGATIVE, F32))
        s = jnp.where(allowed, dot32(query, key_value(i), NT), NEGATIVE)
        s_ref[i] = s
        top = jnp.max(lanes_max(mx, s), -1, keepdims=True)

        def second(j, state):
            total, acc = state
            p = jnp.exp(s_ref[j] - top)
            for c in range(keys // 128):
                total = total + p[:, c * 128 : (c + 1) * 128]
            low_p = p.astype(BF16)
            p_ref[j] = low_p
            return (total, acc + dot32(low_p, key_value(j)))

        total, acc = lax.fori_loop(
            0,
            i + 1,
            second,
            (jnp.zeros((rows, 128), F32), jnp.zeros((rows, PAIR), F32)),
        )
        inverse = 1.0 / jnp.sum(total, -1, keepdims=True)
        attended = acc * inverse
        grad = jnp.where(low, zero, qdo32 * inverse).astype(BF16)
        delta = jnp.sum(grad.astype(F32) * attended, -1, keepdims=True)
        query_t = jnp.transpose(query.astype(F32))[:HEAD].astype(BF16)
        grad_t = jnp.transpose(grad.astype(F32))[HEAD:].astype(BF16)

        def third(j, acc):
            kv = key_value(j)
            low_p = p_ref[j]
            dp = dot32(grad, kv, NT)
            ds = (low_p.astype(F32) * (dp - delta)).astype(BF16)
            dkv_ref[j, :HEAD] += dot32(query_t, ds)
            dkv_ref[j, HEAD:] += dot32(grad_t, low_p)
            return acc + dot32(ds, kv)

        acc = lax.fori_loop(0, i + 1, third, jnp.zeros((rows, PAIR), F32))
        done = jnp.where(low, acc * scale, attended).astype(BF16)
        y_ref[pl.ds(i * group, group), key_rows:, :] = done.reshape(group, query_rows, PAIR)
        return unused

    lax.fori_loop(0, blocks, one_block, 0)

    def finish(i, unused):
        grads = jnp.transpose(dkv_ref[i]).astype(BF16)
        y_ref[pl.ds(i * group, group), :key_rows, :] = grads.reshape(group, key_rows, PAIR)
        return unused

    lax.fori_loop(0, blocks, finish, 0)


def one_head(x, part, key_rows, query_rows):
    count = x.shape[0]
    group = 2 if count % 2 == 0 else 1
    blocks = count // group
    keys, rows = group * key_rows, group * query_rows
    pairs = count * key_rows * count * query_rows // 2
    return pl.pallas_call(
        partial(head_kernel, group=group, key_rows=key_rows, query_rows=query_rows),
        out_shape=jax.ShapeDtypeStruct(x.shape, BF16),
        in_specs=[
            pl.BlockSpec(memory_space=pltpu.SMEM),
            pl.BlockSpec(memory_space=pltpu.VMEM),
        ],
        out_specs=pl.BlockSpec(memory_space=pltpu.VMEM),
        scratch_shapes=[
            pltpu.VMEM((blocks, rows, keys), F32),
            pltpu.VMEM((blocks, rows, keys), BF16),
            pltpu.VMEM((blocks, PAIR, keys), F32),
        ],
        cost_estimate=pl.CostEstimate(
            flops=pairs * 2 * 256 * 6, bytes_accessed=4 * x.size, transcendentals=pairs
        ),
        compiler_params=pltpu.CompilerParams(vmem_limit_bytes=56 * 1024 * 1024),
        name="one_head",
    )(part, x)


def feed_kernel(*refs, count, keep):
    rows_refs, cot_refs = refs[:count], refs[count : 2 * count]
    w1_ref, b1_ref, w2_ref = refs[2 * count : 2 * count + 3]
    hid_ref, gpre_ref, gb_ref = refs[2 * count + 3 : 2 * count + 6]
    outs = refs[2 * count + 6 : -2]
    out_acc, grad_acc = refs[-2:]
    step = pl.program_id(0)

    @pl.when(step == 0)
    def _():
        out_acc[...] = jnp.zeros_like(out_acc)
        grad_acc[...] = jnp.zeros_like(grad_acc)

    bias = b1_ref[...]
    sums = jnp.zeros_like(bias)
    rows = rows_refs[0].shape[0]
    for r in range(count):
        here = slice(r * rows, (r + 1) * rows)
        pre = dot32(rows_refs[r][...], w1_ref[...]) + bias
        grad = dot32(cot_refs[r][...], w2_ref[...], NT)
        cdf = 0.5 + 0.5 * lax.erf(pre * (0.5**0.5))
        density = jnp.exp(-0.5 * pre * pre) * 0.3989422804014327
        hidden = (pre * cdf).astype(BF16)
        grad_pre = (grad * (cdf + pre * density)).astype(BF16)
        hid_ref[here] = hidden
        gpre_ref[here] = grad_pre
        sums = sums + jnp.sum(grad_pre.astype(F32), 0, keepdims=True)
        out_acc[here] += dot32(hidden, w2_ref[...])
        grad_acc[here] += dot32(grad_pre, w1_ref[...], NT)
    gb_ref[...] = sums

    @pl.when(step == pl.num_programs(0) - 1)
    def _():
        if keep:
            own_out, own_grad, other_out, other_grad = outs
            own_out[...] = out_acc[:rows]
            own_grad[...] = grad_acc[:rows]
            other_out[...] = out_acc[rows:].astype(BF16)
            other_grad[...] = grad_acc[rows:].astype(BF16)
        else:
            outs[0][...] = out_acc[...].astype(BF16)
            outs[1][...] = grad_acc[...].astype(BF16)


def feed(rows_list, cot_list, w1, b1, w2):
    width, hidden = w1.shape
    count = len(rows_list)
    rows = rows_list[0].shape[0]
    total = rows * count
    block = 256
    keep = count > 1
    sides = (
        [(rows, F32), (rows, F32), (total - rows, BF16), (total - rows, BF16)]
        if keep
        else [(total, BF16), (total, BF16)]
    )
    once = pl.Buffered(1)
    whole = pl.BlockSpec((rows, width), lambda i: (0, 0), pipeline_mode=once)
    return pl.pallas_call(
        partial(feed_kernel, count=count, keep=keep),
        grid=(hidden // block,),
        out_shape=(
            shape_of((total, hidden), BF16),
            shape_of((total, hidden), BF16),
            shape_of((1, hidden), F32),
            *[shape_of((r, width), d) for r, d in sides],
        ),
        in_specs=[
            *[whole] * (2 * count),
            pl.BlockSpec((width, block), lambda i: (0, i)),
            pl.BlockSpec((1, block), lambda i: (0, i)),
            pl.BlockSpec((block, width), lambda i: (i, 0)),
        ],
        out_specs=(
            pl.BlockSpec((total, block), lambda i: (0, i)),
            pl.BlockSpec((total, block), lambda i: (0, i)),
            pl.BlockSpec((1, block), lambda i: (0, i)),
            *[
                pl.BlockSpec((r, width), lambda i: (0, 0), pipeline_mode=once) for r, d in sides
            ],
        ),
        scratch_shapes=[pltpu.VMEM((total, width), F32), pltpu.VMEM((total, width), F32)],
        cost_estimate=pl.CostEstimate(
            flops=8 * total * width * hidden,
            bytes_accessed=4 * width * hidden + 4 * total * hidden,
            transcendentals=2 * total * hidden,
        ),
        compiler_params=pltpu.CompilerParams(vmem_limit_bytes=VMEM_LIMIT),
        name="feed",
    )(*rows_list, *cot_list, w1, b1.astype(F32).reshape(1, hidden), w2)


def chunk_at(k, bit, value):
    return ((k >> bit) << (bit + 1)) + (value << bit) + (k & ((1 << bit) - 1))


def weight_kernel(me_ref, at_ref, *refs, bit, count):
    b_refs, (send_ref, keep_ref, chunk_ref) = refs[:count], refs[count:]
    rows = b_refs[0].shape[0]
    acc = dot32(at_ref[:, :rows], b_refs[0][...])
    for m in range(1, count):
        acc = acc + dot32(at_ref[:, m * rows : (m + 1) * rows], b_refs[m][...])
    chunk_ref[...] = acc.astype(BF16).reshape(chunk_ref.shape)
    mine = (me_ref[0] >> bit) & 1
    for k in range(send_ref.shape[0]):
        send_ref[k] = chunk_ref[chunk_at(k, bit, 1 - mine)]
        keep_ref[k] = chunk_ref[chunk_at(k, bit, mine)]


def weight_halves(me, at, parts, steps, block, members, bit):
    width, tokens = at.shape
    rows = width // members
    half = (members // 2, rows, steps * block)
    out = pl.BlockSpec((members // 2, rows, block), lambda i: (0, 0, i))
    return pl.pallas_call(
        partial(weight_kernel, bit=bit, count=len(parts)),
        grid=(steps,),
        out_shape=(shape_of(half, BF16), shape_of(half, BF16)),
        in_specs=[
            pl.BlockSpec(memory_space=pltpu.SMEM),
            fixed((width, tokens)),
            *[pl.BlockSpec(shape, index) for _, shape, index in parts],
        ],
        out_specs=(out, out),
        scratch_shapes=[pltpu.VMEM((members, rows, block), BF16)],
        cost_estimate=pl.CostEstimate(
            flops=2 * width * tokens * steps * block,
            bytes_accessed=2 * width * tokens + 2 * (width + tokens) * steps * block,
            transcendentals=0,
        ),
        compiler_params=pltpu.CompilerParams(vmem_limit_bytes=VMEM_LIMIT),
        name="weight_halves",
    )(me, at, *[array for array, _, _ in parts])


def add_kernel(me_ref, a0_ref, b0_ref, a1_ref, b1_ref, send_ref, keep_ref):
    send_ref[...] = (a0_ref[...].astype(F32) + b0_ref[...].astype(F32)).astype(BF16)
    keep_ref[...] = (a1_ref[...].astype(F32) + b1_ref[...].astype(F32)).astype(BF16)


def add_halves(me, held, came, ring_bit, bit):
    chunks, rows, cols = held.shape
    block = (1, rows, cols)

    def at(flip):
        return pl.BlockSpec(
            block, lambda k, me: (chunk_at(k, bit, ((me[0] >> ring_bit) & 1) ^ flip), 0, 0)
        )

    out = pl.BlockSpec(block, lambda k, me: (k, 0, 0))
    half = shape_of((chunks // 2, rows, cols), BF16)
    return pl.pallas_call(
        add_kernel,
        grid_spec=pltpu.PrefetchScalarGridSpec(
            num_scalar_prefetch=1,
            grid=(chunks // 2,),
            in_specs=[at(1), at(1), at(0), at(0)],
            out_specs=(out, out),
        ),
        out_shape=(half, half),
        cost_estimate=pl.CostEstimate(
            flops=held.size, bytes_accessed=6 * held.size, transcendentals=0
        ),
        name="add_halves",
    )(me, held, came, held, came)


def seq_move(x, bit):
    members = lax.axis_size("seq")
    return lax.ppermute(x, "seq", [(s, s ^ (1 << bit)) for s in range(members)])


class Ring:
    def __init__(self, me, send, keep, order):
        self.me, self.keep = me, keep
        members = lax.axis_size("seq")
        bits = members.bit_length() - 1
        order = [b for b in order if b < bits] + [b for b in range(bits) if b not in order]
        self.left = sorted(order, reverse=True)
        self.order = list(order)
        self.send = send
        self.travel()

    def travel(self):
        bit = self.order.pop(0)
        self.left.remove(bit)
        self.came = seq_move(self.send, bit)

    def step(self):
        bit = self.order[0]
        lower = len([b for b in self.left if b < bit])
        self.send, self.keep = add_halves(self.me, self.keep, self.came, bit, lower)
        self.travel()

    def total(self):
        while self.order:
            self.step()
        return self.keep[0].astype(F32) + self.came[0].astype(F32)


def regroup_kernel(back_ref, table_ref, gm_ref, att_ref, *, rows):
    heads, parts = back_ref.shape[:2]
    low = lax.broadcasted_iota(jnp.int32, (rows, PAIR), 1) < HEAD
    kv, qo = [], []
    for h in range(heads):
        kv.append(sum(back_ref[h, p, :rows].astype(F32) for p in range(parts)))
        qo.append(jnp.concatenate([back_ref[h, p, rows:].astype(F32) for p in range(parts)], 0))
    grad_k, grad_v = two_heads(kv[0], kv[1], low)
    grad_q, attended = two_heads(qo[0], qo[1], low)
    tables = (table_ref[0], -table_ref[1], -table_ref[2])
    gm_ref[0, :, :PAIR] = rotate_lanes(grad_q, *tables).astype(BF16)
    gm_ref[0, :, PAIR : 2 * PAIR] = rotate_lanes(grad_k, *tables).astype(BF16)
    gm_ref[0, :, 2 * PAIR :] = grad_v.astype(BF16)
    att_ref[...] = attended.astype(BF16)


def regroup(back, table, rows, parts):
    chunk = back.shape[1]
    return pl.pallas_call(
        partial(regroup_kernel, rows=rows),
        grid=(GROUPS,),
        out_shape=(
            shape_of((GROUPS, rows, 3 * PAIR), BF16),
            shape_of((rows, HEADS * HEAD), BF16),
        ),
        in_specs=[
            pl.BlockSpec((2, parts, chunk, PAIR), lambda i: (i, 0, 0, 0)),
            fixed(table.shape),
        ],
        out_specs=(
            pl.BlockSpec((1, rows, 3 * PAIR), lambda i: (i, 0, 0)),
            pl.BlockSpec((rows, PAIR), lambda i: (0, i)),
        ),
        cost_estimate=pl.CostEstimate(
            flops=back.size, bytes_accessed=4 * back.size, transcendentals=0
        ),
        name="regroup",
    )(back.reshape(HEADS, parts, chunk, PAIR), table)


def close_kernel(
    x_ref, g_ref, ga_ref, gf_ref, bo_ref, bc_ref, gm_ref, att_ref,
    wq_ref, wk_ref, wv_ref, wo_ref, *refs, sides,
):
    feeds, grads = refs[:sides], refs[sides : 2 * sides]
    out_ref, gin_ref, vec_ref, gmb_ref, out_acc, grad_acc = refs[2 * sides :]
    step = pl.program_id(0)

    @pl.when(step == 0)
    def _():
        out_acc[...] = jnp.zeros_like(out_acc)
        grad_acc[...] = jnp.zeros_like(grad_acc)

    out_acc[...] += dot32(att_ref[...], wo_ref[...])
    count = gm_ref.shape[0]
    for third, w_ref in enumerate((wq_ref, wk_ref, wv_ref)):
        grad = jnp.concatenate(
            [gm_ref[c, :, third * PAIR : (third + 1) * PAIR] for c in range(count)], 1
        )
        grad_acc[...] += dot32(grad, w_ref[...], NT)
    for c in range(count):
        gmb_ref[c] = jnp.sum(gm_ref[c].astype(F32), 0, keepdims=True)

    @pl.when(step == pl.num_programs(0) - 1)
    def _():
        x = x_ref[...].astype(F32)
        g = g_ref[...].astype(F32)
        total = x + out_acc[...] + vector_row(bo_ref) + vector_row(bc_ref)
        for ref in feeds:
            total = total + ref[...].astype(F32)
        out_ref[...] = total.astype(BF16)
        unit, root = unit_rows(x)
        one = grad_acc[...]
        two = grads[0][...].astype(F32)
        for ref in grads[1:]:
            two = two + ref[...].astype(F32)
        down = one * vector_row(ga_ref) + two * vector_row(gf_ref)
        mean = jnp.mean(down, -1, keepdims=True)
        slope = jnp.mean(down * unit, -1, keepdims=True)
        gin_ref[...] = g + root * (down - mean - unit * slope)
        for r, rows in enumerate((one * unit, one, g, two * unit, two)):
            vec_ref[r : r + 1] = jnp.sum(rows, 0, keepdims=True)


def close_layer(x, g, vectors, gm, attended, weight, out_weight, feeds, grads):
    rows, width = x.shape
    steps = 4
    cols = width // steps
    per = GROUPS // steps

    def third(t):
        return pl.BlockSpec((width, cols), lambda i: (0, t * steps + i))

    return pl.pallas_call(
        partial(close_kernel, sides=len(feeds)),
        grid=(steps,),
        out_shape=(
            shape_of((rows, width), BF16),
            shape_of((rows, width), F32),
            shape_of((5, width), F32),
            shape_of((GROUPS, 1, 3 * PAIR), F32),
        ),
        in_specs=[
            fixed((rows, width)),
            fixed((rows, width)),
            *[fixed((width,))] * 4,
            pl.BlockSpec((per, rows, 3 * PAIR), lambda i: (i, 0, 0)),
            pl.BlockSpec((rows, cols), lambda i: (0, i)),
            third(0), third(1), third(2),
            pl.BlockSpec((cols, width), lambda i: (i, 0)),
            *[fixed((rows, width))] * (2 * len(feeds)),
        ],
        out_specs=(
            fixed((rows, width)),
            fixed((rows, width)),
            fixed((5, width)),
            pl.BlockSpec((per, 1, 3 * PAIR), lambda i: (i, 0, 0)),
        ),
        scratch_shapes=[pltpu.VMEM((rows, width), F32), pltpu.VMEM((rows, width), F32)],
        cost_estimate=pl.CostEstimate(
            flops=8 * rows * width * width,
            bytes_accessed=8 * width * width + 24 * rows * width,
            transcendentals=0,
        ),
        compiler_params=pltpu.CompilerParams(vmem_limit_bytes=VMEM_LIMIT),
        name="close_layer",
    )(x, g, *vectors, gm, attended, weight, weight, weight, out_weight, *feeds, *grads)


def pair_swap(x):
    return lax.ppermute(x, "mlp", [(0, 1), (1, 0)])


def mlp_list(x, axis=0):
    if lax.axis_size("mlp") == 2:
        return [x, pair_swap(x)]
    return [lax.all_gather(x, "mlp", axis=axis, tiled=True)]


def mlp_pieces(pieces):
    members = lax.axis_size("mlp")
    if members == 2:
        me = lax.axis_index("mlp")
        came = pair_swap(lax.dynamic_index_in_dim(pieces, 1 - me, 0, False))
        return [lax.dynamic_index_in_dim(pieces, me, 0, False), came]
    got = lax.all_to_all(pieces, "mlp", 0, 0, tiled=False)
    return [got[m] for m in range(members)]


def after(value, *others):
    return lax.optimization_barrier((value, *others))[0]


def per_device(
    block_input,
    out_cotangent,
    attend_gain,
    attend_shift,
    query_key_value_weight,
    query_key_value_bias,
    attention_out_weight,
    attention_out_bias,
    feed_gain,
    feed_shift,
    expand_weight,
    expand_bias,
    contract_weight,
    contract_bias,
):
    seq_count, rows, width = block_input.shape
    members = lax.axis_size("seq")
    pairs = lax.axis_size("mlp")
    parts = members // HEADS
    own = width // members
    me = lax.axis_index("seq").astype(jnp.int32).reshape(1)
    pair_me = lax.axis_index("mlp")
    inputs = block_input.reshape(rows, width)
    cot = out_cotangent.reshape(rows, width)

    outgoing, normed_one, normed_two, table, one_t, two_t, cot_t = open_layer(
        inputs,
        cot,
        me * rows,
        (attend_gain, attend_shift, feed_gain, feed_shift),
        query_key_value_weight,
        query_key_value_bias,
        attention_out_weight,
        parts,
    )
    at_head = lax.all_to_all(outgoing, "seq", 0, 0, tiled=True)

    rows_list, cot_list = mlp_list(normed_two), mlp_list(cot)
    two_t, cot_t, one_t = (
        jnp.concatenate(mlp_list(v, 1), 1) if pairs == 2 else mlp_list(v, 1)[0]
        for v in (two_t, cot_t, one_t)
    )
    hidden, grad_pre, grad_hid_bias, *sides = feed(
        rows_list, cot_list, expand_weight, expand_bias, contract_weight
    )
    if pairs == 2:
        feeds = [sides[0], pair_swap(sides[2])]
        grads = [sides[1], pair_swap(sides[3])]
    else:
        feeds, grads = (
            [lax.psum_scatter(v, "mlp", scatter_dimension=0, tiled=True)] for v in sides
        )
    slice_width = expand_weight.shape[1]
    block = min(512, slice_width)

    def ring_of(at, b, order):
        parts_b = [
            (b, (rows, block), lambda i, m=m: (m, i)) for m in range(pairs)
        ]
        send, keep = weight_halves(
            me, at, parts_b, slice_width // block, block, members, order[0]
        )
        return Ring(me, send, keep, order)

    ring_out = ring_of(cot_t, hidden, (0, 1, 2, 3))
    ring_hid = ring_of(two_t, grad_pre, (1, 0, 2, 3))

    part = (me % parts).astype(jnp.int32)
    at_head = after(at_head, ring_out.send, ring_hid.send, *feeds, *grads)
    from_head = one_head(at_head, part, rows, rows // parts)
    back = lax.all_to_all(from_head, "seq", 0, 0, tiled=True)

    ring_out.came, ring_hid.came, from_head = lax.optimization_barrier(
        (ring_out.came, ring_hid.came, from_head)
    )
    ring_out.step()
    ring_hid.step()
    gm, attended = regroup(back, table, rows, parts)
    per = GROUPS // pairs
    gm_pieces = mlp_pieces(gm.reshape(pairs, per, rows, 3 * PAIR))
    att_t = jnp.transpose(attended)
    att_t = jnp.concatenate(mlp_list(att_t, 1), 1) if pairs == 2 else mlp_list(att_t, 1)[0]
    dense_share = width // pairs

    rings = []
    cuts = [(0, per // 2, (0, 1, 2, 3)), (per // 2, per, (1, 0, 2, 3))] if per > 1 else [
        (0, per, (0, 1, 2, 3))
    ]
    for low, high, order in cuts:
        parts_b = [
            (piece, (None, rows, 3 * PAIR), lambda i, low=low: (low + i, 0, 0))
            for piece in gm_pieces
        ]
        send, keep = weight_halves(
            me, one_t, parts_b, high - low, 3 * PAIR, members, order[0]
        )
        rings.append(Ring(me, send, keep, order))
    parts_b = [
        (piece, (rows, dense_share), lambda i: (0, 0))
        for piece in [
            lax.dynamic_slice_in_dim(c, pair_me * dense_share, dense_share, 1)
            for c in (
                cot_list
                if pairs == 2
                else [cot_list[0][m * rows : (m + 1) * rows] for m in range(pairs)]
            )
        ]
    ]
    send, keep = weight_halves(me, att_t, parts_b, 1, dense_share, members, 2)
    rings.append(Ring(me, send, keep, (2, 0, 1, 3)))

    block_output, grad_input, vec, gm_bias = close_layer(
        inputs,
        cot,
        (attend_gain, feed_gain, attention_out_bias, contract_bias),
        gm,
        attended,
        query_key_value_weight,
        attention_out_weight,
        feeds,
        grads,
    )

    bias_full = lax.dynamic_update_slice_in_dim(
        jnp.zeros((pairs * slice_width,), F32), grad_hid_bias[0], pair_me * slice_width, 0
    )
    gm_bias = jnp.transpose(gm_bias.reshape(GROUPS, 3, PAIR), (1, 0, 2)).reshape(-1)
    vectors = [*[vec[r] for r in range(5)], gm_bias, bias_full]
    packed = jnp.concatenate([v.reshape(members, pairs, -1) for v in vectors], -1)
    packed = jnp.sum(lax.all_to_all(packed, "seq", 0, 0, tiled=True), 0)
    if pairs == 2:
        mine = lax.dynamic_index_in_dim(packed, pair_me, 0, False)
        other = lax.dynamic_index_in_dim(packed, 1 - pair_me, 0, False)
        packed = mine + pair_swap(other)
    else:
        packed = lax.psum_scatter(packed, "mlp", scatter_dimension=0, tiled=False)
    outs, start = [], 0
    for v in vectors:
        size = v.shape[0] // (members * pairs)
        outs.append(lax.slice_in_dim(packed, start, start + size))
        start += size
    grad_gain_one, grad_shift_one, grad_dense_bias, grad_gain_two, grad_shift_two = outs[:5]
    grad_merged_bias, out_hid_bias = outs[5:]

    out_weight = jnp.transpose(ring_out.total())
    hid_weight = ring_hid.total()

    totals = jnp.concatenate([r.total() for r in rings], -1)
    pieces = mlp_pieces(totals.reshape(pairs, own // pairs, totals.shape[-1]))
    if pairs == 2:
        first = pair_me == 0
        pieces = [jnp.where(first, pieces[0], pieces[1]), jnp.where(first, pieces[1], pieces[0])]
    share = per * 3 * PAIR
    merged = jnp.stack([p[:, :share].reshape(-1, per, 3, PAIR) for p in pieces], 1)
    merged = jnp.transpose(merged, (0, 3, 1, 2, 4)).reshape(own // pairs, 3 * width)
    dense = jnp.concatenate([p[:, share:] for p in pieces], -1)
    return (
        block_output.reshape(seq_count, rows, width),
        grad_input.reshape(seq_count, rows, width),
        grad_gain_one,
        grad_shift_one,
        merged,
        grad_merged_bias,
        dense,
        grad_dense_bias,
        grad_gain_two,
        grad_shift_two,
        hid_weight,
        out_hid_bias,
        out_weight,
        grad_dense_bias,
    )


def solution(mesh):
    in_specs = (
        P("mlp", "seq", None),
        P("mlp", "seq", None),
        P(),
        P(),
        P(),
        P(),
        P(),
        P(),
        P(),
        P(),
        P(None, "mlp"),
        P("mlp"),
        P("mlp", None),
        P(),
    )
    out_specs = (
        P("mlp", "seq", None),
        P("mlp", "seq", None),
        P(("seq", "mlp")),
        P(("seq", "mlp")),
        P(("seq", "mlp"), None),
        P(("seq", "mlp")),
        P(("seq", "mlp"), None),
        P(("seq", "mlp")),
        P(("seq", "mlp")),
        P(("seq", "mlp")),
        P("seq", "mlp"),
        P(("seq", "mlp")),
        P("mlp", "seq"),
        P(("seq", "mlp")),
    )
    return jax.shard_map(
        per_device, mesh=mesh, in_specs=in_specs, out_specs=out_specs, check_vma=False
    )
```

profile of v0, /device:TPU:1, one launch (start us, length us, event | category | flops | bytes accessed | tf_op | source)
XLA Modules:
  0.0 337.9 jit_solution(15414567417857398029)
XLA Ops:
  1.3 9.4 %open_layer.1 = (bf16[16,1,512,128]{3,2,1,0:T(8,128)(2,1)}, bf16[256,1024]{1,0:T(8,128)(2,1)}, bf16[256,1024]{1,0:T(8,128)(2,1)}, f32[3,256,128]{2,1,0:T(8,128)}...) custom-call(s32[1]{0:T(128)S(6)} %mul.12.first_ref, bf16[256,1024]{1,0:T(8,128)(2,1)} %bitcast.45, ...), custom_call_target="tpu_custom_call" | custom-call | flops 2147483648 | bytes 13107200 | tf_op jit(solution)/shard_map/open_layer/pallas_call | solution.py:133
  10.7 7.6 %all-to-all-start = ((bf16[16,512,128]{2,1,0:T(8,128)(2,1)}), bf16[16,512,128]{2,1,0:T(8,128)(2,1)S(1)}, u32[]{:S(2)}, u32[]{:S(2)}) async-start(bf16[16,512,128]{2,1,0:T(8,128)(2,1)} %bitcast.47), calls=%async_computation | async-start | bytes 4194304 | tf_op jit(solution)/shard_map/all_to_all | solution.py:676
  18.2 1.0 collective-permute-start.1
  21.0 2.0 collective-permute-done.2.refs_3_
  23.9 17.3 %feed.1 = (bf16[512,2048]{1,0:T(8,128)(2,1)}, bf16[512,2048]{1,0:T(8,128)(2,1)}, f32[1,2048]{1,0:T(1,128)}, f32[256,1024]{1,0:T(8,128)}, f32[256,1024]{1,0:T(8,1...) custom-call(bf16[256,1024]{1,0:T(8,128)(2,1)} %get-tuple-element.78.refs_0_, bf16[256,1024]{1,0:T(8,128)(2,1)} %copy-done.29, ...), custom_call_target="tpu_custom_call" | custom-call | flops 8589934592 | bytes 12582912 | tf_op jit(solution)/shard_map/feed/pallas_call | solution.py:345
  41.7 2.2 pad_maximum_fusion.1.at_ref
  44.0 2.1 pad_maximum_fusion.at_ref
  46.1 6.3 %weight_halves.6 = (bf16[8,64,2048]{2,1,0:T(8,128)(2,1)}, bf16[8,64,2048]{2,1,0:T(8,128)(2,1)}) custom-call(s32[1]{0:T(128)} %bitcast.2.me_ref, bf16[1024,512]{1,0:T(8,128)(2,1)} %pad_maximum_fusion.1.at_ref, bf16[512,2048]{1,0:T(8,128)(2,1)} %get-tuple-element.82.refs_0_.refs_1_, bf16[512,2048]{1,0:T(8,128)(2,1)} %get-tuple-element.82.refs_0_.refs_1_), custom_call_target="tpu_custom_call" | custom-call | flops 2147483648 | bytes 7340032 | tf_op jit(solution)/shard_map/weight_halves/pallas_call | solution.py:401
  52.4 6.3 %weight_halves.5 = (bf16[8,64,2048]{2,1,0:T(8,128)(2,1)}, bf16[8,64,2048]{2,1,0:T(8,128)(2,1)}) custom-call(s32[1]{0:T(128)} %bitcast.2.me_ref, bf16[1024,512]{1,0:T(8,128)(2,1)} %pad_maximum_fusion.at_ref, bf16[512,2048]{1,0:T(8,128)(2,1)} %get-tuple-element.79.refs_0_.refs_1_, bf16[512,2048]{1,0:T(8,128)(2,1)} %get-tuple-element.79.refs_0_.refs_1_), custom_call_target="tpu_custom_call" | custom-call | flops 2147483648 | bytes 7340032 | tf_op jit(solution)/shard_map/weight_halves/pallas_call | solution.py:401
  59.7 1.3 copy-done.11
  61.0 59.0 %one_head.1 = bf16[16,512,128]{2,1,0:T(8,128)(2,1)} custom-call(s32[1]{0:T(128)} %constant.56.clone.1.part_ref, bf16[16,512,128]{2,1,0:T(8,128)(2,1)} %copy-done.11), custom_call_target="tpu_custom_call" | custom-call | flops 25769803776 | bytes 4194304 | tf_op jit(solution)/shard_map/one_head/pallas_call | solution.py:266
  120.0 10.8 %all-to-all-start.1 = ((bf16[16,512,128]{2,1,0:T(8,128)(2,1)}), bf16[16,512,128]{2,1,0:T(8,128)(2,1)S(1)}, u32[]{:S(2)}, u32[]{:S(2)}) async-start(bf16[16,512,128]{2,1,0:T(8,128)(2,1)} %one_head.1), calls=%async_computation.1 | async-start | bytes 4194304 | tf_op jit(solution)/shard_map/all_to_all | solution.py:711
  130.8 1.4 collective-permute-start.24
  132.2 1.2 collective-permute-start.23
  133.4 39.0 %all-to-all-done.1 = bf16[16,512,128]{2,1,0:T(8,128)(2,1)S(1)} async-done(((bf16[16,512,128]{2,1,0:T(8,128)(2,1)}), bf16[16,512,128]{2,1,0:T(8,128)(2,1)S(1)}, u32[]{:S(2)}, u32[]{:S(2)}) %all-to-all-start.1) | async-done | bytes 2097184 | tf_op jit(solution)/shard_map/all_to_all | solution.py:711
  172.4 1.3 copy-done
  173.8 6.6 %regroup.1 = (bf16[8,256,384]{2,1,0:T(8,128)(2,1)}, bf16[256,1024]{1,0:T(8,128)(2,1)}) custom-call(bf16[16,1,512,128]{3,2,1,0:T(8,128)(2,1)} %bitcast.39, f32[3,256,128]{2,1,0:T(8,128)} %get-tuple-element.89.table_ref), custom_call_target="tpu_custom_call" | custom-call | flops 1048576 | bytes 4194304 | tf_op jit(solution)/shard_map/regroup/pallas_call | solution.py:505
  180.3 2.7 dynamic-slice_bitcast_fusion
  183.0 2.8 collective-permute-start.8
  185.8 14.3 %collective-permute-done.24.b0_ref.b1_ref = bf16[8,64,2048]{2,1,0:T(8,128)(2,1)} collective-permute-done((bf16[8,64,2048]{2,1,0:T(8,128)(2,1)}, bf16[8,64,2048]{2,1,0:T(8,128)(2,1)}, u32[]{:S(2)}, u32[]{:S(2)}) %collective-permute-start.24) | collective-permute-done | bytes 2097184 | tf_op jit(solution)/shard_map/ppermute | solution.py:456
  200.1 4.2 %add_halves.27 = (bf16[4,64,2048]{2,1,0:T(8,128)(2,1)}, bf16[4,64,2048]{2,1,0:T(8,128)(2,1)}) custom-call(s32[1]{0:T(128)} %bitcast.2.me_ref, bf16[8,64,2048]{2,1,0:T(8,128)(2,1)} %get-tuple-element.130.a0_ref.a1_ref, bf16[8,64,2048]{2,1,0:T(8,128)(2,1)} %collective-permute-done.23.b0_ref.b1_ref, bf16[8,64,2048]{2,1,0:T(8,128)(2,1)} %get-tuple-element.130.a0_ref.a1_ref, ...), custom_call_target="tpu_custom_call" | custom-call | flops 1048576 | bytes 6291456 | tf_op jit(solution)/shard_map/add_halves/pallas_call | solution.py:438
  204.3 1.0 collective-permute-start.28
  205.3 4.3 %add_halves.24 = (bf16[4,64,2048]{2,1,0:T(8,128)(2,1)}, bf16[4,64,2048]{2,1,0:T(8,128)(2,1)}) custom-call(s32[1]{0:T(128)} %bitcast.2.me_ref, bf16[8,64,2048]{2,1,0:T(8,128)(2,1)} %get-tuple-element.122.a0_ref.a1_ref, bf16[8,64,2048]{2,1,0:T(8,128)(2,1)} %collective-permute-done.24.b0_ref.b1_ref, bf16[8,64,2048]{2,1,0:T(8,128)(2,1)} %get-tuple-element.122.a0_ref.a1_ref, ...), custom_call_target="tpu_custom_call" | custom-call | flops 1048576 | bytes 6291456 | tf_op jit(solution)/shard_map/add_halves/pallas_call | solution.py:438
  209.8 1.0 copy.46
  210.8 2.3 collective-permute-start.17
  213.8 2.0 constant_dynamic-update-slice_fusion.1
  215.8 1.7 constant_dynamic-slice_fusion.refs_1_
  217.5 2.0 constant_dynamic-update-slice_fusion.at_ref
  219.4 4.0 %weight_halves.7 = (bf16[8,64,768]{2,1,0:T(8,128)(2,1)}, bf16[8,64,768]{2,1,0:T(8,128)(2,1)}) custom-call(s32[1]{0:T(128)} %bitcast.2.me_ref, bf16[1024,512]{1,0:T(8,128)(2,1)} %constant_dynamic-update-slice_fusion.at_ref, bf16[4,256,384]{2,1,0:T(8,128)(2,1)} %get-tuple-element.146.refs_0_, bf16[4,256,384]{2,1,0:T(8,128)(2,1)} %collective-permute-done.8.refs_1_), custom_call_target="tpu_custom_call" | custom-call | flops 805306368 | bytes 3407872 | tf_op jit(solution)/shard_map/weight_halves/pallas_call | solution.py:401
  223.5 1.7 collective-permute-start.9
  225.2 1.1 pad_maximum_fusion.2.at_ref
  226.2 3.1 weight_halves.9
  230.0 1.0 copy-done.2
  230.9 2.4 add_halves.28
  234.1 1.0 copy-done.1
  235.1 2.4 add_halves.25
  238.1 3.9 %weight_halves.8 = (bf16[8,64,768]{2,1,0:T(8,128)(2,1)}, bf16[8,64,768]{2,1,0:T(8,128)(2,1)}) custom-call(s32[1]{0:T(128)} %bitcast.2.me_ref, bf16[1024,512]{1,0:T(8,128)(2,1)} %constant_dynamic-update-slice_fusion.at_ref, bf16[4,256,384]{2,1,0:T(8,128)(2,1)} %get-tuple-element.146.refs_0_, bf16[4,256,384]{2,1,0:T(8,128)(2,1)} %collective-permute-done.8.refs_1_), custom_call_target="tpu_custom_call" | custom-call | flops 805306368 | bytes 3407872 | tf_op jit(solution)/shard_map/weight_halves/pallas_call | solution.py:401
  243.6 3.2 add_halves.21
  247.6 1.2 collective-permute-done.9.b0_ref.b1_ref
  249.7 3.5 %add_halves.15 = (bf16[4,64,768]{2,1,0:T(8,128)(2,1)}, bf16[4,64,768]{2,1,0:T(8,128)(2,1)}) custom-call(s32[1]{0:T(128)} %bitcast.2.me_ref, bf16[8,64,768]{2,1,0:T(8,128)(2,1)} %get-tuple-element.98.a0_ref.a1_ref, bf16[8,64,768]{2,1,0:T(8,128)(2,1)} %copy-done.6, bf16[8,64,768]{2,1,0:T(8,128)(2,1)} %get-tuple-element.98.a0_ref.a1_ref, ...), custom_call_target="tpu_custom_call" | custom-call | flops 393216 | bytes 2359296 | tf_op jit(solution)/shard_map/add_halves/pallas_call | solution.py:438
  253.2 1.2 collective-permute-start.10
  255.4 2.0 add_halves.29
  257.5 2.1 collective-permute-start.30
  259.6 9.4 %collective-permute-done.26.b0_ref.b1_ref = bf16[2,64,2048]{2,1,0:T(8,128)(2,1)S(1)} collective-permute-done((bf16[2,64,2048]{2,1,0:T(8,128)(2,1)}, bf16[2,64,2048]{2,1,0:T(8,128)(2,1)S(1)}, u32[]{:S(2)}, u32[]{:S(2)}) %collective-permute-start.26) | collective-permute-done | bytes 524320 | tf_op jit(solution)/shard_map/ppermute | solution.py:456
  269.7 2.0 add_halves.26
  272.4 1.7 add_halves.22
  274.2 10.0 %close_layer.1 = (bf16[256,1024]{1,0:T(8,128)(2,1)}, f32[256,1024]{1,0:T(8,128)}, f32[5,1024]{1,0:T(8,128)}, f32[8,1,384]{2,1,0:T(1,128)}) custom-call(bf16[256,1024]{1,0:T(8,128)(2,1)} %bitcast.46, bf16[256,1024]{1,0:T(8,128)(2,1)} %bitcast.43, bf16[1024]{0:T(1024)(128)(2,1)} %ga_ref.3, bf16[1024]{0:T(1024)(128)(2,1)} %gf_ref.3, bf16[1024]{0:T(1024)(128)(2,1)} %bo_ref.1, ...), custom_call_target="tpu_custom_call" | custom-call | flops 2147483648 | bytes 14680064 | tf_op jit(solution)/shard_map/close_layer/pallas_call | solution.py:580
  284.3 1.0 slice_reduce_fusion
  287.3 4.9 %all-to-all-start.2 = ((f32[16,2,384]{2,1,0:T(2,128)}), f32[16,2,384]{2,1,0:T(2,128)S(1)}, u32[]{:S(2)}, u32[]{:S(2)}) async-start(f32[16,2,384]{2,1,0:T(2,128)} %concatenate.24), calls=%async_computation.2 | async-start | bytes 98304 | tf_op jit(solution)/shard_map/all_to_all | solution.py:770
  292.8 1.6 add_halves.23
  294.4 2.3 collective-permute-start.21
  296.7 0.9 copy-done.5
  297.6 3.5 %add_halves.18 = (bf16[4,64,768]{2,1,0:T(8,128)(2,1)}, bf16[4,64,768]{2,1,0:T(8,128)(2,1)}) custom-call(s32[1]{0:T(128)} %bitcast.2.me_ref, bf16[8,64,768]{2,1,0:T(8,128)(2,1)} %get-tuple-element.106.a0_ref.a1_ref, bf16[8,64,768]{2,1,0:T(8,128)(2,1)} %copy-done.5, bf16[8,64,768]{2,1,0:T(8,128)(2,1)} %get-tuple-element.106.a0_ref.a1_ref, ...), custom_call_target="tpu_custom_call" | custom-call | flops 393216 | bytes 2359296 | tf_op jit(solution)/shard_map/add_halves/pallas_call | solution.py:438
  301.2 1.2 collective-permute-start.14
  303.1 1.9 add_halves.16
  305.0 1.2 collective-permute-start.11
  307.2 3.1 collective-permute-start.6
  311.1 1.9 add_halves.19
  314.0 1.8 add_halves.17
  316.1 1.6 collective-permute-done.15.b0_ref.b1_ref
  318.4 1.7 add_halves.20
  320.6 0.9 convert_add_fusion.1
  321.5 6.4 %collective-permute-done.16 = bf16[1,64,768]{2,1,0:T(8,128)(2,1)S(1)} collective-permute-done((bf16[1,64,768]{2,1,0:T(8,128)(2,1)}, bf16[1,64,768]{2,1,0:T(8,128)(2,1)S(1)}, u32[]{:S(2)}, u32[]{:S(2)}) %collective-permute-start.16) | collective-permute-done | bytes 98336 | tf_op jit(solution)/shard_map/ppermute | solution.py:456
  329.0 3.6 %collective-permute-start.22 = (f32[32,2048]{1,0:T(8,128)S(1)}, f32[32,2048]{1,0:T(8,128)S(1)}, u32[]{:S(2)}, u32[]{:S(2)}) collective-permute-start(f32[32,2048]{1,0:T(8,128)S(1)} %dynamic-slice_bitcast_fusion.2), channel_id=1, source_target_pairs={{0,1},{1,0},{2,3},{3,2},{4,5},{5,4},{6,7},{7,6},{8,9},{9,8},{10,11... | collective-permute-start | bytes 786440 | tf_op jit(solution)/shard_map/ppermute | solution.py:617
  (138 shorter events, 27.4 us)
Async XLA Ops:
  10.6 8.6 %copy-start.3 = (bf16[1,256,1024]{2,1,0:T(8,128)(2,1)S(1)}, bf16[1,256,1024]{2,1,0:T(8,128)(2,1)}, u32[]{:S(2)}) copy-start(bf16[1,256,1024]{2,1,0:T(8,128)(2,1)} %param.15) | copy-start | bytes 1572868
  10.7 9.1 %copy-start.21 = (bf16[1024,256]{1,0:T(8,128)(2,1)S(1)}, bf16[1024,256]{1,0:T(8,128)(2,1)}, u32[]{:S(2)}) copy-start(bf16[1024,256]{1,0:T(8,128)(2,1)} %get-tuple-element.77) | copy-start | bytes 1572868
  10.7 9.2 %copy-start.27 = (bf16[2048]{0:T(1024)(128)(2,1)S(1)}, bf16[2048]{0:T(1024)(128)(2,1)}, u32[]{:S(2)}) copy-start(bf16[2048]{0:T(1024)(128)(2,1)} %param.25) | copy-start | bytes 12292
  10.7 49.0 %all-to-all-start = ((bf16[16,512,128]{2,1,0:T(8,128)(2,1)}), bf16[16,512,128]{2,1,0:T(8,128)(2,1)S(1)}, u32[]{:S(2)}, u32[]{:S(2)}) async-start(bf16[16,512,128]{2,1,0:T(8,128)(2,1)} %bitcast.47), calls=%async_computation | async-start | bytes 4194304 | tf_op jit(solution)/shard_map/all_to_all | solution.py:676
  18.2 2.8 collective-permute-start.1
  19.3 3.8 %collective-permute-start.2 = (bf16[256,1024]{1,0:T(8,128)(2,1)S(1)}, bf16[256,1024]{1,0:T(8,128)(2,1)S(1)}, u32[]{:S(2)}, u32[]{:S(2)}) collective-permute-start(bf16[256,1024]{1,0:T(8,128)(2,1)S(1)} %bitcast.44), channel_id=1, source_target_pairs={{0,1},{1,0},{2,3},{3,2},{4,5},{5,4},{6,7},{7,6},{8,9},{9,8},{10,11... | collective-permute-start | bytes 1572872 | tf_op jit(solution)/shard_map/ppermute | solution.py:617
  19.4 22.4 %collective-permute-start.3 = (bf16[1024,256]{1,0:T(8,128)(2,1)}, bf16[1024,256]{1,0:T(8,128)(2,1)}, u32[]{:S(2)}, u32[]{:S(2)}) collective-permute-start(bf16[1024,256]{1,0:T(8,128)(2,1)} %get-tuple-element.81), channel_id=1, source_target_pairs={{0,1},{1,0},{2,3},{3,2},{4,5},{5,4},{6,7},{7,6},{8,9},{9,8},{10,11... | collective-permute-start | bytes 1572872 | tf_op jit(solution)/shard_map/ppermute | solution.py:617
  19.8 24.2 %collective-permute-start = (bf16[1024,256]{1,0:T(8,128)(2,1)S(1)}, bf16[1024,256]{1,0:T(8,128)(2,1)}, u32[]{:S(2)}, u32[]{:S(2)}) collective-permute-start(bf16[1024,256]{1,0:T(8,128)(2,1)S(1)} %copy-done.21), channel_id=1, source_target_pairs={{0,1},{1,0},{2,3},{3,2},{4,5},{5,4},{6,7},{7,6},{8,9},{9,8},{10,11... | collective-permute-start | bytes 1572872 | tf_op jit(solution)/shard_map/ppermute | solution.py:617
  21.0 2.0 copy-start.29
  23.1 0.8 copy-start.24
  41.1 17.5 %collective-permute-start.4 = (bf16[256,1024]{1,0:T(8,128)(2,1)}, bf16[256,1024]{1,0:T(8,128)(2,1)S(1)}, u32[]{:S(2)}, u32[]{:S(2)}) collective-permute-start(bf16[256,1024]{1,0:T(8,128)(2,1)} %get-tuple-element.85), channel_id=1, source_target_pairs={{0,1},{1,0},{2,3},{3,2},{4,5},{5,4},{6,7},{7,6},{8,9},{9,8},{10,11... | collective-permute-start | bytes 1572872 | tf_op jit(solution)/shard_map/ppermute | solution.py:617
  41.6 17.9 %collective-permute-start.5 = (bf16[256,1024]{1,0:T(8,128)(2,1)}, bf16[256,1024]{1,0:T(8,128)(2,1)S(1)}, u32[]{:S(2)}, u32[]{:S(2)}) collective-permute-start(bf16[256,1024]{1,0:T(8,128)(2,1)} %get-tuple-element.87), channel_id=1, source_target_pairs={{0,1},{1,0},{2,3},{3,2},{4,5},{5,4},{6,7},{7,6},{8,9},{9,8},{10,11... | collective-permute-start | bytes 1572872 | tf_op jit(solution)/shard_map/ppermute | solution.py:617
  58.7 0.8 copy-start.18
  59.5 60.5 %copy-start.19 = (bf16[256,1024]{1,0:T(8,128)(2,1)}, bf16[256,1024]{1,0:T(8,128)(2,1)S(1)}, u32[]{:S(2)}) copy-start(bf16[256,1024]{1,0:T(8,128)(2,1)S(1)} %collective-permute-done.5.refs_3_) | copy-start | bytes 1572868
  59.7 1.3 copy-start.11
  120.0 52.4 %all-to-all-start.1 = ((bf16[16,512,128]{2,1,0:T(8,128)(2,1)}), bf16[16,512,128]{2,1,0:T(8,128)(2,1)S(1)}, u32[]{:S(2)}, u32[]{:S(2)}) async-start(bf16[16,512,128]{2,1,0:T(8,128)(2,1)} %one_head.1), calls=%async_computation.1 | async-start | bytes 4194304 | tf_op jit(solution)/shard_map/all_to_all | solution.py:711
  130.8 69.3 %collective-permute-start.24 = (bf16[8,64,2048]{2,1,0:T(8,128)(2,1)}, bf16[8,64,2048]{2,1,0:T(8,128)(2,1)}, u32[]{:S(2)}, u32[]{:S(2)}) collective-permute-start(bf16[8,64,2048]{2,1,0:T(8,128)(2,1)} %get-tuple-element.83), channel_id=1, source_target_pairs={{0,4},{2,6},{4,0},{6,2},{8,12},{10,14},{12,8},{14,10},{16,20},{18,... | collective-permute-start | bytes 6291464 | tf_op jit(solution)/shard_map/ppermute | solution.py:456
  132.2 67.8 %collective-permute-start.23 = (bf16[8,64,2048]{2,1,0:T(8,128)(2,1)}, bf16[8,64,2048]{2,1,0:T(8,128)(2,1)}, u32[]{:S(2)}, u32[]{:S(2)}) collective-permute-start(bf16[8,64,2048]{2,1,0:T(8,128)(2,1)} %get-tuple-element.80), channel_id=1, source_target_pairs={{0,2},{2,0},{4,6},{6,4},{8,10},{10,8},{12,14},{14,12},{16,18},{18,... | collective-permute-start | bytes 6291464 | tf_op jit(solution)/shard_map/ppermute | solution.py:456
  172.4 1.3 copy-start
  183.0 36.4 %collective-permute-start.8 = (bf16[4,256,384]{2,1,0:T(8,128)(2,1)}, bf16[4,256,384]{2,1,0:T(8,128)(2,1)}, u32[]{:S(2)}, u32[]{:S(2)}) collective-permute-start(bf16[4,256,384]{2,1,0:T(8,128)(2,1)} %get-tuple-element.145), channel_id=1, source_target_pairs={{0,1},{1,0},{2,3},{3,2},{4,5},{5,4},{6,7},{7,6},{8,9},{9,8},{10,11... | collective-permute-start | bytes 2359304 | tf_op jit(solution)/shard_map/ppermute | solution.py:617
  185.8 31.7 %collective-permute-start.7 = (bf16[1024,256]{1,0:T(8,128)(2,1)}, bf16[1024,256]{1,0:T(8,128)(2,1)}, u32[]{:S(2)}, u32[]{:S(2)}) collective-permute-start(bf16[1024,256]{1,0:T(8,128)(2,1)} %get-tuple-element.97), channel_id=1, source_target_pairs={{0,1},{1,0},{2,3},{3,2},{4,5},{5,4},{6,7},{7,6},{8,9},{9,8},{10,11... | collective-permute-start | bytes 1572872 | tf_op jit(solution)/shard_map/ppermute | solution.py:617
  204.3 25.7 %collective-permute-start.28 = (bf16[4,64,2048]{2,1,0:T(8,128)(2,1)}, bf16[4,64,2048]{2,1,0:T(8,128)(2,1)S(1)}, u32[]{:S(2)}, u32[]{:S(2)}) collective-permute-start(bf16[4,64,2048]{2,1,0:T(8,128)(2,1)} %get-tuple-element.133), channel_id=1, source_target_pairs={{0,4},{2,6},{4,0},{6,2},{8,12},{10,14},{12,8},{14,10},{16,20},{18,... | collective-permute-start | bytes 3145736 | tf_op jit(solution)/shard_map/ppermute | solution.py:456
  205.3 4.5 %copy-start.10 = (bf16[256,1024]{1,0:T(8,128)(2,1)S(1)}, bf16[256,1024]{1,0:T(8,128)(2,1)}, u32[]{:S(2)}) copy-start(bf16[256,1024]{1,0:T(8,128)(2,1)} %get-tuple-element.91.att_ref) | copy-start | bytes 1572868
  205.3 7.8 %copy-start.4 = (bf16[1,256,1024]{2,1,0:T(8,128)(2,1)S(1)}, bf16[1,256,1024]{2,1,0:T(8,128)(2,1)}, u32[]{:S(2)}) copy-start(bf16[1,256,1024]{2,1,0:T(8,128)(2,1)} %param.15) | copy-start | bytes 1572868
  209.6 24.6 %collective-permute-start.25 = (bf16[4,64,2048]{2,1,0:T(8,128)(2,1)}, bf16[4,64,2048]{2,1,0:T(8,128)(2,1)S(1)}, u32[]{:S(2)}, u32[]{:S(2)}) collective-permute-start(bf16[4,64,2048]{2,1,0:T(8,128)(2,1)} %get-tuple-element.125), channel_id=1, source_target_pairs={{0,2},{2,0},{4,6},{6,4},{8,10},{10,8},{12,14},{14,12},{16,18},{18,... | collective-permute-start | bytes 3145736 | tf_op jit(solution)/shard_map/ppermute | solution.py:456
  210.8 14.3 %collective-permute-start.17 = (bf16[1024,256]{1,0:T(8,128)(2,1)}, bf16[1024,256]{1,0:T(8,128)(2,1)S(1)}, u32[]{:S(2)}, u32[]{:S(2)}) collective-permute-start(bf16[1024,256]{1,0:T(8,128)(2,1)} %bitcast.48), channel_id=1, source_target_pairs={{0,1},{1,0},{2,3},{3,2},{4,5},{5,4},{6,7},{7,6},{8,9},{9,8},{10,11... | collective-permute-start | bytes 1572872 | tf_op jit(solution)/shard_map/ppermute | solution.py:617
  217.5 7.7 %copy-start.12 = (bf16[256,1024]{0,1:T(8,128)(2,1)S(1)}, bf16[256,1024]{0,1:T(8,128)(2,1)}, u32[]{:S(2)}) copy-start(bf16[256,1024]{0,1:T(8,128)(2,1)} %copy.46) | copy-start | bytes 1572868
  223.5 25.3 %collective-permute-start.9 = (bf16[8,64,768]{2,1,0:T(8,128)(2,1)}, bf16[8,64,768]{2,1,0:T(8,128)(2,1)S(1)}, u32[]{:S(2)}, u32[]{:S(2)}) collective-permute-start(bf16[8,64,768]{2,1,0:T(8,128)(2,1)} %get-tuple-element.99), channel_id=1, source_target_pairs={{0,2},{2,0},{4,6},{6,4},{8,10},{10,8},{12,14},{14,12},{16,18},{18,... | collective-permute-start | bytes 2359304 | tf_op jit(solution)/shard_map/ppermute | solution.py:456
  229.3 13.4 %collective-permute-start.18 = (bf16[8,64,512]{2,1,0:T(8,128)(2,1)}, bf16[8,64,512]{2,1,0:T(8,128)(2,1)S(1)}, u32[]{:S(2)}, u32[]{:S(2)}) collective-permute-start(bf16[8,64,512]{2,1,0:T(8,128)(2,1)} %get-tuple-element.115), channel_id=1, source_target_pairs={{0,8},{2,10},{4,12},{6,14},{8,0},{10,2},{12,4},{14,6},{16,24},{18,... | collective-permute-start | bytes 1572872 | tf_op jit(solution)/shard_map/ppermute | solution.py:456
  230.0 1.0 copy-start.2
  233.3 21.3 %collective-permute-start.29 = (bf16[2,64,2048]{2,1,0:T(8,128)(2,1)}, bf16[2,64,2048]{2,1,0:T(8,128)(2,1)S(1)}, u32[]{:S(2)}, u32[]{:S(2)}) collective-permute-start(bf16[2,64,2048]{2,1,0:T(8,128)(2,1)} %get-tuple-element.135), channel_id=1, source_target_pairs={{0,8},{2,10},{4,12},{6,14},{8,0},{10,2},{12,4},{14,6},{16,24},{18,... | collective-permute-start | bytes 1572872 | tf_op jit(solution)/shard_map/ppermute | solution.py:456
  234.1 1.0 copy-start.1
  237.5 31.4 %collective-permute-start.26 = (bf16[2,64,2048]{2,1,0:T(8,128)(2,1)}, bf16[2,64,2048]{2,1,0:T(8,128)(2,1)S(1)}, u32[]{:S(2)}, u32[]{:S(2)}) collective-permute-start(bf16[2,64,2048]{2,1,0:T(8,128)(2,1)} %get-tuple-element.127), channel_id=1, source_target_pairs={{0,8},{2,10},{4,12},{6,14},{8,0},{10,2},{12,4},{14,6},{16,24},{18,... | collective-permute-start | bytes 1572872 | tf_op jit(solution)/shard_map/ppermute | solution.py:456
  242.1 54.6 %collective-permute-start.13 = (bf16[8,64,768]{2,1,0:T(8,128)(2,1)}, bf16[8,64,768]{2,1,0:T(8,128)(2,1)S(1)}, u32[]{:S(2)}, u32[]{:S(2)}) collective-permute-start(bf16[8,64,768]{2,1,0:T(8,128)(2,1)} %get-tuple-element.107), channel_id=1, source_target_pairs={{0,4},{2,6},{4,0},{6,2},{8,12},{10,14},{12,8},{14,10},{16,20},{18,... | collective-permute-start | bytes 2359304 | tf_op jit(solution)/shard_map/ppermute | solution.py:456
  242.8 0.8 copy-start.9
  246.8 7.6 %copy-start.26 = (f32[1,2048]{1,0:T(1,128)S(1)}, f32[1,2048]{1,0:T(1,128)}, u32[]{:S(2)}) copy-start(f32[1,2048]{1,0:T(1,128)} %get-tuple-element.96) | copy-start | bytes 24580
  246.8 25.0 %collective-permute-start.19 = (bf16[4,64,512]{2,1,0:T(8,128)(2,1)}, bf16[4,64,512]{2,1,0:T(8,128)(2,1)S(1)}, u32[]{:S(2)}, u32[]{:S(2)}) collective-permute-start(bf16[4,64,512]{2,1,0:T(8,128)(2,1)} %get-tuple-element.117), channel_id=1, source_target_pairs={{0,2},{2,0},{4,6},{6,4},{8,10},{10,8},{12,14},{14,12},{16,18},{18,... | collective-permute-start | bytes 786440 | tf_op jit(solution)/shard_map/ppermute | solution.py:456
  248.8 0.9 copy-start.6
  253.2 49.2 %collective-permute-start.10 = (bf16[4,64,768]{2,1,0:T(8,128)(2,1)}, bf16[4,64,768]{2,1,0:T(8,128)(2,1)S(1)}, u32[]{:S(2)}, u32[]{:S(2)}) collective-permute-start(bf16[4,64,768]{2,1,0:T(8,128)(2,1)} %get-tuple-element.101), channel_id=1, source_target_pairs={{0,4},{2,6},{4,0},{6,2},{8,12},{10,14},{12,8},{14,10},{16,20},{18,... | collective-permute-start | bytes 1179656 | tf_op jit(solution)/shard_map/ppermute | solution.py:456
  254.6 0.8 copy-start.7
  257.5 48.8 %collective-permute-start.30 = (bf16[1,64,2048]{2,1,0:T(8,128)(2,1)}, bf16[1,64,2048]{2,1,0:T(8,128)(2,1)S(1)}, u32[]{:S(2)}, u32[]{:S(2)}) collective-permute-start(bf16[1,64,2048]{2,1,0:T(8,128)(2,1)} %get-tuple-element.137), channel_id=1, source_target_pairs={{0,16},{2,18},{4,20},{6,22},{8,24},{10,26},{12,28},{14,30},{16,0},... | collective-permute-start | bytes 786440 | tf_op jit(solution)/shard_map/ppermute | solution.py:456
  268.9 0.8 copy-start.8
  271.7 60.9 %collective-permute-start.27 = (bf16[1,64,2048]{2,1,0:T(8,128)(2,1)}, bf16[1,64,2048]{2,1,0:T(8,128)(2,1)S(1)}, u32[]{:S(2)}, u32[]{:S(2)}) collective-permute-start(bf16[1,64,2048]{2,1,0:T(8,128)(2,1)} %get-tuple-element.129), channel_id=1, source_target_pairs={{0,16},{2,18},{4,20},{6,22},{8,24},{10,26},{12,28},{14,30},{16,0},... | collective-permute-start | bytes 786440 | tf_op jit(solution)/shard_map/ppermute | solution.py:456
  271.7 0.7 copy-start.15
  274.2 18.0 %collective-permute-start.20 = (bf16[2,64,512]{2,1,0:T(8,128)(2,1)}, bf16[2,64,512]{2,1,0:T(8,128)(2,1)S(1)}, u32[]{:S(2)}, u32[]{:S(2)}) collective-permute-start(bf16[2,64,512]{2,1,0:T(8,128)(2,1)} %get-tuple-element.119), channel_id=1, source_target_pairs={{0,4},{2,6},{4,0},{6,2},{8,12},{10,14},{12,8},{14,10},{16,20},{18,... | collective-permute-start | bytes 393224 | tf_op jit(solution)/shard_map/ppermute | solution.py:456
  287.3 19.8 %all-to-all-start.2 = ((f32[16,2,384]{2,1,0:T(2,128)}), f32[16,2,384]{2,1,0:T(2,128)S(1)}, u32[]{:S(2)}, u32[]{:S(2)}) async-start(f32[16,2,384]{2,1,0:T(2,128)} %concatenate.24), calls=%async_computation.2 | async-start | bytes 98304 | tf_op jit(solution)/shard_map/all_to_all | solution.py:770
  292.2 0.7 copy-start.20
  294.4 21.6 %collective-permute-start.21 = (bf16[1,64,512]{2,1,0:T(8,128)(2,1)}, bf16[1,64,512]{2,1,0:T(8,128)(2,1)S(1)}, u32[]{:S(2)}, u32[]{:S(2)}) collective-permute-start(bf16[1,64,512]{2,1,0:T(8,128)(2,1)} %get-tuple-element.121), channel_id=1, source_target_pairs={{0,16},{2,18},{4,20},{6,22},{8,24},{10,26},{12,28},{14,30},{16,0},... | collective-permute-start | bytes 196616 | tf_op jit(solution)/shard_map/ppermute | solution.py:456
  296.7 0.9 copy-start.5
  297.6 8.6 %copy-start.23 = (bf16[1,64,2048]{2,1,0:T(8,128)(2,1)S(1)}, bf16[1,64,2048]{2,1,0:T(8,128)(2,1)}, u32[]{:S(2)}) copy-start(bf16[1,64,2048]{2,1,0:T(8,128)(2,1)} %get-tuple-element.136) | copy-start | bytes 786436
  301.2 9.1 %collective-permute-start.14 = (bf16[4,64,768]{2,1,0:T(8,128)(2,1)}, bf16[4,64,768]{2,1,0:T(8,128)(2,1)S(1)}, u32[]{:S(2)}, u32[]{:S(2)}) collective-permute-start(bf16[4,64,768]{2,1,0:T(8,128)(2,1)} %get-tuple-element.109), channel_id=1, source_target_pairs={{0,2},{2,0},{4,6},{6,4},{8,10},{10,8},{12,14},{14,12},{16,18},{18,... | collective-permute-start | bytes 1179656 | tf_op jit(solution)/shard_map/ppermute | solution.py:456
  302.4 0.7 copy-start.13
  305.0 11.0 %copy-start.25 = (bf16[1,64,512]{2,1,0:T(8,128)(2,1)S(1)}, bf16[1,64,512]{2,1,0:T(8,128)(2,1)}, u32[]{:S(2)}) copy-start(bf16[1,64,512]{2,1,0:T(8,128)(2,1)} %get-tuple-element.120) | copy-start | bytes 196612
  305.0 8.3 %collective-permute-start.11 = (bf16[2,64,768]{2,1,0:T(8,128)(2,1)}, bf16[2,64,768]{2,1,0:T(8,128)(2,1)S(1)}, u32[]{:S(2)}, u32[]{:S(2)}) collective-permute-start(bf16[2,64,768]{2,1,0:T(8,128)(2,1)} %get-tuple-element.103), channel_id=1, source_target_pairs={{0,8},{2,10},{4,12},{6,14},{8,0},{10,2},{12,4},{14,6},{16,24},{18,... | collective-permute-start | bytes 589832 | tf_op jit(solution)/shard_map/ppermute | solution.py:456
  307.2 26.3 %collective-permute-start.6 = (f32[384]{0:T(512)S(1)}, f32[384]{0:T(512)S(1)}, u32[]{:S(2)}, u32[]{:S(2)}) collective-permute-start(f32[384]{0:T(512)S(1)} %get-tuple-element.143), channel_id=1, source_target_pairs={{0,1},{1,0},{2,3},{3,2},{4,5},{5,4},{6,7},{7,6},{8,9},{9,8},{10,11... | collective-permute-start | bytes 4616 | tf_op jit(solution)/shard_map/ppermute | solution.py:617
  310.3 0.7 copy-start.14
  313.0 4.7 %collective-permute-start.15 = (bf16[2,64,768]{2,1,0:T(8,128)(2,1)}, bf16[2,64,768]{2,1,0:T(8,128)(2,1)S(1)}, u32[]{:S(2)}, u32[]{:S(2)}) collective-permute-start(bf16[2,64,768]{2,1,0:T(8,128)(2,1)} %get-tuple-element.111), channel_id=1, source_target_pairs={{0,8},{2,10},{4,12},{6,14},{8,0},{10,2},{12,4},{14,6},{16,24},{18,... | collective-permute-start | bytes 589832 | tf_op jit(solution)/shard_map/ppermute | solution.py:456
  313.3 0.7 copy-start.16
  314.0 18.6 %copy-start.22 = (bf16[1,64,2048]{2,1,0:T(8,128)(2,1)S(1)}, bf16[1,64,2048]{2,1,0:T(8,128)(2,1)}, u32[]{:S(2)}) copy-start(bf16[1,64,2048]{2,1,0:T(8,128)(2,1)} %get-tuple-element.128) | copy-start | bytes 786436
  315.8 4.8 %collective-permute-start.12 = (bf16[1,64,768]{2,1,0:T(8,128)(2,1)}, bf16[1,64,768]{2,1,0:T(8,128)(2,1)S(1)}, u32[]{:S(2)}, u32[]{:S(2)}) collective-permute-start(bf16[1,64,768]{2,1,0:T(8,128)(2,1)} %get-tuple-element.105), channel_id=1, source_target_pairs={{0,16},{2,18},{4,20},{6,22},{8,24},{10,26},{12,28},{14,30},{16,0},... | collective-permute-start | bytes 294920 | tf_op jit(solution)/shard_map/ppermute | solution.py:456
  317.7 0.7 copy-start.17
  320.1 7.9 %collective-permute-start.16 = (bf16[1,64,768]{2,1,0:T(8,128)(2,1)}, bf16[1,64,768]{2,1,0:T(8,128)(2,1)S(1)}, u32[]{:S(2)}, u32[]{:S(2)}) collective-permute-start(bf16[1,64,768]{2,1,0:T(8,128)(2,1)} %get-tuple-element.113), channel_id=1, source_target_pairs={{0,16},{2,18},{4,20},{6,22},{8,24},{10,26},{12,28},{14,30},{16,0},... | collective-permute-start | bytes 294920 | tf_op jit(solution)/shard_map/ppermute | solution.py:456
  329.0 6.2 %collective-permute-start.22 = (f32[32,2048]{1,0:T(8,128)S(1)}, f32[32,2048]{1,0:T(8,128)S(1)}, u32[]{:S(2)}, u32[]{:S(2)}) collective-permute-start(f32[32,2048]{1,0:T(8,128)S(1)} %dynamic-slice_bitcast_fusion.2), channel_id=1, source_target_pairs={{0,1},{1,0},{2,3},{3,2},{4,5},{5,4},{6,7},{7,6},{8,9},{9,8},{10,11... | collective-permute-start | bytes 786440 | tf_op jit(solution)/shard_map/ppermute | solution.py:617
  335.2 2.2 copy-start.28
where the time goes:
time: 340 us; the launch traced here: 338 us
  Pallas kernels  164 us (48%)
  waiting for transfers between devices  74.9 us (22%)
  starting transfers between devices  55.3 us (16%)
  local copies, waits for them, and re-layouts  32 us (9%)
  other arithmetic  10.5 us (3%)
    pallas_call x1, Pallas kernels, one_head(): pl.pallas_call(partial(head_kernel, group=group, key_rows=key_rows, query...  59 us
    all_to_all x1, waiting for transfers between devices, per_device(): back = lax.all_to_all(from_head, 'seq', 0, 0, tiled=True)  39 us
    pallas_call x15, Pallas kernels, add_halves(): pl.pallas_call(add_kernel, grid_spec=pltpu.PrefetchScalarGridSpec(num_sca...  38.3 us
    ppermute x20, waiting for transfers between devices, seq_move(): return lax.ppermute(x, 'seq', [(s, s ^ 1 << bit) for s in range(members)])  33.1 us
    pallas_call x5, Pallas kernels, weight_halves(): pl.pallas_call(partial(weight_kernel, bit=bit, count=len(parts)), grid=(s...  23.6 us
    ppermute x20, starting transfers between devices, seq_move(): return lax.ppermute(x, 'seq', [(s, s ^ 1 << bit) for s in range(members)])  18.1 us
    pallas_call x1, Pallas kernels, feed(): pl.pallas_call(partial(feed_kernel, count=count, keep=keep), grid=(hidden...  17.3 us
    unnamed x62, local copies, waits for them, and re-layouts  17.1 us
  transfers between devices with their start and end apart: 34, of which 10 were waited for; matrix products, arithmetic and copies ran while one was open for 7% of the time, Pallas kernels for 28%

commit v1 on v0

v1 whole, which is shorter than its diff:
```python
from functools import partial

import jax
import jax.numpy as jnp
from jax import lax
from jax.experimental import pallas as pl
from jax.experimental.pallas import tpu as pltpu
from jax.sharding import PartitionSpec as P

HEADS = 16
HEAD = 64
ROT = 16
PAIR = 2 * HEAD
EPS = 1e-05
NEGATIVE = -1e30

F32 = jnp.float32
BF16 = jnp.bfloat16
NT = (((1,), (1,)), ((), ()))
NN = (((1,), (0,)), ((), ()))
VMEM_LIMIT = 60 * 1024 * 1024
COST_SHARE = 16


def dot32(a, b, dims=NN):
    return lax.dot_general(a, b, dims, preferred_element_type=F32)


def cost(flops, bytes_accessed, transcendentals):
    return pl.CostEstimate(
        flops=flops // COST_SHARE,
        bytes_accessed=bytes_accessed // COST_SHARE,
        transcendentals=transcendentals // COST_SHARE,
    )


def shape_of(shape, dtype):
    return jax.ShapeDtypeStruct(shape, dtype)


def fixed(shape):
    return pl.BlockSpec(shape, lambda *i: (0,) * len(shape))


def vector_row(ref):
    return ref[...].astype(F32).reshape(1, -1)


def two_heads(pair_a, pair_b, low):
    even = jnp.where(low, pair_a, pltpu.roll(pair_b, HEAD, 1))
    odd = jnp.where(low, pltpu.roll(pair_a, HEAD, 1), pair_b)
    return (even, odd)


def rotary_lanes(first, rows, inverse):
    shape = (rows, PAIR)
    lane = lax.broadcasted_iota(jnp.int32, shape, 1) % HEAD
    position = (lax.broadcasted_iota(jnp.int32, shape, 0) + first).astype(F32)
    angle = position * inverse
    cosine, sine = jnp.cos(angle), jnp.sin(angle)
    zero = jnp.zeros_like(sine)
    return (
        jnp.where(lane < ROT, cosine, 1.0),
        jnp.where(lane < ROT // 2, -sine, zero),
        jnp.where((lane >= ROT // 2) & (lane < ROT), sine, zero),
    )


def rotate_lanes(x, cosine, to_first, to_second):
    ahead = pltpu.roll(x, PAIR - ROT // 2, 1)
    behind = pltpu.roll(x, ROT // 2, 1)
    return x * cosine + ahead * to_first + behind * to_second


def unit_rows(x):
    average = jnp.mean(x, -1, keepdims=True)
    centred = x - average
    spread = jnp.mean(centred * centred, -1, keepdims=True)
    root = lax.rsqrt(spread + EPS)
    return (centred * root, root)


def open_kernel(
    first_ref, x_ref, g_ref, inv_ref, ga_ref, sa_ref, gf_ref, sf_ref, b_ref,
    wq_ref, wk_ref, wv_ref, wo_ref,
    out_ref, n1_ref, n2_ref, table_ref, n1t_ref, n2t_ref, gt_ref, bias_ref, *, parts,
):
    rows, width = x_ref.shape
    step = pl.program_id(0)
    cols = wq_ref.shape[1]

    @pl.when(step == 0)
    def _():
        unit, root = unit_rows(x_ref[...].astype(F32))
        n1_ref[...] = (unit * vector_row(ga_ref) + vector_row(sa_ref)).astype(BF16)
        n2_ref[...] = (unit * vector_row(gf_ref) + vector_row(sf_ref)).astype(BF16)
        for t, table in enumerate(rotary_lanes(first_ref[0], rows, inv_ref[...])):
            table_ref[t] = table
        bias_ref[...] = vector_row(b_ref)

    for at, source, target in ((1, n1_ref, n1t_ref), (2, n2_ref, n2t_ref), (3, g_ref, gt_ref)):

        @pl.when(step == at)
        def _(source=source, target=target):
            target[...] = jnp.transpose(source[...])

    def bias(third):
        return bias_ref[:, pl.ds(pl.multiple_of(third * width + step * cols, cols), cols)]

    normed = n1_ref[...]
    query = dot32(normed, wq_ref[...]) + bias(0)
    key = dot32(normed, wk_ref[...]) + bias(1)
    value = dot32(normed, wv_ref[...]) + bias(2)
    grad = dot32(g_ref[...], wo_ref[...], NT)
    tables = (table_ref[0], table_ref[1], table_ref[2])
    low = lax.broadcasted_iota(jnp.int32, (rows, PAIR), 1) < HEAD
    query_rows = rows // parts
    for c in range(cols // PAIR):
        cut = slice(c * PAIR, (c + 1) * PAIR)
        kv = two_heads(rotate_lanes(key[:, cut], *tables), value[:, cut], low)
        qg = two_heads(rotate_lanes(query[:, cut], *tables), grad[:, cut], low)
        for h in range(2):
            kv_h, qg_h = kv[h].astype(BF16), qg[h].astype(BF16)
            for p in range(parts):
                out_ref[2 * c + h, p, :rows] = kv_h
                out_ref[2 * c + h, p, rows:] = qg_h[p * query_rows : (p + 1) * query_rows]


def open_layer(x, g, first, vectors, weight, bias, out_weight, parts):
    rows, width = x.shape
    steps = 4
    cols = width // steps
    per = HEADS // steps
    inverse = 10000.0 ** (-(jnp.arange(ROT // 2, dtype=F32) * 2.0 / ROT))
    inverse = jnp.tile(inverse, PAIR // (ROT // 2)).reshape(1, PAIR)
    chunk = rows + rows // parts

    def third(t):
        return pl.BlockSpec((width, cols), lambda i: (0, t * steps + i))

    out, *others = pl.pallas_call(
        partial(open_kernel, parts=parts),
        grid=(steps,),
        out_shape=(
            shape_of((HEADS, parts, chunk, PAIR), BF16),
            shape_of((rows, width), BF16),
            shape_of((rows, width), BF16),
            shape_of((3, rows, PAIR), F32),
            shape_of((width, rows), BF16),
            shape_of((width, rows), BF16),
            shape_of((width, rows), BF16),
        ),
        in_specs=[
            pl.BlockSpec(memory_space=pltpu.SMEM),
            fixed((rows, width)),
            fixed((rows, width)),
            fixed((1, PAIR)),
            *[fixed((width,))] * 4,
            fixed((3 * width,)),
            third(0), third(1), third(2),
            pl.BlockSpec((cols, width), lambda i: (i, 0)),
        ],
        out_specs=(
            pl.BlockSpec((per, parts, chunk, PAIR), lambda i: (i, 0, 0, 0)),
            fixed((rows, width)),
            fixed((rows, width)),
            fixed((3, rows, PAIR)),
            fixed((width, rows)),
            fixed((width, rows)),
            fixed((width, rows)),
        ),
        scratch_shapes=[pltpu.VMEM((1, 3 * width), F32)],
        cost_estimate=cost(
            flops=8 * rows * width * width,
            bytes_accessed=8 * width * width + 18 * rows * width,
            transcendentals=0,
        ),
        compiler_params=pltpu.CompilerParams(vmem_limit_bytes=VMEM_LIMIT),
        name="open_layer",
    )(first, x, g, inverse, *vectors, bias, weight, weight, weight, out_weight)
    return (out.reshape(HEADS * parts, chunk, PAIR), *others)


ROW_GROUP = 4
ONES = 16
CUTS = 4
KEY_GROUP = 2


def first_tile(i):
    return i * (i + 1)


def column_chunks(x):
    return [x[:, c : c + 128] for c in range(0, x.shape[1], 128)]


def forward_kernel(
    part_ref, x_ref, y_ref, g_ref, d_ref, p_hbm,
    s_ref, p_ref, dv_ref, vt_ref, mx_ref, top_ref, acc_ref, sem,
    *, key_rows, query_rows,
):
    blocks = x_ref.shape[0] // ROW_GROUP
    keys, rows = KEY_GROUP * key_rows, ROW_GROUP * query_rows
    low = lax.broadcasted_iota(jnp.int32, (rows, PAIR), 1) < HEAD
    key_low = lax.broadcasted_iota(jnp.int32, (keys, PAIR), 1) < HEAD
    cuts = [slice(r, r + rows // CUTS) for r in range(0, rows, rows // CUTS)]

    def key_value(j):
        return x_ref[pl.ds(j * KEY_GROUP, KEY_GROUP), :key_rows, :].reshape(keys, PAIR)

    def query_rows_of(i):
        return x_ref[pl.ds(i * ROW_GROUP, ROW_GROUP), key_rows:, :].reshape(rows, PAIR)

    def query_of(i):
        return jnp.where(low, query_rows_of(i).astype(F32) * HEAD**-0.5, 0.0).astype(BF16)

    def copy_out(i, j):
        return pltpu.make_async_copy(p_ref.at[j], p_hbm.at[first_tile(i) + j], sem.at[j])

    def ones_and_values(j, unused):
        turned = jnp.transpose(key_value(j).astype(F32))
        vt_ref[j, :HEAD] = turned[HEAD:].astype(BF16)
        vt_ref[j, HEAD:] = jnp.ones((ONES, keys), BF16)
        return unused

    def raise_max(cut, s):
        mx = mx_ref[cut]
        for chunk in column_chunks(s):
            mx = jnp.maximum(mx, chunk)
        mx_ref[cut] = mx

    def last_scores(i, query):
        row = lax.broadcasted_iota(jnp.int32, (rows, keys), 0)
        col = lax.broadcasted_iota(jnp.int32, (rows, keys), 1)
        row_pos = (row // query_rows) * key_rows + row % query_rows + part_ref[0] * query_rows
        for d in range(ROW_GROUP // KEY_GROUP):
            j = 2 * i + d
            s = dot32(query, key_value(j), NT)
            s = jnp.where(col + d * keys <= row_pos, s, NEGATIVE)
            s_ref[j] = s
            raise_max(slice(None), s)

    def tile(i, j, query, grad_t):
        kv = key_value(j)
        grads = None
        for cut in cuts:
            if grad_t is not None:
                part = dot32(grad_t[:, cut], p_ref[j, cut])
                grads = part if grads is None else grads + part
            top = top_ref[cut]
            p = jnp.concatenate(
                [jnp.exp(c - top) for c in column_chunks(s_ref[j, cut])], 1
            ).astype(BF16)
            p_ref[j, cut] = p
            acc_ref[:, cut] += dot32(vt_ref[j], p, NT)
            if query is not None:
                s = dot32(query[cut], kv, NT)
                s_ref[j, cut] = s
                raise_max(cut, s)
        if grads is not None:
            dv_ref[j, HEAD:] += grads
        copy_out(i, j).start()

    def block(i, grad_t, ahead):
        query = query_of(i + 1) if ahead else None
        top_ref[...] = jnp.broadcast_to(jnp.max(mx_ref[...], -1, keepdims=True), (rows, PAIR))
        mx_ref[...] = jnp.full_like(mx_ref, NEGATIVE)
        acc_ref[...] = jnp.zeros_like(acc_ref)

        def step(j, unused):
            copy_out(i - 1, j).wait()
            tile(i, j, query, grad_t)
            return unused

        lax.fori_loop(0, 2 * i, step, 0)
        for d in range(2):
            tile(i, 2 * i + d, query, None)
        if ahead:
            last_scores(i + 1, query)
        inverse = 1.0 / acc_ref[HEAD : HEAD + 1]
        attended_t = acc_ref[:HEAD] * inverse
        rows_t = jnp.transpose(query_rows_of(i).astype(F32))
        grad_t = (rows_t[HEAD:] * inverse).astype(BF16)
        both = jnp.transpose(jnp.concatenate([attended_t, grad_t.astype(F32)], 0))
        delta = jnp.sum(grad_t.astype(F32) * attended_t, 0, keepdims=True)
        d_ref[i] = jnp.transpose(jnp.broadcast_to(delta, (PAIR, rows)))
        g_ref[i] = jnp.where(low, 0.0, both).astype(BF16)
        here = pl.ds(i * ROW_GROUP, ROW_GROUP)
        y_ref[here, :query_rows, :] = both.astype(BF16).reshape(ROW_GROUP, query_rows, PAIR)
        if query_rows < key_rows:
            y_ref[here, query_rows:, :] = jnp.zeros(
                (ROW_GROUP, key_rows - query_rows, PAIR), BF16
            )
        return grad_t

    dv_ref[...] = jnp.zeros_like(dv_ref)
    lax.fori_loop(0, 2 * blocks, ones_and_values, 0)
    mx_ref[...] = jnp.full_like(mx_ref, NEGATIVE)
    last_scores(0, query_of(0))
    grad_t = lax.fori_loop(
        0, blocks - 1, lambda i, g: block(i, g, True), jnp.zeros((HEAD, rows), BF16)
    )
    grad_t = block(jnp.int32(blocks - 1), grad_t, False)

    def finish(j, unused):
        here = pl.ds(j * KEY_GROUP, KEY_GROUP)
        held = y_ref[here].reshape(keys, PAIR)
        dv_ref[j, HEAD:] += dot32(grad_t, p_ref[j])
        grads = jnp.transpose(dv_ref[j]).astype(BF16)
        y_ref[here] = jnp.where(key_low, held, grads).reshape(KEY_GROUP, key_rows, PAIR)
        copy_out(blocks - 1, j).wait()
        return unused

    lax.fori_loop(0, 2 * blocks, finish, 0)


def backward_kernel(
    x_ref, g_ref, d_ref, p_hbm, y_ref, p_ref, dp0_ref, dp1_ref, dk_ref, acc_ref, sem,
    *, key_rows, query_rows,
):
    blocks = x_ref.shape[0] // ROW_GROUP
    keys, rows = KEY_GROUP * key_rows, ROW_GROUP * query_rows
    tiles = first_tile(blocks)
    slots = p_ref.shape[0]
    low = lax.broadcasted_iota(jnp.int32, (rows, PAIR), 1) < HEAD
    dp_refs = (dp0_ref, dp1_ref)

    def copy_in(t):
        return pltpu.make_async_copy(p_hbm.at[t], p_ref.at[t % slots], sem.at[t % slots])

    def refill(t):
        @pl.when(t + slots < tiles)
        def _():
            copy_in(t + slots).start()

    for t in range(min(slots, tiles)):
        copy_in(t).start()
    dk_ref[...] = jnp.zeros_like(dk_ref)

    def key_value(j):
        return x_ref[pl.ds(j * KEY_GROUP, KEY_GROUP), :key_rows, :].reshape(keys, PAIR)

    def one_block(i, unused):
        here = pl.ds(i * ROW_GROUP, ROW_GROUP)
        query = x_ref[here, key_rows:, :].reshape(rows, PAIR).astype(F32) * HEAD**-0.5
        query_t = jnp.transpose(query)[:HEAD].astype(BF16)
        grad = g_ref[i]
        first = first_tile(i)
        acc_ref[...] = jnp.zeros_like(acc_ref)

        def raise_probs(j, side):
            dp_refs[side][...] = dot32(grad, key_value(j), NT)

        def tile(j, side):
            delta = d_ref[i]
            p = column_chunks(p_ref[(first + j) % slots].astype(F32))
            dp = column_chunks(dp_refs[side][...])
            ds = jnp.concatenate([a * (b - delta) for a, b in zip(p, dp)], 1).astype(BF16)
            dk_ref[j, HEAD:] += dot32(query_t, ds)
            acc_ref[...] += dot32(ds, key_value(j))

        def two_tiles(m, unused, more=True):
            j = 2 * m
            copy_in(first + j).wait()
            copy_in(first + j + 1).wait()
            raise_probs(j + 1, 1)
            tile(j, 0)
            if more:
                raise_probs(j + 2, 0)
            tile(j + 1, 1)
            refill(first + j)
            refill(first + j + 1)
            return unused

        raise_probs(0, 0)
        lax.fori_loop(0, i, two_tiles, 0)
        two_tiles(i, 0, False)
        done = jnp.where(low, acc_ref[...] * HEAD**-0.5, 0.0).astype(BF16)
        y_ref[here, :query_rows, :] = done.reshape(ROW_GROUP, query_rows, PAIR)
        if query_rows < key_rows:
            y_ref[here, query_rows:, :] = jnp.zeros(
                (ROW_GROUP, key_rows - query_rows, PAIR), BF16
            )
        return unused

    lax.fori_loop(0, blocks, one_block, 0)
    key_low = lax.broadcasted_iota(jnp.int32, (keys, PAIR), 1) < HEAD

    def finish(j, unused):
        here = pl.ds(j * KEY_GROUP, KEY_GROUP)
        held = y_ref[here].reshape(keys, PAIR)
        grads = jnp.transpose(dk_ref[j]).astype(BF16)
        y_ref[here] = jnp.where(key_low, held, grads).reshape(KEY_GROUP, key_rows, PAIR)
        return unused

    lax.fori_loop(0, 2 * blocks, finish, 0)


def head_sizes(x, key_rows, query_rows):
    count = x.shape[0]
    blocks = count // ROW_GROUP
    return count, blocks, KEY_GROUP * key_rows, ROW_GROUP * query_rows


def forward_head(x, part, key_rows, query_rows, behind):
    count, blocks, keys, rows = head_sizes(x, key_rows, query_rows)
    tiles = first_tile(blocks)
    vmem = pl.BlockSpec(memory_space=pltpu.VMEM)
    return pl.pallas_call(
        without(
            partial(forward_kernel, key_rows=key_rows, query_rows=query_rows), 2, len(behind)
        ),
        out_shape=(
            shape_of((count, key_rows, PAIR), BF16),
            shape_of((blocks, rows, PAIR), BF16),
            shape_of((blocks, rows, PAIR), F32),
            shape_of((tiles, rows, keys), BF16),
        ),
        in_specs=[pl.BlockSpec(memory_space=pltpu.SMEM), vmem]
        + [pl.BlockSpec(memory_space=pl.ANY)] * len(behind),
        out_specs=(vmem, vmem, vmem, pl.BlockSpec(memory_space=pl.ANY)),
        scratch_shapes=[
            pltpu.VMEM((2 * blocks, rows, keys), F32),
            pltpu.VMEM((2 * blocks, rows, keys), BF16),
            pltpu.VMEM((2 * blocks, PAIR, keys), F32),
            pltpu.VMEM((2 * blocks, HEAD + ONES, keys), BF16),
            pltpu.VMEM((rows, PAIR), F32),
            pltpu.VMEM((rows, PAIR), F32),
            pltpu.VMEM((HEAD + ONES, rows), F32),
            pltpu.SemaphoreType.DMA((2 * blocks,)),
        ],
        cost_estimate=cost(
            flops=tiles * rows * keys * 2 * 256 * 3,
            bytes_accessed=4 * x.size + 2 * tiles * rows * keys,
            transcendentals=tiles * rows * keys,
        ),
        compiler_params=pltpu.CompilerParams(vmem_limit_bytes=VMEM_LIMIT),
        name="forward_head",
    )(part, x, *behind)


def backward_head(x, grad, delta, probs, key_rows, query_rows):
    count, blocks, keys, rows = head_sizes(x, key_rows, query_rows)
    tiles = first_tile(blocks)
    slots = 6
    vmem = pl.BlockSpec(memory_space=pltpu.VMEM)
    return pl.pallas_call(
        partial(backward_kernel, key_rows=key_rows, query_rows=query_rows),
        out_shape=shape_of((count, key_rows, PAIR), BF16),
        in_specs=[vmem, vmem, vmem, pl.BlockSpec(memory_space=pl.ANY)],
        out_specs=vmem,
        scratch_shapes=[
            pltpu.VMEM((slots, rows, keys), BF16),
            pltpu.VMEM((rows, keys), F32),
            pltpu.VMEM((rows, keys), F32),
            pltpu.VMEM((2 * blocks, PAIR, keys), F32),
            pltpu.VMEM((rows, PAIR), F32),
            pltpu.SemaphoreType.DMA((slots,)),
        ],
        cost_estimate=cost(
            flops=tiles * rows * keys * 2 * 256 * 3,
            bytes_accessed=4 * x.size + 2 * tiles * rows * keys,
            transcendentals=0,
        ),
        compiler_params=pltpu.CompilerParams(vmem_limit_bytes=VMEM_LIMIT),
        name="backward_head",
    )(x, grad, delta, probs)


def feed_kernel(*refs, count, keep):
    rows_refs, cot_refs = refs[:count], refs[count : 2 * count]
    w1_ref, b1_ref, w2_ref = refs[2 * count : 2 * count + 3]
    hid_ref, gpre_ref, gb_ref = refs[2 * count + 3 : 2 * count + 6]
    outs = refs[2 * count + 6 : -2]
    out_acc, grad_acc = refs[-2:]
    step = pl.program_id(0)

    @pl.when(step == 0)
    def _():
        out_acc[...] = jnp.zeros_like(out_acc)
        grad_acc[...] = jnp.zeros_like(grad_acc)

    bias = b1_ref[...]
    sums = jnp.zeros_like(bias)
    rows = rows_refs[0].shape[0]
    for r in range(count):
        here = slice(r * rows, (r + 1) * rows)
        pre = dot32(rows_refs[r][...], w1_ref[...]) + bias
        grad = dot32(cot_refs[r][...], w2_ref[...], NT)
        cdf = 0.5 + 0.5 * lax.erf(pre * (0.5**0.5))
        density = jnp.exp(-0.5 * pre * pre) * 0.3989422804014327
        hidden = (pre * cdf).astype(BF16)
        grad_pre = (grad * (cdf + pre * density)).astype(BF16)
        hid_ref[here] = hidden
        gpre_ref[here] = grad_pre
        sums = sums + jnp.sum(grad_pre.astype(F32), 0, keepdims=True)
        out_acc[here] += dot32(hidden, w2_ref[...])
        grad_acc[here] += dot32(grad_pre, w1_ref[...], NT)
    gb_ref[...] = sums

    @pl.when(step == pl.num_programs(0) - 1)
    def _():
        if keep:
            own_out, own_grad, other_out, other_grad = outs
            own_out[...] = out_acc[:rows]
            own_grad[...] = grad_acc[:rows]
            other_out[...] = out_acc[rows:].astype(BF16)
            other_grad[...] = grad_acc[rows:].astype(BF16)
        else:
            outs[0][...] = out_acc[...].astype(BF16)
            outs[1][...] = grad_acc[...].astype(BF16)


def feed(rows_list, cot_list, w1, b1, w2):
    width, hidden = w1.shape
    count = len(rows_list)
    rows = rows_list[0].shape[0]
    total = rows * count
    block = 256
    keep = count > 1
    sides = (
        [(rows, F32), (rows, F32), (total - rows, BF16), (total - rows, BF16)]
        if keep
        else [(total, BF16), (total, BF16)]
    )
    once = pl.Buffered(1)
    whole = pl.BlockSpec((rows, width), lambda i: (0, 0), pipeline_mode=once)
    return pl.pallas_call(
        partial(feed_kernel, count=count, keep=keep),
        grid=(hidden // block,),
        out_shape=(
            shape_of((total, hidden), BF16),
            shape_of((total, hidden), BF16),
            shape_of((1, hidden), F32),
            *[shape_of((r, width), d) for r, d in sides],
        ),
        in_specs=[
            *[whole] * (2 * count),
            pl.BlockSpec((width, block), lambda i: (0, i)),
            pl.BlockSpec((1, block), lambda i: (0, i)),
            pl.BlockSpec((block, width), lambda i: (i, 0)),
        ],
        out_specs=(
            pl.BlockSpec((total, block), lambda i: (0, i)),
            pl.BlockSpec((total, block), lambda i: (0, i)),
            pl.BlockSpec((1, block), lambda i: (0, i)),
            *[
                pl.BlockSpec((r, width), lambda i: (0, 0), pipeline_mode=once) for r, d in sides
            ],
        ),
        scratch_shapes=[pltpu.VMEM((total, width), F32), pltpu.VMEM((total, width), F32)],
        cost_estimate=cost(
            flops=8 * total * width * hidden,
            bytes_accessed=4 * width * hidden + 4 * total * hidden,
            transcendentals=2 * total * hidden,
        ),
        compiler_params=pltpu.CompilerParams(vmem_limit_bytes=VMEM_LIMIT),
        name="feed",
    )(*rows_list, *cot_list, w1, b1.astype(F32).reshape(1, hidden), w2)


def insert_bits(k, positions, values):
    for position, value in zip(positions, values):
        k = ((k >> position) << (position + 1)) + (value << position) + (k & ((1 << position) - 1))
    return k


def part_chunk(k, p, me, ring_bits, positions):
    values = [((me >> bit) & 1) ^ ((p >> n) & 1) for n, bit in enumerate(ring_bits)]
    return insert_bits(k, positions, values)


def weight_kernel(me_ref, *refs, bits, counts):
    total = sum(counts)
    a_refs, b_refs, parts = refs[:total], refs[total : 2 * total], refs[2 * total :]

    def product(first, count):
        b = jnp.concatenate([r[...] for r in b_refs[first : first + count]], 0)
        for p, ref in enumerate(parts):
            chunks, rows, cols = ref.shape
            a = []
            for k in range(chunks):
                start = part_chunk(k, p, me_ref[0], bits, bits) * rows
                here = pl.ds(pl.multiple_of(start, rows), rows)
                a.append(
                    jnp.concatenate([r[here, :] for r in a_refs[first : first + count]], 1)
                )
            ref[...] = dot32(jnp.concatenate(a, 0), b).astype(BF16).reshape(ref.shape)

    if len(counts) == 1:
        product(0, total)
    else:
        for n, count in enumerate(counts):
            pl.when(pl.program_id(0) == n)(partial(product, sum(counts[:n]), count))


def weight_parts(scalars, products, steps, block, members, bits):
    a_runs = [run for a, _ in products for run in a]
    b_runs = [run for _, b in products for run in b]
    width = a_runs[0][1][0]
    rows = width // members
    tokens = sum(shape[1] for _, shape, _ in products[0][0])
    count = 1 << len(bits)
    each = (members // count, rows, steps * block)
    out = pl.BlockSpec((members // count, rows, block), lambda i, me: (0, 0, i))
    return pl.pallas_call(
        partial(weight_kernel, bits=bits, counts=[len(a) for a, _ in products]),
        grid_spec=pltpu.PrefetchScalarGridSpec(
            num_scalar_prefetch=1,
            grid=(steps,),
            in_specs=[pl.BlockSpec(shape, index) for _, shape, index in (*a_runs, *b_runs)],
            out_specs=[out] * count,
        ),
        out_shape=[shape_of(each, BF16)] * count,
        cost_estimate=cost(
            flops=2 * width * tokens * steps * block,
            bytes_accessed=2 * width * tokens + 2 * (width + tokens) * steps * block,
            transcendentals=0,
        ),
        compiler_params=pltpu.CompilerParams(vmem_limit_bytes=VMEM_LIMIT),
        name="weight_parts",
    )(scalars, *[array for array, _, _ in (*a_runs, *b_runs)])


def weight_once_kernel(me_ref, *refs, bits, forms):
    total = len(forms)
    a_refs, b_refs, parts = refs[:total], refs[total : 2 * total], refs[2 * total : -1]
    cols = parts[0].shape[2]
    for n in range(2):
        refs[-1][n] = me_ref[n]

    def run(ref, form):
        if form == "turned":
            return ref[...]
        start = pl.multiple_of(form(me_ref) * cols, cols)
        return ref[:, pl.ds(start, cols)]

    turned = forms[0] == "turned"
    b = jnp.concatenate([run(r, f) for r, f in zip(b_refs, forms)], 1 if turned else 0)
    for p, ref in enumerate(parts):
        chunks, rows, _ = ref.shape
        a = []
        for k in range(chunks):
            start = part_chunk(k, p, me_ref[0], bits, bits) * rows
            here = pl.ds(pl.multiple_of(start, rows), rows)
            a.append(jnp.concatenate([r[here, :] for r in a_refs], 1))
        product = dot32(jnp.concatenate(a, 0), b, NT if turned else NN)
        ref[...] = product.astype(BF16).reshape(ref.shape)


def weight_once(scalars, a_list, b_list, forms, cols, members, bits, behind=()):
    width = a_list[0].shape[0]
    count = 1 << len(bits)
    each = shape_of((members // count, width // members, cols), BF16)
    return vmem_call(
        partial(weight_once_kernel, bits=bits, forms=forms),
        [each] * count + [shape_of((2,), jnp.int32)],
        scalars,
        [*a_list, *b_list],
        "weight_once",
        behind,
    )


def column_sums(refs, counts):
    groups, start = [], 0
    for count in counts:
        groups.append(refs[start : start + count])
        start += count

    def total(group, c):
        value = group[0][c].astype(F32)
        for ref in group[1:]:
            value = value + ref[c].astype(F32)
        return value

    return [partial(total, group) for group in groups]


def add_kernel(me_ref, *refs, counts, bits, positions):
    ins, outs = refs[: sum(counts)], refs[sum(counts) :]
    at = 0
    for group, total in zip(counts, column_sums(ins, counts)):
        cols = ins[0].shape[2]
        for p, ref in enumerate(outs):
            for k in range(ref.shape[0]):
                c = part_chunk(k, p, me_ref[0], bits, positions)
                ref[k, :, at : at + cols] = total(c).astype(BF16)
        at += cols
        ins = ins[group:]


def last_kernel(me_ref, *refs, count, form):
    value = column_sums(refs[:count], [count])[0](0)
    outs = refs[count:]
    if form == "pair":
        half = value.shape[0] // 2
        first = me_ref[1] == 0
        outs[0][...] = jnp.where(first, value[:half], value[half:])
        outs[1][...] = jnp.where(first, value[half:], value[:half]).astype(BF16)
    else:
        at = 0
        for ref in outs:
            ref[...] = value[:, at : at + ref.shape[1]]
            at += ref.shape[1]


def without(kernel, first, count):
    if not count:
        return kernel
    return lambda *refs: kernel(*refs[:first], *refs[first + count :])


def vmem_call(kernel, out_shape, scalars, arrays, name, behind=()):
    vmem = pl.BlockSpec(memory_space=pltpu.VMEM)
    size = sum(a.size for a in arrays)
    return pl.pallas_call(
        without(kernel, 1 + len(arrays), len(behind)),
        in_specs=[pl.BlockSpec(memory_space=pltpu.SMEM)]
        + [vmem] * len(arrays)
        + [pl.BlockSpec(memory_space=pl.ANY)] * len(behind),
        out_specs=[
            pl.BlockSpec(memory_space=pltpu.SMEM) if o.dtype == jnp.int32 else vmem
            for o in out_shape
        ],
        out_shape=out_shape,
        cost_estimate=cost(flops=size, bytes_accessed=3 * size, transcendentals=0),
        compiler_params=pltpu.CompilerParams(vmem_limit_bytes=VMEM_LIMIT),
        name=name,
    )(scalars, *arrays, *behind)


def seq_move(x, mask):
    members = lax.axis_size("seq")
    return lax.ppermute(x, "seq", [(s, s ^ mask) for s in range(members)])


def ring_stages(stages):
    bits = lax.axis_size("seq").bit_length() - 1
    named = [b for stage in stages for b in stage]
    stages = [tuple(b for b in stage if b < bits) for stage in stages]
    stages[-1] = stages[-1] + tuple(b for b in range(bits) if b not in named)
    return [stage for stage in stages if stage]


class Ring:
    def __init__(self, scalars, parts, stages):
        self.scalars, self.stages, self.behind = scalars, list(stages), ()
        self.me = scalars[0]
        self.left = sorted(b for stage in stages for b in stage)
        self.travel(parts)

    def travel(self, parts):
        stage = self.stages.pop(0)
        self.left = [b for b in self.left if b not in stage]
        self.keep, self.sent = parts[0], parts[1:]
        self.came = [
            seq_move(part, sum(1 << b for n, b in enumerate(stage) if (p >> n) & 1))
            for p, part in enumerate(parts)
            if p
        ]

    def hold(self, *others):
        self.behind = others

    def step(self, *others):
        stage = self.stages[0]
        positions = [self.left.index(b) for b in stage]
        rings = (self, *others)
        chunks, rows = self.keep.shape[:2]
        cols = sum(ring.keep.shape[2] for ring in rings)
        count = 1 << len(stage)
        arrays = [[ring.keep, *ring.came] for ring in rings]
        self.travel(
            vmem_call(
                partial(
                    add_kernel, counts=[len(a) for a in arrays], bits=stage, positions=positions
                ),
                [shape_of((chunks // count, rows, cols), BF16)] * count,
                self.scalars,
                [a for group in arrays for a in group],
                "add_parts",
                self.behind,
            )
        )
        self.behind = ()

    def pass_on(self, me):
        stage = self.stages[0]
        bits = self.left
        shape = self.keep.shape[1:]
        arrays = [a.reshape((2,) * len(bits) + shape) for a in (self.keep, *self.came)]
        parts = []
        for p in range(1 << len(stage)):
            total = None
            for a in arrays:
                for n, bit in reversed(list(enumerate(stage))):
                    axis = len(bits) - 1 - bits.index(bit)
                    index = ((me >> bit) & 1) ^ ((p >> n) & 1)
                    a = lax.dynamic_index_in_dim(a, index, axis, True)
                a = a.reshape((-1,) + shape).astype(F32)
                total = a if total is None else total + a
            parts.append(total.astype(BF16))
        self.travel(parts)

    def total(self, widths=None):
        while self.stages:
            self.step()
        rows, cols = self.keep.shape[1:]
        shapes = (
            [shape_of((rows, w), F32) for w in widths]
            if widths
            else [shape_of((rows // 2, cols), F32), shape_of((rows // 2, cols), BF16)]
        )
        arrays = [self.keep, *self.came]
        return vmem_call(
            partial(last_kernel, count=len(arrays), form="rows" if widths else "pair"),
            shapes,
            self.scalars,
            arrays,
            "last_sum",
        )


def regroup_kernel(me_ref, back_ref, *refs, key_rows, query_rows, turned):
    heads, parts = back_ref.shape[:2]
    low = lax.broadcasted_iota(jnp.int32, (key_rows, PAIR), 1) < HEAD
    if turned:
        one_ref, two_ref, one_t_ref, *sides = refs
    else:
        table_ref, one_ref, two_ref, *sides = refs
        tables = (table_ref[0], -table_ref[1], -table_ref[2])
    first = pl.program_id(0) == 0
    for t in range(heads // 2):
        pair = []
        for h in (2 * t, 2 * t + 1):
            if parts == 1:
                pair.append(back_ref[h, 0].astype(F32))
                continue
            keys = sum(back_ref[h, p].astype(F32) for p in range(parts))
            queries = jnp.concatenate(
                [back_ref[h, p, :query_rows].astype(F32) for p in range(parts)], 0
            )
            pair.append(jnp.where(low, queries, keys))
        one, two = two_heads(pair[0], pair[1], low)
        if not turned:
            one, two = rotate_lanes(one, *tables), rotate_lanes(two, *tables)
        one, two = one.astype(BF16), two.astype(BF16)
        here = slice(t * PAIR, (t + 1) * PAIR)
        one_ref[:, here] = one
        two_ref[:, here] = two
        if turned:
            one_t_ref[here] = jnp.transpose(one)
        if sides:
            half = one_ref.shape[1]
            for n, value in enumerate((two,) if turned else (one, two)):
                there = slice(n * half + t * PAIR, n * half + (t + 1) * PAIR)
                pl.when(first)(partial(sides[1].__setitem__, (slice(None), there), value))
                pl.when(~first)(partial(sides[0].__setitem__, (slice(None), there), value))


def regroup(back, table, scalars, rows, query_rows, split):
    turned = table is None
    chunk = back.shape[1]
    parts = back.shape[0] // HEADS
    half = HEADS * HEAD // 2
    full = shape_of((rows, 2 * half), BF16)

    def side(i, me):
        return (i + me[1] + 1) % 2 if split else i

    whole = pl.BlockSpec((rows, half), lambda i, me: (0, side(i, me)))
    tall = pl.BlockSpec((half, rows), lambda i, me: (side(i, me), 0))
    cols = half * (1 if turned else 2)
    own = pl.BlockSpec((rows, cols), lambda i, me: (0, 0))
    return pl.pallas_call(
        partial(regroup_kernel, key_rows=rows, query_rows=query_rows, turned=turned),
        grid_spec=pltpu.PrefetchScalarGridSpec(
            num_scalar_prefetch=1,
            grid=(2,),
            in_specs=[
                pl.BlockSpec(
                    (HEADS // 2, parts, chunk, PAIR), lambda i, me: (side(i, me), 0, 0, 0)
                )
            ]
            + ([] if turned else [pl.BlockSpec(table.shape, lambda i, me: (0, 0, 0))]),
            out_specs=[whole, whole] + ([tall] if turned else []) + ([own, own] if split else []),
        ),
        out_shape=[full, full]
        + ([shape_of((2 * half, rows), BF16)] if turned else [])
        + ([shape_of((rows, cols), BF16)] * 2 if split else []),
        cost_estimate=cost(
            flops=back.size, bytes_accessed=4 * back.size, transcendentals=0
        ),
        name="regroup",
    )(
        scalars,
        back.reshape(HEADS, parts, chunk, PAIR),
        *([] if turned else [table]),
    )


def regroup_once_kernel(me_ref, *refs, turned):
    if turned:
        back_ref, att_ref, v_ref, send_ref, own_a_ref, own_v_ref = refs
    else:
        back_ref, table_ref, q_ref, k_ref, send_ref, own_ref = refs
        tables = (table_ref[0], -table_ref[1], -table_ref[2])
    heads, rows = back_ref.shape[:2]
    half = heads // 2
    low = lax.broadcasted_iota(jnp.int32, (rows, PAIR), 1) < HEAD
    for side in range(2):
        first = ((me_ref[1] + side) % 2) * half
        for t in range(half // 2):
            pair = [back_ref[first + 2 * t + n].astype(F32) for n in range(2)]
            one, two = two_heads(pair[0], pair[1], low)
            if not turned:
                one, two = rotate_lanes(one, *tables), rotate_lanes(two, *tables)
            one, two = one.astype(BF16), two.astype(BF16)
            start = pl.multiple_of((first // 2 + t) * PAIR, PAIR)
            here = pl.ds(start, PAIR)
            local = slice(t * PAIR, (t + 1) * PAIR)
            width = half * HEAD
            if turned:
                att_ref[:, here] = one
                v_ref[:, here] = two
                turned_one, turned_two = jnp.transpose(one), jnp.transpose(two)
                own_a_ref[here] = turned_one
                send_ref[here] = turned_one
                if side == 0:
                    own_v_ref[local] = turned_two
                else:
                    send_ref[2 * width + t * PAIR : 2 * width + (t + 1) * PAIR] = turned_two
            else:
                q_ref[:, here] = one
                k_ref[:, here] = two
                ref = own_ref if side == 0 else send_ref
                ref[:, local] = one
                ref[:, width + t * PAIR : width + (t + 1) * PAIR] = two


def regroup_once(back, table, scalars, behind=()):
    rows = back.shape[1]
    full = shape_of((rows, HEADS * HEAD), BF16)
    half = HEADS * HEAD // 2
    if table is None:
        sides = [
            shape_of((3 * half, rows), BF16),
            shape_of((2 * half, rows), BF16),
            shape_of((half, rows), BF16),
        ]
    else:
        sides = [shape_of((rows, 2 * half), BF16)] * 2
    return vmem_call(
        partial(regroup_once_kernel, turned=table is None),
        [full, full, *sides],
        scalars,
        [back] if table is None else [back, table],
        "regroup_once",
        behind,
    )


def close_kernel(
    x_ref, g_ref, ga_ref, gf_ref, bo_ref, bc_ref, gq_ref, gk_ref, gv_ref, att_ref,
    wq_ref, wk_ref, wv_ref, wo_ref, me_ref, *refs, sides,
):
    feeds, grads = refs[:sides], refs[sides : 2 * sides]
    out_ref, gin_ref, vec_ref, gb_ref, after_ref, out_acc, grad_acc = refs[2 * sides :]
    step = pl.program_id(0)
    for n in range(2):
        after_ref[n] = me_ref[n]

    @pl.when(step == 0)
    def _():
        out_acc[...] = jnp.zeros_like(out_acc)
        grad_acc[...] = jnp.zeros_like(grad_acc)

    out_acc[...] += dot32(att_ref[...], wo_ref[...])
    total = None
    for third, (g_third, w_ref) in enumerate(
        ((gq_ref, wq_ref), (gk_ref, wk_ref), (gv_ref, wv_ref))
    ):
        grad = g_third[...]
        part = dot32(grad, w_ref[...], NT)
        total = part if total is None else total + part
        gb_ref[third : third + 1] = jnp.sum(grad.astype(F32), 0, keepdims=True)
    grad_acc[...] += total

    @pl.when(step == pl.num_programs(0) - 1)
    def _():
        x = x_ref[...].astype(F32)
        g = g_ref[...].astype(F32)
        total = x + out_acc[...] + vector_row(bo_ref) + vector_row(bc_ref)
        for ref in feeds:
            total = total + ref[...].astype(F32)
        out_ref[...] = total.astype(BF16)
        unit, root = unit_rows(x)
        one = grad_acc[...]
        two = grads[0][...].astype(F32)
        for ref in grads[1:]:
            two = two + ref[...].astype(F32)
        down = one * vector_row(ga_ref) + two * vector_row(gf_ref)
        mean = jnp.mean(down, -1, keepdims=True)
        slope = jnp.mean(down * unit, -1, keepdims=True)
        gin_ref[...] = g + root * (down - mean - unit * slope)
        for r, rows in enumerate((one * unit, one, g, two * unit, two)):
            vec_ref[r : r + 1] = jnp.sum(rows, 0, keepdims=True)


def close_layer(x, g, vectors, gm, attended, weight, out_weight, feeds, grads, scalars, behind):
    rows, width = x.shape
    steps = 4
    cols = width // steps

    def third(t):
        return pl.BlockSpec((width, cols), lambda i: (0, t * steps + i))

    part = pl.BlockSpec((rows, cols), lambda i: (0, i))
    return pl.pallas_call(
        without(partial(close_kernel, sides=len(feeds)), 15 + 2 * len(feeds), len(behind)),
        grid=(steps,),
        out_shape=(
            shape_of((rows, width), BF16),
            shape_of((rows, width), F32),
            shape_of((5, width), F32),
            shape_of((3, width), F32),
            shape_of((2,), jnp.int32),
        ),
        in_specs=[
            fixed((rows, width)),
            fixed((rows, width)),
            *[fixed((width,))] * 4,
            part, part, part, part,
            third(0), third(1), third(2),
            pl.BlockSpec((cols, width), lambda i: (i, 0)),
            pl.BlockSpec(memory_space=pltpu.SMEM),
            *[fixed((rows, width))] * (2 * len(feeds)),
            *[pl.BlockSpec(memory_space=pl.ANY)] * len(behind),
        ],
        out_specs=(
            fixed((rows, width)),
            fixed((rows, width)),
            fixed((5, width)),
            pl.BlockSpec((3, cols), lambda i: (0, i)),
            pl.BlockSpec(memory_space=pltpu.SMEM),
        ),
        scratch_shapes=[pltpu.VMEM((rows, width), F32), pltpu.VMEM((rows, width), F32)],
        cost_estimate=cost(
            flops=8 * rows * width * width,
            bytes_accessed=8 * width * width + 24 * rows * width,
            transcendentals=0,
        ),
        compiler_params=pltpu.CompilerParams(vmem_limit_bytes=VMEM_LIMIT),
        name="close_layer",
    )(x, g, *vectors, *gm, attended, weight, weight, weight, out_weight, scalars, *feeds, *grads, *behind)


def place_kernel(me_ref, own_ref, came_ref, merged_ref, dense_ref):
    half = dense_ref.shape[1] // 2
    for side, ref in enumerate((own_ref, came_ref)):
        at = ((me_ref[1] + side) % 2) * half
        for third in range(3):
            start = pl.multiple_of(third * 2 * half + at, half)
            value = ref[:, third * half : (third + 1) * half]
            merged_ref[:, pl.ds(start, half)] = value.astype(F32)
        dense_ref[:, pl.ds(pl.multiple_of(at, half), half)] = ref[:, 3 * half :].astype(F32)


def pair_swap(x):
    return lax.ppermute(x, "mlp", [(0, 1), (1, 0)])


def mlp_list(x, axis=0):
    if lax.axis_size("mlp") == 2:
        return [x, pair_swap(x)]
    return [lax.all_gather(x, "mlp", axis=axis, tiled=True)]


def after(value, *others):
    return lax.optimization_barrier((value, *others))[0]


def per_device(
    block_input,
    out_cotangent,
    attend_gain,
    attend_shift,
    query_key_value_weight,
    query_key_value_bias,
    attention_out_weight,
    attention_out_bias,
    feed_gain,
    feed_shift,
    expand_weight,
    expand_bias,
    contract_weight,
    contract_bias,
):
    seq_count, rows, width = block_input.shape
    members = lax.axis_size("seq")
    pairs = lax.axis_size("mlp")
    parts = members // HEADS
    own = width // members
    me = lax.axis_index("seq").astype(jnp.int32).reshape(1)
    pair_me = lax.axis_index("mlp")
    scalars = jnp.stack([me[0], pair_me.astype(jnp.int32)])
    inputs = block_input.reshape(rows, width)
    cot = out_cotangent.reshape(rows, width)

    outgoing, normed_one, normed_two, table, one_t, two_t, cot_t = open_layer(
        inputs,
        cot,
        me * rows,
        (attend_gain, attend_shift, feed_gain, feed_shift),
        query_key_value_weight,
        query_key_value_bias,
        attention_out_weight,
        parts,
    )
    at_head = lax.all_to_all(outgoing, "seq", 0, 0, tiled=True)

    rows_list, cot_list = mlp_list(normed_two), mlp_list(cot)
    two_t, cot_t, one_t = (mlp_list(v, 1) for v in (two_t, cot_t, one_t))
    hidden, grad_pre, grad_hid_bias, *sides = feed(
        rows_list, cot_list, expand_weight, expand_bias, contract_weight
    )
    if pairs == 2:
        feeds = [sides[0], pair_swap(sides[2])]
        grads = [sides[1], pair_swap(sides[3])]
    else:
        feeds, grads = (
            [lax.psum_scatter(v, "mlp", scatter_dimension=0, tiled=True)] for v in sides
        )
    slice_width = expand_weight.shape[1]
    block = min(512, slice_width)

    def runs(arrays, shape, index):
        if pairs == 2:
            return [(a, shape, lambda i, me: index(0, i, me)) for a in arrays]
        return [(arrays[0], shape, lambda i, me, m=m: index(m, i, me)) for m in range(pairs)]

    def sides_of(arrays):
        return runs(arrays, (width, rows), lambda m, i, me: (0, m))

    def ring_of(products, steps, block, stages):
        stages = ring_stages(stages)
        parts = weight_parts(scalars, products, steps, block, members, stages[0])
        return Ring(scalars, parts, stages)

    def feed_ring(at, b, stages):
        b_runs = [(b, (rows, block), lambda i, me, m=m: (m, i)) for m in range(pairs)]
        return ring_of([(sides_of(at), b_runs)], slice_width // block, block, stages)

    ring_out = feed_ring(cot_t, hidden, [(0,), (1,), (2,), (3,)])
    ring_hid = feed_ring(two_t, grad_pre, [(1,), (0,), (2,), (3,)])

    part = (me % parts).astype(jnp.int32)
    query_rows = rows // parts
    from_first, head_grad, head_delta, probs = forward_head(
        at_head, part, rows, query_rows, (*ring_out.sent, *ring_hid.sent, *feeds, *grads)
    )
    back_first = lax.all_to_all(from_first, "seq", 0, 0, tiled=True)
    from_second = backward_head(at_head, head_grad, head_delta, probs, rows, query_rows)
    from_second, ring_out.came, ring_hid.came = lax.optimization_barrier(
        (from_second, ring_out.came, ring_hid.came)
    )
    back_second = lax.all_to_all(from_second, "seq", 0, 0, tiled=True)
    ring_out.hold(from_second)
    ring_hid.hold(from_second)
    ring_out.step()
    ring_hid.step()

    split = pairs == 2 and parts == 1
    share = width // pairs
    x_first, y_first = [(0,), (1,), (2,), (3,)], [(1,), (0,), (2,), (3,)]

    def pieces_of(arrays):
        stacked = jnp.stack([a.reshape(rows, pairs, share) for a in arrays], 2)
        stacked = jnp.transpose(stacked, (1, 0, 2, 3)).reshape(pairs, rows, len(arrays) * share)
        if pairs == 2:
            mine = lax.dynamic_index_in_dim(stacked, pair_me, 0, False)
            return [mine, pair_swap(lax.dynamic_index_in_dim(stacked, 1 - pair_me, 0, False))]
        got = lax.all_to_all(stacked, "mlp", 0, 0, tiled=True)
        return [got.reshape(pairs * rows, len(arrays) * share)]

    if split:

        def ring_once(a_list, b_list, forms, stages, behind=()):
            stages = ring_stages(stages)
            *sums, after_it = weight_once(
                scalars, a_list, b_list, forms, share, members, stages[0], behind
            )
            ring = Ring(scalars, sums, stages)
            ring.me = after_it[0]
            return ring

        attended, grad_v, sent, own_a, own_v = regroup_once(
            back_first, None, scalars, (*ring_out.sent, *ring_hid.sent)
        )
        came = pair_swap(sent)
        ring_v = ring_once(one_t, [own_v, came[width:]], ["turned"] * 2, x_first)
        ring_d = ring_once(
            [own_a, came[:width]], cot_list, [lambda me_ref: me_ref[1]] * 2, y_first
        )
        grad_q, grad_k, sent, own_qk = regroup_once(
            back_second, table, scalars, (*ring_v.sent, *ring_d.sent)
        )
        came = pair_swap(sent)
        ring_q = ring_once(one_t, [own_qk, came], [lambda me_ref: 0] * 2, x_first)
        ring_k = ring_once(
            one_t, [own_qk, came], [lambda me_ref: 1] * 2, y_first, tuple(ring_q.sent)
        )
    else:
        attended, grad_v, att_t = regroup(back_first, None, scalars, rows, query_rows, False)
        att_t = mlp_list(att_t, 1)
        v_runs = runs(pieces_of([grad_v]), (rows, share), lambda m, i, me: (m, 0))
        ring_v = ring_of([(sides_of(one_t), v_runs)], 1, share, x_first)
        cot_runs = runs(cot_list, (rows, share), lambda m, i, me: (m, me[1]))
        ring_d = ring_of([(sides_of(att_t), cot_runs)], 1, share, y_first)
        grad_q, grad_k = regroup(back_second, table, scalars, rows, query_rows, False)
        pieces = pieces_of([grad_q, grad_k])
        ring_q, ring_k = (
            ring_of(
                [(sides_of(one_t), runs(pieces, (rows, share), lambda m, i, me, n=n: (m, n)))],
                1,
                share,
                stages,
            )
            for n, stages in enumerate((x_first, y_first))
        )

    for ring in (ring_out, ring_v, ring_d):
        ring.hold(*ring_k.sent)
    ring_v.pass_on(ring_k.me)
    ring_d.pass_on(ring_k.me)
    ring_out.step(ring_hid)
    block_output, grad_input, vec, gm_bias, closed = close_layer(
        inputs,
        cot,
        (attend_gain, feed_gain, attention_out_bias, contract_bias),
        (grad_q, grad_k, grad_v),
        attended,
        query_key_value_weight,
        attention_out_weight,
        feeds,
        grads,
        scalars,
        (*ring_v.sent, *ring_d.sent, *ring_out.sent),
    )
    for ring in (ring_q, ring_k, ring_out):
        ring.hold(vec)
    ring_q.pass_on(closed[0])
    ring_k.pass_on(closed[0])
    ring_out.pass_on(closed[0])

    bias_full = lax.dynamic_update_slice_in_dim(
        jnp.zeros((pairs * slice_width,), F32), grad_hid_bias[0], pair_me * slice_width, 0
    )
    vectors = [*[vec[r] for r in range(5)], gm_bias.reshape(-1), bias_full]
    packed = jnp.concatenate([v.reshape(members, pairs, -1) for v in vectors], -1)
    if pairs == 2:
        mine = lax.dynamic_index_in_dim(packed, pair_me, 1, False)
        other = lax.dynamic_index_in_dim(packed, 1 - pair_me, 1, False)
        packed = mine + pair_swap(other)
    else:
        packed = lax.psum_scatter(packed, "mlp", scatter_dimension=1, tiled=False)
    packed = jnp.sum(lax.all_to_all(packed, "seq", 0, 0, tiled=True), 0)
    ring_q.hold(packed)
    ring_q.step(ring_k, ring_v, ring_d)
    outs, start = [], 0
    for v in vectors:
        size = v.shape[0] // (members * pairs)
        outs.append(lax.slice_in_dim(packed, start, start + size))
        start += size
    grad_gain_one, grad_shift_one, grad_dense_bias, grad_gain_two, grad_shift_two = outs[:5]
    grad_merged_bias, out_hid_bias = outs[5:]

    out_weight, hid_weight = ring_out.total([slice_width, slice_width])
    out_weight = jnp.transpose(out_weight)

    if pairs == 2:
        mine, other = ring_q.total()
        merged, dense = vmem_call(
            place_kernel,
            [shape_of((own // pairs, 3 * width), F32), shape_of((own // pairs, width), F32)],
            scalars,
            [mine, pair_swap(other)],
            "place",
        )
    else:
        got = ring_q.total([4 * share])[0].reshape(pairs, own // pairs, 4 * share)
        got = lax.all_to_all(got, "mlp", 0, 0, tiled=True)
        got = jnp.transpose(got.reshape(pairs, own // pairs, 4, share), (1, 2, 0, 3))
        got = got.reshape(own // pairs, 4 * width)
        merged, dense = got[:, : 3 * width], got[:, 3 * width :]
    return (
        block_output.reshape(seq_count, rows, width),
        grad_input.reshape(seq_count, rows, width),
        grad_gain_one,
        grad_shift_one,
        merged,
        grad_merged_bias,
        dense,
        grad_dense_bias,
        grad_gain_two,
        grad_shift_two,
        hid_weight,
        out_hid_bias,
        out_weight,
        grad_dense_bias,
    )


def solution(mesh):
    in_specs = (
        P("mlp", "seq", None),
        P("mlp", "seq", None),
        P(),
        P(),
        P(),
        P(),
        P(),
        P(),
        P(),
        P(),
        P(None, "mlp"),
        P("mlp"),
        P("mlp", None),
        P(),
    )
    out_specs = (
        P("mlp", "seq", None),
        P("mlp", "seq", None),
        P(("seq", "mlp")),
        P(("seq", "mlp")),
        P(("seq", "mlp"), None),
        P(("seq", "mlp")),
        P(("seq", "mlp"), None),
        P(("seq", "mlp")),
        P(("seq", "mlp")),
        P(("seq", "mlp")),
        P("seq", "mlp"),
        P(("seq", "mlp")),
        P("mlp", "seq"),
        P(("seq", "mlp")),
    )
    return jax.shard_map(
        per_device, mesh=mesh, in_specs=in_specs, out_specs=out_specs, check_vma=False
    )
```

time: 340 us -> 273 us (0.80)
  waiting for transfers between devices: 74.9 us -> 42.4 us
  Pallas kernels: 164 us -> 141 us
  local copies, waits for them, and re-layouts: 32 us -> 16.4 us
  blocking collectives: 0 us -> 11.6 us
  starting transfers between devices: 55.3 us -> 48.2 us
    all_to_all x2, waiting for transfers between devices: 39 us -> 0.01 us  [the longest x1 0.01 us: per_device(): back_second = lax.all_to_all(from_second, 'seq', 0, 0, tiled=True)]
    pallas_call x23 -> x19, Pallas kernels: 138 us -> 115 us  [the longest x14 42.4 us: vmem_call(): pl.pallas_call(without(kernel, 1 + len(arrays), len(behind)), in_specs=[p...]
    all_to_all x0 -> x1, blocking collectives: none -> 11.6 us  [per_device(): packed = jnp.sum(lax.all_to_all(packed, 'seq', 0, 0, tiled=True), 0)]
    unnamed x62 -> x64, local copies, waits for them, and re-layouts: 17.1 us -> 9.9 us
    convert_element_type x0 -> x5, other arithmetic: none -> 7.02 us  [pass_on(): parts.append(total.astype(BF16))]
    concatenate x5 -> x0, other arithmetic: 6.1 us -> none  [the longest x2 4.35 us: per_device(): jnp.concatenate(mlp_list(v, 1), 1)]
    ppermute x11, starting transfers between devices: 14 us -> 8.91 us  [pair_swap(): return lax.ppermute(x, 'mlp', [(0, 1), (1, 0)])]
    ppermute x20 -> x16, waiting for transfers between devices: 33.1 us -> 38.1 us  [seq_move(): return lax.ppermute(x, 'seq', [(s, s ^ mask) for s in range(members)])]
  transfers between devices with their start and end apart: 34 -> 30, of which waited for: 10 -> 7; matrix products, arithmetic and copies ran while one was open for 7% -> 5% of each run, Pallas kernels for 28% -> 48%
where the time goes in v1:
time: 273 us; the launch traced here: 272 us
  Pallas kernels  141 us (52%)
  starting transfers between devices  48.2 us (18%)
  waiting for transfers between devices  42.4 us (16%)
  local copies, waits for them, and re-layouts  16.4 us (6%)
  blocking collectives  11.6 us (4%)
  other arithmetic  8.9 us (3%)
    pallas_call x14, Pallas kernels, vmem_call(): pl.pallas_call(without(kernel, 1 + len(arrays), len(behind)), in_specs=[p...  42.4 us
    ppermute x16, waiting for transfers between devices, seq_move(): return lax.ppermute(x, 'seq', [(s, s ^ mask) for s in range(members)])  38.1 us
    pallas_call x1, Pallas kernels, forward_head(): pl.pallas_call(without(partial(forward_kernel, key_rows=key_rows, query_r...  26.9 us
    pallas_call x1, Pallas kernels, backward_head(): pl.pallas_call(partial(backward_kernel, key_rows=key_rows, query_rows=que...  22.4 us
    pallas_call x1, Pallas kernels, feed(): pl.pallas_call(partial(feed_kernel, count=count, keep=keep), grid=(hidden...  17.3 us
    ppermute x16, starting transfers between devices, seq_move(): return lax.ppermute(x, 'seq', [(s, s ^ mask) for s in range(members)])  14.4 us
    pallas_call x2, Pallas kernels, weight_parts(): pl.pallas_call(partial(weight_kernel, bits=bits, counts=[len(a) for a, _...  12.7 us
    all_to_all x1, blocking collectives, per_device(): packed = jnp.sum(lax.all_to_all(packed, 'seq', 0, 0, tiled=True), 0)  11.6 us
  transfers between devices with their start and end apart: 30, of which 7 were waited for; matrix products, arithmetic and copies ran while one was open for 5% of the time, Pallas kernels for 48%

profile of v1, /device:TPU:1, one launch (start us, length us, event | category | flops | bytes accessed | tf_op | source)
XLA Modules:
  0.0 271.6 jit_solution(5845011929281347424)
XLA Ops:
  1.3 9.4 %open_layer.1 = (bf16[16,1,512,128]{3,2,1,0:T(8,128)(2,1)}, bf16[256,1024]{1,0:T(8,128)(2,1)}, bf16[256,1024]{1,0:T(8,128)(2,1)}, f32[3,256,128]{2,1,0:T(8,128)}...) custom-call(s32[1]{0:T(128)S(6)} %mul.8.first_ref, bf16[256,1024]{1,0:T(8,128)(2,1)} %bitcast.76, ...), custom_call_target="tpu_custom_call" | custom-call | flops 134217728 | bytes 819200 | tf_op jit(solution)/shard_map/open_layer/pallas_call | solution.py:141
  10.7 7.6 %all-to-all-start = ((bf16[16,512,128]{2,1,0:T(8,128)(2,1)}), bf16[16,512,128]{2,1,0:T(8,128)(2,1)S(1)}, u32[]{:S(2)}, u32[]{:S(2)}) async-start(bf16[16,512,128]{2,1,0:T(8,128)(2,1)} %bitcast.78), calls=%async_computation | async-start | bytes 4194304 | tf_op jit(solution)/shard_map/all_to_all | solution.py:1122
  18.3 1.0 collective-permute-start.1
  20.8 1.5 collective-permute-done.2.refs_3_
  22.3 0.8 copy-done.8
  23.1 17.3 %feed.1 = (bf16[512,2048]{1,0:T(8,128)(2,1)}, bf16[512,2048]{1,0:T(8,128)(2,1)}, f32[1,2048]{1,0:T(1,128)}, f32[256,1024]{1,0:T(8,128)}, f32[256,1024]{1,0:T(8,1...) custom-call(bf16[256,1024]{1,0:T(8,128)(2,1)} %get-tuple-element.79.refs_0_, bf16[256,1024]{1,0:T(8,128)(2,1)} %copy-done.15, ...), custom_call_target="tpu_custom_call" | custom-call | flops 536870912 | bytes 786432 | tf_op jit(solution)/shard_map/feed/pallas_call | solution.py:529
  41.7 6.4 %weight_parts.3 = (bf16[8,64,2048]{2,1,0:T(8,128)(2,1)}, bf16[8,64,2048]{2,1,0:T(8,128)(2,1)}) custom-call(s32[2]{0:T(128)} %pad_add_fusion.me_ref.refs_0_.refs_14_, bf16[1024,256]{1,0:T(8,128)(2,1)} %get-tuple-element.82.refs_0_, bf16[1024,256]{1,0:T(8,128)(2,1)} %collective-permute-done.3.refs_1_, bf16[512,2048]{1,0:T(8,128)(2,1)} %get-tuple-element.83.refs_2_.refs_3_, ...), custom_call_target="tpu_custom_call" | custom-call | flops 134217728 | bytes 458752 | tf_op jit(solution)/shard_map/weight_parts/pallas_call | solution.py:607
  48.1 1.6 collective-permute-start.7
  49.7 6.3 %weight_parts.2 = (bf16[8,64,2048]{2,1,0:T(8,128)(2,1)}, bf16[8,64,2048]{2,1,0:T(8,128)(2,1)}) custom-call(s32[2]{0:T(128)} %pad_add_fusion.me_ref.refs_0_.refs_14_, bf16[1024,256]{1,0:T(8,128)(2,1)} %get-tuple-element.78.refs_0_, bf16[1024,256]{1,0:T(8,128)(2,1)} %collective-permute-done.refs_1_, bf16[512,2048]{1,0:T(8,128)(2,1)} %get-tuple-element.80.refs_2_.refs_3_, ...), custom_call_target="tpu_custom_call" | custom-call | flops 134217728 | bytes 458752 | tf_op jit(solution)/shard_map/weight_parts/pallas_call | solution.py:607
  56.0 1.2 collective-permute-start.6
  57.2 2.4 all-to-all-done.refs_1_.x_ref
  59.7 1.3 copy-done
  61.0 26.9 %forward_head.1 = (bf16[16,256,128]{2,1,0:T(8,128)(2,1)}, bf16[4,1024,128]{2,1,0:T(8,128)(2,1)}, f32[4,1024,128]{2,1,0:T(8,128)}, bf16[20,1024,512]{2,1,0:T(8,128)(2,1)}) custom-call(s32[1]{0:T(128)} %constant.101.clone.1.refs_0_, bf16[16,512,128]{2,1,0:T(8,128)(2,1)} %copy-done, bf16[8,64,2048]{2,1,0:T(8,128)(2,1)} %get-tuple-element.81.refs_2_, ...), custom_call_target="tpu_custom_call" | custom-call | flops 1006632960 | bytes 1572864 | tf_op jit(solution)/shard_map/forward_head/pallas_call | solution.py:410
  87.9 10.9 %all-to-all-start.2 = ((bf16[16,256,128]{2,1,0:T(8,128)(2,1)}), bf16[16,256,128]{2,1,0:T(8,128)(2,1)S(1)}, u32[]{:S(2)}, u32[]{:S(2)}) async-start(bf16[16,256,128]{2,1,0:T(8,128)(2,1)} %get-tuple-element.95), calls=%async_computation.2 | async-start | bytes 2097152 | tf_op jit(solution)/shard_map/all_to_all | solution.py:1164
  98.8 22.4 %backward_head.1.refs_3_ = bf16[16,256,128]{2,1,0:T(8,128)(2,1)} custom-call(bf16[16,512,128]{2,1,0:T(8,128)(2,1)} %copy-done, bf16[4,1024,128]{2,1,0:T(8,128)(2,1)} %get-tuple-element.89.g_ref, f32[4,1024,128]{2,1,0:T(8,128)} %get-tuple-element.90.d_ref, bf16[20,1024,512]{2,1,0:T(8,128)(2,1)} %get-tuple-element.91.p_hbm), custom_call_target="tpu_custom_call" | custom-call | flops 1006632960 | bytes 1572864 | tf_op jit(solution)/shard_map/backward_head/pallas_call | solution.py:448
  121.2 6.4 %all-to-all-start.1 = ((bf16[16,256,128]{2,1,0:T(8,128)(2,1)}), bf16[16,256,128]{2,1,0:T(8,128)(2,1)S(1)}, u32[]{:S(2)}, u32[]{:S(2)}) async-start(bf16[16,256,128]{2,1,0:T(8,128)(2,1)} %backward_head.1.refs_3_), calls=%async_computation.1 | async-start | bytes 2097152 | tf_op jit(solution)/shard_map/all_to_all | solution.py:1169
  127.6 3.9 %add_parts.6 = (bf16[4,64,2048]{2,1,0:T(8,128)(2,1)}, bf16[4,64,2048]{2,1,0:T(8,128)(2,1)}) custom-call(s32[2]{0:T(128)} %pad_add_fusion.me_ref.refs_0_.refs_14_, bf16[8,64,2048]{2,1,0:T(8,128)(2,1)} %get-tuple-element.99.refs_1_, bf16[8,64,2048]{2,1,0:T(8,128)(2,1)} %collective-permute-done.7.refs_2_, bf16[16,256,128]{2,1,0:T(8,128)(2,1)} %backward_head.1.refs_3_), custom_call_target="tpu_custom_call" | custom-call | flops 131072 | bytes 393216 | tf_op jit(solution)/shard_map/add_parts/pallas_call | solution.py:718
  131.6 4.0 %add_parts.5 = (bf16[4,64,2048]{2,1,0:T(8,128)(2,1)}, bf16[4,64,2048]{2,1,0:T(8,128)(2,1)}) custom-call(s32[2]{0:T(128)} %pad_add_fusion.me_ref.refs_0_.refs_14_, bf16[8,64,2048]{2,1,0:T(8,128)(2,1)} %get-tuple-element.96.refs_1_, bf16[8,64,2048]{2,1,0:T(8,128)(2,1)} %collective-permute-done.6.refs_2_, bf16[16,256,128]{2,1,0:T(8,128)(2,1)} %backward_head.1.refs_3_), custom_call_target="tpu_custom_call" | custom-call | flops 131072 | bytes 393216 | tf_op jit(solution)/shard_map/add_parts/pallas_call | solution.py:718
  135.6 3.7 %regroup_once.2 = (bf16[256,1024]{1,0:T(8,128)(2,1)}, bf16[256,1024]{1,0:T(8,128)(2,1)}, bf16[1536,256]{1,0:T(8,128)(2,1)}, bf16[1024,256]{1,0:T(8,128)(2,1)}, bf16[512,256]{1,0:T(8,128)(2,1)}) custom-call(s32[2]{0:T(128)} %pad_add_fusion.me_ref.refs_0_.refs_14_, bf16[16,256,128]{2,1,0:T(8,128)(2,1)} %copy-done.5, ...), custom_call_target="tpu_custom_call" | custom-call | flops 32768 | bytes 98304 | tf_op jit(solution)/shard_map/regroup_once/pallas_call | solution.py:718
  139.3 2.5 collective-permute-start.9
  141.8 1.6 collective-permute-start.14
  143.4 1.2 collective-permute-start.13
  144.6 0.7 slice.66.refs_3_
  145.4 0.8 copy-done.3
  146.2 2.9 %weight_once.4 = (bf16[8,64,512]{2,1,0:T(8,128)(2,1)}, bf16[8,64,512]{2,1,0:T(8,128)(2,1)}, s32[2]{0:T(128)}) custom-call(s32[2]{0:T(128)} %pad_add_fusion.me_ref.refs_0_.refs_14_, bf16[1024,256]{1,0:T(8,128)(2,1)} %get-tuple-element.94.refs_0_.refs_1_, bf16[1024,256]{1,0:T(8,128)(2,1)} %copy-done.3, bf16[512,256]{1,0:T(8,128)(2,1)} %get-tuple-element.102.refs_2_, ...), custom_call_target="tpu_custom_call" | custom-call | flops 49152 | bytes 147456 | tf_op jit(solution)/shard_map/weight_once/pallas_call | solution.py:718
  149.1 0.8 slice.67.refs_1_
  149.9 3.2 %weight_once.5 = (bf16[8,64,512]{2,1,0:T(8,128)(2,1)}, bf16[8,64,512]{2,1,0:T(8,128)(2,1)}, s32[2]{0:T(128)}) custom-call(s32[2]{0:T(128)} %pad_add_fusion.me_ref.refs_0_.refs_14_, bf16[1024,256]{1,0:T(8,128)(2,1)} %get-tuple-element.105.refs_0_, bf16[1024,256]{1,0:T(8,128)(2,1)} %slice.67.refs_1_, bf16[256,1024]{1,0:T(8,128)(2,1)} %bitcast.73, ...), custom_call_target="tpu_custom_call" | custom-call | flops 65536 | bytes 196608 | tf_op jit(solution)/shard_map/weight_once/pallas_call | solution.py:718
  153.1 1.0 copy-done.4
  154.0 4.0 %regroup_once.3 = (bf16[256,1024]{1,0:T(8,128)(2,1)}, bf16[256,1024]{1,0:T(8,128)(2,1)}, bf16[256,1024]{1,0:T(8,128)(2,1)}, bf16[256,1024]{1,0:T(8,128)(2,1)}) custom-call(s32[2]{0:T(128)} %pad_add_fusion.me_ref.refs_0_.refs_14_, bf16[16,256,128]{2,1,0:T(8,128)(2,1)} %copy-done.4, f32[3,256,128]{2,1,0:T(8,128)} %get-tuple-element.93.refs_2_, ...), custom_call_target="tpu_custom_call" | custom-call | flops 38912 | bytes 116736 | tf_op jit(solution)/shard_map/regroup_once/pallas_call | solution.py:718
  158.0 1.0 collective-permute-start.10
  159.7 1.2 collective-permute-start.11
  160.8 0.8 copy-done.9
  161.6 3.1 %weight_once.6 = (bf16[8,64,512]{2,1,0:T(8,128)(2,1)}, bf16[8,64,512]{2,1,0:T(8,128)(2,1)}, s32[2]{0:T(128)}) custom-call(s32[2]{0:T(128)} %pad_add_fusion.me_ref.refs_0_.refs_14_, bf16[1024,256]{1,0:T(8,128)(2,1)} %get-tuple-element.94.refs_0_.refs_1_, bf16[1024,256]{1,0:T(8,128)(2,1)} %copy-done.3, bf16[256,1024]{1,0:T(8,128)(2,1)} %get-tuple-element.112.refs_2_.refs_3_, ...), custom_call_target="tpu_custom_call" | custom-call | flops 65536 | bytes 196608 | tf_op jit(solution)/shard_map/weight_once/pallas_call | solution.py:718
  164.7 3.1 %weight_once.7 = (bf16[8,64,512]{2,1,0:T(8,128)(2,1)}, bf16[8,64,512]{2,1,0:T(8,128)(2,1)}, s32[2]{0:T(128)}) custom-call(s32[2]{0:T(128)} %pad_add_fusion.me_ref.refs_0_.refs_14_, bf16[1024,256]{1,0:T(8,128)(2,1)} %get-tuple-element.94.refs_0_.refs_1_, bf16[1024,256]{1,0:T(8,128)(2,1)} %copy-done.3, bf16[256,1024]{1,0:T(8,128)(2,1)} %get-tuple-element.112.refs_2_.refs_3_, ...), custom_call_target="tpu_custom_call" | custom-call | flops 65536 | bytes 196608 | tf_op jit(solution)/shard_map/weight_once/pallas_call | solution.py:718
  168.4 2.8 %collective-permute-done.14.refs_4_ = bf16[4,64,2048]{2,1,0:T(8,128)(2,1)S(1)} collective-permute-done((bf16[4,64,2048]{2,1,0:T(8,128)(2,1)}, bf16[4,64,2048]{2,1,0:T(8,128)(2,1)S(1)}, u32[]{:S(2)}, u32[]{:S(2)}) %collective-permute-start.14) | collective-permute-done | bytes 1048608 | tf_op jit(solution)/shard_map/ppermute | solution.py:736
  171.2 1.0 copy-done.12
  172.2 4.0 %add_parts.7 = (bf16[2,64,4096]{2,1,0:T(8,128)(2,1)}, bf16[2,64,4096]{2,1,0:T(8,128)(2,1)}) custom-call(s32[2]{0:T(128)} %pad_add_fusion.me_ref.refs_0_.refs_14_, bf16[4,64,2048]{2,1,0:T(8,128)(2,1)} %get-tuple-element.117.refs_1_, bf16[4,64,2048]{2,1,0:T(8,128)(2,1)} %collective-permute-done.13.refs_2_, bf16[4,64,2048]{2,1,0:T(8,128)(2,1)} %get-tuple-element.118.refs_3_, ...), custom_call_target="tpu_custom_call" | custom-call | flops 131072 | bytes 393216 | tf_op jit(solution)/shard_map/add_parts/pallas_call | solution.py:718
  176.1 1.1 collective-permute-start.25
  177.5 1.8 collective-permute-start.16
  179.3 2.8 %collective-permute-done.12 = bf16[8,64,512]{2,1,0:T(8,128)(2,1)} collective-permute-done((bf16[8,64,512]{2,1,0:T(8,128)(2,1)}, bf16[8,64,512]{2,1,0:T(8,128)(2,1)}, u32[]{:S(2)}, u32[]{:S(2)}) %collective-permute-start.12) | collective-permute-done | bytes 524320 | tf_op jit(solution)/shard_map/ppermute | solution.py:736
  182.1 2.2 add_convert_fusion.2
  184.3 1.0 add_convert_fusion.3
  185.2 10.4 %close_layer.1 = (bf16[256,1024]{1,0:T(8,128)(2,1)}, f32[256,1024]{1,0:T(8,128)}, f32[5,1024]{1,0:T(8,128)}, f32[3,1024]{1,0:T(4,128)}, s32[2]{0:T(128)}) custom-call(bf16[256,1024]{1,0:T(8,128)(2,1)} %bitcast.77, bf16[256,1024]{1,0:T(8,128)(2,1)} %bitcast.74, bf16[1024]{0:T(1024)(128)(2,1)} %refs_2_.1, bf16[1024]{0:T(1024)(128)(2,1)} %refs_3_.1, ...), custom_call_target="tpu_custom_call" | custom-call | flops 134217728 | bytes 917504 | tf_op jit(solution)/shard_map/close_layer/pallas_call | solution.py:1021
  197.1 0.7 collective-permute-start.20
  197.9 1.0 slice_reduce_fusion
  199.3 0.8 reshape_reshape.3
  200.4 2.4 collective-permute-start.15
  202.8 0.9 add_convert_fusion.4
  203.7 1.2 collective-permute-start.19
  204.8 1.9 add_convert_fusion.6
  207.5 11.6 %all_to_all.24 = f32[16,1,384]{2,1,0:T(1,128)S(1)} all-to-all(f32[16,1,384]{2,1,0:T(1,128)S(1)} %all_to_all.18), channel_id=1, replica_groups=mesh['seq'=16,'mlp'=2] {'seq'}, dimensions={0} | all-to-all | bytes 49152 | tf_op jit(solution)/shard_map/all_to_all | solution.py:1269
  219.8 0.7 copy-done.23
  220.5 2.7 add_parts.8
  223.6 1.1 add_convert_fusion
  225.1 19.3 %collective-permute-done.22.refs_1_ = bf16[2,64,2048]{2,1,0:T(8,128)(2,1)S(1)} collective-permute-done((bf16[2,64,2048]{2,1,0:T(8,128)(2,1)}, bf16[2,64,2048]{2,1,0:T(8,128)(2,1)S(1)}, u32[]{:S(2)}, u32[]{:S(2)}) %collective-permute-start.22) | collective-permute-done | bytes 524320 | tf_op jit(solution)/shard_map/ppermute | solution.py:736
  244.4 0.8 copy-done.16
  245.2 2.1 add_parts.9
  248.4 13.2 %collective-permute-done.23.refs_1_ = bf16[1,64,2048]{2,1,0:T(8,128)(2,1)S(1)} collective-permute-done((bf16[1,64,2048]{2,1,0:T(8,128)(2,1)}, bf16[1,64,2048]{2,1,0:T(8,128)(2,1)S(1)}, u32[]{:S(2)}, u32[]{:S(2)}) %collective-permute-start.23) | collective-permute-done | bytes 262176 | tf_op jit(solution)/shard_map/ppermute | solution.py:736
  261.6 0.7 copy-done.22
  262.3 1.8 last_sum.2
  264.1 0.8 collective-permute-start.24
  265.6 0.8 copy-done.17
  266.3 2.2 last_sum.3
  269.2 1.8 place.1
  (111 shorter events, 10.8 us)
Async XLA Ops:
  10.7 7.6 %copy-start.14 = (bf16[256,1024]{1,0:T(8,128)(2,1)S(1)}, bf16[256,1024]{1,0:T(8,128)(2,1)}, u32[]{:S(2)}) copy-start(bf16[256,1024]{1,0:T(8,128)(2,1)} %get-tuple-element.79.refs_0_) | copy-start | bytes 1572868
  10.7 8.6 %copy-start.1 = (bf16[1,256,1024]{2,1,0:T(8,128)(2,1)S(1)}, bf16[1,256,1024]{2,1,0:T(8,128)(2,1)}, u32[]{:S(2)}) copy-start(bf16[1,256,1024]{2,1,0:T(8,128)(2,1)} %param.15) | copy-start | bytes 1572868
  10.7 9.2 %copy-start.27 = (bf16[2048]{0:T(1024)(128)(2,1)S(1)}, bf16[2048]{0:T(1024)(128)(2,1)}, u32[]{:S(2)}) copy-start(bf16[2048]{0:T(1024)(128)(2,1)} %param.25) | copy-start | bytes 12292
  10.7 49.0 %all-to-all-start = ((bf16[16,512,128]{2,1,0:T(8,128)(2,1)}), bf16[16,512,128]{2,1,0:T(8,128)(2,1)S(1)}, u32[]{:S(2)}, u32[]{:S(2)}) async-start(bf16[16,512,128]{2,1,0:T(8,128)(2,1)} %bitcast.78), calls=%async_computation | async-start | bytes 4194304 | tf_op jit(solution)/shard_map/all_to_all | solution.py:1122
  18.3 2.6 collective-permute-start.1
  19.3 3.0 %collective-permute-start.2 = (bf16[256,1024]{1,0:T(8,128)(2,1)S(1)}, bf16[256,1024]{1,0:T(8,128)(2,1)S(1)}, u32[]{:S(2)}, u32[]{:S(2)}) collective-permute-start(bf16[256,1024]{1,0:T(8,128)(2,1)S(1)} %bitcast.75), channel_id=1, source_target_pairs={{0,1},{1,0},{2,3},{3,2},{4,5},{5,4},{6,7},{7,6},{8,9},{9,8},{10,11... | collective-permute-start | bytes 1572872 | tf_op jit(solution)/shard_map/ppermute | solution.py:1072
  19.4 22.3 %collective-permute-start.3 = (bf16[1024,256]{1,0:T(8,128)(2,1)}, bf16[1024,256]{1,0:T(8,128)(2,1)}, u32[]{:S(2)}, u32[]{:S(2)}) collective-permute-start(bf16[1024,256]{1,0:T(8,128)(2,1)} %get-tuple-element.82.refs_0_), channel_id=1, source_target_pairs={{0,1},{1,0},{2,3},{3,2},{4,5},{5,4},{6,7},{7,6},{8,9},{9,8},{10,11... | collective-permute-start | bytes 1572872 | tf_op jit(solution)/shard_map/ppermute | solution.py:1072
  19.8 29.9 %collective-permute-start = (bf16[1024,256]{1,0:T(8,128)(2,1)}, bf16[1024,256]{1,0:T(8,128)(2,1)}, u32[]{:S(2)}, u32[]{:S(2)}) collective-permute-start(bf16[1024,256]{1,0:T(8,128)(2,1)} %get-tuple-element.78.refs_0_), channel_id=1, source_target_pairs={{0,1},{1,0},{2,3},{3,2},{4,5},{5,4},{6,7},{7,6},{8,9},{9,8},{10,11... | collective-permute-start | bytes 1572872 | tf_op jit(solution)/shard_map/ppermute | solution.py:1072
  20.8 1.5 copy-start.15
  22.3 0.8 copy-start.8
  40.5 16.8 %collective-permute-start.4 = (bf16[256,1024]{1,0:T(8,128)(2,1)}, bf16[256,1024]{1,0:T(8,128)(2,1)S(1)}, u32[]{:S(2)}, u32[]{:S(2)}) collective-permute-start(bf16[256,1024]{1,0:T(8,128)(2,1)} %get-tuple-element.86), channel_id=1, source_target_pairs={{0,1},{1,0},{2,3},{3,2},{4,5},{5,4},{6,7},{7,6},{8,9},{9,8},{10,11... | collective-permute-start | bytes 1572872 | tf_op jit(solution)/shard_map/ppermute | solution.py:1072
  40.9 16.3 %collective-permute-start.5 = (bf16[256,1024]{1,0:T(8,128)(2,1)}, bf16[256,1024]{1,0:T(8,128)(2,1)S(1)}, u32[]{:S(2)}, u32[]{:S(2)}) collective-permute-start(bf16[256,1024]{1,0:T(8,128)(2,1)} %get-tuple-element.88), channel_id=1, source_target_pairs={{0,1},{1,0},{2,3},{3,2},{4,5},{5,4},{6,7},{7,6},{8,9},{9,8},{10,11... | collective-permute-start | bytes 1572872 | tf_op jit(solution)/shard_map/ppermute | solution.py:1072
  48.1 73.1 %collective-permute-start.7 = (bf16[8,64,2048]{2,1,0:T(8,128)(2,1)}, bf16[8,64,2048]{2,1,0:T(8,128)(2,1)}, u32[]{:S(2)}, u32[]{:S(2)}) collective-permute-start(bf16[8,64,2048]{2,1,0:T(8,128)(2,1)} %get-tuple-element.84.refs_3_), channel_id=1, source_target_pairs={{0,4},{2,6},{4,0},{6,2},{8,12},{10,14},{12,8},{14,10},{16,20},{18,... | collective-permute-start | bytes 6291464 | tf_op jit(solution)/shard_map/ppermute | solution.py:736
  56.0 65.2 %collective-permute-start.6 = (bf16[8,64,2048]{2,1,0:T(8,128)(2,1)}, bf16[8,64,2048]{2,1,0:T(8,128)(2,1)}, u32[]{:S(2)}, u32[]{:S(2)}) collective-permute-start(bf16[8,64,2048]{2,1,0:T(8,128)(2,1)} %get-tuple-element.81.refs_2_), channel_id=1, source_target_pairs={{0,2},{2,0},{4,6},{6,4},{8,10},{10,8},{12,14},{14,12},{16,18},{18,... | collective-permute-start | bytes 6291464 | tf_op jit(solution)/shard_map/ppermute | solution.py:736
  57.2 2.4 copy-start.6
  57.2 2.4 copy-start.7
  59.7 1.3 copy-start
  87.9 33.3 %all-to-all-start.2 = ((bf16[16,256,128]{2,1,0:T(8,128)(2,1)}), bf16[16,256,128]{2,1,0:T(8,128)(2,1)S(1)}, u32[]{:S(2)}, u32[]{:S(2)}) async-start(bf16[16,256,128]{2,1,0:T(8,128)(2,1)} %get-tuple-element.95), calls=%async_computation.2 | async-start | bytes 2097152 | tf_op jit(solution)/shard_map/all_to_all | solution.py:1164
  121.2 10.3 %copy-start.5 = (bf16[16,256,128]{2,1,0:T(8,128)(2,1)}, bf16[16,256,128]{2,1,0:T(8,128)(2,1)S(1)}, u32[]{:S(2)}) copy-start(bf16[16,256,128]{2,1,0:T(8,128)(2,1)S(1)} %all-to-all-done.2.refs_1_) | copy-start | bytes 3145732
  121.2 31.8 %all-to-all-start.1 = ((bf16[16,256,128]{2,1,0:T(8,128)(2,1)}), bf16[16,256,128]{2,1,0:T(8,128)(2,1)S(1)}, u32[]{:S(2)}, u32[]{:S(2)}) async-start(bf16[16,256,128]{2,1,0:T(8,128)(2,1)} %backward_head.1.refs_3_), calls=%async_computation.1 | async-start | bytes 2097152 | tf_op jit(solution)/shard_map/all_to_all | solution.py:1169
  135.6 6.2 %copy-start.2 = (bf16[1024,256]{1,0:T(8,128)(2,1)S(1)}, bf16[1024,256]{1,0:T(8,128)(2,1)}, u32[]{:S(2)}) copy-start(bf16[1024,256]{1,0:T(8,128)(2,1)} %get-tuple-element.94.refs_0_.refs_1_) | copy-start | bytes 1572868
  139.3 5.4 %collective-permute-start.9 = (bf16[1536,256]{1,0:T(8,128)(2,1)}, bf16[1536,256]{1,0:T(8,128)(2,1)S(1)}, u32[]{:S(2)}, u32[]{:S(2)}) collective-permute-start(bf16[1536,256]{1,0:T(8,128)(2,1)} %get-tuple-element.103), channel_id=1, source_target_pairs={{0,1},{1,0},{2,3},{3,2},{4,5},{5,4},{6,7},{7,6},{8,9},{9,8},{10,11... | collective-permute-start | bytes 2359304 | tf_op jit(solution)/shard_map/ppermute | solution.py:1072
  141.7 3.6 %collective-permute-start.8 = (bf16[1024,256]{1,0:T(8,128)(2,1)S(1)}, bf16[1024,256]{1,0:T(8,128)(2,1)S(1)}, u32[]{:S(2)}, u32[]{:S(2)}) collective-permute-start(bf16[1024,256]{1,0:T(8,128)(2,1)S(1)} %copy-done.2), channel_id=1, source_target_pairs={{0,1},{1,0},{2,3},{3,2},{4,5},{5,4},{6,7},{7,6},{8,9},{9,8},{10,11... | collective-permute-start | bytes 1572872 | tf_op jit(solution)/shard_map/ppermute | solution.py:1072
  141.8 29.4 %collective-permute-start.14 = (bf16[4,64,2048]{2,1,0:T(8,128)(2,1)}, bf16[4,64,2048]{2,1,0:T(8,128)(2,1)S(1)}, u32[]{:S(2)}, u32[]{:S(2)}) collective-permute-start(bf16[4,64,2048]{2,1,0:T(8,128)(2,1)} %get-tuple-element.101.refs_3_), channel_id=1, source_target_pairs={{0,2},{2,0},{4,6},{6,4},{8,10},{10,8},{12,14},{14,12},{16,18},{18,... | collective-permute-start | bytes 3145736 | tf_op jit(solution)/shard_map/ppermute | solution.py:736
  143.4 27.8 %collective-permute-start.13 = (bf16[4,64,2048]{2,1,0:T(8,128)(2,1)}, bf16[4,64,2048]{2,1,0:T(8,128)(2,1)}, u32[]{:S(2)}, u32[]{:S(2)}) collective-permute-start(bf16[4,64,2048]{2,1,0:T(8,128)(2,1)} %get-tuple-element.98.refs_2_), channel_id=1, source_target_pairs={{0,4},{2,6},{4,0},{6,2},{8,12},{10,14},{12,8},{14,10},{16,20},{18,... | collective-permute-start | bytes 3145736 | tf_op jit(solution)/shard_map/ppermute | solution.py:736
  145.4 0.8 copy-start.3
  149.9 9.8 %copy-start.21 = (bf16[8,64,512]{2,1,0:T(8,128)(2,1)S(1)}, bf16[8,64,512]{2,1,0:T(8,128)(2,1)}, u32[]{:S(2)}) copy-start(bf16[8,64,512]{2,1,0:T(8,128)(2,1)} %get-tuple-element.104.refs_3_) | copy-start | bytes 1572868
  153.1 1.0 copy-start.4
  158.0 2.8 %collective-permute-start.10 = (bf16[256,1024]{1,0:T(8,128)(2,1)}, bf16[256,1024]{1,0:T(8,128)(2,1)S(1)}, u32[]{:S(2)}, u32[]{:S(2)}) collective-permute-start(bf16[256,1024]{1,0:T(8,128)(2,1)} %get-tuple-element.113), channel_id=1, source_target_pairs={{0,1},{1,0},{2,3},{3,2},{4,5},{5,4},{6,7},{7,6},{8,9},{9,8},{10,11... | collective-permute-start | bytes 1572872 | tf_op jit(solution)/shard_map/ppermute | solution.py:1072
  159.0 23.0 %collective-permute-start.12 = (bf16[8,64,512]{2,1,0:T(8,128)(2,1)}, bf16[8,64,512]{2,1,0:T(8,128)(2,1)}, u32[]{:S(2)}, u32[]{:S(2)}) collective-permute-start(bf16[8,64,512]{2,1,0:T(8,128)(2,1)} %get-tuple-element.106.refs_4_), channel_id=1, source_target_pairs={{0,4},{2,6},{4,0},{6,2},{8,12},{10,14},{12,8},{14,10},{16,20},{18,... | collective-permute-start | bytes 1572872 | tf_op jit(solution)/shard_map/ppermute | solution.py:736
  159.7 24.6 %collective-permute-start.11 = (bf16[8,64,512]{2,1,0:T(8,128)(2,1)S(1)}, bf16[8,64,512]{2,1,0:T(8,128)(2,1)S(1)}, u32[]{:S(2)}, u32[]{:S(2)}) collective-permute-start(bf16[8,64,512]{2,1,0:T(8,128)(2,1)S(1)} %copy-done.21), channel_id=1, source_target_pairs={{0,2},{2,0},{4,6},{6,4},{8,10},{10,8},{12,14},{14,12},{16,18},{18,... | collective-permute-start | bytes 1572872 | tf_op jit(solution)/shard_map/ppermute | solution.py:736
  160.8 0.8 copy-start.9
  167.8 32.6 %collective-permute-start.18 = (bf16[8,64,512]{2,1,0:T(8,128)(2,1)}, bf16[8,64,512]{2,1,0:T(8,128)(2,1)S(1)}, u32[]{:S(2)}, u32[]{:S(2)}) collective-permute-start(bf16[8,64,512]{2,1,0:T(8,128)(2,1)} %get-tuple-element.119.refs_5_), channel_id=1, source_target_pairs={{0,4},{2,6},{4,0},{6,2},{8,12},{10,14},{12,8},{14,10},{16,20},{18,... | collective-permute-start | bytes 1572872 | tf_op jit(solution)/shard_map/ppermute | solution.py:736
  171.2 1.0 copy-start.12
  172.2 5.1 %copy-start.26 = (f32[1,2048]{1,0:T(1,128)S(1)}, f32[1,2048]{1,0:T(1,128)}, u32[]{:S(2)}) copy-start(f32[1,2048]{1,0:T(1,128)} %get-tuple-element.125) | copy-start | bytes 24580
  172.2 5.3 %copy-start.30 = (s32[2]{0:T(128)S(1)}, s32[2]{0:T(128)}, u32[]{:S(2)}) copy-start(s32[2]{0:T(128)} %get-tuple-element.115) | copy-start | bytes 28
  172.2 12.1 %copy-start.20 = (bf16[8,64,512]{2,1,0:T(8,128)(2,1)S(1)}, bf16[8,64,512]{2,1,0:T(8,128)(2,1)}, u32[]{:S(2)}) copy-start(bf16[8,64,512]{2,1,0:T(8,128)(2,1)} %get-tuple-element.111) | copy-start | bytes 1572868
  176.1 47.4 %collective-permute-start.25 = (bf16[2,64,4096]{2,1,0:T(8,128)(2,1)}, bf16[2,64,4096]{2,1,0:T(8,128)(2,1)S(1)}, u32[]{:S(2)}, u32[]{:S(2)}) collective-permute-start(bf16[2,64,4096]{2,1,0:T(8,128)(2,1)} %get-tuple-element.120.refs_21_), channel_id=1, source_target_pairs={{0,8},{2,10},{4,12},{6,14},{8,0},{10,2},{12,4},{14,6},{16,24},{18,... | collective-permute-start | bytes 3145736 | tf_op jit(solution)/shard_map/ppermute | solution.py:736
  177.5 26.2 %collective-permute-start.16 = (bf16[8,64,512]{2,1,0:T(8,128)(2,1)}, bf16[8,64,512]{2,1,0:T(8,128)(2,1)}, u32[]{:S(2)}, u32[]{:S(2)}) collective-permute-start(bf16[8,64,512]{2,1,0:T(8,128)(2,1)} %get-tuple-element.114.refs_5_), channel_id=1, source_target_pairs={{0,2},{2,0},{4,6},{6,4},{8,10},{10,8},{12,14},{14,12},{16,18},{18,... | collective-permute-start | bytes 1572872 | tf_op jit(solution)/shard_map/ppermute | solution.py:736
  185.2 11.7 %copy-start.10 = (bf16[2,2,1,64,512]{4,3,1,0,2:T(8,128)(2,1)S(1)}, bf16[2,2,1,64,512]{4,3,1,0,2:T(8,128)(2,1)}, u32[]{:S(2)}) copy-start(bf16[2,2,1,64,512]{4,3,1,0,2:T(8,128)(2,1)} %get-tuple-element.148) | copy-start | bytes 786436
  185.2 11.9 %copy-start.11 = (bf16[2,2,1,64,512]{4,3,1,0,2:T(8,128)(2,1)S(1)}, bf16[2,2,1,64,512]{4,3,1,0,2:T(8,128)(2,1)}, u32[]{:S(2)}) copy-start(bf16[2,2,1,64,512]{4,3,1,0,2:T(8,128)(2,1)} %get-tuple-element.150) | copy-start | bytes 786436
  185.2 17.5 %copy-start.19 = (bf16[8,64,512]{2,1,0:T(8,128)(2,1)S(1)}, bf16[8,64,512]{2,1,0:T(8,128)(2,1)}, u32[]{:S(2)}) copy-start(bf16[8,64,512]{2,1,0:T(8,128)(2,1)} %get-tuple-element.128) | copy-start | bytes 1572868
  195.6 9.2 %copy-start.18 = (bf16[8,64,512]{2,1,0:T(8,128)(2,1)S(1)}, bf16[8,64,512]{2,1,0:T(8,128)(2,1)}, u32[]{:S(2)}) copy-start(bf16[8,64,512]{2,1,0:T(8,128)(2,1)} %get-tuple-element.126) | copy-start | bytes 1572868
  197.0 22.8 %collective-permute-start.21 = (bf16[4,64,512]{2,1,0:T(8,128)(2,1)S(1)}, bf16[4,64,512]{2,1,0:T(8,128)(2,1)}, u32[]{:S(2)}, u32[]{:S(2)}) collective-permute-start(bf16[4,64,512]{2,1,0:T(8,128)(2,1)S(1)} %bitcast.80), channel_id=1, source_target_pairs={{0,2},{2,0},{4,6},{6,4},{8,10},{10,8},{12,14},{14,12},{16,18},{18,... | collective-permute-start | bytes 786440 | tf_op jit(solution)/shard_map/ppermute | solution.py:736
  197.1 22.6 %collective-permute-start.20 = (bf16[4,64,512]{2,1,0:T(8,128)(2,1)S(1)}, bf16[4,64,512]{2,1,0:T(8,128)(2,1)}, u32[]{:S(2)}, u32[]{:S(2)}) collective-permute-start(bf16[4,64,512]{2,1,0:T(8,128)(2,1)S(1)} %bitcast.82), channel_id=1, source_target_pairs={{0,4},{2,6},{4,0},{6,2},{8,12},{10,14},{12,8},{14,10},{16,20},{18,... | collective-permute-start | bytes 786440 | tf_op jit(solution)/shard_map/ppermute | solution.py:736
  200.4 6.4 %collective-permute-start.15 = (f32[16,384]{1,0:T(8,128)S(1)}, f32[16,384]{1,0:T(8,128)S(1)}, u32[]{:S(2)}, u32[]{:S(2)}) collective-permute-start(f32[16,384]{1,0:T(8,128)S(1)} %bitcast.96), channel_id=1, source_target_pairs={{0,1},{1,0},{2,3},{3,2},{4,5},{5,4},{6,7},{7,6},{8,9},{9,8},{10,11... | collective-permute-start | bytes 73736 | tf_op jit(solution)/shard_map/ppermute | solution.py:1072
  203.6 19.8 %copy-start.29 = (s32[2]{0:T(128)S(1)}, s32[2]{0:T(128)}, u32[]{:S(2)}) copy-start(s32[2]{0:T(128)} %get-tuple-element.127) | copy-start | bytes 28
  203.6 19.9 %copy-start.13 = (bf16[2,64,4096]{2,1,0:T(8,128)(2,1)S(1)}, bf16[2,64,4096]{2,1,0:T(8,128)(2,1)}, u32[]{:S(2)}) copy-start(bf16[2,64,4096]{2,1,0:T(8,128)(2,1)} %get-tuple-element.137) | copy-start | bytes 3145732
  203.7 16.1 %collective-permute-start.19 = (bf16[4,64,512]{2,1,0:T(8,128)(2,1)S(1)}, bf16[4,64,512]{2,1,0:T(8,128)(2,1)}, u32[]{:S(2)}, u32[]{:S(2)}) collective-permute-start(bf16[4,64,512]{2,1,0:T(8,128)(2,1)S(1)} %bitcast.93), channel_id=1, source_target_pairs={{0,2},{2,0},{4,6},{6,4},{8,10},{10,8},{12,14},{14,12},{16,18},{18,... | collective-permute-start | bytes 786440 | tf_op jit(solution)/shard_map/ppermute | solution.py:736
  206.8 13.0 %collective-permute-start.17 = (bf16[4,64,512]{2,1,0:T(8,128)(2,1)}, bf16[4,64,512]{2,1,0:T(8,128)(2,1)S(1)}, u32[]{:S(2)}, u32[]{:S(2)}) collective-permute-start(bf16[4,64,512]{2,1,0:T(8,128)(2,1)} %bitcast.22), channel_id=1, source_target_pairs={{0,4},{2,6},{4,0},{6,2},{8,12},{10,14},{12,8},{14,10},{16,20},{18,... | collective-permute-start | bytes 786440 | tf_op jit(solution)/shard_map/ppermute | solution.py:736
  219.8 0.7 copy-start.23
  223.2 21.3 %collective-permute-start.22 = (bf16[2,64,2048]{2,1,0:T(8,128)(2,1)}, bf16[2,64,2048]{2,1,0:T(8,128)(2,1)S(1)}, u32[]{:S(2)}, u32[]{:S(2)}) collective-permute-start(bf16[2,64,2048]{2,1,0:T(8,128)(2,1)} %get-tuple-element.130), channel_id=1, source_target_pairs={{0,8},{2,10},{4,12},{6,14},{8,0},{10,2},{12,4},{14,6},{16,24},{18,... | collective-permute-start | bytes 1572872 | tf_op jit(solution)/shard_map/ppermute | solution.py:736
  223.6 23.8 %copy-start.25 = (f32[384]{0:T(512)S(1)}, f32[384]{0:T(512)}, u32[]{:S(2)}) copy-start(f32[384]{0:T(512)} %reduce_sum.9.refs_9_) | copy-start | bytes 4612
  224.7 40.9 %collective-permute-start.26 = (bf16[1,64,4096]{2,1,0:T(8,128)(2,1)S(1)}, bf16[1,64,4096]{2,1,0:T(8,128)(2,1)S(1)}, u32[]{:S(2)}, u32[]{:S(2)}) collective-permute-start(bf16[1,64,4096]{2,1,0:T(8,128)(2,1)S(1)} %get-tuple-element.145), channel_id=1, source_target_pairs={{0,16},{2,18},{4,20},{6,22},{8,24},{10,26},{12,28},{14,30},{16,0},... | collective-permute-start | bytes 1572872 | tf_op jit(solution)/shard_map/ppermute | solution.py:736
  244.4 0.8 copy-start.16
  247.3 14.3 %collective-permute-start.23 = (bf16[1,64,2048]{2,1,0:T(8,128)(2,1)}, bf16[1,64,2048]{2,1,0:T(8,128)(2,1)S(1)}, u32[]{:S(2)}, u32[]{:S(2)}) collective-permute-start(bf16[1,64,2048]{2,1,0:T(8,128)(2,1)} %get-tuple-element.132), channel_id=1, source_target_pairs={{0,16},{2,18},{4,20},{6,22},{8,24},{10,26},{12,28},{14,30},{16,0},... | collective-permute-start | bytes 786440 | tf_op jit(solution)/shard_map/ppermute | solution.py:736
  261.6 0.7 copy-start.22
  264.1 4.4 %collective-permute-start.24 = (bf16[32,2048]{1,0:T(8,128)(2,1)}, bf16[32,2048]{1,0:T(8,128)(2,1)S(1)}, u32[]{:S(2)}, u32[]{:S(2)}) collective-permute-start(bf16[32,2048]{1,0:T(8,128)(2,1)} %get-tuple-element.134), channel_id=1, source_target_pairs={{0,1},{1,0},{2,3},{3,2},{4,5},{5,4},{6,7},{7,6},{8,9},{9,8},{10,11... | collective-permute-start | bytes 393224 | tf_op jit(solution)/shard_map/ppermute | solution.py:1072
  265.5 6.0 %copy-start.28 = (f32[32]{0:T(128)}, f32[32]{0:T(128)S(1)}, u32[]{:S(2)}) copy-start(f32[32]{0:T(128)S(1)} %get-tuple-element.189) | copy-start | bytes 388
  265.5 0.8 copy-start.17
  268.6 0.7 copy-start.24

commit v2 on v1

--- a/solution.py
+++ b/solution.py
@@ -26,11 +26,11 @@
     return lax.dot_general(a, b, dims, preferred_element_type=F32)
 
 
-def cost(flops, bytes_accessed, transcendentals):
+def cost(flops, bytes_accessed, transcendentals, share=COST_SHARE):
     return pl.CostEstimate(
-        flops=flops // COST_SHARE,
-        bytes_accessed=bytes_accessed // COST_SHARE,
-        transcendentals=transcendentals // COST_SHARE,
+        flops=flops // share,
+        bytes_accessed=bytes_accessed // share,
+        transcendentals=transcendentals // share,
     )
 
 
@@ -83,7 +83,7 @@
 def open_kernel(
     first_ref, x_ref, g_ref, inv_ref, ga_ref, sa_ref, gf_ref, sf_ref, b_ref,
     wq_ref, wk_ref, wv_ref, wo_ref,
-    out_ref, n1_ref, n2_ref, table_ref, n1t_ref, n2t_ref, gt_ref, bias_ref, *, parts,
+    out_ref, n1_ref, n2_ref, table_ref, turned_ref, bias_ref, *, parts,
 ):
     rows, width = x_ref.shape
     step = pl.program_id(0)
@@ -98,11 +98,11 @@
             table_ref[t] = table
         bias_ref[...] = vector_row(b_ref)
 
-    for at, source, target in ((1, n1_ref, n1t_ref), (2, n2_ref, n2t_ref), (3, g_ref, gt_ref)):
-
-        @pl.when(step == at)
-        def _(source=source, target=target):
-            target[...] = jnp.transpose(source[...])
+    for n, source in enumerate((n1_ref, n2_ref, g_ref)):
+
+        @pl.when(step == n + 1)
+        def _(n=n, source=source):
+            turned_ref[n * width : (n + 1) * width] = jnp.transpose(source[...])
 
     def bias(third):
         return bias_ref[:, pl.ds(pl.multiple_of(third * width + step * cols, cols), cols)]
@@ -146,9 +146,7 @@
             shape_of((rows, width), BF16),
             shape_of((rows, width), BF16),
             shape_of((3, rows, PAIR), F32),
-            shape_of((width, rows), BF16),
-            shape_of((width, rows), BF16),
-            shape_of((width, rows), BF16),
+            shape_of((3 * width, rows), BF16),
         ),
         in_specs=[
             pl.BlockSpec(memory_space=pltpu.SMEM),
@@ -165,9 +163,7 @@
             fixed((rows, width)),
             fixed((rows, width)),
             fixed((3, rows, PAIR)),
-            fixed((width, rows)),
-            fixed((width, rows)),
-            fixed((width, rows)),
+            fixed((3 * width, rows)),
         ),
         scratch_shapes=[pltpu.VMEM((1, 3 * width), F32)],
         cost_estimate=cost(
@@ -196,10 +192,11 @@
 
 
 def forward_kernel(
-    part_ref, x_ref, y_ref, g_ref, d_ref, p_hbm,
+    part_ref, x_ref, y_ref, g_ref, d_ref, p_hbm, after_ref,
     s_ref, p_ref, dv_ref, vt_ref, mx_ref, top_ref, acc_ref, sem,
     *, key_rows, query_rows,
 ):
+    after_ref[0] = part_ref[1]
     blocks = x_ref.shape[0] // ROW_GROUP
     keys, rows = KEY_GROUP * key_rows, ROW_GROUP * query_rows
     low = lax.broadcasted_iota(jnp.int32, (rows, PAIR), 1) < HEAD
@@ -316,9 +313,11 @@
 
 
 def backward_kernel(
-    x_ref, g_ref, d_ref, p_hbm, y_ref, p_ref, dp0_ref, dp1_ref, dk_ref, acc_ref, sem,
+    me_ref, x_ref, g_ref, d_ref, p_hbm, y_ref, after_ref,
+    p_ref, dp0_ref, dp1_ref, dk_ref, acc_ref, sem,
     *, key_rows, query_rows,
 ):
+    after_ref[0] = me_ref[0]
     blocks = x_ref.shape[0] // ROW_GROUP
     keys, rows = KEY_GROUP * key_rows, ROW_GROUP * query_rows
     tiles = first_tile(blocks)
@@ -416,10 +415,14 @@
             shape_of((blocks, rows, PAIR), BF16),
             shape_of((blocks, rows, PAIR), F32),
             shape_of((tiles, rows, keys), BF16),
+            shape_of((1,), jnp.int32),
         ),
         in_specs=[pl.BlockSpec(memory_space=pltpu.SMEM), vmem]
         + [pl.BlockSpec(memory_space=pl.ANY)] * len(behind),
-        out_specs=(vmem, vmem, vmem, pl.BlockSpec(memory_space=pl.ANY)),
+        out_specs=(
+            vmem, vmem, vmem, pl.BlockSpec(memory_space=pl.ANY),
+            pl.BlockSpec(memory_space=pltpu.SMEM),
+        ),
         scratch_shapes=[
             pltpu.VMEM((2 * blocks, rows, keys), F32),
             pltpu.VMEM((2 * blocks, rows, keys), BF16),
@@ -434,22 +437,26 @@
             flops=tiles * rows * keys * 2 * 256 * 3,
             bytes_accessed=4 * x.size + 2 * tiles * rows * keys,
             transcendentals=tiles * rows * keys,
+            share=1,
         ),
         compiler_params=pltpu.CompilerParams(vmem_limit_bytes=VMEM_LIMIT),
         name="forward_head",
     )(part, x, *behind)
 
 
-def backward_head(x, grad, delta, probs, key_rows, query_rows):
+def backward_head(scalars, x, grad, delta, probs, key_rows, query_rows, behind):
     count, blocks, keys, rows = head_sizes(x, key_rows, query_rows)
     tiles = first_tile(blocks)
     slots = 6
     vmem = pl.BlockSpec(memory_space=pltpu.VMEM)
     return pl.pallas_call(
-        partial(backward_kernel, key_rows=key_rows, query_rows=query_rows),
-        out_shape=shape_of((count, key_rows, PAIR), BF16),
-        in_specs=[vmem, vmem, vmem, pl.BlockSpec(memory_space=pl.ANY)],
-        out_specs=vmem,
+        without(
+            partial(backward_kernel, key_rows=key_rows, query_rows=query_rows), 5, len(behind)
+        ),
+        out_shape=(shape_of((count, key_rows, PAIR), BF16), shape_of((1,), jnp.int32)),
+        in_specs=[pl.BlockSpec(memory_space=pltpu.SMEM), vmem, vmem, vmem]
+        + [pl.BlockSpec(memory_space=pl.ANY)] * (1 + len(behind)),
+        out_specs=(vmem, pl.BlockSpec(memory_space=pltpu.SMEM)),
         scratch_shapes=[
             pltpu.VMEM((slots, rows, keys), BF16),
             pltpu.VMEM((rows, keys), F32),
@@ -462,10 +469,11 @@
             flops=tiles * rows * keys * 2 * 256 * 3,
             bytes_accessed=4 * x.size + 2 * tiles * rows * keys,
             transcendentals=0,
+            share=1,
         ),
         compiler_params=pltpu.CompilerParams(vmem_limit_bytes=VMEM_LIMIT),
         name="backward_head",
-    )(x, grad, delta, probs)
+    )(scalars, x, grad, delta, probs, *behind)
 
 
 def feed_kernel(*refs, count, keep):
@@ -502,11 +510,11 @@
     @pl.when(step == pl.num_programs(0) - 1)
     def _():
         if keep:
-            own_out, own_grad, other_out, other_grad = outs
+            own_out, own_grad, other = outs
             own_out[...] = out_acc[:rows]
             own_grad[...] = grad_acc[:rows]
-            other_out[...] = out_acc[rows:].astype(BF16)
-            other_grad[...] = grad_acc[rows:].astype(BF16)
+            other[:rows] = out_acc[rows:].astype(BF16)
+            other[rows:] = grad_acc[rows:].astype(BF16)
         else:
             outs[0][...] = out_acc[...].astype(BF16)
             outs[1][...] = grad_acc[...].astype(BF16)
@@ -520,7 +528,7 @@
     block = 256
     keep = count > 1
     sides = (
-        [(rows, F32), (rows, F32), (total - rows, BF16), (total - rows, BF16)]
+        [(rows, F32), (rows, F32), (total, BF16)]
         if keep
         else [(total, BF16), (total, BF16)]
     )
@@ -623,44 +631,59 @@
     )(scalars, *[array for array, _, _ in (*a_runs, *b_runs)])
 
 
-def weight_once_kernel(me_ref, *refs, bits, forms):
-    total = len(forms)
-    a_refs, b_refs, parts = refs[:total], refs[total : 2 * total], refs[2 * total : -1]
-    cols = parts[0].shape[2]
+def weight_once_kernel(me_ref, *refs, products, operands):
+    arrays, outs = refs[:operands], refs[operands:-1]
     for n in range(2):
         refs[-1][n] = me_ref[n]
-
-    def run(ref, form):
-        if form == "turned":
-            return ref[...]
-        start = pl.multiple_of(form(me_ref) * cols, cols)
-        return ref[:, pl.ds(start, cols)]
-
-    turned = forms[0] == "turned"
-    b = jnp.concatenate([run(r, f) for r, f in zip(b_refs, forms)], 1 if turned else 0)
-    for p, ref in enumerate(parts):
-        chunks, rows, _ = ref.shape
-        a = []
-        for k in range(chunks):
-            start = part_chunk(k, p, me_ref[0], bits, bits) * rows
-            here = pl.ds(pl.multiple_of(start, rows), rows)
-            a.append(jnp.concatenate([r[here, :] for r in a_refs], 1))
-        product = dot32(jnp.concatenate(a, 0), b, NT if turned else NN)
-        ref[...] = product.astype(BF16).reshape(ref.shape)
-
-
-def weight_once(scalars, a_list, b_list, forms, cols, members, bits, behind=()):
-    width = a_list[0].shape[0]
-    count = 1 << len(bits)
-    each = shape_of((members // count, width // members, cols), BF16)
-    return vmem_call(
-        partial(weight_once_kernel, bits=bits, forms=forms),
-        [each] * count + [shape_of((2,), jnp.int32)],
+    at = 0
+    for blocks, bits in products:
+        parts = outs[at : at + (1 << len(bits))]
+        at += len(parts)
+        cols = parts[0].shape[2] // len(blocks)
+        for n, block in enumerate(blocks):
+            here = slice(n * cols, (n + 1) * cols)
+            if len(block) == len(parts):
+                for ref, source in zip(parts, block):
+                    ref[:, :, here] = arrays[source][...]
+                continue
+            a_runs, b_runs, turned = block
+            b = jnp.concatenate([run(arrays, me_ref) for run in b_runs], 1 if turned else 0)
+            for p, ref in enumerate(parts):
+                chunks, rows, _ = ref.shape
+                a = []
+                for k in range(chunks):
+                    start = part_chunk(k, p, me_ref[0], bits, bits) * rows
+                    lines = pl.ds(pl.multiple_of(start, rows), rows)
+                    a.append(jnp.concatenate([arrays[m][lines, :] for m in a_runs], 1))
+                product = dot32(jnp.concatenate(a, 0), b, NT if turned else NN)
+                ref[:, :, here] = product.astype(BF16).reshape(chunks, rows, cols)
+
+
+def rows_run(n, first, count):
+    return lambda arrays, me_ref: arrays[n][first : first + count, :]
+
+
+def columns_run(n, cols, block):
+    if block is not None:
+        return lambda arrays, me_ref: arrays[n][:, block * cols : (block + 1) * cols]
+    return lambda arrays, me_ref: arrays[n][:, pl.ds(pl.multiple_of(me_ref[1] * cols, cols), cols)]
+
+
+def weight_once(scalars, arrays, products, width, cols, members, behind):
+    each = [
+        shape_of((members >> len(bits), width // members, cols * len(blocks)), BF16)
+        for blocks, bits in products
+        for _ in range(1 << len(bits))
+    ]
+    outs = vmem_call(
+        partial(weight_once_kernel, products=products, operands=len(arrays)),
+        each + [shape_of((2,), jnp.int32)],
         scalars,
-        [*a_list, *b_list],
+        arrays,
         "weight_once",
         behind,
     )
+    return outs[:2], outs[2:4], outs[4]
 
 
 def column_sums(refs, counts):
@@ -803,6 +826,9 @@
                 total = a if total is None else total + a
             parts.append(total.astype(BF16))
         self.travel(parts)
+
+    def plain_total(self):
+        return sum(a[0].astype(F32) for a in (self.keep, *self.came))
 
     def total(self, widths=None):
         while self.stages:
@@ -1036,7 +1062,9 @@
             third(0), third(1), third(2),
             pl.BlockSpec((cols, width), lambda i: (i, 0)),
             pl.BlockSpec(memory_space=pltpu.SMEM),
-            *[fixed((rows, width))] * (2 * len(feeds)),
+            *[
+                pl.BlockSpec((rows, width), lambda i, n=n: (n, 0)) for _, n in (*feeds, *grads)
+            ],
             *[pl.BlockSpec(memory_space=pl.ANY)] * len(behind),
         ],
         out_specs=(
@@ -1054,16 +1082,16 @@
         ),
         compiler_params=pltpu.CompilerParams(vmem_limit_bytes=VMEM_LIMIT),
         name="close_layer",
-    )(x, g, *vectors, *gm, attended, weight, weight, weight, out_weight, scalars, *feeds, *grads, *behind)
+    )(x, g, *vectors, *gm, attended, weight, weight, weight, out_weight, scalars, *[a for a, _ in (*feeds, *grads)], *behind)
 
 
 def place_kernel(me_ref, own_ref, came_ref, merged_ref, dense_ref):
     half = dense_ref.shape[1] // 2
     for side, ref in enumerate((own_ref, came_ref)):
         at = ((me_ref[1] + side) % 2) * half
-        for third in range(3):
+        for third, block in enumerate((0, 2, 1)):
             start = pl.multiple_of(third * 2 * half + at, half)
-            value = ref[:, third * half : (third + 1) * half]
+            value = ref[:, block * half : (block + 1) * half]
             merged_ref[:, pl.ds(start, half)] = value.astype(F32)
         dense_ref[:, pl.ds(pl.multiple_of(at, half), half)] = ref[:, 3 * half :].astype(F32)
 
@@ -1109,7 +1137,7 @@
     inputs = block_input.reshape(rows, width)
     cot = out_cotangent.reshape(rows, width)
 
-    outgoing, normed_one, normed_two, table, one_t, two_t, cot_t = open_layer(
+    outgoing, normed_one, normed_two, table, turned = open_layer(
         inputs,
         cot,
         me * rows,
@@ -1122,16 +1150,16 @@
     at_head = lax.all_to_all(outgoing, "seq", 0, 0, tiled=True)
 
     rows_list, cot_list = mlp_list(normed_two), mlp_list(cot)
-    two_t, cot_t, one_t = (mlp_list(v, 1) for v in (two_t, cot_t, one_t))
+    turned = mlp_list(turned, 1)
     hidden, grad_pre, grad_hid_bias, *sides = feed(
         rows_list, cot_list, expand_weight, expand_bias, contract_weight
     )
     if pairs == 2:
-        feeds = [sides[0], pair_swap(sides[2])]
-        grads = [sides[1], pair_swap(sides[3])]
+        came = pair_swap(sides[2])
+        feeds, grads = [(sides[0], 0), (came, 0)], [(sides[1], 0), (came, 1)]
     else:
         feeds, grads = (
-            [lax.psum_scatter(v, "mlp", scatter_dimension=0, tiled=True)] for v in sides
+            [(lax.psum_scatter(v, "mlp", scatter_dimension=0, tiled=True), 0)] for v in sides
         )
     slice_width = expand_weight.shape[1]
     block = min(512, slice_width)
@@ -1141,40 +1169,41 @@
             return [(a, shape, lambda i, me: index(0, i, me)) for a in arrays]
         return [(arrays[0], shape, lambda i, me, m=m: index(m, i, me)) for m in range(pairs)]
 
-    def sides_of(arrays):
-        return runs(arrays, (width, rows), lambda m, i, me: (0, m))
+    def sides_of(arrays, part=0):
+        return runs(arrays, (width, rows), lambda m, i, me: (part, m))
 
     def ring_of(products, steps, block, stages):
         stages = ring_stages(stages)
         parts = weight_parts(scalars, products, steps, block, members, stages[0])
         return Ring(scalars, parts, stages)
 
-    def feed_ring(at, b, stages):
+    x_first, y_first = [(0,), (1,), (2,), (3,)], [(1,), (0,), (2,), (3,)]
+
+    def feed_ring(part, b, stages):
         b_runs = [(b, (rows, block), lambda i, me, m=m: (m, i)) for m in range(pairs)]
-        return ring_of([(sides_of(at), b_runs)], slice_width // block, block, stages)
-
-    ring_out = feed_ring(cot_t, hidden, [(0,), (1,), (2,), (3,)])
-    ring_hid = feed_ring(two_t, grad_pre, [(1,), (0,), (2,), (3,)])
-
-    part = (me % parts).astype(jnp.int32)
+        return ring_of([(sides_of(turned, part), b_runs)], slice_width // block, block, stages)
+
+    ring_out = feed_ring(2, hidden, x_first)
+    ring_hid = feed_ring(1, grad_pre, y_first)
+
     query_rows = rows // parts
-    from_first, head_grad, head_delta, probs = forward_head(
-        at_head, part, rows, query_rows, (*ring_out.sent, *ring_hid.sent, *feeds, *grads)
+    part = jnp.stack([me[0] % parts, me[0]]).astype(jnp.int32)
+    from_first, head_grad, head_delta, probs, _ = forward_head(
+        at_head,
+        part,
+        rows,
+        query_rows,
+        (*ring_out.sent, *ring_hid.sent, *[a for a, _ in (*feeds, *grads)], *turned),
     )
     back_first = lax.all_to_all(from_first, "seq", 0, 0, tiled=True)
-    from_second = backward_head(at_head, head_grad, head_delta, probs, rows, query_rows)
-    from_second, ring_out.came, ring_hid.came = lax.optimization_barrier(
-        (from_second, ring_out.came, ring_hid.came)
-    )
+    from_second, after_second = backward_head(
+        scalars, at_head, head_grad, head_delta, probs, rows, query_rows, ()
+    )
+    from_second = after(from_second, *ring_out.came, *ring_hid.came)
     back_second = lax.all_to_all(from_second, "seq", 0, 0, tiled=True)
-    ring_out.hold(from_second)
-    ring_hid.hold(from_second)
-    ring_out.step()
-    ring_hid.step()
-
+    x_first, y_first = [(0,), (1,), (2, 3)], [(1,), (0,), (2, 3)]
     split = pairs == 2 and parts == 1
     share = width // pairs
-    x_first, y_first = [(0,), (1,), (2,), (3,)], [(1,), (0,), (2,), (3,)]
 
     def pieces_of(arrays):
         stacked = jnp.stack([a.reshape(rows, pairs, share) for a in arrays], 2)
@@ -1187,54 +1216,68 @@
 
     if split:
 
-        def ring_once(a_list, b_list, forms, stages, behind=()):
-            stages = ring_stages(stages)
-            *sums, after_it = weight_once(
-                scalars, a_list, b_list, forms, share, members, stages[0], behind
-            )
-            ring = Ring(scalars, sums, stages)
-            ring.me = after_it[0]
-            return ring
-
         attended, grad_v, sent, own_a, own_v = regroup_once(
-            back_first, None, scalars, (*ring_out.sent, *ring_hid.sent)
+            back_first, None, scalars, (from_second,)
         )
         came = pair_swap(sent)
-        ring_v = ring_once(one_t, [own_v, came[width:]], ["turned"] * 2, x_first)
-        ring_d = ring_once(
-            [own_a, came[:width]], cot_list, [lambda me_ref: me_ref[1]] * 2, y_first
+        for ring in (ring_out, ring_hid):
+            ring.hold(sent)
+            ring.step()
+        v_parts, d_parts, _ = weight_once(
+            scalars,
+            [*turned, own_v, came, own_a, *cot_list],
+            [
+                ([((0, 1), (rows_run(2, 0, share), rows_run(3, width, share)), True)], (0,)),
+                (
+                    [((4, 3), (columns_run(5, share, None), columns_run(6, share, None)), False)],
+                    (1,),
+                ),
+            ],
+            width,
+            share,
+            members,
+            (),
         )
         grad_q, grad_k, sent, own_qk = regroup_once(
-            back_second, table, scalars, (*ring_v.sent, *ring_d.sent)
+            back_second, table, scalars, (*v_parts, *d_parts)
         )
         came = pair_swap(sent)
-        ring_q = ring_once(one_t, [own_qk, came], [lambda me_ref: 0] * 2, x_first)
-        ring_k = ring_once(
-            one_t, [own_qk, came], [lambda me_ref: 1] * 2, y_first, tuple(ring_q.sent)
+        qv_parts, kd_parts, weighed = weight_once(
+            scalars,
+            [*turned, own_qk, came, *v_parts, *d_parts],
+            [
+                (
+                    [
+                        ((0, 1), (columns_run(2, share, n), columns_run(3, share, n)), False),
+                        (4 + 2 * n, 5 + 2 * n),
+                    ],
+                    (n,),
+                )
+                for n in range(2)
+            ],
+            width,
+            share,
+            members,
+            (),
         )
+        ring_qv = Ring(scalars, qv_parts, x_first)
+        ring_kd = Ring(scalars, kd_parts, y_first)
     else:
+        for ring in (ring_out, ring_hid):
+            ring.step()
         attended, grad_v, att_t = regroup(back_first, None, scalars, rows, query_rows, False)
         att_t = mlp_list(att_t, 1)
-        v_runs = runs(pieces_of([grad_v]), (rows, share), lambda m, i, me: (m, 0))
-        ring_v = ring_of([(sides_of(one_t), v_runs)], 1, share, x_first)
+        grad_q, grad_k = regroup(back_second, table, scalars, rows, query_rows, False)
+        pieces = [pieces_of([g]) for g in (grad_q, grad_v, grad_k)]
+        q_runs, v_runs, k_runs = (
+            runs(p, (rows, share), lambda m, i, me: (m, 0)) for p in pieces
+        )
         cot_runs = runs(cot_list, (rows, share), lambda m, i, me: (m, me[1]))
-        ring_d = ring_of([(sides_of(att_t), cot_runs)], 1, share, y_first)
-        grad_q, grad_k = regroup(back_second, table, scalars, rows, query_rows, False)
-        pieces = pieces_of([grad_q, grad_k])
-        ring_q, ring_k = (
-            ring_of(
-                [(sides_of(one_t), runs(pieces, (rows, share), lambda m, i, me, n=n: (m, n)))],
-                1,
-                share,
-                stages,
-            )
-            for n, stages in enumerate((x_first, y_first))
-        )
-
-    for ring in (ring_out, ring_v, ring_d):
-        ring.hold(*ring_k.sent)
-    ring_v.pass_on(ring_k.me)
-    ring_d.pass_on(ring_k.me)
+        one = sides_of(turned)
+        ring_qv = ring_of([(one, q_runs), (one, v_runs)], 2, share, x_first)
+        ring_kd = ring_of([(one, k_runs), (sides_of(att_t), cot_runs)], 2, share, y_first)
+
+    ring_out.hold(*ring_kd.sent)
     ring_out.step(ring_hid)
     block_output, grad_input, vec, gm_bias, closed = close_layer(
         inputs,
@@ -1247,12 +1290,11 @@
         feeds,
         grads,
         scalars,
-        (*ring_v.sent, *ring_d.sent, *ring_out.sent),
-    )
-    for ring in (ring_q, ring_k, ring_out):
-        ring.hold(vec)
-    ring_q.pass_on(closed[0])
-    ring_k.pass_on(closed[0])
+        ring_out.sent,
+    )
+    for ring in (ring_qv, ring_kd):
+        ring.pass_on(closed[0])
+    ring_out.came = [after(x, *ring_qv.sent, *ring_kd.sent) for x in ring_out.came]
     ring_out.pass_on(closed[0])
 
     bias_full = lax.dynamic_update_slice_in_dim(
@@ -1263,12 +1305,12 @@
     if pairs == 2:
         mine = lax.dynamic_index_in_dim(packed, pair_me, 1, False)
         other = lax.dynamic_index_in_dim(packed, 1 - pair_me, 1, False)
-        packed = mine + pair_swap(other)
+        packed = mine + pair_swap(after(other, *ring_out.sent))
     else:
         packed = lax.psum_scatter(packed, "mlp", scatter_dimension=1, tiled=False)
+    ring_qv.step(ring_kd)
+    packed = after(packed, *ring_qv.sent)
     packed = jnp.sum(lax.all_to_all(packed, "seq", 0, 0, tiled=True), 0)
-    ring_q.hold(packed)
-    ring_q.step(ring_k, ring_v, ring_d)
     outs, start = [], 0
     for v in vectors:
         size = v.shape[0] // (members * pairs)
@@ -1277,11 +1319,12 @@
     grad_gain_one, grad_shift_one, grad_dense_bias, grad_gain_two, grad_shift_two = outs[:5]
     grad_merged_bias, out_hid_bias = outs[5:]
 
-    out_weight, hid_weight = ring_out.total([slice_width, slice_width])
-    out_weight = jnp.transpose(out_weight)
+    feed_total = ring_out.plain_total()
+    out_weight = jnp.transpose(feed_total[:, :slice_width])
+    hid_weight = feed_total[:, slice_width:]
 
     if pairs == 2:
-        mine, other = ring_q.total()
+        mine, other = ring_qv.total()
         merged, dense = vmem_call(
             place_kernel,
             [shape_of((own // pairs, 3 * width), F32), shape_of((own // pairs, width), F32)],
@@ -1290,11 +1333,11 @@
             "place",
         )
     else:
-        got = ring_q.total([4 * share])[0].reshape(pairs, own // pairs, 4 * share)
+        got = ring_qv.total([4 * share])[0].reshape(pairs, own // pairs, 4 * share)
         got = lax.all_to_all(got, "mlp", 0, 0, tiled=True)
         got = jnp.transpose(got.reshape(pairs, own // pairs, 4, share), (1, 2, 0, 3))
-        got = got.reshape(own // pairs, 4 * width)
-        merged, dense = got[:, : 3 * width], got[:, 3 * width :]
+        merged = jnp.concatenate([got[:, n].reshape(-1, width) for n in (0, 2, 1)], -1)
+        dense = got[:, 3].reshape(-1, width)
     return (
         block_output.reshape(seq_count, rows, width),
         grad_input.reshape(seq_count, rows, width),

time: 273 us -> 262 us (0.960)
  blocking collectives: 11.6 us -> 0 us
  starting transfers between devices: 48.2 us -> 58.5 us
  Pallas kernels: 141 us -> 136 us
    ppermute x16 -> x13, waiting for transfers between devices: 38.1 us -> 23.9 us  [seq_move(): return lax.ppermute(x, 'seq', [(s, s ^ mask) for s in range(members)])]
    all_to_all x1 -> x0, blocking collectives: 11.6 us -> none  [per_device(): packed = jnp.sum(lax.all_to_all(packed, 'seq', 0, 0, tiled=True), 0)]
    all_to_all x0 -> x1, waiting for transfers between devices: none -> 10.3 us  [per_device(): packed = jnp.sum(lax.all_to_all(packed, 'seq', 0, 0, tiled=True), 0)]
    all_to_all x0 -> x1, starting transfers between devices: none -> 6.12 us  [per_device(): packed = jnp.sum(lax.all_to_all(packed, 'seq', 0, 0, tiled=True), 0)]
    pallas_call x14 -> x10, Pallas kernels: 42.4 us -> 36.9 us  [vmem_call(): pl.pallas_call(without(kernel, 1 + len(arrays), len(behind)), in_specs=[p...]
    ppermute x11 -> x8, starting transfers between devices: 8.91 us -> 12.4 us  [pair_swap(): return lax.ppermute(x, 'mlp', [(0, 1), (1, 0)])]
    ppermute x11 -> x8, waiting for transfers between devices: 1.85 us -> 5.34 us  [pair_swap(): return lax.ppermute(x, 'mlp', [(0, 1), (1, 0)])]
    convert_element_type x5 -> x3, other arithmetic: 7.02 us -> 5.14 us  [pass_on(): parts.append(total.astype(BF16))]
  transfers between devices with their start and end apart: 30 -> 25, of which waited for: 7 -> 15; matrix products, arithmetic and copies ran while one was open for 5% -> 4% of each run, Pallas kernels for 48% -> 47%
where the time goes in v2:
time: 262 us; the launch traced here: 260 us
  Pallas kernels  136 us (52%)
  starting transfers between devices  58.5 us (22%)
  waiting for transfers between devices  41.3 us (16%)
  local copies, waits for them, and re-layouts  13.9 us (5%)
  other arithmetic  7.67 us (3%)
  between operations  3 us (1%)
    pallas_call x10, Pallas kernels, vmem_call(): pl.pallas_call(without(kernel, 1 + len(arrays), len(behind)), in_specs=[p...  36.9 us
    pallas_call x1, Pallas kernels, forward_head(): pl.pallas_call(without(partial(forward_kernel, key_rows=key_rows, query_r...  26.9 us
    ppermute x13, waiting for transfers between devices, seq_move(): return lax.ppermute(x, 'seq', [(s, s ^ mask) for s in range(members)])  23.9 us
    pallas_call x1, Pallas kernels, backward_head(): pl.pallas_call(without(partial(backward_kernel, key_rows=key_rows, query_...  22.5 us
    pallas_call x1, Pallas kernels, feed(): pl.pallas_call(partial(feed_kernel, count=count, keep=keep), grid=(hidden...  17.3 us
    ppermute x13, starting transfers between devices, seq_move(): return lax.ppermute(x, 'seq', [(s, s ^ mask) for s in range(members)])  15.1 us
    pallas_call x2, Pallas kernels, weight_parts(): pl.pallas_call(partial(weight_kernel, bits=bits, counts=[len(a) for a, _...  12.6 us
    ppermute x8, starting transfers between devices, pair_swap(): return lax.ppermute(x, 'mlp', [(0, 1), (1, 0)])  12.4 us
  transfers between devices with their start and end apart: 25, of which 15 were waited for; matrix products, arithmetic and copies ran while one was open for 4% of the time, Pallas kernels for 47%

profile of v2, /device:TPU:1, one launch (start us, length us, event | category | flops | bytes accessed | tf_op | source)
XLA Modules:
  0.0 260.2 jit_solution(301270103538166166)
XLA Ops:
  1.3 9.4 %open_layer.1 = (bf16[16,1,512,128]{3,2,1,0:T(8,128)(2,1)}, bf16[256,1024]{1,0:T(8,128)(2,1)}, bf16[256,1024]{1,0:T(8,128)(2,1)}, f32[3,256,128]{2,1,0:T(8,128)}, bf16[3072,256]{1,0:T(8,128)(2,1)}) custom-call(s32[1]{0:T(128)S(6)} %mul.8.first_ref, bf16[256,1024]{1,0:T(8,128)(2,1)} %bitcast.47, bf16[256,1024]{1,0:T(8,128)(2,1)} %bitcast.1.g_ref.refs_2_.refs_5_.refs_1_, ...), custom_call_target="tpu_custom_call" | custom-call | flops 134217728 | bytes 819200 | tf_op jit(solution)/shard_map/open_layer/pallas_call | solution.py:141
  10.7 7.6 %all-to-all-start = ((bf16[16,512,128]{2,1,0:T(8,128)(2,1)}), bf16[16,512,128]{2,1,0:T(8,128)(2,1)}, u32[]{:S(2)}, u32[]{:S(2)}) async-start(bf16[16,512,128]{2,1,0:T(8,128)(2,1)} %bitcast.49), calls=%async_computation | async-start | bytes 4194304 | tf_op jit(solution)/shard_map/all_to_all | solution.py:1150
  18.3 1.0 collective-permute-start.1
  20.4 0.6 collective-permute-done.1.refs_1_
  21.1 1.5 collective-permute-done.2.refs_3_.refs_6_
  22.6 0.8 copy-done.4
  23.4 17.3 %feed.1 = (bf16[512,2048]{1,0:T(8,128)(2,1)}, bf16[512,2048]{1,0:T(8,128)(2,1)}, f32[1,2048]{1,0:T(1,128)}, f32[256,1024]{1,0:T(8,128)}, f32[256,1024]{1,0:T(8,128)}, /*index=5*/bf16[512,1024]{1,0:T(8,128)(2,1)}) custom-call(bf16[256,1024]{1,0:T(8,128)(2,1)} %get-tuple-element.75.refs_0_, bf16[256,1024]{1,0:T(8,128)(2,1)} %copy-done.12, ...), custom_call_target="tpu_custom_call" | custom-call | flops 536870912 | bytes 786432 | tf_op jit(solution)/shard_map/feed/pallas_call | solution.py:537
  41.1 0.7 pad_add_fusion
  41.7 1.1 copy-done.1
  42.9 6.3 %weight_parts.3 = (bf16[8,64,2048]{2,1,0:T(8,128)(2,1)}, bf16[8,64,2048]{2,1,0:T(8,128)(2,1)}) custom-call(s32[2]{0:T(128)} %get-tuple-element.150.me_ref.refs_0_.refs_14_, bf16[3072,256]{1,0:T(8,128)(2,1)} %get-tuple-element.74.refs_0_.refs_8_, bf16[3072,256]{1,0:T(8,128)(2,1)} %copy-done.1, bf16[512,2048]{1,0:T(8,128)(2,1)} %get-tuple-element.78.refs_2_.refs_3_, ...), custom_call_target="tpu_custom_call" | custom-call | flops 134217728 | bytes 458752 | tf_op jit(solution)/shard_map/weight_parts/pallas_call | solution.py:615
  49.2 1.6 collective-permute-start.5
  50.8 6.3 %weight_parts.2 = (bf16[8,64,2048]{2,1,0:T(8,128)(2,1)}, bf16[8,64,2048]{2,1,0:T(8,128)(2,1)}) custom-call(s32[2]{0:T(128)} %get-tuple-element.150.me_ref.refs_0_.refs_14_, bf16[3072,256]{1,0:T(8,128)(2,1)} %get-tuple-element.74.refs_0_.refs_8_, bf16[3072,256]{1,0:T(8,128)(2,1)} %copy-done.1, bf16[512,2048]{1,0:T(8,128)(2,1)} %get-tuple-element.76.refs_2_.refs_3_, ...), custom_call_target="tpu_custom_call" | custom-call | flops 134217728 | bytes 458752 | tf_op jit(solution)/shard_map/weight_parts/pallas_call | solution.py:615
  57.1 1.2 collective-permute-start.4
  58.3 1.5 all-to-all-done.refs_1_.x_ref
  59.8 26.9 %forward_head.1 = (bf16[16,256,128]{2,1,0:T(8,128)(2,1)}, bf16[4,1024,128]{2,1,0:T(8,128)(2,1)}, f32[4,1024,128]{2,1,0:T(8,128)}, bf16[20,1024,512]{2,1,0:T(8,128)(2,1)}, s32[1]{0:T(128)}) custom-call(s32[2]{0:T(128)} %get-tuple-element.151.refs_0_, bf16[16,512,128]{2,1,0:T(8,128)(2,1)} %all-to-all-done.refs_1_.x_ref, ...), custom_call_target="tpu_custom_call" | custom-call | flops 16106127360 | bytes 25165824 | tf_op jit(solution)/shard_map/forward_head/pallas_call | solution.py:409
  86.6 10.9 %all-to-all-start.2 = ((bf16[16,256,128]{2,1,0:T(8,128)(2,1)}), bf16[16,256,128]{2,1,0:T(8,128)(2,1)S(1)}, u32[]{:S(2)}, u32[]{:S(2)}) async-start(bf16[16,256,128]{2,1,0:T(8,128)(2,1)} %get-tuple-element.89), calls=%async_computation.2 | async-start | bytes 2097152 | tf_op jit(solution)/shard_map/all_to_all | solution.py:1198
  97.5 22.5 %backward_head.1 = (bf16[16,256,128]{2,1,0:T(8,128)(2,1)}, s32[1]{0:T(128)}) custom-call(s32[2]{0:T(128)} %get-tuple-element.150.me_ref.refs_0_.refs_14_, bf16[16,512,128]{2,1,0:T(8,128)(2,1)} %all-to-all-done.refs_1_.x_ref, bf16[4,1024,128]{2,1,0:T(8,128)(2,1)} %get-tuple-element.83.g_ref, f32[4,1024,128]{2,1,0:T(8,128)} %get-tuple-element.84.d_ref, ...), custom_call_target="tpu_custom_call" | custom-call | flops 16106127360 | bytes 25165824 | tf_op jit(solution)/shard_map/backward_head/pallas_call | solution.py:452
  120.0 1.3 copy-done.5
  121.4 6.3 %all-to-all-start.1 = ((bf16[16,256,128]{2,1,0:T(8,128)(2,1)}), bf16[16,256,128]{2,1,0:T(8,128)(2,1)S(1)}, u32[]{:S(2)}, u32[]{:S(2)}) async-start(bf16[16,256,128]{2,1,0:T(8,128)(2,1)} %get-tuple-element.87.refs_2_), calls=%async_computation.1 | async-start | bytes 2097152 | tf_op jit(solution)/shard_map/all_to_all | solution.py:1203
  127.7 3.6 %regroup_once.2 = (bf16[256,1024]{1,0:T(8,128)(2,1)}, bf16[256,1024]{1,0:T(8,128)(2,1)}, bf16[1536,256]{1,0:T(8,128)(2,1)}, bf16[1024,256]{1,0:T(8,128)(2,1)}, bf16[512,256]{1,0:T(8,128)(2,1)}) custom-call(s32[2]{0:T(128)} %get-tuple-element.150.me_ref.refs_0_.refs_14_, bf16[16,256,128]{2,1,0:T(8,128)(2,1)} %copy-done.2, ...), custom_call_target="tpu_custom_call" | custom-call | flops 32768 | bytes 98304 | tf_op jit(solution)/shard_map/regroup_once/pallas_call | solution.py:741
  131.4 2.5 collective-permute-start.6
  133.9 4.0 %add_parts.5 = (bf16[4,64,2048]{2,1,0:T(8,128)(2,1)}, bf16[4,64,2048]{2,1,0:T(8,128)(2,1)}) custom-call(s32[2]{0:T(128)} %get-tuple-element.150.me_ref.refs_0_.refs_14_, bf16[8,64,2048]{2,1,0:T(8,128)(2,1)} %get-tuple-element.104.refs_1_, bf16[8,64,2048]{2,1,0:T(8,128)(2,1)} %collective-permute-done.5.refs_2_, bf16[1536,256]{1,0:T(8,128)(2,1)} %get-tuple-element.91.refs_3_), custom_call_target="tpu_custom_call" | custom-call | flops 131072 | bytes 393216 | tf_op jit(solution)/shard_map/add_parts/pallas_call | solution.py:741
  137.9 1.6 collective-permute-start.8
  139.6 4.0 %add_parts.4 = (bf16[4,64,2048]{2,1,0:T(8,128)(2,1)}, bf16[4,64,2048]{2,1,0:T(8,128)(2,1)}) custom-call(s32[2]{0:T(128)} %get-tuple-element.150.me_ref.refs_0_.refs_14_, bf16[8,64,2048]{2,1,0:T(8,128)(2,1)} %get-tuple-element.101.refs_1_, bf16[8,64,2048]{2,1,0:T(8,128)(2,1)} %copy-done.5, bf16[1536,256]{1,0:T(8,128)(2,1)} %get-tuple-element.91.refs_3_), custom_call_target="tpu_custom_call" | custom-call | flops 131072 | bytes 393216 | tf_op jit(solution)/shard_map/add_parts/pallas_call | solution.py:741
  143.6 1.2 collective-permute-start.7
  144.8 4.8 %weight_once.2 = (bf16[8,64,512]{2,1,0:T(8,128)(2,1)}, bf16[8,64,512]{2,1,0:T(8,128)(2,1)}, bf16[8,64,512]{2,1,0:T(8,128)(2,1)}, bf16[8,64,512]{2,1,0:T(8,128)(2,1)}, s32[2]{0:T(128)}) custom-call(s32[2]{0:T(128)} %get-tuple-element.150.me_ref.refs_0_.refs_14_, bf16[3072,256]{1,0:T(8,128)(2,1)} %get-tuple-element.74.refs_0_.refs_8_, ...), custom_call_target="tpu_custom_call" | custom-call | flops 180224 | bytes 540672 | tf_op jit(solution)/shard_map/weight_once/pallas_call | solution.py:741
  149.8 1.0 copy-done.3
  150.8 3.9 %regroup_once.3 = (bf16[256,1024]{1,0:T(8,128)(2,1)}, bf16[256,1024]{1,0:T(8,128)(2,1)}, bf16[256,1024]{1,0:T(8,128)(2,1)}, bf16[256,1024]{1,0:T(8,128)(2,1)}) custom-call(s32[2]{0:T(128)} %get-tuple-element.150.me_ref.refs_0_.refs_14_, bf16[16,256,128]{2,1,0:T(8,128)(2,1)} %copy-done.3, f32[3,256,128]{2,1,0:T(8,128)} %get-tuple-element.88.refs_2_, ...), custom_call_target="tpu_custom_call" | custom-call | flops 38912 | bytes 116736 | tf_op jit(solution)/shard_map/regroup_once/pallas_call | solution.py:741
  154.7 3.2 %collective-permute-start.9 = (bf16[256,1024]{1,0:T(8,128)(2,1)}, bf16[256,1024]{1,0:T(8,128)(2,1)S(1)}, u32[]{:S(2)}, u32[]{:S(2)}) collective-permute-start(bf16[256,1024]{1,0:T(8,128)(2,1)} %get-tuple-element.108), channel_id=1, source_target_pairs={{0,1},{1,0},{2,3},{3,2},{4,5},{5,4},{6,7},{7,6},{8,9},{9,8},{10,11... | collective-permute-start | bytes 1572872 | tf_op jit(solution)/shard_map/ppermute | solution.py:1100
  158.0 1.7 collective-permute-done.9.refs_3_
  159.7 0.8 copy-done.13
  160.5 5.9 %weight_once.3 = (bf16[8,64,1024]{2,1,0:T(8,128)(2,1)}, bf16[8,64,1024]{2,1,0:T(8,128)(2,1)}, bf16[8,64,1024]{2,1,0:T(8,128)(2,1)}, bf16[8,64,1024]{2,1,0:T(8,128)(2,1)}, s32[2]{0:T(128)}) custom-call(s32[2]{0:T(128)} %get-tuple-element.150.me_ref.refs_0_.refs_14_, bf16[3072,256]{1,0:T(8,128)(2,1)} %get-tuple-element.74.refs_0_.refs_8_, ...), custom_call_target="tpu_custom_call" | custom-call | flops 196608 | bytes 589824 | tf_op jit(solution)/shard_map/weight_once/pallas_call | solution.py:741
  166.5 1.7 collective-permute-start.12
  168.5 1.2 collective-permute-done.8.refs_4_
  169.7 1.3 collective-permute-done.7.refs_2_
  171.1 1.0 copy-done.10
  172.1 4.0 %add_parts.6 = (bf16[2,64,4096]{2,1,0:T(8,128)(2,1)}, bf16[2,64,4096]{2,1,0:T(8,128)(2,1)}) custom-call(s32[2]{0:T(128)} %get-tuple-element.150.me_ref.refs_0_.refs_14_, bf16[4,64,2048]{2,1,0:T(8,128)(2,1)} %get-tuple-element.102.refs_1_, bf16[4,64,2048]{2,1,0:T(8,128)(2,1)} %copy-done.10, bf16[4,64,2048]{2,1,0:T(8,128)(2,1)} %get-tuple-element.105.refs_3_, ...), custom_call_target="tpu_custom_call" | custom-call | flops 131072 | bytes 393216 | tf_op jit(solution)/shard_map/add_parts/pallas_call | solution.py:741
  176.0 1.5 collective-permute-start.10
  177.5 10.4 %close_layer.1 = (bf16[256,1024]{1,0:T(8,128)(2,1)}, f32[256,1024]{1,0:T(8,128)}, f32[5,1024]{1,0:T(8,128)}, f32[3,1024]{1,0:T(4,128)}, s32[2]{0:T(128)}) custom-call(bf16[256,1024]{1,0:T(8,128)(2,1)} %bitcast.48, bf16[256,1024]{1,0:T(8,128)(2,1)} %bitcast.1.g_ref.refs_2_.refs_5_.refs_1_, bf16[1024]{0:T(1024)(128)(2,1)} %refs_2_.1, bf16[1024]{0:T(1024)(128)(2,1)} %refs_3_.1, ...), custom_call_target="tpu_custom_call" | custom-call | flops 134217728 | bytes 917504 | tf_op jit(solution)/shard_map/close_layer/pallas_call | solution.py:1047
  189.9 3.8 %collective-permute-done.12 = bf16[8,64,1024]{2,1,0:T(8,128)(2,1)} collective-permute-done((bf16[8,64,1024]{2,1,0:T(8,128)(2,1)}, bf16[8,64,1024]{2,1,0:T(8,128)(2,1)}, u32[]{:S(2)}, u32[]{:S(2)}) %collective-permute-start.12) | collective-permute-done | bytes 1048608 | tf_op jit(solution)/shard_map/ppermute | solution.py:759
  193.7 2.6 add_convert_fusion.1
  196.5 1.4 add_convert_fusion.2
  197.9 0.7 collective-permute-start.14
  198.6 1.5 collective-permute-done.10
  200.1 1.2 add_convert_fusion.3
  201.3 1.2 collective-permute-start.20
  203.6 3.1 %collective-permute-start.13 = (f32[16,384]{1,0:T(8,128)S(1)}, f32[16,384]{1,0:T(8,128)S(1)}, u32[]{:S(2)}, u32[]{:S(2)}) collective-permute-start(f32[16,384]{1,0:T(8,128)S(1)} %bitcast.57), channel_id=1, source_target_pairs={{0,1},{1,0},{2,3},{3,2},{4,5},{5,4},{6,7},{7,6},{8,9},{9,8},{10,11... | collective-permute-start | bytes 73736 | tf_op jit(solution)/shard_map/ppermute | solution.py:1100
  206.7 0.8 collective-permute-done.13
  207.5 1.9 collective-permute-done.15.refs_3_
  209.4 1.1 collective-permute-done.14.refs_1_
  210.5 0.8 copy-done.11
  211.3 2.7 %add_parts.7 = (bf16[1,64,2048]{2,1,0:T(8,128)(2,1)}, bf16[1,64,2048]{2,1,0:T(8,128)(2,1)}, bf16[1,64,2048]{2,1,0:T(8,128)(2,1)}, bf16[1,64,2048]{2,1,0:T(8,128)(2,1)}) custom-call(s32[2]{0:T(128)} %get-tuple-element.150.me_ref.refs_0_.refs_14_, bf16[4,64,1024]{2,1,0:T(8,128)(2,1)} %bitcast.51, bf16[4,64,1024]{2,1,0:T(8,128)(2,1)} %copy-done.11, ...), custom_call_target="tpu_custom_call" | custom-call | flops 65536 | bytes 196608 | tf_op jit(solution)/shard_map/add_parts/pallas_call | solution.py:741
  214.0 1.3 collective-permute-start.16
  215.2 2.6 collective-permute-start.17
  218.4 6.1 %all-to-all-start.3 = ((f32[16,1,384]{2,1,0:T(1,128)}), f32[16,1,384]{2,1,0:T(1,128)S(1)}, u32[]{:S(2)}, u32[]{:S(2)}) async-start(f32[16,1,384]{2,1,0:T(1,128)} %all_to_all.18), calls=%async_computation.3 | async-start | bytes 49152 | tf_op jit(solution)/shard_map/all_to_all | solution.py:1313
  224.6 13.1 %collective-permute-done.20 = bf16[1,64,4096]{2,1,0:T(8,128)(2,1)S(1)} collective-permute-done((bf16[1,64,4096]{2,1,0:T(8,128)(2,1)S(1)}, bf16[1,64,4096]{2,1,0:T(8,128)(2,1)S(1)}, u32[]{:S(2)}, u32[]{:S(2)}) %collective-permute-start.20) | collective-permute-done | bytes 524320 | tf_op jit(solution)/shard_map/ppermute | solution.py:759
  237.7 1.2 add_bitcast_fusion
  238.9 1.0 slice_bitcast_fusion
  239.9 10.3 %all-to-all-done.3 = f32[16,1,384]{2,1,0:T(1,128)S(1)} async-done(((f32[16,1,384]{2,1,0:T(1,128)}), f32[16,1,384]{2,1,0:T(1,128)S(1)}, u32[]{:S(2)}, u32[]{:S(2)}) %all-to-all-start.3) | async-done | bytes 24608 | tf_op jit(solution)/shard_map/all_to_all | solution.py:1313
  251.4 0.7 copy-done.14
  252.3 2.1 last_sum.1
  254.4 1.7 collective-permute-start.19
  257.2 0.7 copy-done.17
  257.9 1.8 place.1
  (78 shorter events, 7.8 us)
Async XLA Ops:
  10.6 8.7 %copy-start = (bf16[3072,256]{1,0:T(8,128)(2,1)S(1)}, bf16[3072,256]{1,0:T(8,128)(2,1)}, u32[]{:S(2)}) copy-start(bf16[3072,256]{1,0:T(8,128)(2,1)} %get-tuple-element.74.refs_0_.refs_8_) | copy-start | bytes 4718596
  10.7 9.2 %copy-start.21 = (bf16[2048]{0:T(1024)(128)(2,1)S(1)}, bf16[2048]{0:T(1024)(128)(2,1)}, u32[]{:S(2)}) copy-start(bf16[2048]{0:T(1024)(128)(2,1)} %param.25) | copy-start | bytes 12292
  10.7 49.1 %all-to-all-start = ((bf16[16,512,128]{2,1,0:T(8,128)(2,1)}), bf16[16,512,128]{2,1,0:T(8,128)(2,1)}, u32[]{:S(2)}, u32[]{:S(2)}) async-start(bf16[16,512,128]{2,1,0:T(8,128)(2,1)} %bitcast.49), calls=%async_computation | async-start | bytes 4194304 | tf_op jit(solution)/shard_map/all_to_all | solution.py:1150
  18.3 2.8 %collective-permute-start.1 = (bf16[256,1024]{1,0:T(8,128)(2,1)}, bf16[256,1024]{1,0:T(8,128)(2,1)S(1)}, u32[]{:S(2)}, u32[]{:S(2)}) collective-permute-start(bf16[256,1024]{1,0:T(8,128)(2,1)} %get-tuple-element.75.refs_0_), channel_id=1, source_target_pairs={{0,1},{1,0},{2,3},{3,2},{4,5},{5,4},{6,7},{7,6},{8,9},{9,8},{10,11... | collective-permute-start | bytes 1572872 | tf_op jit(solution)/shard_map/ppermute | solution.py:1100
  19.3 3.2 %collective-permute-start.2 = (bf16[256,1024]{1,0:T(8,128)(2,1)}, bf16[256,1024]{1,0:T(8,128)(2,1)S(1)}, u32[]{:S(2)}, u32[]{:S(2)}) collective-permute-start(bf16[256,1024]{1,0:T(8,128)(2,1)} %bitcast.1.g_ref.refs_2_.refs_5_.refs_1_), channel_id=1, source_target_pairs={{0,1},{1,0},{2,3},{3,2},{4,5},{5,4},{6,7},{7,6},{8,9},{9,8},{10,11... | collective-permute-start | bytes 1572872 | tf_op jit(solution)/shard_map/ppermute | solution.py:1100
  19.4 22.3 %collective-permute-start = (bf16[3072,256]{1,0:T(8,128)(2,1)S(1)}, bf16[3072,256]{1,0:T(8,128)(2,1)S(1)}, u32[]{:S(2)}, u32[]{:S(2)}) collective-permute-start(bf16[3072,256]{1,0:T(8,128)(2,1)S(1)} %copy-done), channel_id=1, source_target_pairs={{0,1},{1,0},{2,3},{3,2},{4,5},{5,4},{6,7},{7,6},{8,9},{9,8},{10,11... | collective-permute-start | bytes 4718600 | tf_op jit(solution)/shard_map/ppermute | solution.py:1100
  21.1 1.5 copy-start.12
  22.6 0.8 copy-start.4
  40.6 17.7 %collective-permute-start.3 = (bf16[512,1024]{1,0:T(8,128)(2,1)}, bf16[512,1024]{1,0:T(8,128)(2,1)}, u32[]{:S(2)}, u32[]{:S(2)}) collective-permute-start(bf16[512,1024]{1,0:T(8,128)(2,1)} %get-tuple-element.81), channel_id=1, source_target_pairs={{0,1},{1,0},{2,3},{3,2},{4,5},{5,4},{6,7},{7,6},{8,9},{9,8},{10,11... | collective-permute-start | bytes 3145736 | tf_op jit(solution)/shard_map/ppermute | solution.py:1100
  41.7 1.1 copy-start.1
  49.2 70.8 %collective-permute-start.5 = (bf16[8,64,2048]{2,1,0:T(8,128)(2,1)}, bf16[8,64,2048]{2,1,0:T(8,128)(2,1)}, u32[]{:S(2)}, u32[]{:S(2)}) collective-permute-start(bf16[8,64,2048]{2,1,0:T(8,128)(2,1)} %get-tuple-element.79.refs_3_), channel_id=1, source_target_pairs={{0,4},{2,6},{4,0},{6,2},{8,12},{10,14},{12,8},{14,10},{16,20},{18,... | collective-permute-start | bytes 6291464 | tf_op jit(solution)/shard_map/ppermute | solution.py:759
  57.1 62.9 %collective-permute-start.4 = (bf16[8,64,2048]{2,1,0:T(8,128)(2,1)}, bf16[8,64,2048]{2,1,0:T(8,128)(2,1)S(1)}, u32[]{:S(2)}, u32[]{:S(2)}) collective-permute-start(bf16[8,64,2048]{2,1,0:T(8,128)(2,1)} %get-tuple-element.77.refs_2_), channel_id=1, source_target_pairs={{0,2},{2,0},{4,6},{6,4},{8,10},{10,8},{12,14},{14,12},{16,18},{18,... | collective-permute-start | bytes 6291464 | tf_op jit(solution)/shard_map/ppermute | solution.py:759
  86.6 33.4 %all-to-all-start.2 = ((bf16[16,256,128]{2,1,0:T(8,128)(2,1)}), bf16[16,256,128]{2,1,0:T(8,128)(2,1)S(1)}, u32[]{:S(2)}, u32[]{:S(2)}) async-start(bf16[16,256,128]{2,1,0:T(8,128)(2,1)} %get-tuple-element.89), calls=%async_computation.2 | async-start | bytes 2097152 | tf_op jit(solution)/shard_map/all_to_all | solution.py:1198
  120.0 1.3 copy-start.5
  120.0 7.7 %copy-start.2 = (bf16[16,256,128]{2,1,0:T(8,128)(2,1)}, bf16[16,256,128]{2,1,0:T(8,128)(2,1)S(1)}, u32[]{:S(2)}) copy-start(bf16[16,256,128]{2,1,0:T(8,128)(2,1)S(1)} %all-to-all-done.2.refs_1_) | copy-start | bytes 3145732
  121.4 28.5 %all-to-all-start.1 = ((bf16[16,256,128]{2,1,0:T(8,128)(2,1)}), bf16[16,256,128]{2,1,0:T(8,128)(2,1)S(1)}, u32[]{:S(2)}, u32[]{:S(2)}) async-start(bf16[16,256,128]{2,1,0:T(8,128)(2,1)} %get-tuple-element.87.refs_2_), calls=%async_computation.1 | async-start | bytes 2097152 | tf_op jit(solution)/shard_map/all_to_all | solution.py:1203
  131.4 13.4 %collective-permute-start.6 = (bf16[1536,256]{1,0:T(8,128)(2,1)}, bf16[1536,256]{1,0:T(8,128)(2,1)}, u32[]{:S(2)}, u32[]{:S(2)}) collective-permute-start(bf16[1536,256]{1,0:T(8,128)(2,1)} %get-tuple-element.91.refs_3_), channel_id=1, source_target_pairs={{0,1},{1,0},{2,3},{3,2},{4,5},{5,4},{6,7},{7,6},{8,9},{9,8},{10,11... | collective-permute-start | bytes 2359304 | tf_op jit(solution)/shard_map/ppermute | solution.py:1100
  137.9 31.8 %collective-permute-start.8 = (bf16[4,64,2048]{2,1,0:T(8,128)(2,1)}, bf16[4,64,2048]{2,1,0:T(8,128)(2,1)S(1)}, u32[]{:S(2)}, u32[]{:S(2)}) collective-permute-start(bf16[4,64,2048]{2,1,0:T(8,128)(2,1)} %get-tuple-element.106), channel_id=1, source_target_pairs={{0,2},{2,0},{4,6},{6,4},{8,10},{10,8},{12,14},{14,12},{16,18},{18,... | collective-permute-start | bytes 3145736 | tf_op jit(solution)/shard_map/ppermute | solution.py:759
  143.6 27.5 %collective-permute-start.7 = (bf16[4,64,2048]{2,1,0:T(8,128)(2,1)}, bf16[4,64,2048]{2,1,0:T(8,128)(2,1)S(1)}, u32[]{:S(2)}, u32[]{:S(2)}) collective-permute-start(bf16[4,64,2048]{2,1,0:T(8,128)(2,1)} %get-tuple-element.103), channel_id=1, source_target_pairs={{0,4},{2,6},{4,0},{6,2},{8,12},{10,14},{12,8},{14,10},{16,20},{18,... | collective-permute-start | bytes 3145736 | tf_op jit(solution)/shard_map/ppermute | solution.py:759
  149.8 1.0 copy-start.3
  154.7 5.0 %collective-permute-start.9 = (bf16[256,1024]{1,0:T(8,128)(2,1)}, bf16[256,1024]{1,0:T(8,128)(2,1)S(1)}, u32[]{:S(2)}, u32[]{:S(2)}) collective-permute-start(bf16[256,1024]{1,0:T(8,128)(2,1)} %get-tuple-element.108), channel_id=1, source_target_pairs={{0,1},{1,0},{2,3},{3,2},{4,5},{5,4},{6,7},{7,6},{8,9},{9,8},{10,11... | collective-permute-start | bytes 1572872 | tf_op jit(solution)/shard_map/ppermute | solution.py:1100
  159.7 0.8 copy-start.13
  166.5 27.2 %collective-permute-start.12 = (bf16[8,64,1024]{2,1,0:T(8,128)(2,1)}, bf16[8,64,1024]{2,1,0:T(8,128)(2,1)}, u32[]{:S(2)}, u32[]{:S(2)}) collective-permute-start(bf16[8,64,1024]{2,1,0:T(8,128)(2,1)} %get-tuple-element.109.refs_5_), channel_id=1, source_target_pairs={{0,4},{2,6},{4,0},{6,2},{8,12},{10,14},{12,8},{14,10},{16,20},{18,... | collective-permute-start | bytes 3145736 | tf_op jit(solution)/shard_map/ppermute | solution.py:759
  168.2 28.2 %collective-permute-start.11 = (bf16[8,64,1024]{2,1,0:T(8,128)(2,1)}, bf16[8,64,1024]{2,1,0:T(8,128)(2,1)S(1)}, u32[]{:S(2)}, u32[]{:S(2)}) collective-permute-start(bf16[8,64,1024]{2,1,0:T(8,128)(2,1)} %get-tuple-element.119), channel_id=1, source_target_pairs={{0,2},{2,0},{4,6},{6,4},{8,10},{10,8},{12,14},{14,12},{16,18},{18,... | collective-permute-start | bytes 3145736 | tf_op jit(solution)/shard_map/ppermute | solution.py:759
  169.7 1.3 copy-start.9
  171.1 1.0 copy-start.10
  176.0 24.1 %collective-permute-start.10 = (bf16[2,64,4096]{2,1,0:T(8,128)(2,1)}, bf16[2,64,4096]{2,1,0:T(8,128)(2,1)}, u32[]{:S(2)}, u32[]{:S(2)}) collective-permute-start(bf16[2,64,4096]{2,1,0:T(8,128)(2,1)} %get-tuple-element.110.refs_19_), channel_id=1, source_target_pairs={{0,8},{2,10},{4,12},{6,14},{8,0},{10,2},{12,4},{14,6},{16,24},{18,... | collective-permute-start | bytes 3145736 | tf_op jit(solution)/shard_map/ppermute | solution.py:759
  177.5 16.2 %copy-start.7 = (bf16[8,64,1024]{2,1,0:T(8,128)(2,1)S(1)}, bf16[8,64,1024]{2,1,0:T(8,128)(2,1)}, u32[]{:S(2)}) copy-start(bf16[8,64,1024]{2,1,0:T(8,128)(2,1)} %get-tuple-element.120) | copy-start | bytes 3145732
  187.8 8.6 %copy-start.6 = (bf16[8,64,1024]{2,1,0:T(8,128)(2,1)S(1)}, bf16[8,64,1024]{2,1,0:T(8,128)(2,1)}, u32[]{:S(2)}) copy-start(bf16[8,64,1024]{2,1,0:T(8,128)(2,1)} %get-tuple-element.118) | copy-start | bytes 3145732
  196.2 3.9 %copy-start.8 = (bf16[2,64,4096]{2,1,0:T(8,128)(2,1)S(1)}, bf16[2,64,4096]{2,1,0:T(8,128)(2,1)}, u32[]{:S(2)}) copy-start(bf16[2,64,4096]{2,1,0:T(8,128)(2,1)} %get-tuple-element.116) | copy-start | bytes 3145732
  196.2 13.1 %collective-permute-start.15 = (bf16[4,64,1024]{2,1,0:T(8,128)(2,1)}, bf16[4,64,1024]{2,1,0:T(8,128)(2,1)}, u32[]{:S(2)}, u32[]{:S(2)}) collective-permute-start(bf16[4,64,1024]{2,1,0:T(8,128)(2,1)} %bitcast.18), channel_id=1, source_target_pairs={{0,2},{2,0},{4,6},{6,4},{8,10},{10,8},{12,14},{14,12},{16,18},{18,... | collective-permute-start | bytes 1572872 | tf_op jit(solution)/shard_map/ppermute | solution.py:759
  196.5 6.1 %copy-start.20 = (f32[1,2048]{1,0:T(1,128)S(1)}, f32[1,2048]{1,0:T(1,128)}, u32[]{:S(2)}) copy-start(f32[1,2048]{1,0:T(1,128)} %get-tuple-element.115) | copy-start | bytes 24580
  196.5 6.3 %copy-start.19 = (f32[5,1024]{1,0:T(8,128)S(1)}, f32[5,1024]{1,0:T(8,128)}, u32[]{:S(2)}) copy-start(f32[5,1024]{1,0:T(8,128)} %get-tuple-element.113) | copy-start | bytes 61444
  196.5 6.8 %copy-start.18 = (f32[3,1024]{1,0:T(4,128)S(1)}, f32[3,1024]{1,0:T(4,128)}, u32[]{:S(2)}) copy-start(f32[3,1024]{1,0:T(4,128)} %get-tuple-element.114) | copy-start | bytes 36868
  197.9 12.6 %collective-permute-start.14 = (bf16[4,64,1024]{2,1,0:T(8,128)(2,1)}, bf16[4,64,1024]{2,1,0:T(8,128)(2,1)S(1)}, u32[]{:S(2)}, u32[]{:S(2)}) collective-permute-start(bf16[4,64,1024]{2,1,0:T(8,128)(2,1)} %bitcast.14), channel_id=1, source_target_pairs={{0,4},{2,6},{4,0},{6,2},{8,12},{10,14},{12,8},{14,10},{16,20},{18,... | collective-permute-start | bytes 1572872 | tf_op jit(solution)/shard_map/ppermute | solution.py:759
  201.3 36.4 %collective-permute-start.20 = (bf16[1,64,4096]{2,1,0:T(8,128)(2,1)S(1)}, bf16[1,64,4096]{2,1,0:T(8,128)(2,1)S(1)}, u32[]{:S(2)}, u32[]{:S(2)}) collective-permute-start(bf16[1,64,4096]{2,1,0:T(8,128)(2,1)S(1)} %add_convert_fusion.3), channel_id=1, source_target_pairs={{0,16},{2,18},{4,20},{6,22},{8,24},{10,26},{12,28},{14,30},{16,0},... | collective-permute-start | bytes 1572872 | tf_op jit(solution)/shard_map/ppermute | solution.py:759
  203.6 3.9 %collective-permute-start.13 = (f32[16,384]{1,0:T(8,128)S(1)}, f32[16,384]{1,0:T(8,128)S(1)}, u32[]{:S(2)}, u32[]{:S(2)}) collective-permute-start(f32[16,384]{1,0:T(8,128)S(1)} %bitcast.57), channel_id=1, source_target_pairs={{0,1},{1,0},{2,3},{3,2},{4,5},{5,4},{6,7},{7,6},{8,9},{9,8},{10,11... | collective-permute-start | bytes 73736 | tf_op jit(solution)/shard_map/ppermute | solution.py:1100
  210.5 0.8 copy-start.11
  214.0 37.4 %collective-permute-start.16 = (bf16[1,64,2048]{2,1,0:T(8,128)(2,1)}, bf16[1,64,2048]{2,1,0:T(8,128)(2,1)S(1)}, u32[]{:S(2)}, u32[]{:S(2)}) collective-permute-start(bf16[1,64,2048]{2,1,0:T(8,128)(2,1)} %get-tuple-element.123), channel_id=1, source_target_pairs={{0,8},{2,10},{4,12},{6,14},{8,0},{10,2},{12,4},{14,6},{16,24},{18,... | collective-permute-start | bytes 786440 | tf_op jit(solution)/shard_map/ppermute | solution.py:759
  215.2 36.2 %collective-permute-start.17 = (bf16[1,64,2048]{2,1,0:T(8,128)(2,1)}, bf16[1,64,2048]{2,1,0:T(8,128)(2,1)S(1)}, u32[]{:S(2)}, u32[]{:S(2)}) collective-permute-start(bf16[1,64,2048]{2,1,0:T(8,128)(2,1)} %get-tuple-element.124), channel_id=1, source_target_pairs={{0,16},{2,18},{4,20},{6,22},{8,24},{10,26},{12,28},{14,30},{16,0},... | collective-permute-start | bytes 786440 | tf_op jit(solution)/shard_map/ppermute | solution.py:759
  217.8 33.6 %collective-permute-start.18 = (bf16[1,64,2048]{2,1,0:T(8,128)(2,1)}, bf16[1,64,2048]{2,1,0:T(8,128)(2,1)S(1)}, u32[]{:S(2)}, u32[]{:S(2)}) collective-permute-start(bf16[1,64,2048]{2,1,0:T(8,128)(2,1)} %get-tuple-element.125), channel_id=1, source_target_pairs={{0,24},{2,26},{4,28},{6,30},{8,16},{10,18},{12,20},{14,22},{16,8},... | collective-permute-start | bytes 786440 | tf_op jit(solution)/shard_map/ppermute | solution.py:759
  218.4 31.8 %all-to-all-start.3 = ((f32[16,1,384]{2,1,0:T(1,128)}), f32[16,1,384]{2,1,0:T(1,128)S(1)}, u32[]{:S(2)}, u32[]{:S(2)}) async-start(f32[16,1,384]{2,1,0:T(1,128)} %all_to_all.18), calls=%async_computation.3 | async-start | bytes 49152 | tf_op jit(solution)/shard_map/all_to_all | solution.py:1313
  251.4 0.7 copy-start.14
  251.4 0.8 copy-start.15
  251.4 0.9 copy-start.16
  254.4 2.9 %collective-permute-start.19 = (bf16[32,2048]{1,0:T(8,128)(2,1)}, bf16[32,2048]{1,0:T(8,128)(2,1)S(1)}, u32[]{:S(2)}, u32[]{:S(2)}) collective-permute-start(bf16[32,2048]{1,0:T(8,128)(2,1)} %get-tuple-element.129), channel_id=1, source_target_pairs={{0,1},{1,0},{2,3},{3,2},{4,5},{5,4},{6,7},{7,6},{8,9},{9,8},{10,11... | collective-permute-start | bytes 393224 | tf_op jit(solution)/shard_map/ppermute | solution.py:1100
  256.6 3.6 %copy-start.22 = (f32[32]{0:T(128)}, f32[32]{0:T(128)S(1)}, u32[]{:S(2)}) copy-start(f32[32]{0:T(128)S(1)} %get-tuple-element.179) | copy-start | bytes 388
  257.2 0.7 copy-start.17

commit v3 on v2

--- a/solution.py
+++ b/solution.py
@@ -83,7 +83,7 @@
 def open_kernel(
     first_ref, x_ref, g_ref, inv_ref, ga_ref, sa_ref, gf_ref, sf_ref, b_ref,
     wq_ref, wk_ref, wv_ref, wo_ref,
-    out_ref, n1_ref, n2_ref, table_ref, turned_ref, bias_ref, *, parts,
+    out_ref, n1_ref, n2_ref, table_ref, one_ref, turned_ref, bias_ref, *, parts,
 ):
     rows, width = x_ref.shape
     step = pl.program_id(0)
@@ -98,11 +98,17 @@
             table_ref[t] = table
         bias_ref[...] = vector_row(b_ref)
 
-    for n, source in enumerate((n1_ref, n2_ref, g_ref)):
-
-        @pl.when(step == n + 1)
-        def _(n=n, source=source):
-            turned_ref[n * width : (n + 1) * width] = jnp.transpose(source[...])
+    for n, (source, target) in enumerate(
+        (
+            (n1_ref, one_ref),
+            (n2_ref, turned_ref.at[:width]),
+            (g_ref, turned_ref.at[width:]),
+        )
+    ):
+
+        @pl.when(step == pl.num_programs(0) - 1)
+        def _(source=source, target=target):
+            target[...] = jnp.transpose(source[...])
 
     def bias(third):
         return bias_ref[:, pl.ds(pl.multiple_of(third * width + step * cols, cols), cols)]
@@ -128,7 +134,7 @@
 
 def open_layer(x, g, first, vectors, weight, bias, out_weight, parts):
     rows, width = x.shape
-    steps = 4
+    steps = 2
     cols = width // steps
     per = HEADS // steps
     inverse = 10000.0 ** (-(jnp.arange(ROT // 2, dtype=F32) * 2.0 / ROT))
@@ -146,7 +152,8 @@
             shape_of((rows, width), BF16),
             shape_of((rows, width), BF16),
             shape_of((3, rows, PAIR), F32),
-            shape_of((3 * width, rows), BF16),
+            shape_of((width, rows), BF16),
+            shape_of((2 * width, rows), BF16),
         ),
         in_specs=[
             pl.BlockSpec(memory_space=pltpu.SMEM),
@@ -163,7 +170,8 @@
             fixed((rows, width)),
             fixed((rows, width)),
             fixed((3, rows, PAIR)),
-            fixed((3 * width, rows)),
+            fixed((width, rows)),
+            fixed((2 * width, rows)),
         ),
         scratch_shapes=[pltpu.VMEM((1, 3 * width), F32)],
         cost_estimate=cost(
@@ -1137,7 +1145,7 @@
     inputs = block_input.reshape(rows, width)
     cot = out_cotangent.reshape(rows, width)
 
-    outgoing, normed_one, normed_two, table, turned = open_layer(
+    outgoing, _, normed_two, table, one_t, turned = open_layer(
         inputs,
         cot,
         me * rows,
@@ -1151,6 +1159,7 @@
 
     rows_list, cot_list = mlp_list(normed_two), mlp_list(cot)
     turned = mlp_list(turned, 1)
+    one_t = mlp_list(one_t, 1)
     hidden, grad_pre, grad_hid_bias, *sides = feed(
         rows_list, cot_list, expand_weight, expand_bias, contract_weight
     )
@@ -1183,8 +1192,8 @@
         b_runs = [(b, (rows, block), lambda i, me, m=m: (m, i)) for m in range(pairs)]
         return ring_of([(sides_of(turned, part), b_runs)], slice_width // block, block, stages)
 
-    ring_out = feed_ring(2, hidden, x_first)
-    ring_hid = feed_ring(1, grad_pre, y_first)
+    ring_out = feed_ring(1, hidden, x_first)
+    ring_hid = feed_ring(0, grad_pre, y_first)
 
     query_rows = rows // parts
     part = jnp.stack([me[0] % parts, me[0]]).astype(jnp.int32)
@@ -1193,7 +1202,7 @@
         part,
         rows,
         query_rows,
-        (*ring_out.sent, *ring_hid.sent, *[a for a, _ in (*feeds, *grads)], *turned),
+        (*ring_out.sent, *ring_hid.sent, *[a for a, _ in (*feeds, *grads)], *turned, *one_t),
     )
     back_first = lax.all_to_all(from_first, "seq", 0, 0, tiled=True)
     from_second, after_second = backward_head(
@@ -1225,7 +1234,7 @@
             ring.step()
         v_parts, d_parts, _ = weight_once(
             scalars,
-            [*turned, own_v, came, own_a, *cot_list],
+            [*one_t, own_v, came, own_a, *cot_list],
             [
                 ([((0, 1), (rows_run(2, 0, share), rows_run(3, width, share)), True)], (0,)),
                 (
@@ -1244,7 +1253,7 @@
         came = pair_swap(sent)
         qv_parts, kd_parts, weighed = weight_once(
             scalars,
-            [*turned, own_qk, came, *v_parts, *d_parts],
+            [*one_t, own_qk, came, *v_parts, *d_parts],
             [
                 (
                     [
@@ -1273,7 +1282,7 @@
             runs(p, (rows, share), lambda m, i, me: (m, 0)) for p in pieces
         )
         cot_runs = runs(cot_list, (rows, share), lambda m, i, me: (m, me[1]))
-        one = sides_of(turned)
+        one = sides_of(one_t)
         ring_qv = ring_of([(one, q_runs), (one, v_runs)], 2, share, x_first)
         ring_kd = ring_of([(one, k_runs), (sides_of(att_t), cot_runs)], 2, share, y_first)
 
@@ -1310,14 +1319,7 @@
         packed = lax.psum_scatter(packed, "mlp", scatter_dimension=1, tiled=False)
     ring_qv.step(ring_kd)
     packed = after(packed, *ring_qv.sent)
-    packed = jnp.sum(lax.all_to_all(packed, "seq", 0, 0, tiled=True), 0)
-    outs, start = [], 0
-    for v in vectors:
-        size = v.shape[0] // (members * pairs)
-        outs.append(lax.slice_in_dim(packed, start, start + size))
-        start += size
-    grad_gain_one, grad_shift_one, grad_dense_bias, grad_gain_two, grad_shift_two = outs[:5]
-    grad_merged_bias, out_hid_bias = outs[5:]
+    packed = lax.all_to_all(packed, "seq", 0, 0, tiled=True)
 
     feed_total = ring_out.plain_total()
     out_weight = jnp.transpose(feed_total[:, :slice_width])
@@ -1325,6 +1327,7 @@
 
     if pairs == 2:
         mine, other = ring_qv.total()
+        packed = after(packed, other)
         merged, dense = vmem_call(
             place_kernel,
             [shape_of((own // pairs, 3 * width), F32), shape_of((own // pairs, width), F32)],
@@ -1338,6 +1341,14 @@
         got = jnp.transpose(got.reshape(pairs, own // pairs, 4, share), (1, 2, 0, 3))
         merged = jnp.concatenate([got[:, n].reshape(-1, width) for n in (0, 2, 1)], -1)
         dense = got[:, 3].reshape(-1, width)
+    packed = jnp.sum(packed, 0)
+    outs, start = [], 0
+    for v in vectors:
+        size = v.shape[0] // (members * pairs)
+        outs.append(lax.slice_in_dim(packed, start, start + size))
+        start += size
+    grad_gain_one, grad_shift_one, grad_dense_bias, grad_gain_two, grad_shift_two = outs[:5]
+    grad_merged_bias, out_hid_bias = outs[5:]
     return (
         block_output.reshape(seq_count, rows, width),
         grad_input.reshape(seq_count, rows, width),

time: 262 us -> 258 us (0.985)
    ppermute x8 -> x9, waiting for transfers between devices: 5.34 us -> 3.77 us  [pair_swap(): return lax.ppermute(x, 'mlp', [(0, 1), (1, 0)])]
    unnamed x48 -> x51, local copies, waits for them, and re-layouts: 8.89 us -> 7.36 us
    ppermute x8 -> x9, starting transfers between devices: 12.4 us -> 12.1 us  [pair_swap(): return lax.ppermute(x, 'mlp', [(0, 1), (1, 0)])]
  transfers between devices with their start and end apart: 25 -> 26, of which waited for: 15 -> 14; matrix products, arithmetic and copies ran while one was open for 4% -> 4% of each run, Pallas kernels for 47% -> 47%
where the time goes in v3:
time: 258 us; the launch traced here: 257 us
  Pallas kernels  134 us (52%)
  starting transfers between devices  57.2 us (22%)
  waiting for transfers between devices  43.5 us (17%)
  local copies, waits for them, and re-layouts  12.3 us (5%)
  other arithmetic  7.67 us (3%)
  between operations  3.02 us (1%)
    pallas_call x10, Pallas kernels, vmem_call(): pl.pallas_call(without(kernel, 1 + len(arrays), len(behind)), in_specs=[p...  35.6 us
    pallas_call x1, Pallas kernels, forward_head(): pl.pallas_call(without(partial(forward_kernel, key_rows=key_rows, query_r...  26.9 us
    ppermute x13, waiting for transfers between devices, seq_move(): return lax.ppermute(x, 'seq', [(s, s ^ mask) for s in range(members)])  25.8 us
    pallas_call x1, Pallas kernels, backward_head(): pl.pallas_call(without(partial(backward_kernel, key_rows=key_rows, query_...  22.4 us
    pallas_call x1, Pallas kernels, feed(): pl.pallas_call(partial(feed_kernel, count=count, keep=keep), grid=(hidden...  17.3 us
    ppermute x13, starting transfers between devices, seq_move(): return lax.ppermute(x, 'seq', [(s, s ^ mask) for s in range(members)])  14.2 us
    pallas_call x2, Pallas kernels, weight_parts(): pl.pallas_call(partial(weight_kernel, bits=bits, counts=[len(a) for a, _...  12.7 us
    ppermute x9, starting transfers between devices, pair_swap(): return lax.ppermute(x, 'mlp', [(0, 1), (1, 0)])  12.1 us
  transfers between devices with their start and end apart: 26, of which 14 were waited for; matrix products, arithmetic and copies ran while one was open for 4% of the time, Pallas kernels for 47%

profile of v3, /device:TPU:1, one launch (start us, length us, event | category | flops | bytes accessed | tf_op | source)
XLA Modules:
  0.0 257.5 jit_solution(16242203326968431042)
XLA Ops:
  1.3 8.5 %open_layer.1 = (bf16[16,1,512,128]{3,2,1,0:T(8,128)(2,1)}, bf16[256,1024]{1,0:T(8,128)(2,1)}, bf16[256,1024]{1,0:T(8,128)(2,1)}, f32[3,256,128]{2,1,0:T(8,128)}...) custom-call(s32[1]{0:T(128)S(6)} %mul.8.first_ref, bf16[256,1024]{1,0:T(8,128)(2,1)} %bitcast.55, ...), custom_call_target="tpu_custom_call" | custom-call | flops 134217728 | bytes 819200 | tf_op jit(solution)/shard_map/open_layer/pallas_call | solution.py:147
  9.8 7.6 %all-to-all-start = ((bf16[16,512,128]{2,1,0:T(8,128)(2,1)}), bf16[16,512,128]{2,1,0:T(8,128)(2,1)}, u32[]{:S(2)}, u32[]{:S(2)}) async-start(bf16[16,512,128]{2,1,0:T(8,128)(2,1)} %bitcast.57), calls=%async_computation | async-start | bytes 4194304 | tf_op jit(solution)/shard_map/all_to_all | solution.py:1158
  17.5 1.0 collective-permute-start.1
  19.0 0.6 reshape.123
  19.6 0.6 collective-permute-done.1.refs_1_
  21.6 17.3 %feed.1 = (bf16[512,2048]{1,0:T(8,128)(2,1)}, bf16[512,2048]{1,0:T(8,128)(2,1)}, f32[1,2048]{1,0:T(1,128)}, f32[256,1024]{1,0:T(8,128)}, f32[256,1024]{1,0:T(8,128)}, /*index=5*/bf16[512,1024]{1,0:T(8,128)(2,1)}) custom-call(bf16[256,1024]{1,0:T(8,128)(2,1)} %get-tuple-element.77.refs_0_, bf16[256,1024]{1,0:T(8,128)(2,1)} %copy-done.13, ...), custom_call_target="tpu_custom_call" | custom-call | flops 536870912 | bytes 786432 | tf_op jit(solution)/shard_map/feed/pallas_call | solution.py:545
  39.4 0.7 pad_add_fusion
  40.1 1.0 copy-done.3
  41.0 6.3 %weight_parts.3 = (bf16[8,64,2048]{2,1,0:T(8,128)(2,1)}, bf16[8,64,2048]{2,1,0:T(8,128)(2,1)}) custom-call(s32[2]{0:T(128)} %get-tuple-element.154.me_ref.refs_0_.refs_14_, bf16[2048,256]{1,0:T(8,128)(2,1)} %get-tuple-element.76.refs_0_.refs_8_, bf16[2048,256]{1,0:T(8,128)(2,1)} %copy-done.3, bf16[512,2048]{1,0:T(8,128)(2,1)} %get-tuple-element.80.refs_2_.refs_3_, ...), custom_call_target="tpu_custom_call" | custom-call | flops 134217728 | bytes 458752 | tf_op jit(solution)/shard_map/weight_parts/pallas_call | solution.py:623
  47.4 1.6 collective-permute-start.6
  49.0 6.3 %weight_parts.2 = (bf16[8,64,2048]{2,1,0:T(8,128)(2,1)}, bf16[8,64,2048]{2,1,0:T(8,128)(2,1)}) custom-call(s32[2]{0:T(128)} %get-tuple-element.154.me_ref.refs_0_.refs_14_, bf16[2048,256]{1,0:T(8,128)(2,1)} %get-tuple-element.76.refs_0_.refs_8_, bf16[2048,256]{1,0:T(8,128)(2,1)} %copy-done.3, bf16[512,2048]{1,0:T(8,128)(2,1)} %get-tuple-element.78.refs_2_.refs_3_, ...), custom_call_target="tpu_custom_call" | custom-call | flops 134217728 | bytes 458752 | tf_op jit(solution)/shard_map/weight_parts/pallas_call | solution.py:623
  55.3 1.2 collective-permute-start.5
  56.5 2.4 all-to-all-done.refs_1_.x_ref
  58.9 26.9 %forward_head.1 = (bf16[16,256,128]{2,1,0:T(8,128)(2,1)}, bf16[4,1024,128]{2,1,0:T(8,128)(2,1)}, f32[4,1024,128]{2,1,0:T(8,128)}, bf16[20,1024,512]{2,1,0:T(8,128)(2,1)}, s32[1]{0:T(128)}) custom-call(s32[2]{0:T(128)} %get-tuple-element.155.refs_0_, bf16[16,512,128]{2,1,0:T(8,128)(2,1)} %all-to-all-done.refs_1_.x_ref, ...), custom_call_target="tpu_custom_call" | custom-call | flops 16106127360 | bytes 25165824 | tf_op jit(solution)/shard_map/forward_head/pallas_call | solution.py:417
  85.8 10.9 %all-to-all-start.2 = ((bf16[16,256,128]{2,1,0:T(8,128)(2,1)}), bf16[16,256,128]{2,1,0:T(8,128)(2,1)S(1)}, u32[]{:S(2)}, u32[]{:S(2)}) async-start(bf16[16,256,128]{2,1,0:T(8,128)(2,1)} %get-tuple-element.92), calls=%async_computation.2 | async-start | bytes 2097152 | tf_op jit(solution)/shard_map/all_to_all | solution.py:1207
  96.7 22.4 %backward_head.1 = (bf16[16,256,128]{2,1,0:T(8,128)(2,1)}, s32[1]{0:T(128)}) custom-call(s32[2]{0:T(128)} %get-tuple-element.154.me_ref.refs_0_.refs_14_, bf16[16,512,128]{2,1,0:T(8,128)(2,1)} %all-to-all-done.refs_1_.x_ref, bf16[4,1024,128]{2,1,0:T(8,128)(2,1)} %get-tuple-element.86.g_ref, f32[4,1024,128]{2,1,0:T(8,128)} %get-tuple-element.87.d_ref, ...), custom_call_target="tpu_custom_call" | custom-call | flops 16106127360 | bytes 25165824 | tf_op jit(solution)/shard_map/backward_head/pallas_call | solution.py:460
  119.2 6.3 %all-to-all-start.1 = ((bf16[16,256,128]{2,1,0:T(8,128)(2,1)}), bf16[16,256,128]{2,1,0:T(8,128)(2,1)S(1)}, u32[]{:S(2)}, u32[]{:S(2)}) async-start(bf16[16,256,128]{2,1,0:T(8,128)(2,1)} %get-tuple-element.90.refs_2_), calls=%async_computation.1 | async-start | bytes 2097152 | tf_op jit(solution)/shard_map/all_to_all | solution.py:1212
  125.6 3.7 %regroup_once.2 = (bf16[256,1024]{1,0:T(8,128)(2,1)}, bf16[256,1024]{1,0:T(8,128)(2,1)}, bf16[1536,256]{1,0:T(8,128)(2,1)}, bf16[1024,256]{1,0:T(8,128)(2,1)}, bf16[512,256]{1,0:T(8,128)(2,1)}) custom-call(s32[2]{0:T(128)} %get-tuple-element.154.me_ref.refs_0_.refs_14_, bf16[16,256,128]{2,1,0:T(8,128)(2,1)} %copy-done.4, ...), custom_call_target="tpu_custom_call" | custom-call | flops 32768 | bytes 98304 | tf_op jit(solution)/shard_map/regroup_once/pallas_call | solution.py:749
  129.2 2.5 collective-permute-start.7
  131.7 3.9 %add_parts.5 = (bf16[4,64,2048]{2,1,0:T(8,128)(2,1)}, bf16[4,64,2048]{2,1,0:T(8,128)(2,1)}) custom-call(s32[2]{0:T(128)} %get-tuple-element.154.me_ref.refs_0_.refs_14_, bf16[8,64,2048]{2,1,0:T(8,128)(2,1)} %get-tuple-element.107.refs_1_, bf16[8,64,2048]{2,1,0:T(8,128)(2,1)} %collective-permute-done.6.refs_2_, bf16[1536,256]{1,0:T(8,128)(2,1)} %get-tuple-element.94.refs_3_), custom_call_target="tpu_custom_call" | custom-call | flops 131072 | bytes 393216 | tf_op jit(solution)/shard_map/add_parts/pallas_call | solution.py:749
  135.7 1.6 collective-permute-start.9
  137.3 4.0 %add_parts.4 = (bf16[4,64,2048]{2,1,0:T(8,128)(2,1)}, bf16[4,64,2048]{2,1,0:T(8,128)(2,1)}) custom-call(s32[2]{0:T(128)} %get-tuple-element.154.me_ref.refs_0_.refs_14_, bf16[8,64,2048]{2,1,0:T(8,128)(2,1)} %get-tuple-element.104.refs_1_, bf16[8,64,2048]{2,1,0:T(8,128)(2,1)} %collective-permute-done.5.refs_2_, bf16[1536,256]{1,0:T(8,128)(2,1)} %get-tuple-element.94.refs_3_), custom_call_target="tpu_custom_call" | custom-call | flops 131072 | bytes 393216 | tf_op jit(solution)/shard_map/add_parts/pallas_call | solution.py:749
  141.3 1.2 collective-permute-start.8
  142.5 4.1 %weight_once.2 = (bf16[8,64,512]{2,1,0:T(8,128)(2,1)}, bf16[8,64,512]{2,1,0:T(8,128)(2,1)}, bf16[8,64,512]{2,1,0:T(8,128)(2,1)}, bf16[8,64,512]{2,1,0:T(8,128)(2,1)}, s32[2]{0:T(128)}) custom-call(s32[2]{0:T(128)} %get-tuple-element.154.me_ref.refs_0_.refs_14_, bf16[1024,256]{1,0:T(8,128)(2,1)} %get-tuple-element.85.refs_10_.refs_0_, ...), custom_call_target="tpu_custom_call" | custom-call | flops 114688 | bytes 344064 | tf_op jit(solution)/shard_map/weight_once/pallas_call | solution.py:749
  146.6 1.1 all-to-all-done.1.refs_1_
  147.7 1.0 copy-done.5
  148.7 4.0 %regroup_once.3 = (bf16[256,1024]{1,0:T(8,128)(2,1)}, bf16[256,1024]{1,0:T(8,128)(2,1)}, bf16[256,1024]{1,0:T(8,128)(2,1)}, bf16[256,1024]{1,0:T(8,128)(2,1)}) custom-call(s32[2]{0:T(128)} %get-tuple-element.154.me_ref.refs_0_.refs_14_, bf16[16,256,128]{2,1,0:T(8,128)(2,1)} %copy-done.5, f32[3,256,128]{2,1,0:T(8,128)} %get-tuple-element.91.refs_2_, ...), custom_call_target="tpu_custom_call" | custom-call | flops 38912 | bytes 116736 | tf_op jit(solution)/shard_map/regroup_once/pallas_call | solution.py:749
  152.6 3.2 %collective-permute-start.10 = (bf16[256,1024]{1,0:T(8,128)(2,1)}, bf16[256,1024]{1,0:T(8,128)(2,1)S(1)}, u32[]{:S(2)}, u32[]{:S(2)}) collective-permute-start(bf16[256,1024]{1,0:T(8,128)(2,1)} %get-tuple-element.111), channel_id=1, source_target_pairs={{0,1},{1,0},{2,3},{3,2},{4,5},{5,4},{6,7},{7,6},{8,9},{9,8},{10,11... | collective-permute-start | bytes 1572872 | tf_op jit(solution)/shard_map/ppermute | solution.py:1108
  155.9 1.7 collective-permute-done.10.refs_3_
  157.6 0.8 copy-done.14
  158.4 5.5 %weight_once.3 = (bf16[8,64,1024]{2,1,0:T(8,128)(2,1)}, bf16[8,64,1024]{2,1,0:T(8,128)(2,1)}, bf16[8,64,1024]{2,1,0:T(8,128)(2,1)}, bf16[8,64,1024]{2,1,0:T(8,128)(2,1)}, s32[2]{0:T(128)}) custom-call(s32[2]{0:T(128)} %get-tuple-element.154.me_ref.refs_0_.refs_14_, bf16[1024,256]{1,0:T(8,128)(2,1)} %get-tuple-element.85.refs_10_.refs_0_, ...), custom_call_target="tpu_custom_call" | custom-call | flops 131072 | bytes 393216 | tf_op jit(solution)/shard_map/weight_once/pallas_call | solution.py:749
  163.9 1.7 collective-permute-start.13
  165.9 1.7 collective-permute-done.9.refs_4_
  167.6 1.4 collective-permute-done.8.refs_2_
  169.0 1.0 copy-done.11
  169.9 3.9 %add_parts.6 = (bf16[2,64,4096]{2,1,0:T(8,128)(2,1)}, bf16[2,64,4096]{2,1,0:T(8,128)(2,1)}) custom-call(s32[2]{0:T(128)} %get-tuple-element.154.me_ref.refs_0_.refs_14_, bf16[4,64,2048]{2,1,0:T(8,128)(2,1)} %get-tuple-element.105.refs_1_, bf16[4,64,2048]{2,1,0:T(8,128)(2,1)} %copy-done.11, bf16[4,64,2048]{2,1,0:T(8,128)(2,1)} %get-tuple-element.108.refs_3_, ...), custom_call_target="tpu_custom_call" | custom-call | flops 131072 | bytes 393216 | tf_op jit(solution)/shard_map/add_parts/pallas_call | solution.py:749
  173.9 1.3 collective-permute-start.11
  175.1 10.4 %close_layer.1 = (bf16[256,1024]{1,0:T(8,128)(2,1)}, f32[256,1024]{1,0:T(8,128)}, f32[5,1024]{1,0:T(8,128)}, f32[3,1024]{1,0:T(4,128)}, s32[2]{0:T(128)}) custom-call(bf16[256,1024]{1,0:T(8,128)(2,1)} %bitcast.56, bf16[256,1024]{1,0:T(8,128)(2,1)} %bitcast.53, bf16[1024]{0:T(1024)(128)(2,1)} %refs_2_.1, bf16[1024]{0:T(1024)(128)(2,1)} %refs_3_.1, ...), custom_call_target="tpu_custom_call" | custom-call | flops 134217728 | bytes 917504 | tf_op jit(solution)/shard_map/close_layer/pallas_call | solution.py:1055
  187.6 4.0 %collective-permute-done.13 = bf16[8,64,1024]{2,1,0:T(8,128)(2,1)} collective-permute-done((bf16[8,64,1024]{2,1,0:T(8,128)(2,1)}, bf16[8,64,1024]{2,1,0:T(8,128)(2,1)}, u32[]{:S(2)}, u32[]{:S(2)}) %collective-permute-start.13) | collective-permute-done | bytes 1048608 | tf_op jit(solution)/shard_map/ppermute | solution.py:767
  191.5 2.6 %add_convert_fusion.1 = (bf16[2,2,1,64,1024]{4,3,1,0,2:T(8,128)(2,1)}, bf16[2,2,1,64,1024]{4,3,1,0,2:T(8,128)(2,1)}) fusion(bf16[2,2,2,64,1024]{4,3,2,1,0:T(8,128)(2,1)} %bitcast.17, s32[]{:T(128)S(6)} %select_n.48, bf16[2,2,2,64,1024]{4,3,2,1,0:T(8,128)(2,1)S(1)} %bitcast.61, s32[]{:T(128)S(6)} %select_n.46), kind=kLoop, calls=%fused_computation.2 | loop fusion | flops 2097152 | bytes 3145736 | tf_op jit(solution)/shard_map/convert_element_type | solution.py:835
  194.3 1.4 add_convert_fusion.2
  195.7 0.7 collective-permute-start.15
  196.4 1.6 collective-permute-done.11
  198.0 1.2 add_convert_fusion.3
  199.2 1.0 collective-permute-start.21
  201.2 3.1 %collective-permute-start.14 = (f32[16,384]{1,0:T(8,128)S(1)}, f32[16,384]{1,0:T(8,128)S(1)}, u32[]{:S(2)}, u32[]{:S(2)}) collective-permute-start(f32[16,384]{1,0:T(8,128)S(1)} %bitcast.66), channel_id=1, source_target_pairs={{0,1},{1,0},{2,3},{3,2},{4,5},{5,4},{6,7},{7,6},{8,9},{9,8},{10,11... | collective-permute-start | bytes 73736 | tf_op jit(solution)/shard_map/ppermute | solution.py:1108
  204.3 0.8 collective-permute-done.14
  205.2 2.1 collective-permute-done.16.refs_3_
  207.3 1.1 collective-permute-done.15.refs_1_
  208.4 0.8 copy-done.12
  209.2 2.7 %add_parts.7 = (bf16[1,64,2048]{2,1,0:T(8,128)(2,1)}, bf16[1,64,2048]{2,1,0:T(8,128)(2,1)}, bf16[1,64,2048]{2,1,0:T(8,128)(2,1)}, bf16[1,64,2048]{2,1,0:T(8,128)(2,1)}) custom-call(s32[2]{0:T(128)} %get-tuple-element.154.me_ref.refs_0_.refs_14_, bf16[4,64,1024]{2,1,0:T(8,128)(2,1)} %bitcast.59, bf16[4,64,1024]{2,1,0:T(8,128)(2,1)} %copy-done.12, ...), custom_call_target="tpu_custom_call" | custom-call | flops 65536 | bytes 196608 | tf_op jit(solution)/shard_map/add_parts/pallas_call | solution.py:749
  211.9 1.4 collective-permute-start.17
  213.2 2.1 collective-permute-start.18
  215.4 0.6 all_to_all.20
  216.0 6.0 %all-to-all-start.3 = ((f32[16,1,384]{2,1,0:T(1,128)}), f32[16,1,384]{2,1,0:T(1,128)S(1)}, u32[]{:S(2)}, u32[]{:S(2)}) async-start(f32[16,1,384]{2,1,0:T(1,128)} %all_to_all.20), calls=%async_computation.3 | async-start | bytes 49152 | tf_op jit(solution)/shard_map/all_to_all | solution.py:1322
  222.1 13.9 %collective-permute-done.21 = bf16[1,64,4096]{2,1,0:T(8,128)(2,1)S(1)} collective-permute-done((bf16[1,64,4096]{2,1,0:T(8,128)(2,1)S(1)}, bf16[1,64,4096]{2,1,0:T(8,128)(2,1)S(1)}, u32[]{:S(2)}, u32[]{:S(2)}) %collective-permute-start.21) | collective-permute-done | bytes 524320 | tf_op jit(solution)/shard_map/ppermute | solution.py:767
  236.0 1.2 add_bitcast_fusion
  237.2 1.0 slice_bitcast_fusion
  238.2 10.4 %all-to-all-done.3 = f32[16,1,384]{2,1,0:T(1,128)S(1)} async-done(((f32[16,1,384]{2,1,0:T(1,128)}), f32[16,1,384]{2,1,0:T(1,128)S(1)}, u32[]{:S(2)}, u32[]{:S(2)}) %all-to-all-start.3) | async-done | bytes 24608 | tf_op jit(solution)/shard_map/all_to_all | solution.py:1322
  248.7 0.7 copy-done.15
  249.5 2.1 last_sum.1
  251.6 1.2 collective-permute-start.20
  254.5 0.7 copy-done.18
  255.1 1.8 place.1
  (83 shorter events, 7.0 us)
Async XLA Ops:
  9.8 8.7 %copy-start = (bf16[1,256,1024]{2,1,0:T(8,128)(2,1)S(1)}, bf16[1,256,1024]{2,1,0:T(8,128)(2,1)}, u32[]{:S(2)}) copy-start(bf16[1,256,1024]{2,1,0:T(8,128)(2,1)} %param.15) | copy-start | bytes 1572868
  9.8 8.8 %copy-start.2 = (bf16[2048,256]{1,0:T(8,128)(2,1)S(1)}, bf16[2048,256]{1,0:T(8,128)(2,1)}, u32[]{:S(2)}) copy-start(bf16[2048,256]{1,0:T(8,128)(2,1)} %get-tuple-element.76.refs_0_.refs_8_) | copy-start | bytes 3145732
  9.8 9.2 %copy-start.22 = (bf16[2048]{0:T(1024)(128)(2,1)S(1)}, bf16[2048]{0:T(1024)(128)(2,1)}, u32[]{:S(2)}) copy-start(bf16[2048]{0:T(1024)(128)(2,1)} %param.25) | copy-start | bytes 12292
  9.8 49.1 %all-to-all-start = ((bf16[16,512,128]{2,1,0:T(8,128)(2,1)}), bf16[16,512,128]{2,1,0:T(8,128)(2,1)}, u32[]{:S(2)}, u32[]{:S(2)}) async-start(bf16[16,512,128]{2,1,0:T(8,128)(2,1)} %bitcast.57), calls=%async_computation | async-start | bytes 4194304 | tf_op jit(solution)/shard_map/all_to_all | solution.py:1158
  17.5 2.8 %collective-permute-start.1 = (bf16[256,1024]{1,0:T(8,128)(2,1)}, bf16[256,1024]{1,0:T(8,128)(2,1)S(1)}, u32[]{:S(2)}, u32[]{:S(2)}) collective-permute-start(bf16[256,1024]{1,0:T(8,128)(2,1)} %get-tuple-element.77.refs_0_), channel_id=1, source_target_pairs={{0,1},{1,0},{2,3},{3,2},{4,5},{5,4},{6,7},{7,6},{8,9},{9,8},{10,11... | collective-permute-start | bytes 1572872 | tf_op jit(solution)/shard_map/ppermute | solution.py:1108
  18.5 2.3 collective-permute-start.2
  18.6 21.5 %collective-permute-start = (bf16[2048,256]{1,0:T(8,128)(2,1)S(1)}, bf16[2048,256]{1,0:T(8,128)(2,1)S(1)}, u32[]{:S(2)}, u32[]{:S(2)}) collective-permute-start(bf16[2048,256]{1,0:T(8,128)(2,1)S(1)} %copy-done.2), channel_id=1, source_target_pairs={{0,1},{1,0},{2,3},{3,2},{4,5},{5,4},{6,7},{7,6},{8,9},{9,8},{10,11... | collective-permute-start | bytes 3145736 | tf_op jit(solution)/shard_map/ppermute | solution.py:1108
  20.2 0.8 copy-start.13
  20.8 0.8 copy-start.6
  38.8 17.6 %collective-permute-start.3 = (bf16[512,1024]{1,0:T(8,128)(2,1)}, bf16[512,1024]{1,0:T(8,128)(2,1)S(1)}, u32[]{:S(2)}, u32[]{:S(2)}) collective-permute-start(bf16[512,1024]{1,0:T(8,128)(2,1)} %get-tuple-element.83), channel_id=1, source_target_pairs={{0,1},{1,0},{2,3},{3,2},{4,5},{5,4},{6,7},{7,6},{8,9},{9,8},{10,11... | collective-permute-start | bytes 3145736 | tf_op jit(solution)/shard_map/ppermute | solution.py:1108
  39.3 17.2 %collective-permute-start.4 = (bf16[1024,256]{1,0:T(8,128)(2,1)}, bf16[1024,256]{1,0:T(8,128)(2,1)}, u32[]{:S(2)}, u32[]{:S(2)}) collective-permute-start(bf16[1024,256]{1,0:T(8,128)(2,1)} %get-tuple-element.85.refs_10_.refs_0_), channel_id=1, source_target_pairs={{0,1},{1,0},{2,3},{3,2},{4,5},{5,4},{6,7},{7,6},{8,9},{9,8},{10,11... | collective-permute-start | bytes 1572872 | tf_op jit(solution)/shard_map/ppermute | solution.py:1108
  40.1 1.0 copy-start.3
  47.4 71.8 %collective-permute-start.6 = (bf16[8,64,2048]{2,1,0:T(8,128)(2,1)}, bf16[8,64,2048]{2,1,0:T(8,128)(2,1)}, u32[]{:S(2)}, u32[]{:S(2)}) collective-permute-start(bf16[8,64,2048]{2,1,0:T(8,128)(2,1)} %get-tuple-element.81.refs_3_), channel_id=1, source_target_pairs={{0,4},{2,6},{4,0},{6,2},{8,12},{10,14},{12,8},{14,10},{16,20},{18,... | collective-permute-start | bytes 6291464 | tf_op jit(solution)/shard_map/ppermute | solution.py:767
  55.3 63.9 %collective-permute-start.5 = (bf16[8,64,2048]{2,1,0:T(8,128)(2,1)}, bf16[8,64,2048]{2,1,0:T(8,128)(2,1)}, u32[]{:S(2)}, u32[]{:S(2)}) collective-permute-start(bf16[8,64,2048]{2,1,0:T(8,128)(2,1)} %get-tuple-element.79.refs_2_), channel_id=1, source_target_pairs={{0,2},{2,0},{4,6},{6,4},{8,10},{10,8},{12,14},{14,12},{16,18},{18,... | collective-permute-start | bytes 6291464 | tf_op jit(solution)/shard_map/ppermute | solution.py:767
  56.5 2.5 copy-start.1
  85.8 33.4 %all-to-all-start.2 = ((bf16[16,256,128]{2,1,0:T(8,128)(2,1)}), bf16[16,256,128]{2,1,0:T(8,128)(2,1)S(1)}, u32[]{:S(2)}, u32[]{:S(2)}) async-start(bf16[16,256,128]{2,1,0:T(8,128)(2,1)} %get-tuple-element.92), calls=%async_computation.2 | async-start | bytes 2097152 | tf_op jit(solution)/shard_map/all_to_all | solution.py:1207
  119.2 6.4 %copy-start.4 = (bf16[16,256,128]{2,1,0:T(8,128)(2,1)}, bf16[16,256,128]{2,1,0:T(8,128)(2,1)S(1)}, u32[]{:S(2)}) copy-start(bf16[16,256,128]{2,1,0:T(8,128)(2,1)S(1)} %all-to-all-done.2.refs_1_) | copy-start | bytes 3145732
  119.2 28.5 %all-to-all-start.1 = ((bf16[16,256,128]{2,1,0:T(8,128)(2,1)}), bf16[16,256,128]{2,1,0:T(8,128)(2,1)S(1)}, u32[]{:S(2)}, u32[]{:S(2)}) async-start(bf16[16,256,128]{2,1,0:T(8,128)(2,1)} %get-tuple-element.90.refs_2_), calls=%async_computation.1 | async-start | bytes 2097152 | tf_op jit(solution)/shard_map/all_to_all | solution.py:1212
  129.2 13.2 %collective-permute-start.7 = (bf16[1536,256]{1,0:T(8,128)(2,1)}, bf16[1536,256]{1,0:T(8,128)(2,1)}, u32[]{:S(2)}, u32[]{:S(2)}) collective-permute-start(bf16[1536,256]{1,0:T(8,128)(2,1)} %get-tuple-element.94.refs_3_), channel_id=1, source_target_pairs={{0,1},{1,0},{2,3},{3,2},{4,5},{5,4},{6,7},{7,6},{8,9},{9,8},{10,11... | collective-permute-start | bytes 2359304 | tf_op jit(solution)/shard_map/ppermute | solution.py:1108
  135.7 31.9 %collective-permute-start.9 = (bf16[4,64,2048]{2,1,0:T(8,128)(2,1)}, bf16[4,64,2048]{2,1,0:T(8,128)(2,1)S(1)}, u32[]{:S(2)}, u32[]{:S(2)}) collective-permute-start(bf16[4,64,2048]{2,1,0:T(8,128)(2,1)} %get-tuple-element.109), channel_id=1, source_target_pairs={{0,2},{2,0},{4,6},{6,4},{8,10},{10,8},{12,14},{14,12},{16,18},{18,... | collective-permute-start | bytes 3145736 | tf_op jit(solution)/shard_map/ppermute | solution.py:767
  141.3 27.7 %collective-permute-start.8 = (bf16[4,64,2048]{2,1,0:T(8,128)(2,1)}, bf16[4,64,2048]{2,1,0:T(8,128)(2,1)S(1)}, u32[]{:S(2)}, u32[]{:S(2)}) collective-permute-start(bf16[4,64,2048]{2,1,0:T(8,128)(2,1)} %get-tuple-element.106), channel_id=1, source_target_pairs={{0,4},{2,6},{4,0},{6,2},{8,12},{10,14},{12,8},{14,10},{16,20},{18,... | collective-permute-start | bytes 3145736 | tf_op jit(solution)/shard_map/ppermute | solution.py:767
  147.7 1.0 copy-start.5
  152.6 5.0 %collective-permute-start.10 = (bf16[256,1024]{1,0:T(8,128)(2,1)}, bf16[256,1024]{1,0:T(8,128)(2,1)S(1)}, u32[]{:S(2)}, u32[]{:S(2)}) collective-permute-start(bf16[256,1024]{1,0:T(8,128)(2,1)} %get-tuple-element.111), channel_id=1, source_target_pairs={{0,1},{1,0},{2,3},{3,2},{4,5},{5,4},{6,7},{7,6},{8,9},{9,8},{10,11... | collective-permute-start | bytes 1572872 | tf_op jit(solution)/shard_map/ppermute | solution.py:1108
  157.6 0.8 copy-start.14
  163.9 27.7 %collective-permute-start.13 = (bf16[8,64,1024]{2,1,0:T(8,128)(2,1)}, bf16[8,64,1024]{2,1,0:T(8,128)(2,1)}, u32[]{:S(2)}, u32[]{:S(2)}) collective-permute-start(bf16[8,64,1024]{2,1,0:T(8,128)(2,1)} %get-tuple-element.112.refs_5_), channel_id=1, source_target_pairs={{0,4},{2,6},{4,0},{6,2},{8,12},{10,14},{12,8},{14,10},{16,20},{18,... | collective-permute-start | bytes 3145736 | tf_op jit(solution)/shard_map/ppermute | solution.py:767
  165.6 28.6 %collective-permute-start.12 = (bf16[8,64,1024]{2,1,0:T(8,128)(2,1)}, bf16[8,64,1024]{2,1,0:T(8,128)(2,1)S(1)}, u32[]{:S(2)}, u32[]{:S(2)}) collective-permute-start(bf16[8,64,1024]{2,1,0:T(8,128)(2,1)} %get-tuple-element.122), channel_id=1, source_target_pairs={{0,2},{2,0},{4,6},{6,4},{8,10},{10,8},{12,14},{14,12},{16,18},{18,... | collective-permute-start | bytes 3145736 | tf_op jit(solution)/shard_map/ppermute | solution.py:767
  167.6 1.4 copy-start.10
  169.0 1.0 copy-start.11
  173.9 24.2 %collective-permute-start.11 = (bf16[2,64,4096]{2,1,0:T(8,128)(2,1)}, bf16[2,64,4096]{2,1,0:T(8,128)(2,1)}, u32[]{:S(2)}, u32[]{:S(2)}) collective-permute-start(bf16[2,64,4096]{2,1,0:T(8,128)(2,1)} %get-tuple-element.113.refs_19_), channel_id=1, source_target_pairs={{0,8},{2,10},{4,12},{6,14},{8,0},{10,2},{12,4},{14,6},{16,24},{18,... | collective-permute-start | bytes 3145736 | tf_op jit(solution)/shard_map/ppermute | solution.py:767
  175.1 16.4 %copy-start.8 = (bf16[8,64,1024]{2,1,0:T(8,128)(2,1)S(1)}, bf16[8,64,1024]{2,1,0:T(8,128)(2,1)}, u32[]{:S(2)}) copy-start(bf16[8,64,1024]{2,1,0:T(8,128)(2,1)} %get-tuple-element.123) | copy-start | bytes 3145732
  185.5 8.8 %copy-start.7 = (bf16[8,64,1024]{2,1,0:T(8,128)(2,1)S(1)}, bf16[8,64,1024]{2,1,0:T(8,128)(2,1)}, u32[]{:S(2)}) copy-start(bf16[8,64,1024]{2,1,0:T(8,128)(2,1)} %get-tuple-element.121) | copy-start | bytes 3145732
  194.1 3.9 %copy-start.9 = (bf16[2,64,4096]{2,1,0:T(8,128)(2,1)S(1)}, bf16[2,64,4096]{2,1,0:T(8,128)(2,1)}, u32[]{:S(2)}) copy-start(bf16[2,64,4096]{2,1,0:T(8,128)(2,1)} %get-tuple-element.119) | copy-start | bytes 3145732
  194.2 13.2 %collective-permute-start.16 = (bf16[4,64,1024]{2,1,0:T(8,128)(2,1)}, bf16[4,64,1024]{2,1,0:T(8,128)(2,1)}, u32[]{:S(2)}, u32[]{:S(2)}) collective-permute-start(bf16[4,64,1024]{2,1,0:T(8,128)(2,1)} %bitcast.18), channel_id=1, source_target_pairs={{0,2},{2,0},{4,6},{6,4},{8,10},{10,8},{12,14},{14,12},{16,18},{18,... | collective-permute-start | bytes 1572872 | tf_op jit(solution)/shard_map/ppermute | solution.py:767
  194.3 5.9 %copy-start.21 = (f32[1,2048]{1,0:T(1,128)S(1)}, f32[1,2048]{1,0:T(1,128)}, u32[]{:S(2)}) copy-start(f32[1,2048]{1,0:T(1,128)} %get-tuple-element.118) | copy-start | bytes 24580
  194.3 6.1 %copy-start.20 = (f32[5,1024]{1,0:T(8,128)S(1)}, f32[5,1024]{1,0:T(8,128)}, u32[]{:S(2)}) copy-start(f32[5,1024]{1,0:T(8,128)} %get-tuple-element.116) | copy-start | bytes 61444
  194.3 6.6 %copy-start.19 = (f32[3,1024]{1,0:T(4,128)S(1)}, f32[3,1024]{1,0:T(4,128)}, u32[]{:S(2)}) copy-start(f32[3,1024]{1,0:T(4,128)} %get-tuple-element.117) | copy-start | bytes 36868
  195.7 12.7 %collective-permute-start.15 = (bf16[4,64,1024]{2,1,0:T(8,128)(2,1)}, bf16[4,64,1024]{2,1,0:T(8,128)(2,1)S(1)}, u32[]{:S(2)}, u32[]{:S(2)}) collective-permute-start(bf16[4,64,1024]{2,1,0:T(8,128)(2,1)} %bitcast.14), channel_id=1, source_target_pairs={{0,4},{2,6},{4,0},{6,2},{8,12},{10,14},{12,8},{14,10},{16,20},{18,... | collective-permute-start | bytes 1572872 | tf_op jit(solution)/shard_map/ppermute | solution.py:767
  199.2 36.8 %collective-permute-start.21 = (bf16[1,64,4096]{2,1,0:T(8,128)(2,1)S(1)}, bf16[1,64,4096]{2,1,0:T(8,128)(2,1)S(1)}, u32[]{:S(2)}, u32[]{:S(2)}) collective-permute-start(bf16[1,64,4096]{2,1,0:T(8,128)(2,1)S(1)} %add_convert_fusion.3), channel_id=1, source_target_pairs={{0,16},{2,18},{4,20},{6,22},{8,24},{10,26},{12,28},{14,30},{16,0},... | collective-permute-start | bytes 1572872 | tf_op jit(solution)/shard_map/ppermute | solution.py:767
  201.2 4.0 %collective-permute-start.14 = (f32[16,384]{1,0:T(8,128)S(1)}, f32[16,384]{1,0:T(8,128)S(1)}, u32[]{:S(2)}, u32[]{:S(2)}) collective-permute-start(f32[16,384]{1,0:T(8,128)S(1)} %bitcast.66), channel_id=1, source_target_pairs={{0,1},{1,0},{2,3},{3,2},{4,5},{5,4},{6,7},{7,6},{8,9},{9,8},{10,11... | collective-permute-start | bytes 73736 | tf_op jit(solution)/shard_map/ppermute | solution.py:1108
  208.4 0.8 copy-start.12
  211.9 36.8 %collective-permute-start.17 = (bf16[1,64,2048]{2,1,0:T(8,128)(2,1)}, bf16[1,64,2048]{2,1,0:T(8,128)(2,1)S(1)}, u32[]{:S(2)}, u32[]{:S(2)}) collective-permute-start(bf16[1,64,2048]{2,1,0:T(8,128)(2,1)} %get-tuple-element.126), channel_id=1, source_target_pairs={{0,8},{2,10},{4,12},{6,14},{8,0},{10,2},{12,4},{14,6},{16,24},{18,... | collective-permute-start | bytes 786440 | tf_op jit(solution)/shard_map/ppermute | solution.py:767
  213.2 35.4 %collective-permute-start.18 = (bf16[1,64,2048]{2,1,0:T(8,128)(2,1)}, bf16[1,64,2048]{2,1,0:T(8,128)(2,1)S(1)}, u32[]{:S(2)}, u32[]{:S(2)}) collective-permute-start(bf16[1,64,2048]{2,1,0:T(8,128)(2,1)} %get-tuple-element.127), channel_id=1, source_target_pairs={{0,16},{2,18},{4,20},{6,22},{8,24},{10,26},{12,28},{14,30},{16,0},... | collective-permute-start | bytes 786440 | tf_op jit(solution)/shard_map/ppermute | solution.py:767
  215.4 33.3 %collective-permute-start.19 = (bf16[1,64,2048]{2,1,0:T(8,128)(2,1)}, bf16[1,64,2048]{2,1,0:T(8,128)(2,1)S(1)}, u32[]{:S(2)}, u32[]{:S(2)}) collective-permute-start(bf16[1,64,2048]{2,1,0:T(8,128)(2,1)} %get-tuple-element.128), channel_id=1, source_target_pairs={{0,24},{2,26},{4,28},{6,30},{8,16},{10,18},{12,20},{14,22},{16,8},... | collective-permute-start | bytes 786440 | tf_op jit(solution)/shard_map/ppermute | solution.py:767
  216.0 32.6 %all-to-all-start.3 = ((f32[16,1,384]{2,1,0:T(1,128)}), f32[16,1,384]{2,1,0:T(1,128)S(1)}, u32[]{:S(2)}, u32[]{:S(2)}) async-start(f32[16,1,384]{2,1,0:T(1,128)} %all_to_all.20), calls=%async_computation.3 | async-start | bytes 49152 | tf_op jit(solution)/shard_map/all_to_all | solution.py:1322
  248.7 0.7 copy-start.15
  248.7 0.8 copy-start.16
  248.7 0.8 copy-start.17
  251.6 2.9 %collective-permute-start.20 = (bf16[32,2048]{1,0:T(8,128)(2,1)}, bf16[32,2048]{1,0:T(8,128)(2,1)S(1)}, u32[]{:S(2)}, u32[]{:S(2)}) collective-permute-start(bf16[32,2048]{1,0:T(8,128)(2,1)} %get-tuple-element.131), channel_id=1, source_target_pairs={{0,1},{1,0},{2,3},{3,2},{4,5},{5,4},{6,7},{7,6},{8,9},{9,8},{10,11... | collective-permute-start | bytes 393224 | tf_op jit(solution)/shard_map/ppermute | solution.py:1108
  254.5 3.0 %copy-start.23 = (f32[32]{0:T(128)}, f32[32]{0:T(128)S(1)}, u32[]{:S(2)}) copy-start(f32[32]{0:T(128)S(1)} %get-tuple-element.183) | copy-start | bytes 388
  254.5 0.7 copy-start.18

commit v4 on v3

--- a/solution.py
+++ b/solution.py
@@ -639,24 +639,22 @@
     )(scalars, *[array for array, _, _ in (*a_runs, *b_runs)])
 
 
-def weight_once_kernel(me_ref, *refs, products, operands):
-    arrays, outs = refs[:operands], refs[operands:-1]
-    for n in range(2):
-        refs[-1][n] = me_ref[n]
+def weight_once_kernel(me_ref, *refs, products, operands, only):
+    arrays, outs = refs[:operands], refs[operands:]
     at = 0
     for blocks, bits in products:
-        parts = outs[at : at + (1 << len(bits))]
+        parts = outs[at : at + len(only)]
         at += len(parts)
         cols = parts[0].shape[2] // len(blocks)
         for n, block in enumerate(blocks):
             here = slice(n * cols, (n + 1) * cols)
-            if len(block) == len(parts):
+            if isinstance(block[0], int):
                 for ref, source in zip(parts, block):
                     ref[:, :, here] = arrays[source][...]
                 continue
             a_runs, b_runs, turned = block
             b = jnp.concatenate([run(arrays, me_ref) for run in b_runs], 1 if turned else 0)
-            for p, ref in enumerate(parts):
+            for p, ref in zip(only, parts):
                 chunks, rows, _ = ref.shape
                 a = []
                 for k in range(chunks):
@@ -677,21 +675,21 @@
     return lambda arrays, me_ref: arrays[n][:, pl.ds(pl.multiple_of(me_ref[1] * cols, cols), cols)]
 
 
-def weight_once(scalars, arrays, products, width, cols, members, behind):
+def weight_once(scalars, arrays, products, width, cols, members, only, behind=()):
     each = [
-        shape_of((members >> len(bits), width // members, cols * len(blocks)), BF16)
+        shape_of((members // 2, width // members, cols * len(blocks)), BF16)
         for blocks, bits in products
-        for _ in range(1 << len(bits))
+        for _ in only
     ]
     outs = vmem_call(
-        partial(weight_once_kernel, products=products, operands=len(arrays)),
-        each + [shape_of((2,), jnp.int32)],
+        partial(weight_once_kernel, products=products, operands=len(arrays), only=only),
+        each,
         scalars,
         arrays,
         "weight_once",
         behind,
     )
-    return outs[:2], outs[2:4], outs[4]
+    return outs[: len(only)], outs[len(only) :]
 
 
 def column_sums(refs, counts):
@@ -1232,7 +1230,7 @@
         for ring in (ring_out, ring_hid):
             ring.hold(sent)
             ring.step()
-        v_parts, d_parts, _ = weight_once(
+        v_parts, d_parts = weight_once(
             scalars,
             [*one_t, own_v, came, own_a, *cot_list],
             [
@@ -1245,30 +1243,34 @@
             width,
             share,
             members,
-            (),
+            (0, 1),
         )
         grad_q, grad_k, sent, own_qk = regroup_once(
             back_second, table, scalars, (*v_parts, *d_parts)
         )
         came = pair_swap(sent)
-        qv_parts, kd_parts, weighed = weight_once(
-            scalars,
-            [*one_t, own_qk, came, *v_parts, *d_parts],
-            [
-                (
-                    [
-                        ((0, 1), (columns_run(2, share, n), columns_run(3, share, n)), False),
-                        (4 + 2 * n, 5 + 2 * n),
-                    ],
-                    (n,),
-                )
-                for n in range(2)
-            ],
-            width,
-            share,
-            members,
-            (),
-        )
+        halves = [
+            weight_once(
+                scalars,
+                [*one_t, own_qk, came, v_parts[p], d_parts[p]],
+                [
+                    (
+                        [
+                            ((0, 1), (columns_run(2, share, n), columns_run(3, share, n)), False),
+                            (4 + n,),
+                        ],
+                        (n,),
+                    )
+                    for n in range(2)
+                ],
+                width,
+                share,
+                members,
+                (p,),
+            )
+            for p in range(2)
+        ]
+        qv_parts, kd_parts = ([h[n][0] for h in halves] for n in range(2))
         ring_qv = Ring(scalars, qv_parts, x_first)
         ring_kd = Ring(scalars, kd_parts, y_first)
     else:

time: 258 us -> 258 us (level)
    ppermute x13, waiting for transfers between devices: 25.8 us -> 23.2 us  [seq_move(): return lax.ppermute(x, 'seq', [(s, s ^ mask) for s in range(members)])]
    pallas_call x10 -> x11, Pallas kernels: 35.6 us -> 37.9 us  [vmem_call(): pl.pallas_call(without(kernel, 1 + len(arrays), len(behind)), in_specs=[p...]
    unnamed x51 -> x53, local copies, waits for them, and re-layouts: 7.36 us -> 6.41 us
  transfers between devices with their start and end apart: 26 -> 26, of which waited for: 14 -> 14; matrix products, arithmetic and copies ran while one was open for 4% -> 4% of each run, Pallas kernels for 47% -> 48%
where the time goes in v4:
time: 258 us; the launch traced here: 257 us
  Pallas kernels  136 us (53%)
  starting transfers between devices  57.4 us (22%)
  waiting for transfers between devices  41.8 us (16%)
  local copies, waits for them, and re-layouts  11.4 us (4%)
  other arithmetic  7.73 us (3%)
  between operations  3.03 us (1%)
    pallas_call x11, Pallas kernels, vmem_call(): pl.pallas_call(without(kernel, 1 + len(arrays), len(behind)), in_specs=[p...  37.9 us
    pallas_call x1, Pallas kernels, forward_head(): pl.pallas_call(without(partial(forward_kernel, key_rows=key_rows, query_r...  26.9 us
    ppermute x13, waiting for transfers between devices, seq_move(): return lax.ppermute(x, 'seq', [(s, s ^ mask) for s in range(members)])  23.2 us
    pallas_call x1, Pallas kernels, backward_head(): pl.pallas_call(without(partial(backward_kernel, key_rows=key_rows, query_...  22.4 us
    pallas_call x1, Pallas kernels, feed(): pl.pallas_call(partial(feed_kernel, count=count, keep=keep), grid=(hidden...  17.3 us
    ppermute x13, starting transfers between devices, seq_move(): return lax.ppermute(x, 'seq', [(s, s ^ mask) for s in range(members)])  15.3 us
    pallas_call x2, Pallas kernels, weight_parts(): pl.pallas_call(partial(weight_kernel, bits=bits, counts=[len(a) for a, _...  12.7 us
    all_to_all x1, waiting for transfers between devices, per_device(): packed = lax.all_to_all(packed, 'seq', 0, 0, tiled=True)  11.4 us
  transfers between devices with their start and end apart: 26, of which 14 were waited for; matrix products, arithmetic and copies ran while one was open for 4% of the time, Pallas kernels for 48%

profile of v4, /device:TPU:1, one launch (start us, length us, event | category | flops | bytes accessed | tf_op | source)
XLA Modules:
  0.0 257.4 jit_solution(12235479189262759539)
XLA Ops:
  1.3 8.5 %open_layer.1 = (bf16[16,1,512,128]{3,2,1,0:T(8,128)(2,1)}, bf16[256,1024]{1,0:T(8,128)(2,1)}, bf16[256,1024]{1,0:T(8,128)(2,1)}, f32[3,256,128]{2,1,0:T(8,128)}...) custom-call(s32[1]{0:T(128)S(6)} %mul.8.first_ref, bf16[256,1024]{1,0:T(8,128)(2,1)} %bitcast.55, ...), custom_call_target="tpu_custom_call" | custom-call | flops 134217728 | bytes 819200 | tf_op jit(solution)/shard_map/open_layer/pallas_call | solution.py:147
  9.8 7.6 %all-to-all-start = ((bf16[16,512,128]{2,1,0:T(8,128)(2,1)}), bf16[16,512,128]{2,1,0:T(8,128)(2,1)}, u32[]{:S(2)}, u32[]{:S(2)}) async-start(bf16[16,512,128]{2,1,0:T(8,128)(2,1)} %bitcast.57), calls=%async_computation | async-start | bytes 4194304 | tf_op jit(solution)/shard_map/all_to_all | solution.py:1156
  17.5 1.0 collective-permute-start.1
  19.0 0.6 reshape.123
  20.0 1.5 collective-permute-done.2.refs_3_.refs_6_
  21.6 0.8 copy-done.7
  22.3 17.3 %feed.1 = (bf16[512,2048]{1,0:T(8,128)(2,1)}, bf16[512,2048]{1,0:T(8,128)(2,1)}, f32[1,2048]{1,0:T(1,128)}, f32[256,1024]{1,0:T(8,128)}, f32[256,1024]{1,0:T(8,128)}, /*index=5*/bf16[512,1024]{1,0:T(8,128)(2,1)}) custom-call(bf16[256,1024]{1,0:T(8,128)(2,1)} %get-tuple-element.77.refs_0_, bf16[256,1024]{1,0:T(8,128)(2,1)} %copy-done.15, ...), custom_call_target="tpu_custom_call" | custom-call | flops 536870912 | bytes 786432 | tf_op jit(solution)/shard_map/feed/pallas_call | solution.py:545
  40.2 0.7 pad_add_fusion
  40.9 6.3 %weight_parts.3 = (bf16[8,64,2048]{2,1,0:T(8,128)(2,1)}, bf16[8,64,2048]{2,1,0:T(8,128)(2,1)}) custom-call(s32[2]{0:T(128)} %get-tuple-element.154.me_ref.refs_0_.refs_14_, bf16[2048,256]{1,0:T(8,128)(2,1)} %get-tuple-element.76.refs_0_.refs_8_, bf16[2048,256]{1,0:T(8,128)(2,1)} %collective-permute-done.refs_1_.refs_9_, ...), custom_call_target="tpu_custom_call" | custom-call | flops 134217728 | bytes 458752 | tf_op jit(solution)/shard_map/weight_parts/pallas_call | solution.py:623
  47.2 1.6 collective-permute-start.6
  48.8 6.3 %weight_parts.2 = (bf16[8,64,2048]{2,1,0:T(8,128)(2,1)}, bf16[8,64,2048]{2,1,0:T(8,128)(2,1)}) custom-call(s32[2]{0:T(128)} %get-tuple-element.154.me_ref.refs_0_.refs_14_, bf16[2048,256]{1,0:T(8,128)(2,1)} %get-tuple-element.76.refs_0_.refs_8_, bf16[2048,256]{1,0:T(8,128)(2,1)} %collective-permute-done.refs_1_.refs_9_, ...), custom_call_target="tpu_custom_call" | custom-call | flops 134217728 | bytes 458752 | tf_op jit(solution)/shard_map/weight_parts/pallas_call | solution.py:623
  55.1 1.2 collective-permute-start.5
  56.3 2.6 %all-to-all-done.refs_1_.x_ref = bf16[16,512,128]{2,1,0:T(8,128)(2,1)} async-done(((bf16[16,512,128]{2,1,0:T(8,128)(2,1)}), bf16[16,512,128]{2,1,0:T(8,128)(2,1)}, u32[]{:S(2)}, u32[]{:S(2)}) %all-to-all-start) | async-done | bytes 2097184 | tf_op jit(solution)/shard_map/all_to_all | solution.py:1156
  58.9 26.9 %forward_head.1 = (bf16[16,256,128]{2,1,0:T(8,128)(2,1)}, bf16[4,1024,128]{2,1,0:T(8,128)(2,1)}, f32[4,1024,128]{2,1,0:T(8,128)}, bf16[20,1024,512]{2,1,0:T(8,128)(2,1)}, s32[1]{0:T(128)}) custom-call(s32[2]{0:T(128)} %get-tuple-element.155.refs_0_, bf16[16,512,128]{2,1,0:T(8,128)(2,1)} %all-to-all-done.refs_1_.x_ref, ...), custom_call_target="tpu_custom_call" | custom-call | flops 16106127360 | bytes 25165824 | tf_op jit(solution)/shard_map/forward_head/pallas_call | solution.py:417
  85.9 10.9 %all-to-all-start.2 = ((bf16[16,256,128]{2,1,0:T(8,128)(2,1)}), bf16[16,256,128]{2,1,0:T(8,128)(2,1)S(1)}, u32[]{:S(2)}, u32[]{:S(2)}) async-start(bf16[16,256,128]{2,1,0:T(8,128)(2,1)} %get-tuple-element.92), calls=%async_computation.2 | async-start | bytes 2097152 | tf_op jit(solution)/shard_map/all_to_all | solution.py:1205
  96.8 22.4 %backward_head.1 = (bf16[16,256,128]{2,1,0:T(8,128)(2,1)}, s32[1]{0:T(128)}) custom-call(s32[2]{0:T(128)} %get-tuple-element.154.me_ref.refs_0_.refs_14_, bf16[16,512,128]{2,1,0:T(8,128)(2,1)} %all-to-all-done.refs_1_.x_ref, bf16[4,1024,128]{2,1,0:T(8,128)(2,1)} %get-tuple-element.86.g_ref, f32[4,1024,128]{2,1,0:T(8,128)} %get-tuple-element.87.d_ref, ...), custom_call_target="tpu_custom_call" | custom-call | flops 16106127360 | bytes 25165824 | tf_op jit(solution)/shard_map/backward_head/pallas_call | solution.py:460
  119.3 6.3 %all-to-all-start.1 = ((bf16[16,256,128]{2,1,0:T(8,128)(2,1)}), bf16[16,256,128]{2,1,0:T(8,128)(2,1)S(1)}, u32[]{:S(2)}, u32[]{:S(2)}) async-start(bf16[16,256,128]{2,1,0:T(8,128)(2,1)} %get-tuple-element.90.refs_2_), calls=%async_computation.1 | async-start | bytes 2097152 | tf_op jit(solution)/shard_map/all_to_all | solution.py:1210
  125.6 3.7 %regroup_once.2 = (bf16[256,1024]{1,0:T(8,128)(2,1)}, bf16[256,1024]{1,0:T(8,128)(2,1)}, bf16[1536,256]{1,0:T(8,128)(2,1)}, bf16[1024,256]{1,0:T(8,128)(2,1)}, bf16[512,256]{1,0:T(8,128)(2,1)}) custom-call(s32[2]{0:T(128)} %get-tuple-element.154.me_ref.refs_0_.refs_14_, bf16[16,256,128]{2,1,0:T(8,128)(2,1)} %copy-done.5, ...), custom_call_target="tpu_custom_call" | custom-call | flops 32768 | bytes 98304 | tf_op jit(solution)/shard_map/regroup_once/pallas_call | solution.py:747
  129.3 2.5 collective-permute-start.7
  131.7 3.9 %add_parts.5 = (bf16[4,64,2048]{2,1,0:T(8,128)(2,1)}, bf16[4,64,2048]{2,1,0:T(8,128)(2,1)}) custom-call(s32[2]{0:T(128)} %get-tuple-element.154.me_ref.refs_0_.refs_14_, bf16[8,64,2048]{2,1,0:T(8,128)(2,1)} %get-tuple-element.107.refs_1_, bf16[8,64,2048]{2,1,0:T(8,128)(2,1)} %collective-permute-done.6.refs_2_, bf16[1536,256]{1,0:T(8,128)(2,1)} %get-tuple-element.94.refs_3_), custom_call_target="tpu_custom_call" | custom-call | flops 131072 | bytes 393216 | tf_op jit(solution)/shard_map/add_parts/pallas_call | solution.py:747
  135.7 1.6 collective-permute-start.9
  137.3 4.0 %add_parts.4 = (bf16[4,64,2048]{2,1,0:T(8,128)(2,1)}, bf16[4,64,2048]{2,1,0:T(8,128)(2,1)}) custom-call(s32[2]{0:T(128)} %get-tuple-element.154.me_ref.refs_0_.refs_14_, bf16[8,64,2048]{2,1,0:T(8,128)(2,1)} %get-tuple-element.104.refs_1_, bf16[8,64,2048]{2,1,0:T(8,128)(2,1)} %collective-permute-done.5.refs_2_, bf16[1536,256]{1,0:T(8,128)(2,1)} %get-tuple-element.94.refs_3_), custom_call_target="tpu_custom_call" | custom-call | flops 131072 | bytes 393216 | tf_op jit(solution)/shard_map/add_parts/pallas_call | solution.py:747
  141.3 1.2 collective-permute-start.8
  142.5 0.9 copy-done.12
  143.4 4.2 %weight_once.3 = (bf16[8,64,512]{2,1,0:T(8,128)(2,1)}, bf16[8,64,512]{2,1,0:T(8,128)(2,1)}, bf16[8,64,512]{2,1,0:T(8,128)(2,1)}, bf16[8,64,512]{2,1,0:T(8,128)(2,1)}) custom-call(s32[2]{0:T(128)} %get-tuple-element.154.me_ref.refs_0_.refs_14_, bf16[1024,256]{1,0:T(8,128)(2,1)} %get-tuple-element.85.refs_10_.refs_0_, bf16[1024,256]{1,0:T(8,128)(2,1)} %copy-done.2, ...), custom_call_target="tpu_custom_call" | custom-call | flops 114688 | bytes 344064 | tf_op jit(solution)/shard_map/weight_once/pallas_call | solution.py:747
  147.7 1.0 copy-done.6
  148.7 4.0 %regroup_once.3 = (bf16[256,1024]{1,0:T(8,128)(2,1)}, bf16[256,1024]{1,0:T(8,128)(2,1)}, bf16[256,1024]{1,0:T(8,128)(2,1)}, bf16[256,1024]{1,0:T(8,128)(2,1)}) custom-call(s32[2]{0:T(128)} %get-tuple-element.154.me_ref.refs_0_.refs_14_, bf16[16,256,128]{2,1,0:T(8,128)(2,1)} %copy-done.6, f32[3,256,128]{2,1,0:T(8,128)} %get-tuple-element.91.refs_2_, ...), custom_call_target="tpu_custom_call" | custom-call | flops 38912 | bytes 116736 | tf_op jit(solution)/shard_map/regroup_once/pallas_call | solution.py:747
  152.7 3.2 %collective-permute-start.10 = (bf16[256,1024]{1,0:T(8,128)(2,1)}, bf16[256,1024]{1,0:T(8,128)(2,1)S(1)}, u32[]{:S(2)}, u32[]{:S(2)}) collective-permute-start(bf16[256,1024]{1,0:T(8,128)(2,1)} %get-tuple-element.111), channel_id=1, source_target_pairs={{0,1},{1,0},{2,3},{3,2},{4,5},{5,4},{6,7},{7,6},{8,9},{9,8},{10,11... | collective-permute-start | bytes 1572872 | tf_op jit(solution)/shard_map/ppermute | solution.py:1106
  155.9 1.7 collective-permute-done.10.refs_3_
  157.7 0.8 copy-done.8
  158.5 3.9 %weight_once.4 = (bf16[8,64,1024]{2,1,0:T(8,128)(2,1)}, bf16[8,64,1024]{2,1,0:T(8,128)(2,1)}) custom-call(s32[2]{0:T(128)} %get-tuple-element.154.me_ref.refs_0_.refs_14_, bf16[1024,256]{1,0:T(8,128)(2,1)} %get-tuple-element.85.refs_10_.refs_0_, bf16[1024,256]{1,0:T(8,128)(2,1)} %copy-done.2, bf16[256,1024]{1,0:T(8,128)(2,1)} %get-tuple-element.110.refs_2_, ...), custom_call_target="tpu_custom_call" | custom-call | flops 98304 | bytes 294912 | tf_op jit(solution)/shard_map/weight_once/pallas_call | solution.py:747
  162.4 1.7 collective-permute-start.13
  164.4 3.4 %collective-permute-done.9.refs_4_ = bf16[4,64,2048]{2,1,0:T(8,128)(2,1)S(1)} collective-permute-done((bf16[4,64,2048]{2,1,0:T(8,128)(2,1)}, bf16[4,64,2048]{2,1,0:T(8,128)(2,1)S(1)}, u32[]{:S(2)}, u32[]{:S(2)}) %collective-permute-start.9) | collective-permute-done | bytes 1048608 | tf_op jit(solution)/shard_map/ppermute | solution.py:765
  167.7 1.4 collective-permute-done.8.refs_2_
  169.1 3.9 %add_parts.6 = (bf16[2,64,4096]{2,1,0:T(8,128)(2,1)}, bf16[2,64,4096]{2,1,0:T(8,128)(2,1)}) custom-call(s32[2]{0:T(128)} %get-tuple-element.154.me_ref.refs_0_.refs_14_, bf16[4,64,2048]{2,1,0:T(8,128)(2,1)} %get-tuple-element.105.refs_1_, bf16[4,64,2048]{2,1,0:T(8,128)(2,1)} %collective-permute-done.8.refs_2_, ...), custom_call_target="tpu_custom_call" | custom-call | flops 131072 | bytes 393216 | tf_op jit(solution)/shard_map/add_parts/pallas_call | solution.py:747
  173.0 1.3 collective-permute-start.11
  174.3 3.8 %weight_once.5 = (bf16[8,64,1024]{2,1,0:T(8,128)(2,1)}, bf16[8,64,1024]{2,1,0:T(8,128)(2,1)}) custom-call(s32[2]{0:T(128)} %get-tuple-element.154.me_ref.refs_0_.refs_14_, bf16[1024,256]{1,0:T(8,128)(2,1)} %get-tuple-element.85.refs_10_.refs_0_, bf16[1024,256]{1,0:T(8,128)(2,1)} %copy-done.2, bf16[256,1024]{1,0:T(8,128)(2,1)} %get-tuple-element.110.refs_2_, ...), custom_call_target="tpu_custom_call" | custom-call | flops 98304 | bytes 294912 | tf_op jit(solution)/shard_map/weight_once/pallas_call | solution.py:747
  178.1 10.3 %close_layer.1 = (bf16[256,1024]{1,0:T(8,128)(2,1)}, f32[256,1024]{1,0:T(8,128)}, f32[5,1024]{1,0:T(8,128)}, f32[3,1024]{1,0:T(4,128)}, s32[2]{0:T(128)}) custom-call(bf16[256,1024]{1,0:T(8,128)(2,1)} %bitcast.56, bf16[256,1024]{1,0:T(8,128)(2,1)} %bitcast.53, bf16[1024]{0:T(1024)(128)(2,1)} %refs_2_.1, bf16[1024]{0:T(1024)(128)(2,1)} %refs_3_.1, ...), custom_call_target="tpu_custom_call" | custom-call | flops 134217728 | bytes 917504 | tf_op jit(solution)/shard_map/close_layer/pallas_call | solution.py:1053
  190.4 1.2 collective-permute-done.13
  191.6 2.7 %add_convert_fusion.1 = (bf16[2,2,1,64,1024]{4,3,1,0,2:T(8,128)(2,1)}, bf16[2,2,1,64,1024]{4,3,1,0,2:T(8,128)(2,1)}) fusion(bf16[2,2,2,64,1024]{4,3,2,1,0:T(8,128)(2,1)S(1)} %bitcast.61, s32[]{:T(128)S(6)} %select_n.48, bf16[2,2,2,64,1024]{4,3,2,1,0:T(8,128)(2,1)} %bitcast.63, s32[]{:T(128)S(6)} %select_n.46), kind=kLoop, calls=%fused_computation.2 | loop fusion | flops 2097152 | bytes 3145736 | tf_op jit(solution)/shard_map/convert_element_type | solution.py:833
  194.4 1.4 add_convert_fusion.2
  195.8 0.7 collective-permute-start.15
  196.5 0.7 collective-permute-done.11
  197.2 1.2 add_convert_fusion.3
  198.4 2.1 collective-permute-start.21
  201.6 2.5 collective-permute-start.14
  204.1 0.8 collective-permute-done.14
  205.0 2.6 %collective-permute-done.16.refs_3_ = bf16[4,64,1024]{2,1,0:T(8,128)(2,1)} collective-permute-done((bf16[4,64,1024]{2,1,0:T(8,128)(2,1)}, bf16[4,64,1024]{2,1,0:T(8,128)(2,1)}, u32[]{:S(2)}, u32[]{:S(2)}) %collective-permute-start.16) | collective-permute-done | bytes 524320 | tf_op jit(solution)/shard_map/ppermute | solution.py:765
  207.6 0.9 collective-permute-done.15.refs_1_
  208.5 0.8 copy-done.13
  209.3 2.7 %add_parts.7 = (bf16[1,64,2048]{2,1,0:T(8,128)(2,1)}, bf16[1,64,2048]{2,1,0:T(8,128)(2,1)}, bf16[1,64,2048]{2,1,0:T(8,128)(2,1)}, bf16[1,64,2048]{2,1,0:T(8,128)(2,1)}) custom-call(s32[2]{0:T(128)} %get-tuple-element.154.me_ref.refs_0_.refs_14_, bf16[4,64,1024]{2,1,0:T(8,128)(2,1)} %bitcast.59, bf16[4,64,1024]{2,1,0:T(8,128)(2,1)} %copy-done.13, ...), custom_call_target="tpu_custom_call" | custom-call | flops 65536 | bytes 196608 | tf_op jit(solution)/shard_map/add_parts/pallas_call | solution.py:747
  212.0 1.4 collective-permute-start.17
  213.4 2.1 collective-permute-start.18
  215.5 0.6 all_to_all.20
  216.2 6.1 %all-to-all-start.3 = ((f32[16,1,384]{2,1,0:T(1,128)}), f32[16,1,384]{2,1,0:T(1,128)S(1)}, u32[]{:S(2)}, u32[]{:S(2)}) async-start(f32[16,1,384]{2,1,0:T(1,128)} %all_to_all.20), calls=%async_computation.3 | async-start | bytes 49152 | tf_op jit(solution)/shard_map/all_to_all | solution.py:1324
  222.2 13.0 %collective-permute-done.21 = bf16[1,64,4096]{2,1,0:T(8,128)(2,1)S(1)} collective-permute-done((bf16[1,64,4096]{2,1,0:T(8,128)(2,1)S(1)}, bf16[1,64,4096]{2,1,0:T(8,128)(2,1)S(1)}, u32[]{:S(2)}, u32[]{:S(2)}) %collective-permute-start.21) | collective-permute-done | bytes 524320 | tf_op jit(solution)/shard_map/ppermute | solution.py:765
  235.2 1.2 add_bitcast_fusion
  236.4 1.0 slice_bitcast_fusion
  237.5 11.4 %all-to-all-done.3 = f32[16,1,384]{2,1,0:T(1,128)S(1)} async-done(((f32[16,1,384]{2,1,0:T(1,128)}), f32[16,1,384]{2,1,0:T(1,128)S(1)}, u32[]{:S(2)}, u32[]{:S(2)}) %all-to-all-start.3) | async-done | bytes 24608 | tf_op jit(solution)/shard_map/all_to_all | solution.py:1324
  248.9 0.7 copy-done.16
  249.8 2.1 last_sum.1
  251.9 0.9 collective-permute-start.20
  254.5 0.6 copy-done.19
  255.1 1.8 place.1
  (86 shorter events, 6.2 us)
Async XLA Ops:
  9.8 7.7 %copy-start.14 = (bf16[256,1024]{1,0:T(8,128)(2,1)S(1)}, bf16[256,1024]{1,0:T(8,128)(2,1)}, u32[]{:S(2)}) copy-start(bf16[256,1024]{1,0:T(8,128)(2,1)} %get-tuple-element.77.refs_0_) | copy-start | bytes 1572868
  9.8 8.7 %copy-start = (bf16[1,256,1024]{2,1,0:T(8,128)(2,1)S(1)}, bf16[1,256,1024]{2,1,0:T(8,128)(2,1)}, u32[]{:S(2)}) copy-start(bf16[1,256,1024]{2,1,0:T(8,128)(2,1)} %param.15) | copy-start | bytes 1572868
  9.8 8.8 %copy-start.4 = (bf16[2048,256]{1,0:T(8,128)(2,1)S(1)}, bf16[2048,256]{1,0:T(8,128)(2,1)}, u32[]{:S(2)}) copy-start(bf16[2048,256]{1,0:T(8,128)(2,1)} %get-tuple-element.76.refs_0_.refs_8_) | copy-start | bytes 3145732
  9.8 9.2 %copy-start.23 = (bf16[2048]{0:T(1024)(128)(2,1)S(1)}, bf16[2048]{0:T(1024)(128)(2,1)}, u32[]{:S(2)}) copy-start(bf16[2048]{0:T(1024)(128)(2,1)} %param.25) | copy-start | bytes 12292
  9.8 49.1 %all-to-all-start = ((bf16[16,512,128]{2,1,0:T(8,128)(2,1)}), bf16[16,512,128]{2,1,0:T(8,128)(2,1)}, u32[]{:S(2)}, u32[]{:S(2)}) async-start(bf16[16,512,128]{2,1,0:T(8,128)(2,1)} %bitcast.57), calls=%async_computation | async-start | bytes 4194304 | tf_op jit(solution)/shard_map/all_to_all | solution.py:1156
  17.5 2.6 collective-permute-start.1
  18.5 3.0 %collective-permute-start.2 = (bf16[256,1024]{1,0:T(8,128)(2,1)S(1)}, bf16[256,1024]{1,0:T(8,128)(2,1)S(1)}, u32[]{:S(2)}, u32[]{:S(2)}) collective-permute-start(bf16[256,1024]{1,0:T(8,128)(2,1)S(1)} %bitcast.54), channel_id=1, source_target_pairs={{0,1},{1,0},{2,3},{3,2},{4,5},{5,4},{6,7},{7,6},{8,9},{9,8},{10,11... | collective-permute-start | bytes 1572872 | tf_op jit(solution)/shard_map/ppermute | solution.py:1106
  18.6 22.3 %collective-permute-start = (bf16[2048,256]{1,0:T(8,128)(2,1)S(1)}, bf16[2048,256]{1,0:T(8,128)(2,1)}, u32[]{:S(2)}, u32[]{:S(2)}) collective-permute-start(bf16[2048,256]{1,0:T(8,128)(2,1)S(1)} %copy-done.4), channel_id=1, source_target_pairs={{0,1},{1,0},{2,3},{3,2},{4,5},{5,4},{6,7},{7,6},{8,9},{9,8},{10,11... | collective-permute-start | bytes 3145736 | tf_op jit(solution)/shard_map/ppermute | solution.py:1106
  20.0 1.5 copy-start.15
  21.5 0.8 copy-start.7
  22.3 17.7 %copy-start.1 = (bf16[1024,256]{1,0:T(8,128)(2,1)S(1)}, bf16[1024,256]{1,0:T(8,128)(2,1)}, u32[]{:S(2)}) copy-start(bf16[1024,256]{1,0:T(8,128)(2,1)} %get-tuple-element.85.refs_10_.refs_0_) | copy-start | bytes 1572868
  39.6 16.7 %collective-permute-start.3 = (bf16[512,1024]{1,0:T(8,128)(2,1)}, bf16[512,1024]{1,0:T(8,128)(2,1)S(1)}, u32[]{:S(2)}, u32[]{:S(2)}) collective-permute-start(bf16[512,1024]{1,0:T(8,128)(2,1)} %get-tuple-element.83), channel_id=1, source_target_pairs={{0,1},{1,0},{2,3},{3,2},{4,5},{5,4},{6,7},{7,6},{8,9},{9,8},{10,11... | collective-permute-start | bytes 3145736 | tf_op jit(solution)/shard_map/ppermute | solution.py:1106
  40.1 16.2 %collective-permute-start.4 = (bf16[1024,256]{1,0:T(8,128)(2,1)S(1)}, bf16[1024,256]{1,0:T(8,128)(2,1)S(1)}, u32[]{:S(2)}, u32[]{:S(2)}) collective-permute-start(bf16[1024,256]{1,0:T(8,128)(2,1)S(1)} %copy-done.1), channel_id=1, source_target_pairs={{0,1},{1,0},{2,3},{3,2},{4,5},{5,4},{6,7},{7,6},{8,9},{9,8},{10,11... | collective-permute-start | bytes 1572872 | tf_op jit(solution)/shard_map/ppermute | solution.py:1106
  47.2 72.0 %collective-permute-start.6 = (bf16[8,64,2048]{2,1,0:T(8,128)(2,1)}, bf16[8,64,2048]{2,1,0:T(8,128)(2,1)}, u32[]{:S(2)}, u32[]{:S(2)}) collective-permute-start(bf16[8,64,2048]{2,1,0:T(8,128)(2,1)} %get-tuple-element.81.refs_3_), channel_id=1, source_target_pairs={{0,4},{2,6},{4,0},{6,2},{8,12},{10,14},{12,8},{14,10},{16,20},{18,... | collective-permute-start | bytes 6291464 | tf_op jit(solution)/shard_map/ppermute | solution.py:765
  55.1 64.1 %collective-permute-start.5 = (bf16[8,64,2048]{2,1,0:T(8,128)(2,1)}, bf16[8,64,2048]{2,1,0:T(8,128)(2,1)}, u32[]{:S(2)}, u32[]{:S(2)}) collective-permute-start(bf16[8,64,2048]{2,1,0:T(8,128)(2,1)} %get-tuple-element.79.refs_2_), channel_id=1, source_target_pairs={{0,2},{2,0},{4,6},{6,4},{8,10},{10,8},{12,14},{14,12},{16,18},{18,... | collective-permute-start | bytes 6291464 | tf_op jit(solution)/shard_map/ppermute | solution.py:765
  56.3 2.6 %copy-start.2 = (bf16[1024,256]{1,0:T(8,128)(2,1)}, bf16[1024,256]{1,0:T(8,128)(2,1)S(1)}, u32[]{:S(2)}) copy-start(bf16[1024,256]{1,0:T(8,128)(2,1)S(1)} %collective-permute-done.4.refs_11_.refs_1_) | copy-start | bytes 1572868
  56.3 2.6 %copy-start.3 = (bf16[512,1024]{1,0:T(8,128)(2,1)}, bf16[512,1024]{1,0:T(8,128)(2,1)S(1)}, u32[]{:S(2)}) copy-start(bf16[512,1024]{1,0:T(8,128)(2,1)S(1)} %collective-permute-done.3.refs_5_.refs_7_.refs_16_.refs_18_) | copy-start | bytes 3145732
  85.9 33.4 %all-to-all-start.2 = ((bf16[16,256,128]{2,1,0:T(8,128)(2,1)}), bf16[16,256,128]{2,1,0:T(8,128)(2,1)S(1)}, u32[]{:S(2)}, u32[]{:S(2)}) async-start(bf16[16,256,128]{2,1,0:T(8,128)(2,1)} %get-tuple-element.92), calls=%async_computation.2 | async-start | bytes 2097152 | tf_op jit(solution)/shard_map/all_to_all | solution.py:1205
  119.2 6.4 %copy-start.5 = (bf16[16,256,128]{2,1,0:T(8,128)(2,1)}, bf16[16,256,128]{2,1,0:T(8,128)(2,1)S(1)}, u32[]{:S(2)}) copy-start(bf16[16,256,128]{2,1,0:T(8,128)(2,1)S(1)} %all-to-all-done.2.refs_1_) | copy-start | bytes 3145732
  119.3 28.5 %all-to-all-start.1 = ((bf16[16,256,128]{2,1,0:T(8,128)(2,1)}), bf16[16,256,128]{2,1,0:T(8,128)(2,1)S(1)}, u32[]{:S(2)}, u32[]{:S(2)}) async-start(bf16[16,256,128]{2,1,0:T(8,128)(2,1)} %get-tuple-element.90.refs_2_), calls=%async_computation.1 | async-start | bytes 2097152 | tf_op jit(solution)/shard_map/all_to_all | solution.py:1210
  129.3 13.2 %collective-permute-start.7 = (bf16[1536,256]{1,0:T(8,128)(2,1)}, bf16[1536,256]{1,0:T(8,128)(2,1)S(1)}, u32[]{:S(2)}, u32[]{:S(2)}) collective-permute-start(bf16[1536,256]{1,0:T(8,128)(2,1)} %get-tuple-element.94.refs_3_), channel_id=1, source_target_pairs={{0,1},{1,0},{2,3},{3,2},{4,5},{5,4},{6,7},{7,6},{8,9},{9,8},{10,11... | collective-permute-start | bytes 2359304 | tf_op jit(solution)/shard_map/ppermute | solution.py:1106
  135.7 32.0 %collective-permute-start.9 = (bf16[4,64,2048]{2,1,0:T(8,128)(2,1)}, bf16[4,64,2048]{2,1,0:T(8,128)(2,1)S(1)}, u32[]{:S(2)}, u32[]{:S(2)}) collective-permute-start(bf16[4,64,2048]{2,1,0:T(8,128)(2,1)} %get-tuple-element.109), channel_id=1, source_target_pairs={{0,2},{2,0},{4,6},{6,4},{8,10},{10,8},{12,14},{14,12},{16,18},{18,... | collective-permute-start | bytes 3145736 | tf_op jit(solution)/shard_map/ppermute | solution.py:765
  141.3 27.8 %collective-permute-start.8 = (bf16[4,64,2048]{2,1,0:T(8,128)(2,1)}, bf16[4,64,2048]{2,1,0:T(8,128)(2,1)}, u32[]{:S(2)}, u32[]{:S(2)}) collective-permute-start(bf16[4,64,2048]{2,1,0:T(8,128)(2,1)} %get-tuple-element.106), channel_id=1, source_target_pairs={{0,4},{2,6},{4,0},{6,2},{8,12},{10,14},{12,8},{14,10},{16,20},{18,... | collective-permute-start | bytes 3145736 | tf_op jit(solution)/shard_map/ppermute | solution.py:765
  142.5 0.9 copy-start.12
  147.7 1.0 copy-start.6
  152.7 5.0 %collective-permute-start.10 = (bf16[256,1024]{1,0:T(8,128)(2,1)}, bf16[256,1024]{1,0:T(8,128)(2,1)S(1)}, u32[]{:S(2)}, u32[]{:S(2)}) collective-permute-start(bf16[256,1024]{1,0:T(8,128)(2,1)} %get-tuple-element.111), channel_id=1, source_target_pairs={{0,1},{1,0},{2,3},{3,2},{4,5},{5,4},{6,7},{7,6},{8,9},{9,8},{10,11... | collective-permute-start | bytes 1572872 | tf_op jit(solution)/shard_map/ppermute | solution.py:1106
  157.7 0.8 copy-start.8
  162.4 29.2 %collective-permute-start.13 = (bf16[8,64,1024]{2,1,0:T(8,128)(2,1)}, bf16[8,64,1024]{2,1,0:T(8,128)(2,1)S(1)}, u32[]{:S(2)}, u32[]{:S(2)}) collective-permute-start(bf16[8,64,1024]{2,1,0:T(8,128)(2,1)} %get-tuple-element.112.refs_5_), channel_id=1, source_target_pairs={{0,4},{2,6},{4,0},{6,2},{8,12},{10,14},{12,8},{14,10},{16,20},{18,... | collective-permute-start | bytes 3145736 | tf_op jit(solution)/shard_map/ppermute | solution.py:765
  164.1 30.3 %collective-permute-start.12 = (bf16[8,64,1024]{2,1,0:T(8,128)(2,1)}, bf16[8,64,1024]{2,1,0:T(8,128)(2,1)S(1)}, u32[]{:S(2)}, u32[]{:S(2)}) collective-permute-start(bf16[8,64,1024]{2,1,0:T(8,128)(2,1)} %get-tuple-element.122), channel_id=1, source_target_pairs={{0,2},{2,0},{4,6},{6,4},{8,10},{10,8},{12,14},{14,12},{16,18},{18,... | collective-permute-start | bytes 3145736 | tf_op jit(solution)/shard_map/ppermute | solution.py:765
  167.7 1.4 copy-start.11
  173.0 24.2 %collective-permute-start.11 = (bf16[2,64,4096]{2,1,0:T(8,128)(2,1)}, bf16[2,64,4096]{2,1,0:T(8,128)(2,1)}, u32[]{:S(2)}, u32[]{:S(2)}) collective-permute-start(bf16[2,64,4096]{2,1,0:T(8,128)(2,1)} %get-tuple-element.113.refs_19_), channel_id=1, source_target_pairs={{0,8},{2,10},{4,12},{6,14},{8,0},{10,2},{12,4},{14,6},{16,24},{18,... | collective-permute-start | bytes 3145736 | tf_op jit(solution)/shard_map/ppermute | solution.py:765
  188.4 6.0 %copy-start.9 = (bf16[8,64,1024]{2,1,0:T(8,128)(2,1)S(1)}, bf16[8,64,1024]{2,1,0:T(8,128)(2,1)}, u32[]{:S(2)}) copy-start(bf16[8,64,1024]{2,1,0:T(8,128)(2,1)} %get-tuple-element.121) | copy-start | bytes 3145732
  194.3 3.0 %copy-start.10 = (bf16[2,64,4096]{2,1,0:T(8,128)(2,1)S(1)}, bf16[2,64,4096]{2,1,0:T(8,128)(2,1)}, u32[]{:S(2)}) copy-start(bf16[2,64,4096]{2,1,0:T(8,128)(2,1)} %get-tuple-element.119) | copy-start | bytes 3145732
  194.3 13.3 %collective-permute-start.16 = (bf16[4,64,1024]{2,1,0:T(8,128)(2,1)}, bf16[4,64,1024]{2,1,0:T(8,128)(2,1)}, u32[]{:S(2)}, u32[]{:S(2)}) collective-permute-start(bf16[4,64,1024]{2,1,0:T(8,128)(2,1)} %bitcast.18), channel_id=1, source_target_pairs={{0,2},{2,0},{4,6},{6,4},{8,10},{10,8},{12,14},{14,12},{16,18},{18,... | collective-permute-start | bytes 1572872 | tf_op jit(solution)/shard_map/ppermute | solution.py:765
  194.4 6.2 %copy-start.22 = (f32[1,2048]{1,0:T(1,128)S(1)}, f32[1,2048]{1,0:T(1,128)}, u32[]{:S(2)}) copy-start(f32[1,2048]{1,0:T(1,128)} %get-tuple-element.118) | copy-start | bytes 24580
  194.4 6.4 %copy-start.21 = (f32[5,1024]{1,0:T(8,128)S(1)}, f32[5,1024]{1,0:T(8,128)}, u32[]{:S(2)}) copy-start(f32[5,1024]{1,0:T(8,128)} %get-tuple-element.116) | copy-start | bytes 61444
  194.4 6.9 %copy-start.20 = (f32[3,1024]{1,0:T(4,128)S(1)}, f32[3,1024]{1,0:T(4,128)}, u32[]{:S(2)}) copy-start(f32[3,1024]{1,0:T(4,128)} %get-tuple-element.117) | copy-start | bytes 36868
  195.8 12.8 %collective-permute-start.15 = (bf16[4,64,1024]{2,1,0:T(8,128)(2,1)}, bf16[4,64,1024]{2,1,0:T(8,128)(2,1)S(1)}, u32[]{:S(2)}, u32[]{:S(2)}) collective-permute-start(bf16[4,64,1024]{2,1,0:T(8,128)(2,1)} %bitcast.14), channel_id=1, source_target_pairs={{0,4},{2,6},{4,0},{6,2},{8,12},{10,14},{12,8},{14,10},{16,20},{18,... | collective-permute-start | bytes 1572872 | tf_op jit(solution)/shard_map/ppermute | solution.py:765
  198.4 36.8 %collective-permute-start.21 = (bf16[1,64,4096]{2,1,0:T(8,128)(2,1)S(1)}, bf16[1,64,4096]{2,1,0:T(8,128)(2,1)S(1)}, u32[]{:S(2)}, u32[]{:S(2)}) collective-permute-start(bf16[1,64,4096]{2,1,0:T(8,128)(2,1)S(1)} %add_convert_fusion.3), channel_id=1, source_target_pairs={{0,16},{2,18},{4,20},{6,22},{8,24},{10,26},{12,28},{14,30},{16,0},... | collective-permute-start | bytes 1572872 | tf_op jit(solution)/shard_map/ppermute | solution.py:765
  201.6 3.3 %collective-permute-start.14 = (f32[16,384]{1,0:T(8,128)S(1)}, f32[16,384]{1,0:T(8,128)S(1)}, u32[]{:S(2)}, u32[]{:S(2)}) collective-permute-start(f32[16,384]{1,0:T(8,128)S(1)} %bitcast.67), channel_id=1, source_target_pairs={{0,1},{1,0},{2,3},{3,2},{4,5},{5,4},{6,7},{7,6},{8,9},{9,8},{10,11... | collective-permute-start | bytes 73736 | tf_op jit(solution)/shard_map/ppermute | solution.py:1106
  208.5 0.8 copy-start.13
  212.0 36.9 %collective-permute-start.17 = (bf16[1,64,2048]{2,1,0:T(8,128)(2,1)}, bf16[1,64,2048]{2,1,0:T(8,128)(2,1)S(1)}, u32[]{:S(2)}, u32[]{:S(2)}) collective-permute-start(bf16[1,64,2048]{2,1,0:T(8,128)(2,1)} %get-tuple-element.126), channel_id=1, source_target_pairs={{0,8},{2,10},{4,12},{6,14},{8,0},{10,2},{12,4},{14,6},{16,24},{18,... | collective-permute-start | bytes 786440 | tf_op jit(solution)/shard_map/ppermute | solution.py:765
  213.4 35.5 %collective-permute-start.18 = (bf16[1,64,2048]{2,1,0:T(8,128)(2,1)}, bf16[1,64,2048]{2,1,0:T(8,128)(2,1)S(1)}, u32[]{:S(2)}, u32[]{:S(2)}) collective-permute-start(bf16[1,64,2048]{2,1,0:T(8,128)(2,1)} %get-tuple-element.127), channel_id=1, source_target_pairs={{0,16},{2,18},{4,20},{6,22},{8,24},{10,26},{12,28},{14,30},{16,0},... | collective-permute-start | bytes 786440 | tf_op jit(solution)/shard_map/ppermute | solution.py:765
  215.5 33.4 %collective-permute-start.19 = (bf16[1,64,2048]{2,1,0:T(8,128)(2,1)}, bf16[1,64,2048]{2,1,0:T(8,128)(2,1)S(1)}, u32[]{:S(2)}, u32[]{:S(2)}) collective-permute-start(bf16[1,64,2048]{2,1,0:T(8,128)(2,1)} %get-tuple-element.128), channel_id=1, source_target_pairs={{0,24},{2,26},{4,28},{6,30},{8,16},{10,18},{12,20},{14,22},{16,8},... | collective-permute-start | bytes 786440 | tf_op jit(solution)/shard_map/ppermute | solution.py:765
  216.2 32.7 %all-to-all-start.3 = ((f32[16,1,384]{2,1,0:T(1,128)}), f32[16,1,384]{2,1,0:T(1,128)S(1)}, u32[]{:S(2)}, u32[]{:S(2)}) async-start(f32[16,1,384]{2,1,0:T(1,128)} %all_to_all.20), calls=%async_computation.3 | async-start | bytes 49152 | tf_op jit(solution)/shard_map/all_to_all | solution.py:1324
  248.9 0.7 copy-start.16
  248.9 0.8 copy-start.17
  248.9 0.9 copy-start.18
  251.9 2.6 %collective-permute-start.20 = (bf16[32,2048]{1,0:T(8,128)(2,1)}, bf16[32,2048]{1,0:T(8,128)(2,1)S(1)}, u32[]{:S(2)}, u32[]{:S(2)}) collective-permute-start(bf16[32,2048]{1,0:T(8,128)(2,1)} %get-tuple-element.131), channel_id=1, source_target_pairs={{0,1},{1,0},{2,3},{3,2},{4,5},{5,4},{6,7},{7,6},{8,9},{9,8},{10,11... | collective-permute-start | bytes 393224 | tf_op jit(solution)/shard_map/ppermute | solution.py:1106
  254.5 3.0 %copy-start.24 = (f32[32]{0:T(128)}, f32[32]{0:T(128)S(1)}, u32[]{:S(2)}) copy-start(f32[32]{0:T(128)S(1)} %get-tuple-element.183) | copy-start | bytes 388
  254.5 0.6 copy-start.19

commit v5 on v4

--- a/solution.py
+++ b/solution.py
@@ -707,12 +707,12 @@
     return [partial(total, group) for group in groups]
 
 
-def add_kernel(me_ref, *refs, counts, bits, positions):
+def add_kernel(me_ref, *refs, counts, bits, positions, only):
     ins, outs = refs[: sum(counts)], refs[sum(counts) :]
     at = 0
     for group, total in zip(counts, column_sums(ins, counts)):
         cols = ins[0].shape[2]
-        for p, ref in enumerate(outs):
+        for p, ref in zip(only, outs):
             for k in range(ref.shape[0]):
                 c = part_chunk(k, p, me_ref[0], bits, positions)
                 ref[k, :, at : at + cols] = total(c).astype(BF16)
@@ -793,7 +793,7 @@
     def hold(self, *others):
         self.behind = others
 
-    def step(self, *others):
+    def step(self, *others, apart=False):
         stage = self.stages[0]
         positions = [self.left.index(b) for b in stage]
         rings = (self, *others)
@@ -801,18 +801,28 @@
         cols = sum(ring.keep.shape[2] for ring in rings)
         count = 1 << len(stage)
         arrays = [[ring.keep, *ring.came] for ring in rings]
-        self.travel(
-            vmem_call(
+
+        def parts(only):
+            return vmem_call(
                 partial(
-                    add_kernel, counts=[len(a) for a in arrays], bits=stage, positions=positions
+                    add_kernel,
+                    counts=[len(a) for a in arrays],
+                    bits=stage,
+                    positions=positions,
+                    only=only,
                 ),
-                [shape_of((chunks // count, rows, cols), BF16)] * count,
+                [shape_of((chunks // count, rows, cols), BF16)] * len(only),
                 self.scalars,
                 [a for group in arrays for a in group],
                 "add_parts",
                 self.behind,
             )
-        )
+
+        if apart:
+            sent = parts(range(1, count))
+            self.travel([*parts((0,)), *sent])
+        else:
+            self.travel(parts(range(count)))
         self.behind = ()
 
     def pass_on(self, me):
@@ -1229,7 +1239,7 @@
         came = pair_swap(sent)
         for ring in (ring_out, ring_hid):
             ring.hold(sent)
-            ring.step()
+            ring.step(apart=True)
         v_parts, d_parts = weight_once(
             scalars,
             [*one_t, own_v, came, own_a, *cot_list],

time: 258 us -> 261 us (1.012)
  Pallas kernels: 136 us -> 142 us
    pallas_call x11 -> x13, Pallas kernels: 37.9 us -> 43.8 us  [vmem_call(): pl.pallas_call(without(kernel, 1 + len(arrays), len(behind)), in_specs=[p...]
    unnamed x53 -> x51, local copies, waits for them, and re-layouts: 6.41 us -> 6.38 us
  transfers between devices with their start and end apart: 26 -> 26, of which waited for: 14 -> 11; matrix products, arithmetic and copies ran while one was open for 4% -> 4% of each run, Pallas kernels for 48% -> 50%
where the time goes in v5:
time: 261 us; the launch traced here: 260 us
  Pallas kernels  142 us (54%)
  starting transfers between devices  56.6 us (22%)
  waiting for transfers between devices  39.2 us (15%)
  local copies, waits for them, and re-layouts  11.4 us (4%)
  other arithmetic  7.62 us (3%)
  between operations  3.04 us (1%)
    pallas_call x13, Pallas kernels, vmem_call(): pl.pallas_call(without(kernel, 1 + len(arrays), len(behind)), in_specs=[p...  43.8 us
    pallas_call x1, Pallas kernels, forward_head(): pl.pallas_call(without(partial(forward_kernel, key_rows=key_rows, query_r...  26.8 us
    pallas_call x1, Pallas kernels, backward_head(): pl.pallas_call(without(partial(backward_kernel, key_rows=key_rows, query_...  22.4 us
    ppermute x13, waiting for transfers between devices, seq_move(): return lax.ppermute(x, 'seq', [(s, s ^ mask) for s in range(members)])  20.9 us
    pallas_call x1, Pallas kernels, feed(): pl.pallas_call(partial(feed_kernel, count=count, keep=keep), grid=(hidden...  17.4 us
    ppermute x13, starting transfers between devices, seq_move(): return lax.ppermute(x, 'seq', [(s, s ^ mask) for s in range(members)])  16.5 us
    pallas_call x2, Pallas kernels, weight_parts(): pl.pallas_call(partial(weight_kernel, bits=bits, counts=[len(a) for a, _...  12.7 us
    ppermute x9, starting transfers between devices, pair_swap(): return lax.ppermute(x, 'mlp', [(0, 1), (1, 0)])  11.5 us
  transfers between devices with their start and end apart: 26, of which 11 were waited for; matrix products, arithmetic and copies ran while one was open for 4% of the time, Pallas kernels for 50%

profile of v5, /device:TPU:1, one launch (start us, length us, event | category | flops | bytes accessed | tf_op | source)
XLA Modules:
  0.0 259.8 jit_solution(2011616840096324210)
XLA Ops:
  1.3 8.5 %open_layer.1 = (bf16[16,1,512,128]{3,2,1,0:T(8,128)(2,1)}, bf16[256,1024]{1,0:T(8,128)(2,1)}, bf16[256,1024]{1,0:T(8,128)(2,1)}, f32[3,256,128]{2,1,0:T(8,128)}...) custom-call(s32[1]{0:T(128)S(6)} %mul.8.first_ref, bf16[256,1024]{1,0:T(8,128)(2,1)} %bitcast.55, ...), custom_call_target="tpu_custom_call" | custom-call | flops 134217728 | bytes 819200 | tf_op jit(solution)/shard_map/open_layer/pallas_call | solution.py:147
  9.8 7.6 %all-to-all-start = ((bf16[16,512,128]{2,1,0:T(8,128)(2,1)}), bf16[16,512,128]{2,1,0:T(8,128)(2,1)}, u32[]{:S(2)}, u32[]{:S(2)}) async-start(bf16[16,512,128]{2,1,0:T(8,128)(2,1)} %bitcast.57), calls=%async_computation | async-start | bytes 4194304 | tf_op jit(solution)/shard_map/all_to_all | solution.py:1166
  17.5 1.0 collective-permute-start.1
  19.0 0.6 reshape.123
  20.0 1.5 collective-permute-done.2.refs_3_.refs_6_
  21.5 0.8 copy-done.6
  22.3 17.4 %feed.1 = (bf16[512,2048]{1,0:T(8,128)(2,1)}, bf16[512,2048]{1,0:T(8,128)(2,1)}, f32[1,2048]{1,0:T(1,128)}, f32[256,1024]{1,0:T(8,128)}, f32[256,1024]{1,0:T(8,128)}, /*index=5*/bf16[512,1024]{1,0:T(8,128)(2,1)}) custom-call(bf16[256,1024]{1,0:T(8,128)(2,1)} %get-tuple-element.73.refs_0_, bf16[256,1024]{1,0:T(8,128)(2,1)} %copy-done.14, ...), custom_call_target="tpu_custom_call" | custom-call | flops 536870912 | bytes 786432 | tf_op jit(solution)/shard_map/feed/pallas_call | solution.py:545
  40.3 0.6 pad_add_fusion
  40.9 6.3 %weight_parts.3 = (bf16[8,64,2048]{2,1,0:T(8,128)(2,1)}, bf16[8,64,2048]{2,1,0:T(8,128)(2,1)}) custom-call(s32[2]{0:T(128)} %get-tuple-element.146.me_ref.refs_0_.refs_14_, bf16[2048,256]{1,0:T(8,128)(2,1)} %get-tuple-element.72.refs_0_.refs_8_, bf16[2048,256]{1,0:T(8,128)(2,1)} %collective-permute-done.refs_1_.refs_9_, ...), custom_call_target="tpu_custom_call" | custom-call | flops 134217728 | bytes 458752 | tf_op jit(solution)/shard_map/weight_parts/pallas_call | solution.py:623
  47.2 1.6 collective-permute-start.6
  48.8 6.3 %weight_parts.2 = (bf16[8,64,2048]{2,1,0:T(8,128)(2,1)}, bf16[8,64,2048]{2,1,0:T(8,128)(2,1)}) custom-call(s32[2]{0:T(128)} %get-tuple-element.146.me_ref.refs_0_.refs_14_, bf16[2048,256]{1,0:T(8,128)(2,1)} %get-tuple-element.72.refs_0_.refs_8_, bf16[2048,256]{1,0:T(8,128)(2,1)} %collective-permute-done.refs_1_.refs_9_, ...), custom_call_target="tpu_custom_call" | custom-call | flops 134217728 | bytes 458752 | tf_op jit(solution)/shard_map/weight_parts/pallas_call | solution.py:623
  55.2 1.2 collective-permute-start.5
  56.3 2.6 all-to-all-done.refs_1_.x_ref
  58.9 26.8 %forward_head.1 = (bf16[16,256,128]{2,1,0:T(8,128)(2,1)}, bf16[4,1024,128]{2,1,0:T(8,128)(2,1)}, f32[4,1024,128]{2,1,0:T(8,128)}, bf16[20,1024,512]{2,1,0:T(8,128)(2,1)}, s32[1]{0:T(128)}) custom-call(s32[2]{0:T(128)} %get-tuple-element.147.refs_0_, bf16[16,512,128]{2,1,0:T(8,128)(2,1)} %all-to-all-done.refs_1_.x_ref, ...), custom_call_target="tpu_custom_call" | custom-call | flops 16106127360 | bytes 25165824 | tf_op jit(solution)/shard_map/forward_head/pallas_call | solution.py:417
  85.7 10.9 %all-to-all-start.2 = ((bf16[16,256,128]{2,1,0:T(8,128)(2,1)}), bf16[16,256,128]{2,1,0:T(8,128)(2,1)S(1)}, u32[]{:S(2)}, u32[]{:S(2)}) async-start(bf16[16,256,128]{2,1,0:T(8,128)(2,1)} %get-tuple-element.88), calls=%async_computation.2 | async-start | bytes 2097152 | tf_op jit(solution)/shard_map/all_to_all | solution.py:1215
  96.6 22.4 %backward_head.1 = (bf16[16,256,128]{2,1,0:T(8,128)(2,1)}, s32[1]{0:T(128)}) custom-call(s32[2]{0:T(128)} %get-tuple-element.146.me_ref.refs_0_.refs_14_, bf16[16,512,128]{2,1,0:T(8,128)(2,1)} %all-to-all-done.refs_1_.x_ref, bf16[4,1024,128]{2,1,0:T(8,128)(2,1)} %get-tuple-element.82.g_ref, f32[4,1024,128]{2,1,0:T(8,128)} %get-tuple-element.83.d_ref, ...), custom_call_target="tpu_custom_call" | custom-call | flops 16106127360 | bytes 25165824 | tf_op jit(solution)/shard_map/backward_head/pallas_call | solution.py:460
  119.1 6.4 %all-to-all-start.1 = ((bf16[16,256,128]{2,1,0:T(8,128)(2,1)}), bf16[16,256,128]{2,1,0:T(8,128)(2,1)}, u32[]{:S(2)}, u32[]{:S(2)}) async-start(bf16[16,256,128]{2,1,0:T(8,128)(2,1)} %get-tuple-element.86.refs_2_), calls=%async_computation.1 | async-start | bytes 2097152 | tf_op jit(solution)/shard_map/all_to_all | solution.py:1220
  125.6 3.7 %regroup_once.2 = (bf16[256,1024]{1,0:T(8,128)(2,1)}, bf16[256,1024]{1,0:T(8,128)(2,1)}, bf16[1536,256]{1,0:T(8,128)(2,1)}, bf16[1024,256]{1,0:T(8,128)(2,1)}, bf16[512,256]{1,0:T(8,128)(2,1)}) custom-call(s32[2]{0:T(128)} %get-tuple-element.146.me_ref.refs_0_.refs_14_, bf16[16,256,128]{2,1,0:T(8,128)(2,1)} %copy-done.5, ...), custom_call_target="tpu_custom_call" | custom-call | flops 32768 | bytes 98304 | tf_op jit(solution)/shard_map/regroup_once/pallas_call | solution.py:747
  129.2 2.5 collective-permute-start.7
  131.7 3.5 %add_parts.9 = bf16[4,64,2048]{2,1,0:T(8,128)(2,1)} custom-call(s32[2]{0:T(128)} %get-tuple-element.146.me_ref.refs_0_.refs_14_, bf16[8,64,2048]{2,1,0:T(8,128)(2,1)} %get-tuple-element.101.refs_1_, bf16[8,64,2048]{2,1,0:T(8,128)(2,1)} %copy-done.1, bf16[1536,256]{1,0:T(8,128)(2,1)} %get-tuple-element.90.refs_3_), custom_call_target="tpu_custom_call" | custom-call | flops 131072 | bytes 393216 | tf_op jit(solution)/shard_map/add_parts/pallas_call | solution.py:747
  135.2 1.6 collective-permute-start.9
  136.8 3.4 %add_parts.7 = bf16[4,64,2048]{2,1,0:T(8,128)(2,1)} custom-call(s32[2]{0:T(128)} %get-tuple-element.146.me_ref.refs_0_.refs_14_, bf16[8,64,2048]{2,1,0:T(8,128)(2,1)} %get-tuple-element.100.refs_1_, bf16[8,64,2048]{2,1,0:T(8,128)(2,1)} %collective-permute-done.5.refs_2_, bf16[1536,256]{1,0:T(8,128)(2,1)} %get-tuple-element.90.refs_3_), custom_call_target="tpu_custom_call" | custom-call | flops 131072 | bytes 393216 | tf_op jit(solution)/shard_map/add_parts/pallas_call | solution.py:747
  140.2 1.2 collective-permute-start.8
  141.4 0.9 copy-done.11
  142.3 4.2 %weight_once.3 = (bf16[8,64,512]{2,1,0:T(8,128)(2,1)}, bf16[8,64,512]{2,1,0:T(8,128)(2,1)}, bf16[8,64,512]{2,1,0:T(8,128)(2,1)}, bf16[8,64,512]{2,1,0:T(8,128)(2,1)}) custom-call(s32[2]{0:T(128)} %get-tuple-element.146.me_ref.refs_0_.refs_14_, bf16[1024,256]{1,0:T(8,128)(2,1)} %get-tuple-element.81.refs_10_.refs_0_, bf16[1024,256]{1,0:T(8,128)(2,1)} %copy-done.3, ...), custom_call_target="tpu_custom_call" | custom-call | flops 114688 | bytes 344064 | tf_op jit(solution)/shard_map/weight_once/pallas_call | solution.py:747
  146.5 1.2 all-to-all-done.1.refs_1_
  147.7 3.9 %regroup_once.3 = (bf16[256,1024]{1,0:T(8,128)(2,1)}, bf16[256,1024]{1,0:T(8,128)(2,1)}, bf16[256,1024]{1,0:T(8,128)(2,1)}, bf16[256,1024]{1,0:T(8,128)(2,1)}) custom-call(s32[2]{0:T(128)} %get-tuple-element.146.me_ref.refs_0_.refs_14_, bf16[16,256,128]{2,1,0:T(8,128)(2,1)} %all-to-all-done.1.refs_1_, f32[3,256,128]{2,1,0:T(8,128)} %get-tuple-element.87.refs_2_, ...), custom_call_target="tpu_custom_call" | custom-call | flops 38912 | bytes 116736 | tf_op jit(solution)/shard_map/regroup_once/pallas_call | solution.py:747
  151.7 3.2 %collective-permute-start.10 = (bf16[256,1024]{1,0:T(8,128)(2,1)}, bf16[256,1024]{1,0:T(8,128)(2,1)S(1)}, u32[]{:S(2)}, u32[]{:S(2)}) collective-permute-start(bf16[256,1024]{1,0:T(8,128)(2,1)} %get-tuple-element.103), channel_id=1, source_target_pairs={{0,1},{1,0},{2,3},{3,2},{4,5},{5,4},{6,7},{7,6},{8,9},{9,8},{10,11... | collective-permute-start | bytes 1572872 | tf_op jit(solution)/shard_map/ppermute | solution.py:1116
  154.9 1.7 collective-permute-done.10.refs_3_
  156.7 0.8 copy-done.7
  157.5 3.9 %weight_once.4 = (bf16[8,64,1024]{2,1,0:T(8,128)(2,1)}, bf16[8,64,1024]{2,1,0:T(8,128)(2,1)}) custom-call(s32[2]{0:T(128)} %get-tuple-element.146.me_ref.refs_0_.refs_14_, bf16[1024,256]{1,0:T(8,128)(2,1)} %get-tuple-element.81.refs_10_.refs_0_, bf16[1024,256]{1,0:T(8,128)(2,1)} %copy-done.3, bf16[256,1024]{1,0:T(8,128)(2,1)} %get-tuple-element.102.refs_2_, ...), custom_call_target="tpu_custom_call" | custom-call | flops 98304 | bytes 294912 | tf_op jit(solution)/shard_map/weight_once/pallas_call | solution.py:747
  161.4 1.7 collective-permute-start.13
  163.3 3.4 %add_parts.8.refs_3_ = bf16[4,64,2048]{2,1,0:T(8,128)(2,1)} custom-call(s32[2]{0:T(128)} %get-tuple-element.146.me_ref.refs_0_.refs_14_, bf16[8,64,2048]{2,1,0:T(8,128)(2,1)} %get-tuple-element.101.refs_1_, bf16[8,64,2048]{2,1,0:T(8,128)(2,1)} %copy-done.1, bf16[1536,256]{1,0:T(8,128)(2,1)} %get-tuple-element.90.refs_3_), custom_call_target="tpu_custom_call" | custom-call | flops 131072 | bytes 393216 | tf_op jit(solution)/shard_map/add_parts/pallas_call | solution.py:747
  166.8 3.4 %add_parts.6.refs_1_ = bf16[4,64,2048]{2,1,0:T(8,128)(2,1)} custom-call(s32[2]{0:T(128)} %get-tuple-element.146.me_ref.refs_0_.refs_14_, bf16[8,64,2048]{2,1,0:T(8,128)(2,1)} %get-tuple-element.100.refs_1_, bf16[8,64,2048]{2,1,0:T(8,128)(2,1)} %collective-permute-done.5.refs_2_, bf16[1536,256]{1,0:T(8,128)(2,1)} %get-tuple-element.90.refs_3_), custom_call_target="tpu_custom_call" | custom-call | flops 131072 | bytes 393216 | tf_op jit(solution)/shard_map/add_parts/pallas_call | solution.py:747
  170.2 1.0 copy-done.10
  171.2 3.9 %add_parts.10 = (bf16[2,64,4096]{2,1,0:T(8,128)(2,1)}, bf16[2,64,4096]{2,1,0:T(8,128)(2,1)}) custom-call(s32[2]{0:T(128)} %get-tuple-element.146.me_ref.refs_0_.refs_14_, bf16[4,64,2048]{2,1,0:T(8,128)(2,1)} %add_parts.6.refs_1_, bf16[4,64,2048]{2,1,0:T(8,128)(2,1)} %collective-permute-done.8.refs_2_, bf16[4,64,2048]{2,1,0:T(8,128)(2,1)} %add_parts.8.refs_3_, ...), custom_call_target="tpu_custom_call" | custom-call | flops 131072 | bytes 393216 | tf_op jit(solution)/shard_map/add_parts/pallas_call | solution.py:747
  175.1 2.2 collective-permute-start.11
  177.3 3.8 %weight_once.5 = (bf16[8,64,1024]{2,1,0:T(8,128)(2,1)}, bf16[8,64,1024]{2,1,0:T(8,128)(2,1)}) custom-call(s32[2]{0:T(128)} %get-tuple-element.146.me_ref.refs_0_.refs_14_, bf16[1024,256]{1,0:T(8,128)(2,1)} %get-tuple-element.81.refs_10_.refs_0_, bf16[1024,256]{1,0:T(8,128)(2,1)} %copy-done.3, bf16[256,1024]{1,0:T(8,128)(2,1)} %get-tuple-element.102.refs_2_, ...), custom_call_target="tpu_custom_call" | custom-call | flops 98304 | bytes 294912 | tf_op jit(solution)/shard_map/weight_once/pallas_call | solution.py:747
  181.2 10.3 %close_layer.1 = (bf16[256,1024]{1,0:T(8,128)(2,1)}, f32[256,1024]{1,0:T(8,128)}, f32[5,1024]{1,0:T(8,128)}, f32[3,1024]{1,0:T(4,128)}, s32[2]{0:T(128)}) custom-call(bf16[256,1024]{1,0:T(8,128)(2,1)} %bitcast.56, bf16[256,1024]{1,0:T(8,128)(2,1)} %bitcast.53, bf16[1024]{0:T(1024)(128)(2,1)} %refs_2_.1, bf16[1024]{0:T(1024)(128)(2,1)} %refs_3_.1, ...), custom_call_target="tpu_custom_call" | custom-call | flops 134217728 | bytes 917504 | tf_op jit(solution)/shard_map/close_layer/pallas_call | solution.py:1063
  193.5 2.6 %add_convert_fusion.1 = (bf16[2,2,1,64,1024]{4,3,1,0,2:T(8,128)(2,1)}, bf16[2,2,1,64,1024]{4,3,1,0,2:T(8,128)(2,1)}) fusion(bf16[2,2,2,64,1024]{4,3,2,1,0:T(8,128)(2,1)S(1)} %bitcast.61, s32[]{:T(128)S(6)} %select_n.48, bf16[2,2,2,64,1024]{4,3,2,1,0:T(8,128)(2,1)} %bitcast.63, s32[]{:T(128)S(6)} %select_n.46), kind=kLoop, calls=%fused_computation.2 | loop fusion | flops 2097152 | bytes 3145736 | tf_op jit(solution)/shard_map/convert_element_type | solution.py:843
  196.1 1.2 collective-permute-start.16
  197.3 1.4 add_convert_fusion.2
  199.3 1.0 collective-permute-done.11
  200.2 1.2 add_convert_fusion.3
  201.4 1.5 collective-permute-start.21
  204.0 1.9 collective-permute-start.14
  205.9 0.8 collective-permute-done.14
  206.8 1.9 collective-permute-done.16.refs_3_
  208.7 2.2 collective-permute-done.15.refs_1_
  210.9 0.8 copy-done.12
  211.7 2.7 %add_parts.11 = (bf16[1,64,2048]{2,1,0:T(8,128)(2,1)}, bf16[1,64,2048]{2,1,0:T(8,128)(2,1)}, bf16[1,64,2048]{2,1,0:T(8,128)(2,1)}, bf16[1,64,2048]{2,1,0:T(8,128)(2,1)}) custom-call(s32[2]{0:T(128)} %get-tuple-element.146.me_ref.refs_0_.refs_14_, bf16[4,64,1024]{2,1,0:T(8,128)(2,1)} %bitcast.59, bf16[4,64,1024]{2,1,0:T(8,128)(2,1)} %copy-done.12, ...), custom_call_target="tpu_custom_call" | custom-call | flops 65536 | bytes 196608 | tf_op jit(solution)/shard_map/add_parts/pallas_call | solution.py:747
  214.6 1.3 collective-permute-start.18
  215.9 2.0 collective-permute-start.19
  217.9 0.6 all_to_all.20
  218.5 3.7 %all-to-all-start.3 = ((f32[16,1,384]{2,1,0:T(1,128)}), f32[16,1,384]{2,1,0:T(1,128)S(1)}, u32[]{:S(2)}, u32[]{:S(2)}) async-start(f32[16,1,384]{2,1,0:T(1,128)} %all_to_all.20), calls=%async_computation.3 | async-start | bytes 49152 | tf_op jit(solution)/shard_map/all_to_all | solution.py:1334
  222.2 15.8 %collective-permute-done.21 = bf16[1,64,4096]{2,1,0:T(8,128)(2,1)S(1)} collective-permute-done((bf16[1,64,4096]{2,1,0:T(8,128)(2,1)S(1)}, bf16[1,64,4096]{2,1,0:T(8,128)(2,1)S(1)}, u32[]{:S(2)}, u32[]{:S(2)}) %collective-permute-start.21) | collective-permute-done | bytes 524320 | tf_op jit(solution)/shard_map/ppermute | solution.py:765
  238.1 1.2 add_bitcast_fusion
  239.3 1.0 slice_bitcast_fusion
  240.3 10.0 %all-to-all-done.3 = f32[16,1,384]{2,1,0:T(1,128)S(1)} async-done(((f32[16,1,384]{2,1,0:T(1,128)}), f32[16,1,384]{2,1,0:T(1,128)S(1)}, u32[]{:S(2)}, u32[]{:S(2)}) %all-to-all-start.3) | async-done | bytes 24608 | tf_op jit(solution)/shard_map/all_to_all | solution.py:1334
  250.4 0.6 copy-done.15
  251.2 2.1 last_sum.1
  253.3 1.8 collective-permute-start.20
  256.8 0.6 copy-done.18
  257.4 1.8 place.1
  (86 shorter events, 6.8 us)
Async XLA Ops:
  9.8 7.7 %copy-start.13 = (bf16[256,1024]{1,0:T(8,128)(2,1)S(1)}, bf16[256,1024]{1,0:T(8,128)(2,1)}, u32[]{:S(2)}) copy-start(bf16[256,1024]{1,0:T(8,128)(2,1)} %get-tuple-element.73.refs_0_) | copy-start | bytes 1572868
  9.8 8.7 %copy-start = (bf16[1,256,1024]{2,1,0:T(8,128)(2,1)S(1)}, bf16[1,256,1024]{2,1,0:T(8,128)(2,1)}, u32[]{:S(2)}) copy-start(bf16[1,256,1024]{2,1,0:T(8,128)(2,1)} %param.15) | copy-start | bytes 1572868
  9.8 8.8 %copy-start.4 = (bf16[2048,256]{1,0:T(8,128)(2,1)S(1)}, bf16[2048,256]{1,0:T(8,128)(2,1)}, u32[]{:S(2)}) copy-start(bf16[2048,256]{1,0:T(8,128)(2,1)} %get-tuple-element.72.refs_0_.refs_8_) | copy-start | bytes 3145732
  9.8 9.2 %copy-start.22 = (bf16[2048]{0:T(1024)(128)(2,1)S(1)}, bf16[2048]{0:T(1024)(128)(2,1)}, u32[]{:S(2)}) copy-start(bf16[2048]{0:T(1024)(128)(2,1)} %param.25) | copy-start | bytes 12292
  9.8 49.1 %all-to-all-start = ((bf16[16,512,128]{2,1,0:T(8,128)(2,1)}), bf16[16,512,128]{2,1,0:T(8,128)(2,1)}, u32[]{:S(2)}, u32[]{:S(2)}) async-start(bf16[16,512,128]{2,1,0:T(8,128)(2,1)} %bitcast.57), calls=%async_computation | async-start | bytes 4194304 | tf_op jit(solution)/shard_map/all_to_all | solution.py:1166
  17.5 2.6 collective-permute-start.1
  18.5 3.0 %collective-permute-start.2 = (bf16[256,1024]{1,0:T(8,128)(2,1)S(1)}, bf16[256,1024]{1,0:T(8,128)(2,1)S(1)}, u32[]{:S(2)}, u32[]{:S(2)}) collective-permute-start(bf16[256,1024]{1,0:T(8,128)(2,1)S(1)} %bitcast.54), channel_id=1, source_target_pairs={{0,1},{1,0},{2,3},{3,2},{4,5},{5,4},{6,7},{7,6},{8,9},{9,8},{10,11... | collective-permute-start | bytes 1572872 | tf_op jit(solution)/shard_map/ppermute | solution.py:1116
  18.6 22.3 %collective-permute-start = (bf16[2048,256]{1,0:T(8,128)(2,1)S(1)}, bf16[2048,256]{1,0:T(8,128)(2,1)}, u32[]{:S(2)}, u32[]{:S(2)}) collective-permute-start(bf16[2048,256]{1,0:T(8,128)(2,1)S(1)} %copy-done.4), channel_id=1, source_target_pairs={{0,1},{1,0},{2,3},{3,2},{4,5},{5,4},{6,7},{7,6},{8,9},{9,8},{10,11... | collective-permute-start | bytes 3145736 | tf_op jit(solution)/shard_map/ppermute | solution.py:1116
  20.0 1.5 copy-start.14
  21.5 0.8 copy-start.6
  22.3 17.8 %copy-start.2 = (bf16[1024,256]{1,0:T(8,128)(2,1)S(1)}, bf16[1024,256]{1,0:T(8,128)(2,1)}, u32[]{:S(2)}) copy-start(bf16[1024,256]{1,0:T(8,128)(2,1)} %get-tuple-element.81.refs_10_.refs_0_) | copy-start | bytes 1572868
  39.7 16.6 %collective-permute-start.3 = (bf16[512,1024]{1,0:T(8,128)(2,1)}, bf16[512,1024]{1,0:T(8,128)(2,1)}, u32[]{:S(2)}, u32[]{:S(2)}) collective-permute-start(bf16[512,1024]{1,0:T(8,128)(2,1)} %get-tuple-element.79), channel_id=1, source_target_pairs={{0,1},{1,0},{2,3},{3,2},{4,5},{5,4},{6,7},{7,6},{8,9},{9,8},{10,11... | collective-permute-start | bytes 3145736 | tf_op jit(solution)/shard_map/ppermute | solution.py:1116
  40.1 16.2 %collective-permute-start.4 = (bf16[1024,256]{1,0:T(8,128)(2,1)S(1)}, bf16[1024,256]{1,0:T(8,128)(2,1)S(1)}, u32[]{:S(2)}, u32[]{:S(2)}) collective-permute-start(bf16[1024,256]{1,0:T(8,128)(2,1)S(1)} %copy-done.2), channel_id=1, source_target_pairs={{0,1},{1,0},{2,3},{3,2},{4,5},{5,4},{6,7},{7,6},{8,9},{9,8},{10,11... | collective-permute-start | bytes 1572872 | tf_op jit(solution)/shard_map/ppermute | solution.py:1116
  47.2 71.8 %collective-permute-start.6 = (bf16[8,64,2048]{2,1,0:T(8,128)(2,1)}, bf16[8,64,2048]{2,1,0:T(8,128)(2,1)S(1)}, u32[]{:S(2)}, u32[]{:S(2)}) collective-permute-start(bf16[8,64,2048]{2,1,0:T(8,128)(2,1)} %get-tuple-element.77.refs_3_), channel_id=1, source_target_pairs={{0,4},{2,6},{4,0},{6,2},{8,12},{10,14},{12,8},{14,10},{16,20},{18,... | collective-permute-start | bytes 6291464 | tf_op jit(solution)/shard_map/ppermute | solution.py:765
  55.2 63.9 %collective-permute-start.5 = (bf16[8,64,2048]{2,1,0:T(8,128)(2,1)}, bf16[8,64,2048]{2,1,0:T(8,128)(2,1)}, u32[]{:S(2)}, u32[]{:S(2)}) collective-permute-start(bf16[8,64,2048]{2,1,0:T(8,128)(2,1)} %get-tuple-element.75.refs_2_), channel_id=1, source_target_pairs={{0,2},{2,0},{4,6},{6,4},{8,10},{10,8},{12,14},{14,12},{16,18},{18,... | collective-permute-start | bytes 6291464 | tf_op jit(solution)/shard_map/ppermute | solution.py:765
  56.3 2.6 copy-start.3
  85.7 33.4 %all-to-all-start.2 = ((bf16[16,256,128]{2,1,0:T(8,128)(2,1)}), bf16[16,256,128]{2,1,0:T(8,128)(2,1)S(1)}, u32[]{:S(2)}, u32[]{:S(2)}) async-start(bf16[16,256,128]{2,1,0:T(8,128)(2,1)} %get-tuple-element.88), calls=%async_computation.2 | async-start | bytes 2097152 | tf_op jit(solution)/shard_map/all_to_all | solution.py:1215
  119.1 10.1 %copy-start.1 = (bf16[8,64,2048]{2,1,0:T(8,128)(2,1)}, bf16[8,64,2048]{2,1,0:T(8,128)(2,1)S(1)}, u32[]{:S(2)}) copy-start(bf16[8,64,2048]{2,1,0:T(8,128)(2,1)S(1)} %collective-permute-done.6.refs_2_) | copy-start | bytes 6291460
  119.1 6.4 %copy-start.5 = (bf16[16,256,128]{2,1,0:T(8,128)(2,1)}, bf16[16,256,128]{2,1,0:T(8,128)(2,1)S(1)}, u32[]{:S(2)}) copy-start(bf16[16,256,128]{2,1,0:T(8,128)(2,1)S(1)} %all-to-all-done.2.refs_1_) | copy-start | bytes 3145732
  119.1 28.6 %all-to-all-start.1 = ((bf16[16,256,128]{2,1,0:T(8,128)(2,1)}), bf16[16,256,128]{2,1,0:T(8,128)(2,1)}, u32[]{:S(2)}, u32[]{:S(2)}) async-start(bf16[16,256,128]{2,1,0:T(8,128)(2,1)} %get-tuple-element.86.refs_2_), calls=%async_computation.1 | async-start | bytes 2097152 | tf_op jit(solution)/shard_map/all_to_all | solution.py:1220
  129.2 12.2 %collective-permute-start.7 = (bf16[1536,256]{1,0:T(8,128)(2,1)}, bf16[1536,256]{1,0:T(8,128)(2,1)S(1)}, u32[]{:S(2)}, u32[]{:S(2)}) collective-permute-start(bf16[1536,256]{1,0:T(8,128)(2,1)} %get-tuple-element.90.refs_3_), channel_id=1, source_target_pairs={{0,1},{1,0},{2,3},{3,2},{4,5},{5,4},{6,7},{7,6},{8,9},{9,8},{10,11... | collective-permute-start | bytes 2359304 | tf_op jit(solution)/shard_map/ppermute | solution.py:1116
  135.2 35.1 %collective-permute-start.9 = (bf16[4,64,2048]{2,1,0:T(8,128)(2,1)}, bf16[4,64,2048]{2,1,0:T(8,128)(2,1)S(1)}, u32[]{:S(2)}, u32[]{:S(2)}) collective-permute-start(bf16[4,64,2048]{2,1,0:T(8,128)(2,1)} %add_parts.9), channel_id=1, source_target_pairs={{0,2},{2,0},{4,6},{6,4},{8,10},{10,8},{12,14},{14,12},{16,18},{18,... | collective-permute-start | bytes 3145736 | tf_op jit(solution)/shard_map/ppermute | solution.py:765
  140.2 30.0 %collective-permute-start.8 = (bf16[4,64,2048]{2,1,0:T(8,128)(2,1)}, bf16[4,64,2048]{2,1,0:T(8,128)(2,1)}, u32[]{:S(2)}, u32[]{:S(2)}) collective-permute-start(bf16[4,64,2048]{2,1,0:T(8,128)(2,1)} %add_parts.7), channel_id=1, source_target_pairs={{0,4},{2,6},{4,0},{6,2},{8,12},{10,14},{12,8},{14,10},{16,20},{18,... | collective-permute-start | bytes 3145736 | tf_op jit(solution)/shard_map/ppermute | solution.py:765
  141.4 0.9 copy-start.11
  151.7 5.0 %collective-permute-start.10 = (bf16[256,1024]{1,0:T(8,128)(2,1)}, bf16[256,1024]{1,0:T(8,128)(2,1)S(1)}, u32[]{:S(2)}, u32[]{:S(2)}) collective-permute-start(bf16[256,1024]{1,0:T(8,128)(2,1)} %get-tuple-element.103), channel_id=1, source_target_pairs={{0,1},{1,0},{2,3},{3,2},{4,5},{5,4},{6,7},{7,6},{8,9},{9,8},{10,11... | collective-permute-start | bytes 1572872 | tf_op jit(solution)/shard_map/ppermute | solution.py:1116
  156.7 0.8 copy-start.7
  161.4 32.2 %collective-permute-start.13 = (bf16[8,64,1024]{2,1,0:T(8,128)(2,1)}, bf16[8,64,1024]{2,1,0:T(8,128)(2,1)S(1)}, u32[]{:S(2)}, u32[]{:S(2)}) collective-permute-start(bf16[8,64,1024]{2,1,0:T(8,128)(2,1)} %get-tuple-element.104.refs_5_), channel_id=1, source_target_pairs={{0,4},{2,6},{4,0},{6,2},{8,12},{10,14},{12,8},{14,10},{16,20},{18,... | collective-permute-start | bytes 3145736 | tf_op jit(solution)/shard_map/ppermute | solution.py:765
  163.1 34.3 %collective-permute-start.12 = (bf16[8,64,1024]{2,1,0:T(8,128)(2,1)}, bf16[8,64,1024]{2,1,0:T(8,128)(2,1)S(1)}, u32[]{:S(2)}, u32[]{:S(2)}) collective-permute-start(bf16[8,64,1024]{2,1,0:T(8,128)(2,1)} %get-tuple-element.114), channel_id=1, source_target_pairs={{0,2},{2,0},{4,6},{6,4},{8,10},{10,8},{12,14},{14,12},{16,18},{18,... | collective-permute-start | bytes 3145736 | tf_op jit(solution)/shard_map/ppermute | solution.py:765
  170.2 1.0 copy-start.10
  175.1 25.1 %collective-permute-start.11 = (bf16[2,64,4096]{2,1,0:T(8,128)(2,1)}, bf16[2,64,4096]{2,1,0:T(8,128)(2,1)}, u32[]{:S(2)}, u32[]{:S(2)}) collective-permute-start(bf16[2,64,4096]{2,1,0:T(8,128)(2,1)} %get-tuple-element.105.refs_19_), channel_id=1, source_target_pairs={{0,8},{2,10},{4,12},{6,14},{8,0},{10,2},{12,4},{14,6},{16,24},{18,... | collective-permute-start | bytes 3145736 | tf_op jit(solution)/shard_map/ppermute | solution.py:765
  191.5 5.9 %copy-start.8 = (bf16[8,64,1024]{2,1,0:T(8,128)(2,1)S(1)}, bf16[8,64,1024]{2,1,0:T(8,128)(2,1)}, u32[]{:S(2)}) copy-start(bf16[8,64,1024]{2,1,0:T(8,128)(2,1)} %get-tuple-element.113) | copy-start | bytes 3145732
  196.1 4.1 %copy-start.9 = (bf16[2,64,4096]{2,1,0:T(8,128)(2,1)S(1)}, bf16[2,64,4096]{2,1,0:T(8,128)(2,1)}, u32[]{:S(2)}) copy-start(bf16[2,64,4096]{2,1,0:T(8,128)(2,1)} %get-tuple-element.111) | copy-start | bytes 3145732
  196.1 12.5 %collective-permute-start.16 = (bf16[4,64,1024]{2,1,0:T(8,128)(2,1)}, bf16[4,64,1024]{2,1,0:T(8,128)(2,1)}, u32[]{:S(2)}, u32[]{:S(2)}) collective-permute-start(bf16[4,64,1024]{2,1,0:T(8,128)(2,1)} %bitcast.18), channel_id=1, source_target_pairs={{0,2},{2,0},{4,6},{6,4},{8,10},{10,8},{12,14},{14,12},{16,18},{18,... | collective-permute-start | bytes 1572872 | tf_op jit(solution)/shard_map/ppermute | solution.py:765
  197.3 5.6 %copy-start.21 = (f32[1,2048]{1,0:T(1,128)S(1)}, f32[1,2048]{1,0:T(1,128)}, u32[]{:S(2)}) copy-start(f32[1,2048]{1,0:T(1,128)} %get-tuple-element.110) | copy-start | bytes 24580
  197.3 5.8 %copy-start.20 = (f32[5,1024]{1,0:T(8,128)S(1)}, f32[5,1024]{1,0:T(8,128)}, u32[]{:S(2)}) copy-start(f32[5,1024]{1,0:T(8,128)} %get-tuple-element.108) | copy-start | bytes 61444
  197.3 6.3 %copy-start.19 = (f32[3,1024]{1,0:T(4,128)S(1)}, f32[3,1024]{1,0:T(4,128)}, u32[]{:S(2)}) copy-start(f32[3,1024]{1,0:T(4,128)} %get-tuple-element.109) | copy-start | bytes 36868
  198.7 12.1 %collective-permute-start.15 = (bf16[4,64,1024]{2,1,0:T(8,128)(2,1)}, bf16[4,64,1024]{2,1,0:T(8,128)(2,1)S(1)}, u32[]{:S(2)}, u32[]{:S(2)}) collective-permute-start(bf16[4,64,1024]{2,1,0:T(8,128)(2,1)} %bitcast.14), channel_id=1, source_target_pairs={{0,4},{2,6},{4,0},{6,2},{8,12},{10,14},{12,8},{14,10},{16,20},{18,... | collective-permute-start | bytes 1572872 | tf_op jit(solution)/shard_map/ppermute | solution.py:765
  201.4 36.7 %collective-permute-start.21 = (bf16[1,64,4096]{2,1,0:T(8,128)(2,1)S(1)}, bf16[1,64,4096]{2,1,0:T(8,128)(2,1)S(1)}, u32[]{:S(2)}, u32[]{:S(2)}) collective-permute-start(bf16[1,64,4096]{2,1,0:T(8,128)(2,1)S(1)} %add_convert_fusion.3), channel_id=1, source_target_pairs={{0,16},{2,18},{4,20},{6,22},{8,24},{10,26},{12,28},{14,30},{16,0},... | collective-permute-start | bytes 1572872 | tf_op jit(solution)/shard_map/ppermute | solution.py:765
  204.0 2.8 %collective-permute-start.14 = (f32[16,384]{1,0:T(8,128)S(1)}, f32[16,384]{1,0:T(8,128)S(1)}, u32[]{:S(2)}, u32[]{:S(2)}) collective-permute-start(f32[16,384]{1,0:T(8,128)S(1)} %bitcast.67), channel_id=1, source_target_pairs={{0,1},{1,0},{2,3},{3,2},{4,5},{5,4},{6,7},{7,6},{8,9},{9,8},{10,11... | collective-permute-start | bytes 73736 | tf_op jit(solution)/shard_map/ppermute | solution.py:1116
  210.9 0.8 copy-start.12
  214.3 36.0 %collective-permute-start.17 = (bf16[1,64,2048]{2,1,0:T(8,128)(2,1)}, bf16[1,64,2048]{2,1,0:T(8,128)(2,1)S(1)}, u32[]{:S(2)}, u32[]{:S(2)}) collective-permute-start(bf16[1,64,2048]{2,1,0:T(8,128)(2,1)} %get-tuple-element.118), channel_id=1, source_target_pairs={{0,8},{2,10},{4,12},{6,14},{8,0},{10,2},{12,4},{14,6},{16,24},{18,... | collective-permute-start | bytes 786440 | tf_op jit(solution)/shard_map/ppermute | solution.py:765
  214.6 35.7 %collective-permute-start.18 = (bf16[1,64,2048]{2,1,0:T(8,128)(2,1)}, bf16[1,64,2048]{2,1,0:T(8,128)(2,1)S(1)}, u32[]{:S(2)}, u32[]{:S(2)}) collective-permute-start(bf16[1,64,2048]{2,1,0:T(8,128)(2,1)} %get-tuple-element.119), channel_id=1, source_target_pairs={{0,16},{2,18},{4,20},{6,22},{8,24},{10,26},{12,28},{14,30},{16,0},... | collective-permute-start | bytes 786440 | tf_op jit(solution)/shard_map/ppermute | solution.py:765
  215.9 34.5 %collective-permute-start.19 = (bf16[1,64,2048]{2,1,0:T(8,128)(2,1)}, bf16[1,64,2048]{2,1,0:T(8,128)(2,1)S(1)}, u32[]{:S(2)}, u32[]{:S(2)}) collective-permute-start(bf16[1,64,2048]{2,1,0:T(8,128)(2,1)} %get-tuple-element.120), channel_id=1, source_target_pairs={{0,24},{2,26},{4,28},{6,30},{8,16},{10,18},{12,20},{14,22},{16,8},... | collective-permute-start | bytes 786440 | tf_op jit(solution)/shard_map/ppermute | solution.py:765
  218.5 31.8 %all-to-all-start.3 = ((f32[16,1,384]{2,1,0:T(1,128)}), f32[16,1,384]{2,1,0:T(1,128)S(1)}, u32[]{:S(2)}, u32[]{:S(2)}) async-start(f32[16,1,384]{2,1,0:T(1,128)} %all_to_all.20), calls=%async_computation.3 | async-start | bytes 49152 | tf_op jit(solution)/shard_map/all_to_all | solution.py:1334
  250.3 0.7 copy-start.15
  250.3 0.8 copy-start.16
  250.4 0.9 copy-start.17
  253.3 3.5 %collective-permute-start.20 = (bf16[32,2048]{1,0:T(8,128)(2,1)}, bf16[32,2048]{1,0:T(8,128)(2,1)S(1)}, u32[]{:S(2)}, u32[]{:S(2)}) collective-permute-start(bf16[32,2048]{1,0:T(8,128)(2,1)} %get-tuple-element.123), channel_id=1, source_target_pairs={{0,1},{1,0},{2,3},{3,2},{4,5},{5,4},{6,7},{7,6},{8,9},{9,8},{10,11... | collective-permute-start | bytes 393224 | tf_op jit(solution)/shard_map/ppermute | solution.py:1116
  256.8 3.0 %copy-start.23 = (f32[32]{0:T(128)}, f32[32]{0:T(128)S(1)}, u32[]{:S(2)}) copy-start(f32[32]{0:T(128)S(1)} %get-tuple-element.175) | copy-start | bytes 388
  256.8 0.6 copy-start.18

commit v6 on v4

--- a/solution.py
+++ b/solution.py
@@ -1319,9 +1319,9 @@
         packed = mine + pair_swap(after(other, *ring_out.sent))
     else:
         packed = lax.psum_scatter(packed, "mlp", scatter_dimension=1, tiled=False)
+    packed = after(packed, *ring_qv.sent, *ring_kd.sent)
+    packed = lax.all_to_all(packed, "seq", 0, 0, tiled=True)
     ring_qv.step(ring_kd)
-    packed = after(packed, *ring_qv.sent)
-    packed = lax.all_to_all(packed, "seq", 0, 0, tiled=True)
 
     feed_total = ring_out.plain_total()
     out_weight = jnp.transpose(feed_total[:, :slice_width])

time: 258 us -> 264 us (1.023); the launches traced: 257 us -> 260 us
  waiting for transfers between devices: 41.8 us -> 44.5 us
    all_to_all x1, waiting for transfers between devices: 11.4 us -> 17.5 us  [per_device(): packed = lax.all_to_all(packed, 'seq', 0, 0, tiled=True)]
    ppermute x13, waiting for transfers between devices: 23.2 us -> 19.8 us  [seq_move(): return lax.ppermute(x, 'seq', [(s, s ^ mask) for s in range(members)])]
    ppermute x9, starting transfers between devices: 11.2 us -> 14.3 us  [pair_swap(): return lax.ppermute(x, 'mlp', [(0, 1), (1, 0)])]
  transfers between devices with their start and end apart: 26 -> 26, of which waited for: 14 -> 13; matrix products, arithmetic and copies ran while one was open for 4% -> 4% of each run, Pallas kernels for 48% -> 47%
where the time goes in v6:
time: 264 us; the launch traced here: 260 us
  Pallas kernels  136 us (52%)
  starting transfers between devices  58 us (22%)
  waiting for transfers between devices  44.5 us (17%)
  local copies, waits for them, and re-layouts  11.2 us (4%)
  other arithmetic  7.65 us (3%)
  between operations  3 us (1%)
    pallas_call x11, Pallas kernels, vmem_call(): pl.pallas_call(without(kernel, 1 + len(arrays), len(behind)), in_specs=[p...  38 us
    pallas_call x1, Pallas kernels, forward_head(): pl.pallas_call(without(partial(forward_kernel, key_rows=key_rows, query_r...  26.9 us
    pallas_call x1, Pallas kernels, backward_head(): pl.pallas_call(without(partial(backward_kernel, key_rows=key_rows, query_...  22.4 us
    ppermute x13, waiting for transfers between devices, seq_move(): return lax.ppermute(x, 'seq', [(s, s ^ mask) for s in range(members)])  19.8 us
    all_to_all x1, waiting for transfers between devices, per_device(): packed = lax.all_to_all(packed, 'seq', 0, 0, tiled=True)  17.5 us
    pallas_call x1, Pallas kernels, feed(): pl.pallas_call(partial(feed_kernel, count=count, keep=keep), grid=(hidden...  17.3 us
    ppermute x13, starting transfers between devices, seq_move(): return lax.ppermute(x, 'seq', [(s, s ^ mask) for s in range(members)])  15.3 us
    ppermute x9, starting transfers between devices, pair_swap(): return lax.ppermute(x, 'mlp', [(0, 1), (1, 0)])  14.3 us
  transfers between devices with their start and end apart: 26, of which 13 were waited for; matrix products, arithmetic and copies ran while one was open for 4% of the time, Pallas kernels for 47%

profile of v6, /device:TPU:1, one launch (start us, length us, event | category | flops | bytes accessed | tf_op | source)
XLA Modules:
  0.0 260.4 jit_solution(15308326637698446579)
XLA Ops:
  0.7 0.6 reshape_tile.3.inv_ref
  1.3 8.5 %open_layer.1 = (bf16[16,1,512,128]{3,2,1,0:T(8,128)(2,1)}, bf16[256,1024]{1,0:T(8,128)(2,1)}, bf16[256,1024]{1,0:T(8,128)(2,1)}, f32[3,256,128]{2,1,0:T(8,128)}...) custom-call(s32[1]{0:T(128)S(6)} %mul.8.first_ref, bf16[256,1024]{1,0:T(8,128)(2,1)} %bitcast.55, ...), custom_call_target="tpu_custom_call" | custom-call | flops 134217728 | bytes 819200 | tf_op jit(solution)/shard_map/open_layer/pallas_call | solution.py:147
  9.8 7.6 %all-to-all-start = ((bf16[16,512,128]{2,1,0:T(8,128)(2,1)}), bf16[16,512,128]{2,1,0:T(8,128)(2,1)}, u32[]{:S(2)}, u32[]{:S(2)}) async-start(bf16[16,512,128]{2,1,0:T(8,128)(2,1)} %bitcast.57), calls=%async_computation | async-start | bytes 4194304 | tf_op jit(solution)/shard_map/all_to_all | solution.py:1156
  17.5 1.0 collective-permute-start.1
  19.0 0.6 reshape.123
  20.0 1.5 collective-permute-done.2.refs_3_.refs_6_
  21.6 0.8 copy-done.7
  22.3 17.3 %feed.1 = (bf16[512,2048]{1,0:T(8,128)(2,1)}, bf16[512,2048]{1,0:T(8,128)(2,1)}, f32[1,2048]{1,0:T(1,128)}, f32[256,1024]{1,0:T(8,128)}, f32[256,1024]{1,0:T(8,128)}, /*index=5*/bf16[512,1024]{1,0:T(8,128)(2,1)}) custom-call(bf16[256,1024]{1,0:T(8,128)(2,1)} %get-tuple-element.77.refs_0_, bf16[256,1024]{1,0:T(8,128)(2,1)} %copy-done.15, ...), custom_call_target="tpu_custom_call" | custom-call | flops 536870912 | bytes 786432 | tf_op jit(solution)/shard_map/feed/pallas_call | solution.py:545
  40.2 0.7 pad_add_fusion
  40.9 6.3 %weight_parts.3 = (bf16[8,64,2048]{2,1,0:T(8,128)(2,1)}, bf16[8,64,2048]{2,1,0:T(8,128)(2,1)}) custom-call(s32[2]{0:T(128)} %get-tuple-element.154.me_ref.refs_0_.refs_14_, bf16[2048,256]{1,0:T(8,128)(2,1)} %get-tuple-element.76.refs_0_.refs_8_, bf16[2048,256]{1,0:T(8,128)(2,1)} %collective-permute-done.refs_1_.refs_9_, ...), custom_call_target="tpu_custom_call" | custom-call | flops 134217728 | bytes 458752 | tf_op jit(solution)/shard_map/weight_parts/pallas_call | solution.py:623
  47.2 1.6 collective-permute-start.6
  48.8 6.3 %weight_parts.2 = (bf16[8,64,2048]{2,1,0:T(8,128)(2,1)}, bf16[8,64,2048]{2,1,0:T(8,128)(2,1)}) custom-call(s32[2]{0:T(128)} %get-tuple-element.154.me_ref.refs_0_.refs_14_, bf16[2048,256]{1,0:T(8,128)(2,1)} %get-tuple-element.76.refs_0_.refs_8_, bf16[2048,256]{1,0:T(8,128)(2,1)} %collective-permute-done.refs_1_.refs_9_, ...), custom_call_target="tpu_custom_call" | custom-call | flops 134217728 | bytes 458752 | tf_op jit(solution)/shard_map/weight_parts/pallas_call | solution.py:623
  55.1 1.2 collective-permute-start.5
  56.3 2.6 all-to-all-done.refs_1_.x_ref
  58.9 26.9 %forward_head.1 = (bf16[16,256,128]{2,1,0:T(8,128)(2,1)}, bf16[4,1024,128]{2,1,0:T(8,128)(2,1)}, f32[4,1024,128]{2,1,0:T(8,128)}, bf16[20,1024,512]{2,1,0:T(8,128)(2,1)}, s32[1]{0:T(128)}) custom-call(s32[2]{0:T(128)} %get-tuple-element.155.refs_0_, bf16[16,512,128]{2,1,0:T(8,128)(2,1)} %all-to-all-done.refs_1_.x_ref, ...), custom_call_target="tpu_custom_call" | custom-call | flops 16106127360 | bytes 25165824 | tf_op jit(solution)/shard_map/forward_head/pallas_call | solution.py:417
  85.9 10.9 %all-to-all-start.2 = ((bf16[16,256,128]{2,1,0:T(8,128)(2,1)}), bf16[16,256,128]{2,1,0:T(8,128)(2,1)S(1)}, u32[]{:S(2)}, u32[]{:S(2)}) async-start(bf16[16,256,128]{2,1,0:T(8,128)(2,1)} %get-tuple-element.92), calls=%async_computation.2 | async-start | bytes 2097152 | tf_op jit(solution)/shard_map/all_to_all | solution.py:1205
  96.8 22.4 %backward_head.1 = (bf16[16,256,128]{2,1,0:T(8,128)(2,1)}, s32[1]{0:T(128)}) custom-call(s32[2]{0:T(128)} %get-tuple-element.154.me_ref.refs_0_.refs_14_, bf16[16,512,128]{2,1,0:T(8,128)(2,1)} %all-to-all-done.refs_1_.x_ref, bf16[4,1024,128]{2,1,0:T(8,128)(2,1)} %get-tuple-element.86.g_ref, f32[4,1024,128]{2,1,0:T(8,128)} %get-tuple-element.87.d_ref, ...), custom_call_target="tpu_custom_call" | custom-call | flops 16106127360 | bytes 25165824 | tf_op jit(solution)/shard_map/backward_head/pallas_call | solution.py:460
  119.3 6.3 %all-to-all-start.1 = ((bf16[16,256,128]{2,1,0:T(8,128)(2,1)}), bf16[16,256,128]{2,1,0:T(8,128)(2,1)S(1)}, u32[]{:S(2)}, u32[]{:S(2)}) async-start(bf16[16,256,128]{2,1,0:T(8,128)(2,1)} %get-tuple-element.90.refs_2_), calls=%async_computation.1 | async-start | bytes 2097152 | tf_op jit(solution)/shard_map/all_to_all | solution.py:1210
  125.6 3.7 %regroup_once.2 = (bf16[256,1024]{1,0:T(8,128)(2,1)}, bf16[256,1024]{1,0:T(8,128)(2,1)}, bf16[1536,256]{1,0:T(8,128)(2,1)}, bf16[1024,256]{1,0:T(8,128)(2,1)}, bf16[512,256]{1,0:T(8,128)(2,1)}) custom-call(s32[2]{0:T(128)} %get-tuple-element.154.me_ref.refs_0_.refs_14_, bf16[16,256,128]{2,1,0:T(8,128)(2,1)} %copy-done.5, ...), custom_call_target="tpu_custom_call" | custom-call | flops 32768 | bytes 98304 | tf_op jit(solution)/shard_map/regroup_once/pallas_call | solution.py:747
  129.3 2.5 collective-permute-start.7
  131.7 3.9 %add_parts.5 = (bf16[4,64,2048]{2,1,0:T(8,128)(2,1)}, bf16[4,64,2048]{2,1,0:T(8,128)(2,1)}) custom-call(s32[2]{0:T(128)} %get-tuple-element.154.me_ref.refs_0_.refs_14_, bf16[8,64,2048]{2,1,0:T(8,128)(2,1)} %get-tuple-element.107.refs_1_, bf16[8,64,2048]{2,1,0:T(8,128)(2,1)} %collective-permute-done.6.refs_2_, bf16[1536,256]{1,0:T(8,128)(2,1)} %get-tuple-element.94.refs_3_), custom_call_target="tpu_custom_call" | custom-call | flops 131072 | bytes 393216 | tf_op jit(solution)/shard_map/add_parts/pallas_call | solution.py:747
  135.7 1.6 collective-permute-start.9
  137.3 4.0 %add_parts.4 = (bf16[4,64,2048]{2,1,0:T(8,128)(2,1)}, bf16[4,64,2048]{2,1,0:T(8,128)(2,1)}) custom-call(s32[2]{0:T(128)} %get-tuple-element.154.me_ref.refs_0_.refs_14_, bf16[8,64,2048]{2,1,0:T(8,128)(2,1)} %get-tuple-element.104.refs_1_, bf16[8,64,2048]{2,1,0:T(8,128)(2,1)} %collective-permute-done.5.refs_2_, bf16[1536,256]{1,0:T(8,128)(2,1)} %get-tuple-element.94.refs_3_), custom_call_target="tpu_custom_call" | custom-call | flops 131072 | bytes 393216 | tf_op jit(solution)/shard_map/add_parts/pallas_call | solution.py:747
  141.3 1.2 collective-permute-start.8
  142.5 0.9 copy-done.12
  143.4 4.2 %weight_once.3 = (bf16[8,64,512]{2,1,0:T(8,128)(2,1)}, bf16[8,64,512]{2,1,0:T(8,128)(2,1)}, bf16[8,64,512]{2,1,0:T(8,128)(2,1)}, bf16[8,64,512]{2,1,0:T(8,128)(2,1)}) custom-call(s32[2]{0:T(128)} %get-tuple-element.154.me_ref.refs_0_.refs_14_, bf16[1024,256]{1,0:T(8,128)(2,1)} %get-tuple-element.85.refs_10_.refs_0_, bf16[1024,256]{1,0:T(8,128)(2,1)} %copy-done.2, ...), custom_call_target="tpu_custom_call" | custom-call | flops 114688 | bytes 344064 | tf_op jit(solution)/shard_map/weight_once/pallas_call | solution.py:747
  147.7 1.0 copy-done.6
  148.7 4.0 %regroup_once.3 = (bf16[256,1024]{1,0:T(8,128)(2,1)}, bf16[256,1024]{1,0:T(8,128)(2,1)}, bf16[256,1024]{1,0:T(8,128)(2,1)}, bf16[256,1024]{1,0:T(8,128)(2,1)}) custom-call(s32[2]{0:T(128)} %get-tuple-element.154.me_ref.refs_0_.refs_14_, bf16[16,256,128]{2,1,0:T(8,128)(2,1)} %copy-done.6, f32[3,256,128]{2,1,0:T(8,128)} %get-tuple-element.91.refs_2_, ...), custom_call_target="tpu_custom_call" | custom-call | flops 38912 | bytes 116736 | tf_op jit(solution)/shard_map/regroup_once/pallas_call | solution.py:747
  152.7 3.2 %collective-permute-start.10 = (bf16[256,1024]{1,0:T(8,128)(2,1)}, bf16[256,1024]{1,0:T(8,128)(2,1)S(1)}, u32[]{:S(2)}, u32[]{:S(2)}) collective-permute-start(bf16[256,1024]{1,0:T(8,128)(2,1)} %get-tuple-element.111), channel_id=1, source_target_pairs={{0,1},{1,0},{2,3},{3,2},{4,5},{5,4},{6,7},{7,6},{8,9},{9,8},{10,11... | collective-permute-start | bytes 1572872 | tf_op jit(solution)/shard_map/ppermute | solution.py:1106
  155.9 1.7 collective-permute-done.10.refs_3_
  157.7 0.8 copy-done.8
  158.5 3.9 %weight_once.4 = (bf16[8,64,1024]{2,1,0:T(8,128)(2,1)}, bf16[8,64,1024]{2,1,0:T(8,128)(2,1)}) custom-call(s32[2]{0:T(128)} %get-tuple-element.154.me_ref.refs_0_.refs_14_, bf16[1024,256]{1,0:T(8,128)(2,1)} %get-tuple-element.85.refs_10_.refs_0_, bf16[1024,256]{1,0:T(8,128)(2,1)} %copy-done.2, bf16[256,1024]{1,0:T(8,128)(2,1)} %get-tuple-element.110.refs_2_, ...), custom_call_target="tpu_custom_call" | custom-call | flops 98304 | bytes 294912 | tf_op jit(solution)/shard_map/weight_once/pallas_call | solution.py:747
  162.4 1.7 collective-permute-start.13
  164.4 3.4 %collective-permute-done.9.refs_4_ = bf16[4,64,2048]{2,1,0:T(8,128)(2,1)S(1)} collective-permute-done((bf16[4,64,2048]{2,1,0:T(8,128)(2,1)}, bf16[4,64,2048]{2,1,0:T(8,128)(2,1)S(1)}, u32[]{:S(2)}, u32[]{:S(2)}) %collective-permute-start.9) | collective-permute-done | bytes 1048608 | tf_op jit(solution)/shard_map/ppermute | solution.py:765
  167.7 1.4 collective-permute-done.8.refs_2_
  169.1 3.9 %add_parts.6 = (bf16[2,64,4096]{2,1,0:T(8,128)(2,1)}, bf16[2,64,4096]{2,1,0:T(8,128)(2,1)}) custom-call(s32[2]{0:T(128)} %get-tuple-element.154.me_ref.refs_0_.refs_14_, bf16[4,64,2048]{2,1,0:T(8,128)(2,1)} %get-tuple-element.105.refs_1_, bf16[4,64,2048]{2,1,0:T(8,128)(2,1)} %collective-permute-done.8.refs_2_, ...), custom_call_target="tpu_custom_call" | custom-call | flops 131072 | bytes 393216 | tf_op jit(solution)/shard_map/add_parts/pallas_call | solution.py:747
  173.0 1.3 collective-permute-start.11
  174.5 3.8 %weight_once.5 = (bf16[8,64,1024]{2,1,0:T(8,128)(2,1)}, bf16[8,64,1024]{2,1,0:T(8,128)(2,1)}) custom-call(s32[2]{0:T(128)} %get-tuple-element.154.me_ref.refs_0_.refs_14_, bf16[1024,256]{1,0:T(8,128)(2,1)} %get-tuple-element.85.refs_10_.refs_0_, bf16[1024,256]{1,0:T(8,128)(2,1)} %copy-done.2, bf16[256,1024]{1,0:T(8,128)(2,1)} %get-tuple-element.110.refs_2_, ...), custom_call_target="tpu_custom_call" | custom-call | flops 98304 | bytes 294912 | tf_op jit(solution)/shard_map/weight_once/pallas_call | solution.py:747
  178.4 10.3 %close_layer.1 = (bf16[256,1024]{1,0:T(8,128)(2,1)}, f32[256,1024]{1,0:T(8,128)}, f32[5,1024]{1,0:T(8,128)}, f32[3,1024]{1,0:T(4,128)}, s32[2]{0:T(128)}) custom-call(bf16[256,1024]{1,0:T(8,128)(2,1)} %bitcast.56, bf16[256,1024]{1,0:T(8,128)(2,1)} %bitcast.53, bf16[1024]{0:T(1024)(128)(2,1)} %refs_2_.1, bf16[1024]{0:T(1024)(128)(2,1)} %refs_3_.1, ...), custom_call_target="tpu_custom_call" | custom-call | flops 134217728 | bytes 917504 | tf_op jit(solution)/shard_map/close_layer/pallas_call | solution.py:1053
  190.7 0.9 collective-permute-done.13
  191.6 2.6 add_convert_fusion.1
  194.3 1.4 add_convert_fusion.2
  195.7 0.7 collective-permute-start.15
  196.4 0.8 collective-permute-done.11
  197.2 1.2 add_convert_fusion.3
  198.4 2.1 collective-permute-start.21
  201.4 2.5 collective-permute-start.14
  203.8 0.8 collective-permute-done.14
  204.7 0.6 all_to_all.20
  205.3 3.5 %all-to-all-start.3 = ((f32[16,1,384]{2,1,0:T(1,128)}), f32[16,1,384]{2,1,0:T(1,128)S(1)}, u32[]{:S(2)}, u32[]{:S(2)}) async-start(f32[16,1,384]{2,1,0:T(1,128)} %all_to_all.20), calls=%async_computation.3 | async-start | bytes 49152 | tf_op jit(solution)/shard_map/all_to_all | solution.py:1323
  208.8 17.5 %all-to-all-done.3 = f32[16,1,384]{2,1,0:T(1,128)S(1)} async-done(((f32[16,1,384]{2,1,0:T(1,128)}), f32[16,1,384]{2,1,0:T(1,128)S(1)}, u32[]{:S(2)}, u32[]{:S(2)}) %all-to-all-start.3) | async-done | bytes 24608 | tf_op jit(solution)/shard_map/all_to_all | solution.py:1323
  226.3 0.8 copy-done.13
  227.1 2.7 %add_parts.7 = (bf16[1,64,2048]{2,1,0:T(8,128)(2,1)}, bf16[1,64,2048]{2,1,0:T(8,128)(2,1)}, bf16[1,64,2048]{2,1,0:T(8,128)(2,1)}, bf16[1,64,2048]{2,1,0:T(8,128)(2,1)}) custom-call(s32[2]{0:T(128)} %get-tuple-element.154.me_ref.refs_0_.refs_14_, bf16[4,64,1024]{2,1,0:T(8,128)(2,1)} %bitcast.59, bf16[4,64,1024]{2,1,0:T(8,128)(2,1)} %copy-done.13, ...), custom_call_target="tpu_custom_call" | custom-call | flops 65536 | bytes 196608 | tf_op jit(solution)/shard_map/add_parts/pallas_call | solution.py:747
  230.1 1.9 collective-permute-start.18
  232.0 1.3 collective-permute-start.19
  233.3 1.2 add_bitcast_fusion
  234.6 1.0 slice_bitcast_fusion
  235.6 6.0 %collective-permute-done.17.refs_1_ = bf16[1,64,2048]{2,1,0:T(8,128)(2,1)S(1)} collective-permute-done((bf16[1,64,2048]{2,1,0:T(8,128)(2,1)}, bf16[1,64,2048]{2,1,0:T(8,128)(2,1)S(1)}, u32[]{:S(2)}, u32[]{:S(2)}) %collective-permute-start.17) | collective-permute-done | bytes 262176 | tf_op jit(solution)/shard_map/ppermute | solution.py:765
  241.6 7.3 %collective-permute-done.19.refs_3_ = bf16[1,64,2048]{2,1,0:T(8,128)(2,1)S(1)} collective-permute-done((bf16[1,64,2048]{2,1,0:T(8,128)(2,1)}, bf16[1,64,2048]{2,1,0:T(8,128)(2,1)S(1)}, u32[]{:S(2)}, u32[]{:S(2)}) %collective-permute-start.19) | collective-permute-done | bytes 262176 | tf_op jit(solution)/shard_map/ppermute | solution.py:765
  248.9 0.7 copy-done.18
  249.6 2.1 last_sum.1
  251.7 4.1 %collective-permute-start.20 = (bf16[32,2048]{1,0:T(8,128)(2,1)}, bf16[32,2048]{1,0:T(8,128)(2,1)S(1)}, u32[]{:S(2)}, u32[]{:S(2)}) collective-permute-start(bf16[32,2048]{1,0:T(8,128)(2,1)} %get-tuple-element.131), channel_id=1, source_target_pairs={{0,1},{1,0},{2,3},{3,2},{4,5},{5,4},{6,7},{7,6},{8,9},{9,8},{10,11... | collective-permute-start | bytes 393224 | tf_op jit(solution)/shard_map/ppermute | solution.py:1106
  257.4 0.6 copy-done.19
  258.1 1.8 place.1
  (86 shorter events, 5.7 us)
Async XLA Ops:
  9.8 7.7 %copy-start.14 = (bf16[256,1024]{1,0:T(8,128)(2,1)S(1)}, bf16[256,1024]{1,0:T(8,128)(2,1)}, u32[]{:S(2)}) copy-start(bf16[256,1024]{1,0:T(8,128)(2,1)} %get-tuple-element.77.refs_0_) | copy-start | bytes 1572868
  9.8 8.7 %copy-start = (bf16[1,256,1024]{2,1,0:T(8,128)(2,1)S(1)}, bf16[1,256,1024]{2,1,0:T(8,128)(2,1)}, u32[]{:S(2)}) copy-start(bf16[1,256,1024]{2,1,0:T(8,128)(2,1)} %param.15) | copy-start | bytes 1572868
  9.8 8.8 %copy-start.4 = (bf16[2048,256]{1,0:T(8,128)(2,1)S(1)}, bf16[2048,256]{1,0:T(8,128)(2,1)}, u32[]{:S(2)}) copy-start(bf16[2048,256]{1,0:T(8,128)(2,1)} %get-tuple-element.76.refs_0_.refs_8_) | copy-start | bytes 3145732
  9.8 9.2 %copy-start.23 = (bf16[2048]{0:T(1024)(128)(2,1)S(1)}, bf16[2048]{0:T(1024)(128)(2,1)}, u32[]{:S(2)}) copy-start(bf16[2048]{0:T(1024)(128)(2,1)} %param.25) | copy-start | bytes 12292
  9.8 49.1 %all-to-all-start = ((bf16[16,512,128]{2,1,0:T(8,128)(2,1)}), bf16[16,512,128]{2,1,0:T(8,128)(2,1)}, u32[]{:S(2)}, u32[]{:S(2)}) async-start(bf16[16,512,128]{2,1,0:T(8,128)(2,1)} %bitcast.57), calls=%async_computation | async-start | bytes 4194304 | tf_op jit(solution)/shard_map/all_to_all | solution.py:1156
  17.5 2.6 collective-permute-start.1
  18.5 3.0 %collective-permute-start.2 = (bf16[256,1024]{1,0:T(8,128)(2,1)S(1)}, bf16[256,1024]{1,0:T(8,128)(2,1)S(1)}, u32[]{:S(2)}, u32[]{:S(2)}) collective-permute-start(bf16[256,1024]{1,0:T(8,128)(2,1)S(1)} %bitcast.54), channel_id=1, source_target_pairs={{0,1},{1,0},{2,3},{3,2},{4,5},{5,4},{6,7},{7,6},{8,9},{9,8},{10,11... | collective-permute-start | bytes 1572872 | tf_op jit(solution)/shard_map/ppermute | solution.py:1106
  18.6 22.3 %collective-permute-start = (bf16[2048,256]{1,0:T(8,128)(2,1)S(1)}, bf16[2048,256]{1,0:T(8,128)(2,1)}, u32[]{:S(2)}, u32[]{:S(2)}) collective-permute-start(bf16[2048,256]{1,0:T(8,128)(2,1)S(1)} %copy-done.4), channel_id=1, source_target_pairs={{0,1},{1,0},{2,3},{3,2},{4,5},{5,4},{6,7},{7,6},{8,9},{9,8},{10,11... | collective-permute-start | bytes 3145736 | tf_op jit(solution)/shard_map/ppermute | solution.py:1106
  20.0 1.5 copy-start.15
  21.5 0.8 copy-start.7
  22.3 17.7 %copy-start.1 = (bf16[1024,256]{1,0:T(8,128)(2,1)S(1)}, bf16[1024,256]{1,0:T(8,128)(2,1)}, u32[]{:S(2)}) copy-start(bf16[1024,256]{1,0:T(8,128)(2,1)} %get-tuple-element.85.refs_10_.refs_0_) | copy-start | bytes 1572868
  39.6 16.7 %collective-permute-start.3 = (bf16[512,1024]{1,0:T(8,128)(2,1)}, bf16[512,1024]{1,0:T(8,128)(2,1)S(1)}, u32[]{:S(2)}, u32[]{:S(2)}) collective-permute-start(bf16[512,1024]{1,0:T(8,128)(2,1)} %get-tuple-element.83), channel_id=1, source_target_pairs={{0,1},{1,0},{2,3},{3,2},{4,5},{5,4},{6,7},{7,6},{8,9},{9,8},{10,11... | collective-permute-start | bytes 3145736 | tf_op jit(solution)/shard_map/ppermute | solution.py:1106
  40.1 16.2 %collective-permute-start.4 = (bf16[1024,256]{1,0:T(8,128)(2,1)S(1)}, bf16[1024,256]{1,0:T(8,128)(2,1)S(1)}, u32[]{:S(2)}, u32[]{:S(2)}) collective-permute-start(bf16[1024,256]{1,0:T(8,128)(2,1)S(1)} %copy-done.1), channel_id=1, source_target_pairs={{0,1},{1,0},{2,3},{3,2},{4,5},{5,4},{6,7},{7,6},{8,9},{9,8},{10,11... | collective-permute-start | bytes 1572872 | tf_op jit(solution)/shard_map/ppermute | solution.py:1106
  47.2 72.0 %collective-permute-start.6 = (bf16[8,64,2048]{2,1,0:T(8,128)(2,1)}, bf16[8,64,2048]{2,1,0:T(8,128)(2,1)}, u32[]{:S(2)}, u32[]{:S(2)}) collective-permute-start(bf16[8,64,2048]{2,1,0:T(8,128)(2,1)} %get-tuple-element.81.refs_3_), channel_id=1, source_target_pairs={{0,4},{2,6},{4,0},{6,2},{8,12},{10,14},{12,8},{14,10},{16,20},{18,... | collective-permute-start | bytes 6291464 | tf_op jit(solution)/shard_map/ppermute | solution.py:765
  55.1 64.1 %collective-permute-start.5 = (bf16[8,64,2048]{2,1,0:T(8,128)(2,1)}, bf16[8,64,2048]{2,1,0:T(8,128)(2,1)}, u32[]{:S(2)}, u32[]{:S(2)}) collective-permute-start(bf16[8,64,2048]{2,1,0:T(8,128)(2,1)} %get-tuple-element.79.refs_2_), channel_id=1, source_target_pairs={{0,2},{2,0},{4,6},{6,4},{8,10},{10,8},{12,14},{14,12},{16,18},{18,... | collective-permute-start | bytes 6291464 | tf_op jit(solution)/shard_map/ppermute | solution.py:765
  56.3 2.6 %copy-start.2 = (bf16[1024,256]{1,0:T(8,128)(2,1)}, bf16[1024,256]{1,0:T(8,128)(2,1)S(1)}, u32[]{:S(2)}) copy-start(bf16[1024,256]{1,0:T(8,128)(2,1)S(1)} %collective-permute-done.4.refs_11_.refs_1_) | copy-start | bytes 1572868
  56.3 2.6 %copy-start.3 = (bf16[512,1024]{1,0:T(8,128)(2,1)}, bf16[512,1024]{1,0:T(8,128)(2,1)S(1)}, u32[]{:S(2)}) copy-start(bf16[512,1024]{1,0:T(8,128)(2,1)S(1)} %collective-permute-done.3.refs_5_.refs_7_.refs_16_.refs_18_) | copy-start | bytes 3145732
  85.9 33.4 %all-to-all-start.2 = ((bf16[16,256,128]{2,1,0:T(8,128)(2,1)}), bf16[16,256,128]{2,1,0:T(8,128)(2,1)S(1)}, u32[]{:S(2)}, u32[]{:S(2)}) async-start(bf16[16,256,128]{2,1,0:T(8,128)(2,1)} %get-tuple-element.92), calls=%async_computation.2 | async-start | bytes 2097152 | tf_op jit(solution)/shard_map/all_to_all | solution.py:1205
  119.2 6.4 %copy-start.5 = (bf16[16,256,128]{2,1,0:T(8,128)(2,1)}, bf16[16,256,128]{2,1,0:T(8,128)(2,1)S(1)}, u32[]{:S(2)}) copy-start(bf16[16,256,128]{2,1,0:T(8,128)(2,1)S(1)} %all-to-all-done.2.refs_1_) | copy-start | bytes 3145732
  119.3 28.5 %all-to-all-start.1 = ((bf16[16,256,128]{2,1,0:T(8,128)(2,1)}), bf16[16,256,128]{2,1,0:T(8,128)(2,1)S(1)}, u32[]{:S(2)}, u32[]{:S(2)}) async-start(bf16[16,256,128]{2,1,0:T(8,128)(2,1)} %get-tuple-element.90.refs_2_), calls=%async_computation.1 | async-start | bytes 2097152 | tf_op jit(solution)/shard_map/all_to_all | solution.py:1210
  129.3 13.2 %collective-permute-start.7 = (bf16[1536,256]{1,0:T(8,128)(2,1)}, bf16[1536,256]{1,0:T(8,128)(2,1)S(1)}, u32[]{:S(2)}, u32[]{:S(2)}) collective-permute-start(bf16[1536,256]{1,0:T(8,128)(2,1)} %get-tuple-element.94.refs_3_), channel_id=1, source_target_pairs={{0,1},{1,0},{2,3},{3,2},{4,5},{5,4},{6,7},{7,6},{8,9},{9,8},{10,11... | collective-permute-start | bytes 2359304 | tf_op jit(solution)/shard_map/ppermute | solution.py:1106
  135.7 32.0 %collective-permute-start.9 = (bf16[4,64,2048]{2,1,0:T(8,128)(2,1)}, bf16[4,64,2048]{2,1,0:T(8,128)(2,1)S(1)}, u32[]{:S(2)}, u32[]{:S(2)}) collective-permute-start(bf16[4,64,2048]{2,1,0:T(8,128)(2,1)} %get-tuple-element.109), channel_id=1, source_target_pairs={{0,2},{2,0},{4,6},{6,4},{8,10},{10,8},{12,14},{14,12},{16,18},{18,... | collective-permute-start | bytes 3145736 | tf_op jit(solution)/shard_map/ppermute | solution.py:765
  141.3 27.8 %collective-permute-start.8 = (bf16[4,64,2048]{2,1,0:T(8,128)(2,1)}, bf16[4,64,2048]{2,1,0:T(8,128)(2,1)}, u32[]{:S(2)}, u32[]{:S(2)}) collective-permute-start(bf16[4,64,2048]{2,1,0:T(8,128)(2,1)} %get-tuple-element.106), channel_id=1, source_target_pairs={{0,4},{2,6},{4,0},{6,2},{8,12},{10,14},{12,8},{14,10},{16,20},{18,... | collective-permute-start | bytes 3145736 | tf_op jit(solution)/shard_map/ppermute | solution.py:765
  142.5 0.9 copy-start.12
  147.7 1.0 copy-start.6
  152.7 5.0 %collective-permute-start.10 = (bf16[256,1024]{1,0:T(8,128)(2,1)}, bf16[256,1024]{1,0:T(8,128)(2,1)S(1)}, u32[]{:S(2)}, u32[]{:S(2)}) collective-permute-start(bf16[256,1024]{1,0:T(8,128)(2,1)} %get-tuple-element.111), channel_id=1, source_target_pairs={{0,1},{1,0},{2,3},{3,2},{4,5},{5,4},{6,7},{7,6},{8,9},{9,8},{10,11... | collective-permute-start | bytes 1572872 | tf_op jit(solution)/shard_map/ppermute | solution.py:1106
  157.7 0.8 copy-start.8
  162.4 29.2 %collective-permute-start.13 = (bf16[8,64,1024]{2,1,0:T(8,128)(2,1)}, bf16[8,64,1024]{2,1,0:T(8,128)(2,1)S(1)}, u32[]{:S(2)}, u32[]{:S(2)}) collective-permute-start(bf16[8,64,1024]{2,1,0:T(8,128)(2,1)} %get-tuple-element.112.refs_5_), channel_id=1, source_target_pairs={{0,4},{2,6},{4,0},{6,2},{8,12},{10,14},{12,8},{14,10},{16,20},{18,... | collective-permute-start | bytes 3145736 | tf_op jit(solution)/shard_map/ppermute | solution.py:765
  164.1 30.2 %collective-permute-start.12 = (bf16[8,64,1024]{2,1,0:T(8,128)(2,1)}, bf16[8,64,1024]{2,1,0:T(8,128)(2,1)S(1)}, u32[]{:S(2)}, u32[]{:S(2)}) collective-permute-start(bf16[8,64,1024]{2,1,0:T(8,128)(2,1)} %get-tuple-element.122), channel_id=1, source_target_pairs={{0,2},{2,0},{4,6},{6,4},{8,10},{10,8},{12,14},{14,12},{16,18},{18,... | collective-permute-start | bytes 3145736 | tf_op jit(solution)/shard_map/ppermute | solution.py:765
  167.7 1.4 copy-start.11
  169.1 5.2 %copy-start.22 = (f32[1,2048]{1,0:T(1,128)S(1)}, f32[1,2048]{1,0:T(1,128)}, u32[]{:S(2)}) copy-start(f32[1,2048]{1,0:T(1,128)} %get-tuple-element.118) | copy-start | bytes 24580
  173.0 24.2 %collective-permute-start.11 = (bf16[2,64,4096]{2,1,0:T(8,128)(2,1)}, bf16[2,64,4096]{2,1,0:T(8,128)(2,1)}, u32[]{:S(2)}, u32[]{:S(2)}) collective-permute-start(bf16[2,64,4096]{2,1,0:T(8,128)(2,1)} %get-tuple-element.113.refs_19_), channel_id=1, source_target_pairs={{0,8},{2,10},{4,12},{6,14},{8,0},{10,2},{12,4},{14,6},{16,24},{18,... | collective-permute-start | bytes 3145736 | tf_op jit(solution)/shard_map/ppermute | solution.py:765
  188.7 5.6 %copy-start.9 = (bf16[8,64,1024]{2,1,0:T(8,128)(2,1)S(1)}, bf16[8,64,1024]{2,1,0:T(8,128)(2,1)}, u32[]{:S(2)}) copy-start(bf16[8,64,1024]{2,1,0:T(8,128)(2,1)} %get-tuple-element.121) | copy-start | bytes 3145732
  194.2 3.1 %copy-start.10 = (bf16[2,64,4096]{2,1,0:T(8,128)(2,1)S(1)}, bf16[2,64,4096]{2,1,0:T(8,128)(2,1)}, u32[]{:S(2)}) copy-start(bf16[2,64,4096]{2,1,0:T(8,128)(2,1)} %get-tuple-element.119) | copy-start | bytes 3145732
  194.2 32.1 %collective-permute-start.16 = (bf16[4,64,1024]{2,1,0:T(8,128)(2,1)}, bf16[4,64,1024]{2,1,0:T(8,128)(2,1)}, u32[]{:S(2)}, u32[]{:S(2)}) collective-permute-start(bf16[4,64,1024]{2,1,0:T(8,128)(2,1)} %bitcast.18), channel_id=1, source_target_pairs={{0,2},{2,0},{4,6},{6,4},{8,10},{10,8},{12,14},{14,12},{16,18},{18,... | collective-permute-start | bytes 1572872 | tf_op jit(solution)/shard_map/ppermute | solution.py:765
  194.3 6.3 %copy-start.21 = (f32[5,1024]{1,0:T(8,128)S(1)}, f32[5,1024]{1,0:T(8,128)}, u32[]{:S(2)}) copy-start(f32[5,1024]{1,0:T(8,128)} %get-tuple-element.116) | copy-start | bytes 61444
  194.3 6.7 %copy-start.20 = (f32[3,1024]{1,0:T(4,128)S(1)}, f32[3,1024]{1,0:T(4,128)}, u32[]{:S(2)}) copy-start(f32[3,1024]{1,0:T(4,128)} %get-tuple-element.117) | copy-start | bytes 36868
  195.7 30.6 %collective-permute-start.15 = (bf16[4,64,1024]{2,1,0:T(8,128)(2,1)}, bf16[4,64,1024]{2,1,0:T(8,128)(2,1)S(1)}, u32[]{:S(2)}, u32[]{:S(2)}) collective-permute-start(bf16[4,64,1024]{2,1,0:T(8,128)(2,1)} %bitcast.14), channel_id=1, source_target_pairs={{0,4},{2,6},{4,0},{6,2},{8,12},{10,14},{12,8},{14,10},{16,20},{18,... | collective-permute-start | bytes 1572872 | tf_op jit(solution)/shard_map/ppermute | solution.py:765
  198.4 34.9 %collective-permute-start.21 = (bf16[1,64,4096]{2,1,0:T(8,128)(2,1)S(1)}, bf16[1,64,4096]{2,1,0:T(8,128)(2,1)S(1)}, u32[]{:S(2)}, u32[]{:S(2)}) collective-permute-start(bf16[1,64,4096]{2,1,0:T(8,128)(2,1)S(1)} %add_convert_fusion.3), channel_id=1, source_target_pairs={{0,16},{2,18},{4,20},{6,22},{8,24},{10,26},{12,28},{14,30},{16,0},... | collective-permute-start | bytes 1572872 | tf_op jit(solution)/shard_map/ppermute | solution.py:765
  201.4 3.3 %collective-permute-start.14 = (f32[16,384]{1,0:T(8,128)S(1)}, f32[16,384]{1,0:T(8,128)S(1)}, u32[]{:S(2)}, u32[]{:S(2)}) collective-permute-start(f32[16,384]{1,0:T(8,128)S(1)} %bitcast.67), channel_id=1, source_target_pairs={{0,1},{1,0},{2,3},{3,2},{4,5},{5,4},{6,7},{7,6},{8,9},{9,8},{10,11... | collective-permute-start | bytes 73736 | tf_op jit(solution)/shard_map/ppermute | solution.py:1106
  205.3 21.0 %all-to-all-start.3 = ((f32[16,1,384]{2,1,0:T(1,128)}), f32[16,1,384]{2,1,0:T(1,128)S(1)}, u32[]{:S(2)}, u32[]{:S(2)}) async-start(f32[16,1,384]{2,1,0:T(1,128)} %all_to_all.20), calls=%async_computation.3 | async-start | bytes 49152 | tf_op jit(solution)/shard_map/all_to_all | solution.py:1323
  226.3 0.8 copy-start.13
  229.8 11.8 %collective-permute-start.17 = (bf16[1,64,2048]{2,1,0:T(8,128)(2,1)}, bf16[1,64,2048]{2,1,0:T(8,128)(2,1)S(1)}, u32[]{:S(2)}, u32[]{:S(2)}) collective-permute-start(bf16[1,64,2048]{2,1,0:T(8,128)(2,1)} %get-tuple-element.128), channel_id=1, source_target_pairs={{0,8},{2,10},{4,12},{6,14},{8,0},{10,2},{12,4},{14,6},{16,24},{18,... | collective-permute-start | bytes 786440 | tf_op jit(solution)/shard_map/ppermute | solution.py:765
  230.1 11.4 %collective-permute-start.18 = (bf16[1,64,2048]{2,1,0:T(8,128)(2,1)}, bf16[1,64,2048]{2,1,0:T(8,128)(2,1)S(1)}, u32[]{:S(2)}, u32[]{:S(2)}) collective-permute-start(bf16[1,64,2048]{2,1,0:T(8,128)(2,1)} %get-tuple-element.129), channel_id=1, source_target_pairs={{0,16},{2,18},{4,20},{6,22},{8,24},{10,26},{12,28},{14,30},{16,0},... | collective-permute-start | bytes 786440 | tf_op jit(solution)/shard_map/ppermute | solution.py:765
  232.0 16.9 %collective-permute-start.19 = (bf16[1,64,2048]{2,1,0:T(8,128)(2,1)}, bf16[1,64,2048]{2,1,0:T(8,128)(2,1)S(1)}, u32[]{:S(2)}, u32[]{:S(2)}) collective-permute-start(bf16[1,64,2048]{2,1,0:T(8,128)(2,1)} %get-tuple-element.130), channel_id=1, source_target_pairs={{0,24},{2,26},{4,28},{6,30},{8,16},{10,18},{12,20},{14,22},{16,8},... | collective-permute-start | bytes 786440 | tf_op jit(solution)/shard_map/ppermute | solution.py:765
  241.6 7.3 %copy-start.16 = (bf16[1,64,2048]{2,1,0:T(8,128)(2,1)}, bf16[1,64,2048]{2,1,0:T(8,128)(2,1)S(1)}, u32[]{:S(2)}) copy-start(bf16[1,64,2048]{2,1,0:T(8,128)(2,1)S(1)} %collective-permute-done.17.refs_1_) | copy-start | bytes 786436
  241.6 7.3 %copy-start.17 = (bf16[1,64,2048]{2,1,0:T(8,128)(2,1)}, bf16[1,64,2048]{2,1,0:T(8,128)(2,1)S(1)}, u32[]{:S(2)}) copy-start(bf16[1,64,2048]{2,1,0:T(8,128)(2,1)S(1)} %collective-permute-done.18.refs_2_) | copy-start | bytes 786436
  248.9 0.7 copy-start.18
  251.7 5.8 %collective-permute-start.20 = (bf16[32,2048]{1,0:T(8,128)(2,1)}, bf16[32,2048]{1,0:T(8,128)(2,1)S(1)}, u32[]{:S(2)}, u32[]{:S(2)}) collective-permute-start(bf16[32,2048]{1,0:T(8,128)(2,1)} %get-tuple-element.131), channel_id=1, source_target_pairs={{0,1},{1,0},{2,3},{3,2},{4,5},{5,4},{6,7},{7,6},{8,9},{9,8},{10,11... | collective-permute-start | bytes 393224 | tf_op jit(solution)/shard_map/ppermute | solution.py:1106
  257.4 3.0 %copy-start.24 = (f32[32]{0:T(128)}, f32[32]{0:T(128)S(1)}, u32[]{:S(2)}) copy-start(f32[32]{0:T(128)S(1)} %get-tuple-element.183) | copy-start | bytes 388
  257.4 0.6 copy-start.19

commit v7 on v3

--- a/solution.py
+++ b/solution.py
@@ -250,17 +250,17 @@
         kv = key_value(j)
         grads = None
         for cut in cuts:
+            old = s_ref[j, cut]
+            if query is not None:
+                s = dot32(query[cut], kv, NT)
             if grad_t is not None:
                 part = dot32(grad_t[:, cut], p_ref[j, cut])
                 grads = part if grads is None else grads + part
             top = top_ref[cut]
-            p = jnp.concatenate(
-                [jnp.exp(c - top) for c in column_chunks(s_ref[j, cut])], 1
-            ).astype(BF16)
+            p = jnp.concatenate([jnp.exp(c - top) for c in column_chunks(old)], 1).astype(BF16)
             p_ref[j, cut] = p
             acc_ref[:, cut] += dot32(vt_ref[j], p, NT)
             if query is not None:
-                s = dot32(query[cut], kv, NT)
                 s_ref[j, cut] = s
                 raise_max(cut, s)
         if grads is not None:

time: 258 us -> 258 us (level)
  no operation moved by 1% of the time
where the time goes in v7:
time: 258 us; the launch traced here: 257 us
  Pallas kernels  133 us (52%)
  starting transfers between devices  57.1 us (22%)
  waiting for transfers between devices  43.6 us (17%)
  local copies, waits for them, and re-layouts  12.3 us (5%)
  other arithmetic  7.68 us (3%)
  between operations  3.02 us (1%)
    pallas_call x10, Pallas kernels, vmem_call(): pl.pallas_call(without(kernel, 1 + len(arrays), len(behind)), in_specs=[p...  35.6 us
    pallas_call x1, Pallas kernels, forward_head(): pl.pallas_call(without(partial(forward_kernel, key_rows=key_rows, query_r...  26.5 us
    ppermute x13, waiting for transfers between devices, seq_move(): return lax.ppermute(x, 'seq', [(s, s ^ mask) for s in range(members)])  26 us
    pallas_call x1, Pallas kernels, backward_head(): pl.pallas_call(without(partial(backward_kernel, key_rows=key_rows, query_...  22.4 us
    pallas_call x1, Pallas kernels, feed(): pl.pallas_call(partial(feed_kernel, count=count, keep=keep), grid=(hidden...  17.3 us
    ppermute x13, starting transfers between devices, seq_move(): return lax.ppermute(x, 'seq', [(s, s ^ mask) for s in range(members)])  14.1 us
    pallas_call x2, Pallas kernels, weight_parts(): pl.pallas_call(partial(weight_kernel, bits=bits, counts=[len(a) for a, _...  12.7 us
    ppermute x9, starting transfers between devices, pair_swap(): return lax.ppermute(x, 'mlp', [(0, 1), (1, 0)])  12.1 us
  transfers between devices with their start and end apart: 26, of which 14 were waited for; matrix products, arithmetic and copies ran while one was open for 4% of the time, Pallas kernels for 47%

profile of v7, /device:TPU:1, one launch (start us, length us, event | category | flops | bytes accessed | tf_op | source)
XLA Modules:
  0.0 257.0 jit_solution(1575584016859180412)
XLA Ops:
  1.3 8.5 %open_layer.1 = (bf16[16,1,512,128]{3,2,1,0:T(8,128)(2,1)}, bf16[256,1024]{1,0:T(8,128)(2,1)}, bf16[256,1024]{1,0:T(8,128)(2,1)}, f32[3,256,128]{2,1,0:T(8,128)}...) custom-call(s32[1]{0:T(128)S(6)} %mul.8.first_ref, bf16[256,1024]{1,0:T(8,128)(2,1)} %bitcast.55, ...), custom_call_target="tpu_custom_call" | custom-call | flops 134217728 | bytes 819200 | tf_op jit(solution)/shard_map/open_layer/pallas_call | solution.py:147
  9.8 7.6 %all-to-all-start = ((bf16[16,512,128]{2,1,0:T(8,128)(2,1)}), bf16[16,512,128]{2,1,0:T(8,128)(2,1)}, u32[]{:S(2)}, u32[]{:S(2)}) async-start(bf16[16,512,128]{2,1,0:T(8,128)(2,1)} %bitcast.57), calls=%async_computation | async-start | bytes 4194304 | tf_op jit(solution)/shard_map/all_to_all | solution.py:1158
  17.5 1.0 collective-permute-start.1
  19.0 0.6 reshape.123
  19.6 0.6 collective-permute-done.1.refs_1_
  21.6 17.3 %feed.1 = (bf16[512,2048]{1,0:T(8,128)(2,1)}, bf16[512,2048]{1,0:T(8,128)(2,1)}, f32[1,2048]{1,0:T(1,128)}, f32[256,1024]{1,0:T(8,128)}, f32[256,1024]{1,0:T(8,128)}, /*index=5*/bf16[512,1024]{1,0:T(8,128)(2,1)}) custom-call(bf16[256,1024]{1,0:T(8,128)(2,1)} %get-tuple-element.77.refs_0_, bf16[256,1024]{1,0:T(8,128)(2,1)} %copy-done.13, ...), custom_call_target="tpu_custom_call" | custom-call | flops 536870912 | bytes 786432 | tf_op jit(solution)/shard_map/feed/pallas_call | solution.py:545
  39.4 0.7 pad_add_fusion
  40.1 1.0 copy-done.3
  41.0 6.3 %weight_parts.3 = (bf16[8,64,2048]{2,1,0:T(8,128)(2,1)}, bf16[8,64,2048]{2,1,0:T(8,128)(2,1)}) custom-call(s32[2]{0:T(128)} %get-tuple-element.154.me_ref.refs_0_.refs_14_, bf16[2048,256]{1,0:T(8,128)(2,1)} %get-tuple-element.76.refs_0_.refs_8_, bf16[2048,256]{1,0:T(8,128)(2,1)} %copy-done.3, bf16[512,2048]{1,0:T(8,128)(2,1)} %get-tuple-element.80.refs_2_.refs_3_, ...), custom_call_target="tpu_custom_call" | custom-call | flops 134217728 | bytes 458752 | tf_op jit(solution)/shard_map/weight_parts/pallas_call | solution.py:623
  47.4 1.6 collective-permute-start.6
  49.0 6.3 %weight_parts.2 = (bf16[8,64,2048]{2,1,0:T(8,128)(2,1)}, bf16[8,64,2048]{2,1,0:T(8,128)(2,1)}) custom-call(s32[2]{0:T(128)} %get-tuple-element.154.me_ref.refs_0_.refs_14_, bf16[2048,256]{1,0:T(8,128)(2,1)} %get-tuple-element.76.refs_0_.refs_8_, bf16[2048,256]{1,0:T(8,128)(2,1)} %copy-done.3, bf16[512,2048]{1,0:T(8,128)(2,1)} %get-tuple-element.78.refs_2_.refs_3_, ...), custom_call_target="tpu_custom_call" | custom-call | flops 134217728 | bytes 458752 | tf_op jit(solution)/shard_map/weight_parts/pallas_call | solution.py:623
  55.3 1.2 collective-permute-start.5
  56.5 2.4 all-to-all-done.refs_1_.x_ref
  58.9 26.5 %forward_head.1 = (bf16[16,256,128]{2,1,0:T(8,128)(2,1)}, bf16[4,1024,128]{2,1,0:T(8,128)(2,1)}, f32[4,1024,128]{2,1,0:T(8,128)}, bf16[20,1024,512]{2,1,0:T(8,128)(2,1)}, s32[1]{0:T(128)}) custom-call(s32[2]{0:T(128)} %get-tuple-element.155.refs_0_, bf16[16,512,128]{2,1,0:T(8,128)(2,1)} %all-to-all-done.refs_1_.x_ref, ...), custom_call_target="tpu_custom_call" | custom-call | flops 16106127360 | bytes 25165824 | tf_op jit(solution)/shard_map/forward_head/pallas_call | solution.py:417
  85.4 10.9 %all-to-all-start.2 = ((bf16[16,256,128]{2,1,0:T(8,128)(2,1)}), bf16[16,256,128]{2,1,0:T(8,128)(2,1)S(1)}, u32[]{:S(2)}, u32[]{:S(2)}) async-start(bf16[16,256,128]{2,1,0:T(8,128)(2,1)} %get-tuple-element.92), calls=%async_computation.2 | async-start | bytes 2097152 | tf_op jit(solution)/shard_map/all_to_all | solution.py:1207
  96.3 22.4 %backward_head.1 = (bf16[16,256,128]{2,1,0:T(8,128)(2,1)}, s32[1]{0:T(128)}) custom-call(s32[2]{0:T(128)} %get-tuple-element.154.me_ref.refs_0_.refs_14_, bf16[16,512,128]{2,1,0:T(8,128)(2,1)} %all-to-all-done.refs_1_.x_ref, bf16[4,1024,128]{2,1,0:T(8,128)(2,1)} %get-tuple-element.86.g_ref, f32[4,1024,128]{2,1,0:T(8,128)} %get-tuple-element.87.d_ref, ...), custom_call_target="tpu_custom_call" | custom-call | flops 16106127360 | bytes 25165824 | tf_op jit(solution)/shard_map/backward_head/pallas_call | solution.py:460
  118.8 6.4 %all-to-all-start.1 = ((bf16[16,256,128]{2,1,0:T(8,128)(2,1)}), bf16[16,256,128]{2,1,0:T(8,128)(2,1)S(1)}, u32[]{:S(2)}, u32[]{:S(2)}) async-start(bf16[16,256,128]{2,1,0:T(8,128)(2,1)} %get-tuple-element.90.refs_2_), calls=%async_computation.1 | async-start | bytes 2097152 | tf_op jit(solution)/shard_map/all_to_all | solution.py:1212
  125.1 3.7 %regroup_once.2 = (bf16[256,1024]{1,0:T(8,128)(2,1)}, bf16[256,1024]{1,0:T(8,128)(2,1)}, bf16[1536,256]{1,0:T(8,128)(2,1)}, bf16[1024,256]{1,0:T(8,128)(2,1)}, bf16[512,256]{1,0:T(8,128)(2,1)}) custom-call(s32[2]{0:T(128)} %get-tuple-element.154.me_ref.refs_0_.refs_14_, bf16[16,256,128]{2,1,0:T(8,128)(2,1)} %copy-done.4, ...), custom_call_target="tpu_custom_call" | custom-call | flops 32768 | bytes 98304 | tf_op jit(solution)/shard_map/regroup_once/pallas_call | solution.py:749
  128.8 2.5 collective-permute-start.7
  131.3 3.9 %add_parts.5 = (bf16[4,64,2048]{2,1,0:T(8,128)(2,1)}, bf16[4,64,2048]{2,1,0:T(8,128)(2,1)}) custom-call(s32[2]{0:T(128)} %get-tuple-element.154.me_ref.refs_0_.refs_14_, bf16[8,64,2048]{2,1,0:T(8,128)(2,1)} %get-tuple-element.107.refs_1_, bf16[8,64,2048]{2,1,0:T(8,128)(2,1)} %collective-permute-done.6.refs_2_, bf16[1536,256]{1,0:T(8,128)(2,1)} %get-tuple-element.94.refs_3_), custom_call_target="tpu_custom_call" | custom-call | flops 131072 | bytes 393216 | tf_op jit(solution)/shard_map/add_parts/pallas_call | solution.py:749
  135.2 1.6 collective-permute-start.9
  136.8 4.0 %add_parts.4 = (bf16[4,64,2048]{2,1,0:T(8,128)(2,1)}, bf16[4,64,2048]{2,1,0:T(8,128)(2,1)}) custom-call(s32[2]{0:T(128)} %get-tuple-element.154.me_ref.refs_0_.refs_14_, bf16[8,64,2048]{2,1,0:T(8,128)(2,1)} %get-tuple-element.104.refs_1_, bf16[8,64,2048]{2,1,0:T(8,128)(2,1)} %collective-permute-done.5.refs_2_, bf16[1536,256]{1,0:T(8,128)(2,1)} %get-tuple-element.94.refs_3_), custom_call_target="tpu_custom_call" | custom-call | flops 131072 | bytes 393216 | tf_op jit(solution)/shard_map/add_parts/pallas_call | solution.py:749
  140.9 1.2 collective-permute-start.8
  142.0 4.1 %weight_once.2 = (bf16[8,64,512]{2,1,0:T(8,128)(2,1)}, bf16[8,64,512]{2,1,0:T(8,128)(2,1)}, bf16[8,64,512]{2,1,0:T(8,128)(2,1)}, bf16[8,64,512]{2,1,0:T(8,128)(2,1)}, s32[2]{0:T(128)}) custom-call(s32[2]{0:T(128)} %get-tuple-element.154.me_ref.refs_0_.refs_14_, bf16[1024,256]{1,0:T(8,128)(2,1)} %get-tuple-element.85.refs_10_.refs_0_, ...), custom_call_target="tpu_custom_call" | custom-call | flops 114688 | bytes 344064 | tf_op jit(solution)/shard_map/weight_once/pallas_call | solution.py:749
  146.2 1.1 all-to-all-done.1.refs_1_
  147.3 1.0 copy-done.5
  148.2 4.0 %regroup_once.3 = (bf16[256,1024]{1,0:T(8,128)(2,1)}, bf16[256,1024]{1,0:T(8,128)(2,1)}, bf16[256,1024]{1,0:T(8,128)(2,1)}, bf16[256,1024]{1,0:T(8,128)(2,1)}) custom-call(s32[2]{0:T(128)} %get-tuple-element.154.me_ref.refs_0_.refs_14_, bf16[16,256,128]{2,1,0:T(8,128)(2,1)} %copy-done.5, f32[3,256,128]{2,1,0:T(8,128)} %get-tuple-element.91.refs_2_, ...), custom_call_target="tpu_custom_call" | custom-call | flops 38912 | bytes 116736 | tf_op jit(solution)/shard_map/regroup_once/pallas_call | solution.py:749
  152.2 3.2 %collective-permute-start.10 = (bf16[256,1024]{1,0:T(8,128)(2,1)}, bf16[256,1024]{1,0:T(8,128)(2,1)S(1)}, u32[]{:S(2)}, u32[]{:S(2)}) collective-permute-start(bf16[256,1024]{1,0:T(8,128)(2,1)} %get-tuple-element.111), channel_id=1, source_target_pairs={{0,1},{1,0},{2,3},{3,2},{4,5},{5,4},{6,7},{7,6},{8,9},{9,8},{10,11... | collective-permute-start | bytes 1572872 | tf_op jit(solution)/shard_map/ppermute | solution.py:1108
  155.4 1.7 collective-permute-done.10.refs_3_
  157.2 0.8 copy-done.14
  158.0 5.4 %weight_once.3 = (bf16[8,64,1024]{2,1,0:T(8,128)(2,1)}, bf16[8,64,1024]{2,1,0:T(8,128)(2,1)}, bf16[8,64,1024]{2,1,0:T(8,128)(2,1)}, bf16[8,64,1024]{2,1,0:T(8,128)(2,1)}, s32[2]{0:T(128)}) custom-call(s32[2]{0:T(128)} %get-tuple-element.154.me_ref.refs_0_.refs_14_, bf16[1024,256]{1,0:T(8,128)(2,1)} %get-tuple-element.85.refs_10_.refs_0_, ...), custom_call_target="tpu_custom_call" | custom-call | flops 131072 | bytes 393216 | tf_op jit(solution)/shard_map/weight_once/pallas_call | solution.py:749
  163.4 1.7 collective-permute-start.13
  165.5 1.7 collective-permute-done.9.refs_4_
  167.1 1.4 collective-permute-done.8.refs_2_
  168.6 1.0 copy-done.11
  169.5 3.9 %add_parts.6 = (bf16[2,64,4096]{2,1,0:T(8,128)(2,1)}, bf16[2,64,4096]{2,1,0:T(8,128)(2,1)}) custom-call(s32[2]{0:T(128)} %get-tuple-element.154.me_ref.refs_0_.refs_14_, bf16[4,64,2048]{2,1,0:T(8,128)(2,1)} %get-tuple-element.105.refs_1_, bf16[4,64,2048]{2,1,0:T(8,128)(2,1)} %copy-done.11, bf16[4,64,2048]{2,1,0:T(8,128)(2,1)} %get-tuple-element.108.refs_3_, ...), custom_call_target="tpu_custom_call" | custom-call | flops 131072 | bytes 393216 | tf_op jit(solution)/shard_map/add_parts/pallas_call | solution.py:749
  173.4 1.3 collective-permute-start.11
  174.7 10.4 %close_layer.1 = (bf16[256,1024]{1,0:T(8,128)(2,1)}, f32[256,1024]{1,0:T(8,128)}, f32[5,1024]{1,0:T(8,128)}, f32[3,1024]{1,0:T(4,128)}, s32[2]{0:T(128)}) custom-call(bf16[256,1024]{1,0:T(8,128)(2,1)} %bitcast.56, bf16[256,1024]{1,0:T(8,128)(2,1)} %bitcast.53, bf16[1024]{0:T(1024)(128)(2,1)} %refs_2_.1, bf16[1024]{0:T(1024)(128)(2,1)} %refs_3_.1, ...), custom_call_target="tpu_custom_call" | custom-call | flops 134217728 | bytes 917504 | tf_op jit(solution)/shard_map/close_layer/pallas_call | solution.py:1055
  187.1 4.0 %collective-permute-done.13 = bf16[8,64,1024]{2,1,0:T(8,128)(2,1)} collective-permute-done((bf16[8,64,1024]{2,1,0:T(8,128)(2,1)}, bf16[8,64,1024]{2,1,0:T(8,128)(2,1)}, u32[]{:S(2)}, u32[]{:S(2)}) %collective-permute-start.13) | collective-permute-done | bytes 1048608 | tf_op jit(solution)/shard_map/ppermute | solution.py:767
  191.1 2.6 %add_convert_fusion.1 = (bf16[2,2,1,64,1024]{4,3,1,0,2:T(8,128)(2,1)}, bf16[2,2,1,64,1024]{4,3,1,0,2:T(8,128)(2,1)}) fusion(bf16[2,2,2,64,1024]{4,3,2,1,0:T(8,128)(2,1)} %bitcast.17, s32[]{:T(128)S(6)} %select_n.48, bf16[2,2,2,64,1024]{4,3,2,1,0:T(8,128)(2,1)S(1)} %bitcast.61, s32[]{:T(128)S(6)} %select_n.46), kind=kLoop, calls=%fused_computation.2 | loop fusion | flops 2097152 | bytes 3145736 | tf_op jit(solution)/shard_map/convert_element_type | solution.py:835
  193.9 1.4 add_convert_fusion.2
  195.3 0.7 collective-permute-start.15
  196.0 1.7 collective-permute-done.11
  197.6 1.2 add_convert_fusion.3
  198.8 0.9 collective-permute-start.21
  200.8 3.1 %collective-permute-start.14 = (f32[16,384]{1,0:T(8,128)S(1)}, f32[16,384]{1,0:T(8,128)S(1)}, u32[]{:S(2)}, u32[]{:S(2)}) collective-permute-start(f32[16,384]{1,0:T(8,128)S(1)} %bitcast.66), channel_id=1, source_target_pairs={{0,1},{1,0},{2,3},{3,2},{4,5},{5,4},{6,7},{7,6},{8,9},{9,8},{10,11... | collective-permute-start | bytes 73736 | tf_op jit(solution)/shard_map/ppermute | solution.py:1108
  203.9 0.8 collective-permute-done.14
  204.8 2.2 collective-permute-done.16.refs_3_
  206.9 1.1 collective-permute-done.15.refs_1_
  208.0 0.8 copy-done.12
  208.8 2.7 %add_parts.7 = (bf16[1,64,2048]{2,1,0:T(8,128)(2,1)}, bf16[1,64,2048]{2,1,0:T(8,128)(2,1)}, bf16[1,64,2048]{2,1,0:T(8,128)(2,1)}, bf16[1,64,2048]{2,1,0:T(8,128)(2,1)}) custom-call(s32[2]{0:T(128)} %get-tuple-element.154.me_ref.refs_0_.refs_14_, bf16[4,64,1024]{2,1,0:T(8,128)(2,1)} %bitcast.59, bf16[4,64,1024]{2,1,0:T(8,128)(2,1)} %copy-done.12, ...), custom_call_target="tpu_custom_call" | custom-call | flops 65536 | bytes 196608 | tf_op jit(solution)/shard_map/add_parts/pallas_call | solution.py:749
  211.4 1.4 collective-permute-start.17
  212.8 2.1 collective-permute-start.18
  215.0 0.6 all_to_all.20
  215.6 6.0 %all-to-all-start.3 = ((f32[16,1,384]{2,1,0:T(1,128)}), f32[16,1,384]{2,1,0:T(1,128)S(1)}, u32[]{:S(2)}, u32[]{:S(2)}) async-start(f32[16,1,384]{2,1,0:T(1,128)} %all_to_all.20), calls=%async_computation.3 | async-start | bytes 49152 | tf_op jit(solution)/shard_map/all_to_all | solution.py:1322
  221.6 14.0 %collective-permute-done.21 = bf16[1,64,4096]{2,1,0:T(8,128)(2,1)S(1)} collective-permute-done((bf16[1,64,4096]{2,1,0:T(8,128)(2,1)S(1)}, bf16[1,64,4096]{2,1,0:T(8,128)(2,1)S(1)}, u32[]{:S(2)}, u32[]{:S(2)}) %collective-permute-start.21) | collective-permute-done | bytes 524320 | tf_op jit(solution)/shard_map/ppermute | solution.py:767
  235.6 1.2 add_bitcast_fusion
  236.9 1.0 slice_bitcast_fusion
  237.9 10.3 %all-to-all-done.3 = f32[16,1,384]{2,1,0:T(1,128)S(1)} async-done(((f32[16,1,384]{2,1,0:T(1,128)}), f32[16,1,384]{2,1,0:T(1,128)S(1)}, u32[]{:S(2)}, u32[]{:S(2)}) %all-to-all-start.3) | async-done | bytes 24608 | tf_op jit(solution)/shard_map/all_to_all | solution.py:1322
  248.3 0.7 copy-done.15
  249.1 2.1 last_sum.1
  251.2 1.2 collective-permute-start.20
  254.0 0.7 copy-done.18
  254.7 1.8 place.1
  (83 shorter events, 7.0 us)
Async XLA Ops:
  9.8 8.7 %copy-start = (bf16[1,256,1024]{2,1,0:T(8,128)(2,1)S(1)}, bf16[1,256,1024]{2,1,0:T(8,128)(2,1)}, u32[]{:S(2)}) copy-start(bf16[1,256,1024]{2,1,0:T(8,128)(2,1)} %param.15) | copy-start | bytes 1572868
  9.8 8.8 %copy-start.2 = (bf16[2048,256]{1,0:T(8,128)(2,1)S(1)}, bf16[2048,256]{1,0:T(8,128)(2,1)}, u32[]{:S(2)}) copy-start(bf16[2048,256]{1,0:T(8,128)(2,1)} %get-tuple-element.76.refs_0_.refs_8_) | copy-start | bytes 3145732
  9.8 9.2 %copy-start.22 = (bf16[2048]{0:T(1024)(128)(2,1)S(1)}, bf16[2048]{0:T(1024)(128)(2,1)}, u32[]{:S(2)}) copy-start(bf16[2048]{0:T(1024)(128)(2,1)} %param.25) | copy-start | bytes 12292
  9.8 49.1 %all-to-all-start = ((bf16[16,512,128]{2,1,0:T(8,128)(2,1)}), bf16[16,512,128]{2,1,0:T(8,128)(2,1)}, u32[]{:S(2)}, u32[]{:S(2)}) async-start(bf16[16,512,128]{2,1,0:T(8,128)(2,1)} %bitcast.57), calls=%async_computation | async-start | bytes 4194304 | tf_op jit(solution)/shard_map/all_to_all | solution.py:1158
  17.5 2.8 %collective-permute-start.1 = (bf16[256,1024]{1,0:T(8,128)(2,1)}, bf16[256,1024]{1,0:T(8,128)(2,1)S(1)}, u32[]{:S(2)}, u32[]{:S(2)}) collective-permute-start(bf16[256,1024]{1,0:T(8,128)(2,1)} %get-tuple-element.77.refs_0_), channel_id=1, source_target_pairs={{0,1},{1,0},{2,3},{3,2},{4,5},{5,4},{6,7},{7,6},{8,9},{9,8},{10,11... | collective-permute-start | bytes 1572872 | tf_op jit(solution)/shard_map/ppermute | solution.py:1108
  18.5 2.3 collective-permute-start.2
  18.6 21.5 %collective-permute-start = (bf16[2048,256]{1,0:T(8,128)(2,1)S(1)}, bf16[2048,256]{1,0:T(8,128)(2,1)S(1)}, u32[]{:S(2)}, u32[]{:S(2)}) collective-permute-start(bf16[2048,256]{1,0:T(8,128)(2,1)S(1)} %copy-done.2), channel_id=1, source_target_pairs={{0,1},{1,0},{2,3},{3,2},{4,5},{5,4},{6,7},{7,6},{8,9},{9,8},{10,11... | collective-permute-start | bytes 3145736 | tf_op jit(solution)/shard_map/ppermute | solution.py:1108
  20.2 0.8 copy-start.13
  20.8 0.8 copy-start.6
  38.8 17.6 %collective-permute-start.3 = (bf16[512,1024]{1,0:T(8,128)(2,1)}, bf16[512,1024]{1,0:T(8,128)(2,1)S(1)}, u32[]{:S(2)}, u32[]{:S(2)}) collective-permute-start(bf16[512,1024]{1,0:T(8,128)(2,1)} %get-tuple-element.83), channel_id=1, source_target_pairs={{0,1},{1,0},{2,3},{3,2},{4,5},{5,4},{6,7},{7,6},{8,9},{9,8},{10,11... | collective-permute-start | bytes 3145736 | tf_op jit(solution)/shard_map/ppermute | solution.py:1108
  39.3 17.2 %collective-permute-start.4 = (bf16[1024,256]{1,0:T(8,128)(2,1)}, bf16[1024,256]{1,0:T(8,128)(2,1)}, u32[]{:S(2)}, u32[]{:S(2)}) collective-permute-start(bf16[1024,256]{1,0:T(8,128)(2,1)} %get-tuple-element.85.refs_10_.refs_0_), channel_id=1, source_target_pairs={{0,1},{1,0},{2,3},{3,2},{4,5},{5,4},{6,7},{7,6},{8,9},{9,8},{10,11... | collective-permute-start | bytes 1572872 | tf_op jit(solution)/shard_map/ppermute | solution.py:1108
  40.1 1.0 copy-start.3
  47.4 71.3 %collective-permute-start.6 = (bf16[8,64,2048]{2,1,0:T(8,128)(2,1)}, bf16[8,64,2048]{2,1,0:T(8,128)(2,1)}, u32[]{:S(2)}, u32[]{:S(2)}) collective-permute-start(bf16[8,64,2048]{2,1,0:T(8,128)(2,1)} %get-tuple-element.81.refs_3_), channel_id=1, source_target_pairs={{0,4},{2,6},{4,0},{6,2},{8,12},{10,14},{12,8},{14,10},{16,20},{18,... | collective-permute-start | bytes 6291464 | tf_op jit(solution)/shard_map/ppermute | solution.py:767
  55.3 63.5 %collective-permute-start.5 = (bf16[8,64,2048]{2,1,0:T(8,128)(2,1)}, bf16[8,64,2048]{2,1,0:T(8,128)(2,1)}, u32[]{:S(2)}, u32[]{:S(2)}) collective-permute-start(bf16[8,64,2048]{2,1,0:T(8,128)(2,1)} %get-tuple-element.79.refs_2_), channel_id=1, source_target_pairs={{0,2},{2,0},{4,6},{6,4},{8,10},{10,8},{12,14},{14,12},{16,18},{18,... | collective-permute-start | bytes 6291464 | tf_op jit(solution)/shard_map/ppermute | solution.py:767
  56.5 2.5 copy-start.1
  85.4 33.4 %all-to-all-start.2 = ((bf16[16,256,128]{2,1,0:T(8,128)(2,1)}), bf16[16,256,128]{2,1,0:T(8,128)(2,1)S(1)}, u32[]{:S(2)}, u32[]{:S(2)}) async-start(bf16[16,256,128]{2,1,0:T(8,128)(2,1)} %get-tuple-element.92), calls=%async_computation.2 | async-start | bytes 2097152 | tf_op jit(solution)/shard_map/all_to_all | solution.py:1207
  118.8 6.4 %copy-start.4 = (bf16[16,256,128]{2,1,0:T(8,128)(2,1)}, bf16[16,256,128]{2,1,0:T(8,128)(2,1)S(1)}, u32[]{:S(2)}) copy-start(bf16[16,256,128]{2,1,0:T(8,128)(2,1)S(1)} %all-to-all-done.2.refs_1_) | copy-start | bytes 3145732
  118.8 28.5 %all-to-all-start.1 = ((bf16[16,256,128]{2,1,0:T(8,128)(2,1)}), bf16[16,256,128]{2,1,0:T(8,128)(2,1)S(1)}, u32[]{:S(2)}, u32[]{:S(2)}) async-start(bf16[16,256,128]{2,1,0:T(8,128)(2,1)} %get-tuple-element.90.refs_2_), calls=%async_computation.1 | async-start | bytes 2097152 | tf_op jit(solution)/shard_map/all_to_all | solution.py:1212
  128.8 13.2 %collective-permute-start.7 = (bf16[1536,256]{1,0:T(8,128)(2,1)}, bf16[1536,256]{1,0:T(8,128)(2,1)}, u32[]{:S(2)}, u32[]{:S(2)}) collective-permute-start(bf16[1536,256]{1,0:T(8,128)(2,1)} %get-tuple-element.94.refs_3_), channel_id=1, source_target_pairs={{0,1},{1,0},{2,3},{3,2},{4,5},{5,4},{6,7},{7,6},{8,9},{9,8},{10,11... | collective-permute-start | bytes 2359304 | tf_op jit(solution)/shard_map/ppermute | solution.py:1108
  135.2 31.9 %collective-permute-start.9 = (bf16[4,64,2048]{2,1,0:T(8,128)(2,1)}, bf16[4,64,2048]{2,1,0:T(8,128)(2,1)S(1)}, u32[]{:S(2)}, u32[]{:S(2)}) collective-permute-start(bf16[4,64,2048]{2,1,0:T(8,128)(2,1)} %get-tuple-element.109), channel_id=1, source_target_pairs={{0,2},{2,0},{4,6},{6,4},{8,10},{10,8},{12,14},{14,12},{16,18},{18,... | collective-permute-start | bytes 3145736 | tf_op jit(solution)/shard_map/ppermute | solution.py:767
  140.9 27.7 %collective-permute-start.8 = (bf16[4,64,2048]{2,1,0:T(8,128)(2,1)}, bf16[4,64,2048]{2,1,0:T(8,128)(2,1)S(1)}, u32[]{:S(2)}, u32[]{:S(2)}) collective-permute-start(bf16[4,64,2048]{2,1,0:T(8,128)(2,1)} %get-tuple-element.106), channel_id=1, source_target_pairs={{0,4},{2,6},{4,0},{6,2},{8,12},{10,14},{12,8},{14,10},{16,20},{18,... | collective-permute-start | bytes 3145736 | tf_op jit(solution)/shard_map/ppermute | solution.py:767
  147.3 1.0 copy-start.5
  152.2 5.0 %collective-permute-start.10 = (bf16[256,1024]{1,0:T(8,128)(2,1)}, bf16[256,1024]{1,0:T(8,128)(2,1)S(1)}, u32[]{:S(2)}, u32[]{:S(2)}) collective-permute-start(bf16[256,1024]{1,0:T(8,128)(2,1)} %get-tuple-element.111), channel_id=1, source_target_pairs={{0,1},{1,0},{2,3},{3,2},{4,5},{5,4},{6,7},{7,6},{8,9},{9,8},{10,11... | collective-permute-start | bytes 1572872 | tf_op jit(solution)/shard_map/ppermute | solution.py:1108
  157.2 0.8 copy-start.14
  163.4 27.7 %collective-permute-start.13 = (bf16[8,64,1024]{2,1,0:T(8,128)(2,1)}, bf16[8,64,1024]{2,1,0:T(8,128)(2,1)}, u32[]{:S(2)}, u32[]{:S(2)}) collective-permute-start(bf16[8,64,1024]{2,1,0:T(8,128)(2,1)} %get-tuple-element.112.refs_5_), channel_id=1, source_target_pairs={{0,4},{2,6},{4,0},{6,2},{8,12},{10,14},{12,8},{14,10},{16,20},{18,... | collective-permute-start | bytes 3145736 | tf_op jit(solution)/shard_map/ppermute | solution.py:767
  165.2 28.6 %collective-permute-start.12 = (bf16[8,64,1024]{2,1,0:T(8,128)(2,1)}, bf16[8,64,1024]{2,1,0:T(8,128)(2,1)S(1)}, u32[]{:S(2)}, u32[]{:S(2)}) collective-permute-start(bf16[8,64,1024]{2,1,0:T(8,128)(2,1)} %get-tuple-element.122), channel_id=1, source_target_pairs={{0,2},{2,0},{4,6},{6,4},{8,10},{10,8},{12,14},{14,12},{16,18},{18,... | collective-permute-start | bytes 3145736 | tf_op jit(solution)/shard_map/ppermute | solution.py:767
  167.1 1.4 copy-start.10
  168.5 1.0 copy-start.11
  173.4 24.2 %collective-permute-start.11 = (bf16[2,64,4096]{2,1,0:T(8,128)(2,1)}, bf16[2,64,4096]{2,1,0:T(8,128)(2,1)}, u32[]{:S(2)}, u32[]{:S(2)}) collective-permute-start(bf16[2,64,4096]{2,1,0:T(8,128)(2,1)} %get-tuple-element.113.refs_19_), channel_id=1, source_target_pairs={{0,8},{2,10},{4,12},{6,14},{8,0},{10,2},{12,4},{14,6},{16,24},{18,... | collective-permute-start | bytes 3145736 | tf_op jit(solution)/shard_map/ppermute | solution.py:767
  174.7 16.4 %copy-start.8 = (bf16[8,64,1024]{2,1,0:T(8,128)(2,1)S(1)}, bf16[8,64,1024]{2,1,0:T(8,128)(2,1)}, u32[]{:S(2)}) copy-start(bf16[8,64,1024]{2,1,0:T(8,128)(2,1)} %get-tuple-element.123) | copy-start | bytes 3145732
  185.1 8.8 %copy-start.7 = (bf16[8,64,1024]{2,1,0:T(8,128)(2,1)S(1)}, bf16[8,64,1024]{2,1,0:T(8,128)(2,1)}, u32[]{:S(2)}) copy-start(bf16[8,64,1024]{2,1,0:T(8,128)(2,1)} %get-tuple-element.121) | copy-start | bytes 3145732
  193.7 3.9 %copy-start.9 = (bf16[2,64,4096]{2,1,0:T(8,128)(2,1)S(1)}, bf16[2,64,4096]{2,1,0:T(8,128)(2,1)}, u32[]{:S(2)}) copy-start(bf16[2,64,4096]{2,1,0:T(8,128)(2,1)} %get-tuple-element.119) | copy-start | bytes 3145732
  193.7 13.2 %collective-permute-start.16 = (bf16[4,64,1024]{2,1,0:T(8,128)(2,1)}, bf16[4,64,1024]{2,1,0:T(8,128)(2,1)}, u32[]{:S(2)}, u32[]{:S(2)}) collective-permute-start(bf16[4,64,1024]{2,1,0:T(8,128)(2,1)} %bitcast.18), channel_id=1, source_target_pairs={{0,2},{2,0},{4,6},{6,4},{8,10},{10,8},{12,14},{14,12},{16,18},{18,... | collective-permute-start | bytes 1572872 | tf_op jit(solution)/shard_map/ppermute | solution.py:767
  193.8 5.9 %copy-start.21 = (f32[1,2048]{1,0:T(1,128)S(1)}, f32[1,2048]{1,0:T(1,128)}, u32[]{:S(2)}) copy-start(f32[1,2048]{1,0:T(1,128)} %get-tuple-element.118) | copy-start | bytes 24580
  193.8 6.1 %copy-start.20 = (f32[5,1024]{1,0:T(8,128)S(1)}, f32[5,1024]{1,0:T(8,128)}, u32[]{:S(2)}) copy-start(f32[5,1024]{1,0:T(8,128)} %get-tuple-element.116) | copy-start | bytes 61444
  193.8 6.6 %copy-start.19 = (f32[3,1024]{1,0:T(4,128)S(1)}, f32[3,1024]{1,0:T(4,128)}, u32[]{:S(2)}) copy-start(f32[3,1024]{1,0:T(4,128)} %get-tuple-element.117) | copy-start | bytes 36868
  195.3 12.7 %collective-permute-start.15 = (bf16[4,64,1024]{2,1,0:T(8,128)(2,1)}, bf16[4,64,1024]{2,1,0:T(8,128)(2,1)S(1)}, u32[]{:S(2)}, u32[]{:S(2)}) collective-permute-start(bf16[4,64,1024]{2,1,0:T(8,128)(2,1)} %bitcast.14), channel_id=1, source_target_pairs={{0,4},{2,6},{4,0},{6,2},{8,12},{10,14},{12,8},{14,10},{16,20},{18,... | collective-permute-start | bytes 1572872 | tf_op jit(solution)/shard_map/ppermute | solution.py:767
  198.8 36.8 %collective-permute-start.21 = (bf16[1,64,4096]{2,1,0:T(8,128)(2,1)S(1)}, bf16[1,64,4096]{2,1,0:T(8,128)(2,1)S(1)}, u32[]{:S(2)}, u32[]{:S(2)}) collective-permute-start(bf16[1,64,4096]{2,1,0:T(8,128)(2,1)S(1)} %add_convert_fusion.3), channel_id=1, source_target_pairs={{0,16},{2,18},{4,20},{6,22},{8,24},{10,26},{12,28},{14,30},{16,0},... | collective-permute-start | bytes 1572872 | tf_op jit(solution)/shard_map/ppermute | solution.py:767
  200.8 4.0 %collective-permute-start.14 = (f32[16,384]{1,0:T(8,128)S(1)}, f32[16,384]{1,0:T(8,128)S(1)}, u32[]{:S(2)}, u32[]{:S(2)}) collective-permute-start(f32[16,384]{1,0:T(8,128)S(1)} %bitcast.66), channel_id=1, source_target_pairs={{0,1},{1,0},{2,3},{3,2},{4,5},{5,4},{6,7},{7,6},{8,9},{9,8},{10,11... | collective-permute-start | bytes 73736 | tf_op jit(solution)/shard_map/ppermute | solution.py:1108
  208.0 0.8 copy-start.12
  211.4 36.8 %collective-permute-start.17 = (bf16[1,64,2048]{2,1,0:T(8,128)(2,1)}, bf16[1,64,2048]{2,1,0:T(8,128)(2,1)S(1)}, u32[]{:S(2)}, u32[]{:S(2)}) collective-permute-start(bf16[1,64,2048]{2,1,0:T(8,128)(2,1)} %get-tuple-element.126), channel_id=1, source_target_pairs={{0,8},{2,10},{4,12},{6,14},{8,0},{10,2},{12,4},{14,6},{16,24},{18,... | collective-permute-start | bytes 786440 | tf_op jit(solution)/shard_map/ppermute | solution.py:767
  212.8 35.4 %collective-permute-start.18 = (bf16[1,64,2048]{2,1,0:T(8,128)(2,1)}, bf16[1,64,2048]{2,1,0:T(8,128)(2,1)S(1)}, u32[]{:S(2)}, u32[]{:S(2)}) collective-permute-start(bf16[1,64,2048]{2,1,0:T(8,128)(2,1)} %get-tuple-element.127), channel_id=1, source_target_pairs={{0,16},{2,18},{4,20},{6,22},{8,24},{10,26},{12,28},{14,30},{16,0},... | collective-permute-start | bytes 786440 | tf_op jit(solution)/shard_map/ppermute | solution.py:767
  214.9 33.3 %collective-permute-start.19 = (bf16[1,64,2048]{2,1,0:T(8,128)(2,1)}, bf16[1,64,2048]{2,1,0:T(8,128)(2,1)S(1)}, u32[]{:S(2)}, u32[]{:S(2)}) collective-permute-start(bf16[1,64,2048]{2,1,0:T(8,128)(2,1)} %get-tuple-element.128), channel_id=1, source_target_pairs={{0,24},{2,26},{4,28},{6,30},{8,16},{10,18},{12,20},{14,22},{16,8},... | collective-permute-start | bytes 786440 | tf_op jit(solution)/shard_map/ppermute | solution.py:767
  215.6 32.6 %all-to-all-start.3 = ((f32[16,1,384]{2,1,0:T(1,128)}), f32[16,1,384]{2,1,0:T(1,128)S(1)}, u32[]{:S(2)}, u32[]{:S(2)}) async-start(f32[16,1,384]{2,1,0:T(1,128)} %all_to_all.20), calls=%async_computation.3 | async-start | bytes 49152 | tf_op jit(solution)/shard_map/all_to_all | solution.py:1322
  248.2 0.7 copy-start.15
  248.2 0.8 copy-start.16
  248.2 0.8 copy-start.17
  251.2 2.9 %collective-permute-start.20 = (bf16[32,2048]{1,0:T(8,128)(2,1)}, bf16[32,2048]{1,0:T(8,128)(2,1)S(1)}, u32[]{:S(2)}, u32[]{:S(2)}) collective-permute-start(bf16[32,2048]{1,0:T(8,128)(2,1)} %get-tuple-element.131), channel_id=1, source_target_pairs={{0,1},{1,0},{2,3},{3,2},{4,5},{5,4},{6,7},{7,6},{8,9},{9,8},{10,11... | collective-permute-start | bytes 393224 | tf_op jit(solution)/shard_map/ppermute | solution.py:1108
  254.0 3.0 %copy-start.23 = (f32[32]{0:T(128)}, f32[32]{0:T(128)S(1)}, u32[]{:S(2)}) copy-start(f32[32]{0:T(128)S(1)} %get-tuple-element.183) | copy-start | bytes 388
  254.0 0.7 copy-start.18
